TPU v7x, 256 devices: a whole 4x4x8 slice. The times are simulated.
256 devices in a mesh: dp: 64 (over y, z, core), tp: 4 (over x).
Axes of the slice: x: 4, y: 4, z: 8, core: 2. Of those that a mesh axis runs over, the one named last changes fastest.
Arguments:
- hidden: bfloat16 [128, 4096], P('dp'), may hold values from -6 to 6
- attention_norm_gain: bfloat16 [4096], replicated, may hold values from 0.5 to 1.5
- query_key_value_weight: bfloat16 [4096, 4, 1280], P('dp', 'tp'), may hold values from -0.09375 to 0.09375
- key_value_cache: bfloat16 [128, 2048, 4, 256], P('dp', None, 'tp'), may hold values from -6 to 6
- cache_fill_lengths: int32 [128], P('dp'), may hold values from 2 to 2048
- output_weight_frozen: bfloat16 [4, 1024, 4096], P('tp', None, 'dp'), may hold values from -0.09375 to 0.09375
- adapter_down_transposed: bfloat16 [64, 4, 1024], P(None, 'tp', 'dp'), may hold values from -0.09375 to 0.09375
- adapter_up_matrix: bfloat16 [64, 4, 1024], P(None, 'tp', 'dp'), may hold values from -0.75 to 0.75
- attention_rows: bfloat16 [32768, 4096], P('dp', 'tp'), may hold values from -6 to 6
- upstream: bfloat16 [32768, 4096], P('dp', 'tp'), may hold values from -6 to 6
- rewards: float32 [128], P('dp'), may hold values from 0 to 2
- prompt_group_index: int32 [128], P('dp'), may hold values from 0 to 31, as said below
- completion_live_lengths: int32 [128], P('dp'), may hold values from 1 to 256
Outputs:
- decoded: float32 [128, 4096], P('dp')
- adapted_output_rows: float32 [32768, 4096], P('dp', 'tp')
- grad_lora_a_t: float32 [64, 4, 1024], P(None, 'tp', 'dp')
- grad_lora_b: float32 [64, 4, 1024], P(None, 'tp', 'dp')
Inputs may be any that keep to these rules, and one draw needn't show every extreme that they name: `prompt_group_index`: each prompt holds exactly 4 rollouts.
All inputs are finite; a program needn't handle non-finite values.
Results may differ from a plain program's by a relative error of at most 0.0041.
Values may be sent and summed in bfloat16 or wider, within the bound.
No kernel may reach another device: no remote copies, remote signals or barrier semaphores. Data moves between devices by JAX's collectives and lax.ppermute only.
A program may use at most 128 MiB of HBM per device.

v0:
```python
import math

import jax
import jax.numpy as jnp
from jax import lax
from jax.sharding import PartitionSpec as P

HD = 128
HEADS_TP = 8
GROUP = 4
COMP = 256


adapter_scale = 2.0


def turned_gather(arrays, axis, dims):
    turned = [jnp.moveaxis(a, dim, 0) for a, dim in zip(arrays, dims)]
    both = jnp.concatenate([t.reshape(len(t), -1) for t in turned], axis=1)
    out, at, finished = (lax.all_gather(both, axis, axis=0, tiled=True), 0, [])
    for t, dim in zip(turned, dims):
        slab = out[:, at : at + t[0].size].reshape(-1, *t.shape[1:])
        finished.append(jnp.moveaxis(slab, 0, dim))
        at += t[0].size
    return tuple(finished)


def laid_out(tiles, dim):
    shape = list(tiles.shape[1:])
    shape[dim] *= tiles.shape[0]
    return jnp.moveaxis(tiles, 0, dim).reshape(shape)


def sent_to_all(array, axis):
    copies = jnp.broadcast_to(array, (lax.axis_size(axis), *array.shape))
    return lax.all_to_all(copies, axis, split_axis=0, concat_axis=0, tiled=True)


def collect(array, axis, dim):
    return laid_out(sent_to_all(array, axis), dim)


def cut_along(array, dim, count):
    shape = array.shape
    tiles = array.reshape(*shape[:dim], count, shape[dim] // count, *shape[dim + 1 :])
    return jnp.moveaxis(tiles, dim, 0)


def sent_and_summed(array, axis, dim):
    tiles = cut_along(array, dim, lax.axis_size(axis))
    arrived = lax.all_to_all(tiles, axis, split_axis=0, concat_axis=0, tiled=True)
    return arrived.sum(axis=0)


def of_everyone(array, axis):
    return sent_to_all(array, axis).sum(axis=0)


def in_one(arrays, axis):
    ends = [0]
    for a in arrays:
        ends.append(ends[-1] + a.size)
    so_far = of_everyone(jnp.concatenate([a.ravel() for a in arrays]), axis)
    return tuple((so_far[b:e].reshape(a.shape) for a, b, e in zip(arrays, ends, ends[1:])))


def sent_together(arrays, axis, dim, along):
    both = jnp.concatenate(arrays, axis=along)
    out, at, finished = (sent_and_summed(both, axis, dim), 0, [])
    for a in arrays:
        finished.append(lax.slice_in_dim(out, at, at + a.shape[along], axis=along))
        at += a.shape[along]
    return tuple(finished)


def rms_norm(decode_state, gain):
    scale = lax.rsqrt(jnp.mean(decode_state * decode_state, axis=-1, keepdims=True) + 1e-05)
    return decode_state * scale * gain.astype(jnp.float32)


def attend(query, cache, lengths, new_keys, new_values):
    head = query.shape[-1]
    slots = cache.shape[1]
    factor = 1.0 / math.sqrt(head)
    keys = cache[:, :, :head].astype(jnp.float32)
    values = cache[:, :, head:]
    scores = jnp.einsum("bhd,bcd->bhc", query, keys, precision=lax.Precision.HIGHEST) * factor
    valid = jnp.arange(slots, dtype=jnp.int32)[None, None, :] < lengths[:, None, None]
    scores = jnp.where(valid, scores, -1e30)
    extra = jnp.einsum("bhd,bed->bhe", query, new_keys, precision=lax.Precision.HIGHEST) * factor
    joined = jnp.concatenate([scores, extra], axis=-1)
    top = jnp.max(joined, axis=-1, keepdims=True)
    expo = jnp.exp(joined - top)
    probs = (expo / jnp.sum(expo, axis=-1, keepdims=True)).astype(jnp.bfloat16)
    out = jnp.einsum("bhc,bcd->bhd", probs[..., :slots], values, preferred_element_type=jnp.float32)
    out = out + jnp.einsum(
        "bhe,bed->bhd",
        probs[..., slots:].astype(jnp.float32),
        new_values,
        precision=lax.Precision.HIGHEST,
    )
    return out.astype(jnp.bfloat16).reshape(query.shape[0], -1)


def shards(
    hidden,
    attention_norm_gain,
    query_key_value_weight,
    key_value_cache,
    cache_fill_lengths,
    output_weight_frozen,
    adapter_down_transposed,
    adapter_up_matrix,
    attention_rows,
    upstream,
    rewards,
    prompt_group_index,
    completion_live_lengths,
):
    a_piece, b_piece = turned_gather((adapter_down_transposed, adapter_up_matrix), "dp", (2, 2))
    b_whole = collect(b_piece, "tp", 1)
    up_matrix_flat = b_whole.reshape(b_whole.shape[0], -1).astype(jnp.float32)
    a_local = a_piece[:, 0, :]
    up_matrix_columns = b_piece[:, 0, :]
    w_rows = query_key_value_weight[:, 0, :].astype(jnp.float32)
    w_cols = output_weight_frozen[0]
    query_width = HEADS_TP * HD
    local_rolls = hidden.shape[0]
    decode_state = hidden.astype(jnp.float32)
    keys_new = []
    values_new = []
    for step in range(2):
        normed = rms_norm(decode_state, attention_norm_gain)
        spread = lax.all_to_all(normed, "dp", split_axis=1, concat_axis=0, tiled=True)
        partial_value = jnp.dot(spread, w_rows, precision=lax.Precision.HIGHEST)
        qkv = sent_and_summed(partial_value, "dp", 0)
        query = qkv[:, :query_width].reshape(local_rolls, HEADS_TP, HD)
        keys_new.append(qkv[:, query_width : query_width + HD])
        values_new.append(qkv[:, query_width + HD :])
        attended = attend(
            query,
            key_value_cache[:, :, 0, :],
            cache_fill_lengths,
            jnp.stack(keys_new, axis=1),
            jnp.stack(values_new, axis=1),
        )
        columns = jnp.dot(collect(attended, "dp", 0), w_cols, preferred_element_type=jnp.float32)
        returned_values = lax.all_to_all(columns, "dp", split_axis=0, concat_axis=1, tiled=True)
        low_rank_decode = jnp.dot(attended, a_local.T, preferred_element_type=jnp.float32)
        state_update = returned_values + adapter_scale * jnp.dot(
            low_rank_decode, up_matrix_flat, precision=lax.Precision.HIGHEST
        )
        decode_state = decode_state + of_everyone(state_update, "tp")
    groups = local_rolls * lax.axis_size("dp") // GROUP
    onehot = (prompt_group_index[:, None] == jnp.arange(groups, dtype=jnp.int32)[None, :]).astype(
        jnp.float32
    )
    totals, squares = in_one(
        (
            jnp.sum(onehot * rewards[:, None], axis=0),
            jnp.sum(onehot * (rewards * rewards)[:, None], axis=0),
        ),
        "dp",
    )
    mean = totals / GROUP
    std = jnp.sqrt(jnp.maximum(squares / GROUP - mean * mean, 0.09))
    advantage = (rewards - jnp.sum(onehot * mean[None, :], axis=1)) / jnp.sum(
        onehot * std[None, :], axis=1
    )
    per_roll = advantage / completion_live_lengths.astype(jnp.float32)
    rows = attention_rows.shape[0]
    slot = jnp.arange(rows, dtype=jnp.int32) % COMP
    limit = jnp.repeat(completion_live_lengths, COMP)
    row_w = jnp.where(slot < limit, jnp.repeat(per_roll, COMP), 0.0)
    whole_rows = jnp.dot(
        attention_rows,
        lax.all_gather(output_weight_frozen, "dp", axis=2, tiled=True)[0],
        preferred_element_type=jnp.float32,
    )
    frozen_output_rows = lax.psum_scatter(whole_rows, "tp", scatter_dimension=1, tiled=True)
    low_sum = of_everyone(
        jnp.dot(attention_rows, a_local.T, preferred_element_type=jnp.float32), "tp"
    )
    low_rank_rows = low_sum.astype(jnp.bfloat16)
    adapted_output_rows = frozen_output_rows + adapter_scale * jnp.dot(
        low_rank_rows, up_matrix_columns, preferred_element_type=jnp.float32
    )
    advantage_weighted = (row_w[:, None] * upstream.astype(jnp.float32)).astype(jnp.bfloat16)
    backward_result = of_everyone(
        jnp.dot(advantage_weighted, up_matrix_columns.T, preferred_element_type=jnp.float32), "tp"
    ).astype(jnp.bfloat16)
    down_gradient = adapter_scale * lax.dot_general(
        backward_result,
        attention_rows,
        (((0,), (0,)), ((), ())),
        preferred_element_type=jnp.float32,
    )
    up_gradient = adapter_scale * lax.dot_general(
        low_rank_rows,
        advantage_weighted,
        (((0,), (0,)), ((), ())),
        preferred_element_type=jnp.float32,
    )
    grad_a_part, grad_b_part = sent_together(
        (down_gradient[:, None, :], up_gradient[:, None, :]), "dp", 2, 0
    )
    return (decode_state, adapted_output_rows, grad_a_part, grad_b_part)


def solution(mesh):
    placed = (
        P("dp", None),
        P(),
        P("dp", "tp", None),
        P("dp", None, "tp", None),
        P("dp"),
        P("tp", None, "dp"),
        P(None, "tp", "dp"),
        P(None, "tp", "dp"),
        P("dp", "tp"),
        P("dp", "tp"),
        P("dp"),
        P("dp"),
        P("dp"),
    )
    return jax.shard_map(
        shards,
        mesh=mesh,
        in_specs=placed,
        out_specs=(P("dp", None), P("dp", "tp"), P(None, "tp", "dp"), P(None, "tp", "dp")),
        check_vma=False,
    )
```

profile of v0, /device:TPU:8, one launch (start us, length us, event | category | flops | bytes accessed | tf_op | source)
XLA Modules:
  0.0 425.4 jit_solution(12396205886223945543)
XLA Ops:
  8.0 87.5 %all-gather.2.cloned.1.call-done = bf16[1,1024,4096]{1,2,0:T(8,128)(2,1)} async-done(((bf16[1,1024,64]{1,2,0:T(8,128)(2,1)}), bf16[1,1024,4096]{1,2,0:T(8,128)(2,1)}) %all-gather.2.cloned.1.call-update) | async-done | bytes 8388624 | tf_op jit(solution)/shard_map/all_gather | solution.py:177
  95.5 10.1 %fusion = f32[512,4096]{1,0:T(8,128)} fusion(bf16[512,1024]{1,0:T(8,128)(2,1)S(1)} %copy-done, bf16[1,1024,4096]{1,2,0:T(8,128)(2,1)} %all-gather.2.cloned.1.call-done), kind=kOutput, calls=%fused_computation | convolution fusion | flops 4294967296 | bytes 17825792 | tf_op jit(solution)/shard_map/dot_general | solution.py:175
  107.5 7.8 %all-to-all-start = ((f32[64,1,128]{2,1,0:T(1,128)}), f32[64,1,128]{2,1,0:T(1,128)S(1)}, u32[]{:S(2)}, u32[]{:S(2)}) async-start(f32[64,1,128]{2,1,0:T(1,128)} %reshape.178), calls=%async_computation | async-start | bytes 65536 | tf_op jit(solution)/shard_map/all_to_all | solution.py:134
  115.6 8.2 %all-to-all-done = f32[64,1,128]{2,1,0:T(1,128)S(1)} async-done(((f32[64,1,128]{2,1,0:T(1,128)}), f32[64,1,128]{2,1,0:T(1,128)S(1)}, u32[]{:S(2)}, u32[]{:S(2)}) %all-to-all-start) | async-done | bytes 32800 | tf_op jit(solution)/shard_map/all_to_all | solution.py:134
  124.5 5.5 %all-to-all-start.12 = ((f32[64,1,64]{2,1,0:T(1,128)}), f32[64,1,64]{2,1,0:T(1,128)S(1)}, u32[]{:S(2)}, u32[]{:S(2)}) async-start(f32[64,1,64]{2,1,0:T(1,128)} %broadcast_in_dim.80), calls=%async_computation.13 | async-start | bytes 65536 | tf_op jit(solution)/shard_map/all_to_all | solution.py:36
  133.0 5.4 %all-to-all-done.12 = f32[64,1,64]{2,1,0:T(1,128)S(1)} async-done(((f32[64,1,64]{2,1,0:T(1,128)}), f32[64,1,64]{2,1,0:T(1,128)S(1)}, u32[]{:S(2)}, u32[]{:S(2)}) %all-to-all-start.12) | async-done | bytes 16416 | tf_op jit(solution)/shard_map/all_to_all | solution.py:36
  138.5 6.3 %all-to-all-start.1 = ((f32[64,2,1280]{2,1,0:T(2,128)}), f32[64,2,1280]{2,1,0:T(2,128)}, u32[]{:S(2)}, u32[]{:S(2)}) async-start(f32[64,2,1280]{2,1,0:T(2,128)} %copy.121), calls=%async_computation.1 | async-start | bytes 1310720 | tf_op jit(solution)/shard_map/all_to_all | solution.py:51
  145.5 51.7 %all_gather.6 = bf16[1024,128]{1,0:T(8,128)(2,1)S(1)} all-gather(bf16[16,128]{1,0:T(8,128)(2,1)S(1)} %pad_maximum_fusion), channel_id=1, replica_groups=mesh['dp'=64,'tp'=4] {'dp'}, dimensions={0}, use_global_device_ids=true | all-gather | bytes 266240 | tf_op jit(solution)/shard_map/all_gather | solution.py:20
  205.1 4.2 all-to-all-start.4
  211.8 1.7 fusion.64
  219.6 1.5 broadcast_in_dim.73
  221.1 9.4 %all-to-all-start.2 = ((bf16[64,2,1024]{2,1,0:T(2,128)(2,1)}), bf16[64,2,1024]{2,1,0:T(2,128)(2,1)}, u32[]{:S(2)}, u32[]{:S(2)}) async-start(bf16[64,2,1024]{2,1,0:T(2,128)(2,1)} %broadcast_in_dim.73), calls=%async_computation.2 | async-start | bytes 524288 | tf_op jit(solution)/shard_map/all_to_all | solution.py:36
  232.7 1.4 copy.127
  235.1 6.8 %all-to-all-done.2 = bf16[64,2,1024]{2,1,0:T(2,128)(2,1)} async-done(((bf16[64,2,1024]{2,1,0:T(2,128)(2,1)}), bf16[64,2,1024]{2,1,0:T(2,128)(2,1)}, u32[]{:S(2)}, u32[]{:S(2)}) %all-to-all-start.2) | async-done | bytes 262176 | tf_op jit(solution)/shard_map/all_to_all | solution.py:36
  243.9 6.5 %all-to-all-start.3 = ((f32[64,1,128]{2,1,0:T(1,128)}), f32[64,1,128]{2,1,0:T(1,128)S(1)}, u32[]{:S(2)}, u32[]{:S(2)}) async-start(f32[64,1,128]{2,1,0:T(1,128)} %reshape.180), calls=%async_computation.3 | async-start | bytes 65536 | tf_op jit(solution)/shard_map/all_to_all | solution.py:148
  250.4 1.4 fusion.21
  251.8 7.1 %all-to-all-done.3 = f32[64,1,128]{2,1,0:T(1,128)S(1)} async-done(((f32[64,1,128]{2,1,0:T(1,128)}), f32[64,1,128]{2,1,0:T(1,128)S(1)}, u32[]{:S(2)}, u32[]{:S(2)}) %all-to-all-start.3) | async-done | bytes 32800 | tf_op jit(solution)/shard_map/all_to_all | solution.py:148
  259.8 1.4 fusion.3
  261.9 4.5 %all-to-all-start.5 = ((f32[4,2,4096]{2,1,0:T(2,128)}), f32[4,2,4096]{2,1,0:T(2,128)S(1)}, u32[]{:S(2)}, u32[]{:S(2)}) async-start(f32[4,2,4096]{2,1,0:T(2,128)} %broadcast_in_dim.75), calls=%async_computation.5 | async-start | bytes 262144 | tf_op jit(solution)/shard_map/all_to_all | solution.py:36
  267.7 4.7 %all-to-all-done.5 = f32[4,2,4096]{2,1,0:T(2,128)S(1)} async-done(((f32[4,2,4096]{2,1,0:T(2,128)}), f32[4,2,4096]{2,1,0:T(2,128)S(1)}, u32[]{:S(2)}, u32[]{:S(2)}) %all-to-all-start.5) | async-done | bytes 131104 | tf_op jit(solution)/shard_map/all_to_all | solution.py:36
  272.4 1.8 broadcast_in_dim.78
  274.2 4.1 all-to-all-start.11
  281.0 1.6 reshape.182
  282.6 4.1 all-to-all-done.11
  286.7 5.5 %all-to-all-start.6 = ((f32[64,1,128]{2,1,0:T(1,128)}), f32[64,1,128]{2,1,0:T(1,128)S(1)}, u32[]{:S(2)}, u32[]{:S(2)}) async-start(f32[64,1,128]{2,1,0:T(1,128)} %reshape.182), calls=%async_computation.6 | async-start | bytes 65536 | tf_op jit(solution)/shard_map/all_to_all | solution.py:134
  292.2 2.5 fusion.15
  294.7 6.1 %all-to-all-done.6 = f32[64,1,128]{2,1,0:T(1,128)S(1)} async-done(((f32[64,1,128]{2,1,0:T(1,128)}), f32[64,1,128]{2,1,0:T(1,128)S(1)}, u32[]{:S(2)}, u32[]{:S(2)}) %all-to-all-start.6) | async-done | bytes 32800 | tf_op jit(solution)/shard_map/all_to_all | solution.py:134
  300.7 1.8 broadcast_in_dim.83
  302.5 4.1 all-to-all-start.13
  310.1 6.4 %all-to-all-done.13 = f32[4,512,64]{1,2,0:T(8,128)} async-done(((f32[4,512,64]{1,2,0:T(8,128)}), f32[4,512,64]{1,2,0:T(8,128)}, u32[]{:S(2)}, u32[]{:S(2)}) %all-to-all-start.13) | async-done | bytes 524320 | tf_op jit(solution)/shard_map/all_to_all | solution.py:36
  316.5 6.3 %all-to-all-start.7 = ((f32[64,2,1280]{2,1,0:T(2,128)}), f32[64,2,1280]{2,1,0:T(2,128)}, u32[]{:S(2)}, u32[]{:S(2)}) async-start(f32[64,2,1280]{2,1,0:T(2,128)} %copy.131), calls=%async_computation.7 | async-start | bytes 1310720 | tf_op jit(solution)/shard_map/all_to_all | solution.py:51
  323.9 2.3 convolution_multiply_fusion.4
  326.2 1.9 copy.142
  328.2 1.7 reduce_sum.158
  329.9 1.8 convolution_multiply_fusion.5
  331.7 2.0 copy.141
  333.7 2.2 maximum_bitcast_fusion
  335.9 6.1 %all-to-all-done.7 = f32[64,2,1280]{2,1,0:T(2,128)} async-done(((f32[64,2,1280]{2,1,0:T(2,128)}), f32[64,2,1280]{2,1,0:T(2,128)}, u32[]{:S(2)}, u32[]{:S(2)}) %all-to-all-start.7) | async-done | bytes 655392 | tf_op jit(solution)/shard_map/all_to_all | solution.py:51
  342.0 7.3 %all-to-all-start.14 = ((f32[64,128,1,16]{1,3,2,0:T(8,128)}), f32[64,128,1,16]{1,3,2,0:T(8,128)}, u32[]{:S(2)}, u32[]{:S(2)}) async-start(f32[64,128,1,16]{1,3,2,0:T(8,128)} %maximum_bitcast_fusion), calls=%async_computation.15 | async-start | bytes 1048576 | tf_op jit(solution)/shard_map/all_to_all | solution.py:51
  353.3 12.7 %all-to-all-done.14 = f32[64,128,1,16]{1,3,2,0:T(8,128)} async-done(((f32[64,128,1,16]{1,3,2,0:T(8,128)}), f32[64,128,1,16]{1,3,2,0:T(8,128)}, u32[]{:S(2)}, u32[]{:S(2)}) %all-to-all-start.14) | async-done | bytes 524320 | tf_op jit(solution)/shard_map/all_to_all | solution.py:51
  366.8 6.9 %all-to-all-start.8 = ((bf16[64,2,1024]{2,1,0:T(2,128)(2,1)}), bf16[64,2,1024]{2,1,0:T(2,128)(2,1)S(1)}, u32[]{:S(2)}, u32[]{:S(2)}) async-start(bf16[64,2,1024]{2,1,0:T(2,128)(2,1)} %broadcast_in_dim.76), calls=%async_computation.8 | async-start | bytes 524288 | tf_op jit(solution)/shard_map/all_to_all | solution.py:36
  374.8 10.4 %all-to-all-done.8 = bf16[64,2,1024]{2,1,0:T(2,128)(2,1)S(1)} async-done(((bf16[64,2,1024]{2,1,0:T(2,128)(2,1)}), bf16[64,2,1024]{2,1,0:T(2,128)(2,1)S(1)}, u32[]{:S(2)}, u32[]{:S(2)}) %all-to-all-start.8) | async-done | bytes 262176 | tf_op jit(solution)/shard_map/all_to_all | solution.py:36
  387.2 6.5 %all-to-all-start.9 = ((f32[64,1,128]{2,1,0:T(1,128)}), f32[64,1,128]{2,1,0:T(1,128)S(1)}, u32[]{:S(2)}, u32[]{:S(2)}) async-start(f32[64,1,128]{2,1,0:T(1,128)} %reshape.184), calls=%async_computation.9 | async-start | bytes 65536 | tf_op jit(solution)/shard_map/all_to_all | solution.py:148
  393.8 8.4 %all-to-all-done.9 = f32[64,1,128]{2,1,0:T(1,128)S(1)} async-done(((f32[64,1,128]{2,1,0:T(1,128)}), f32[64,1,128]{2,1,0:T(1,128)S(1)}, u32[]{:S(2)}, u32[]{:S(2)}) %all-to-all-start.9) | async-done | bytes 32800 | tf_op jit(solution)/shard_map/all_to_all | solution.py:148
  403.1 1.4 fusion.2
  405.1 3.3 all-to-all-start.10
  409.1 5.3 %all-to-all-done.10 = f32[4,2,4096]{2,1,0:T(2,128)S(1)} async-done(((f32[4,2,4096]{2,1,0:T(2,128)}), f32[4,2,4096]{2,1,0:T(2,128)S(1)}, u32[]{:S(2)}, u32[]{:S(2)}) %all-to-all-start.10) | async-done | bytes 131104 | tf_op jit(solution)/shard_map/all_to_all | solution.py:36
  415.1 3.4 multiply_add_fusion
  (133 shorter events, 49.7 us)
Async XLA Ops:
  7.2 88.3 %copy-start = (bf16[512,1024]{1,0:T(8,128)(2,1)S(1)}, bf16[512,1024]{1,0:T(8,128)(2,1)}, u32[]{:S(2)}) copy-start(bf16[512,1024]{1,0:T(8,128)(2,1)} %param.21) | copy-start | bytes 3145732
  7.2 88.3 %all-gather.2.cloned.1.call-start = ((), (), s32[]{:S(2)}) async-start(), calls=%async_computation.16 | async-start | bytes 8519680 | tf_op jit(solution)/shard_map/all_gather | solution.py:177
  7.9 407.2 %reduce-scatter.2.cloned.1.call-start = ((), (), s32[]{:S(2)}) async-start(), calls=%async_computation.17 | async-start | bytes 10485760 | tf_op jit(solution)/shard_map/reduce_scatter | solution.py:180
  105.6 0.7 copy-start.13
  105.6 0.7 copy-start.4
  105.6 9.7 %copy-start.17 = (f32[2]{0:T(128)S(1)}, f32[2]{0:T(128)}, u32[]{:S(2)}) copy-start(f32[2]{0:T(128)} %param.23) | copy-start | bytes 28
  105.6 9.7 %copy-start.16 = (s32[2]{0:T(128)S(1)}, s32[2]{0:T(128)}, u32[]{:S(2)}) copy-start(s32[2]{0:T(128)} %param.24) | copy-start | bytes 28
  105.6 9.8 %copy-start.18 = (s32[2]{0:T(128)S(1)}, s32[2]{0:T(128)}, u32[]{:S(2)}) copy-start(s32[2]{0:T(128)} %param.25) | copy-start | bytes 28
  105.6 25.7 %copy-start.2 = (bf16[64,1,1280]{2,0,1:T(8,128)(2,1)S(1)}, bf16[64,1,1280]{2,0,1:T(8,128)(2,1)}, u32[]{:S(2)}) copy-start(bf16[64,1,1280]{2,0,1:T(8,128)(2,1)} %param.15) | copy-start | bytes 491524
  106.3 25.0 %copy-start.5 = (f32[4096]{0:T(1024)}, f32[4096]{0:T(1024)S(1)}, u32[]{:S(2)}) copy-start(f32[4096]{0:T(1024)S(1)} %convert_element_type.42) | copy-start | bytes 49156
  106.6 38.2 %copy-start.14 = (bf16[64,1,16]{0,2,1:T(8,128)(2,1)S(1)}, bf16[64,1,16]{0,2,1:T(8,128)(2,1)}, u32[]{:S(2)}) copy-start(bf16[64,1,16]{0,2,1:T(8,128)(2,1)} %param.20) | copy-start | bytes 6148
  106.6 38.2 %copy-start.15 = (bf16[64,1,16]{0,2,1:T(8,128)(2,1)S(1)}, bf16[64,1,16]{0,2,1:T(8,128)(2,1)}, u32[]{:S(2)}) copy-start(bf16[64,1,16]{0,2,1:T(8,128)(2,1)} %param.19) | copy-start | bytes 6148
  107.5 16.3 %all-to-all-start = ((f32[64,1,128]{2,1,0:T(1,128)}), f32[64,1,128]{2,1,0:T(1,128)S(1)}, u32[]{:S(2)}, u32[]{:S(2)}) async-start(f32[64,1,128]{2,1,0:T(1,128)} %reshape.178), calls=%async_computation | async-start | bytes 65536 | tf_op jit(solution)/shard_map/all_to_all | solution.py:134
  124.5 14.0 %all-to-all-start.12 = ((f32[64,1,64]{2,1,0:T(1,128)}), f32[64,1,64]{2,1,0:T(1,128)S(1)}, u32[]{:S(2)}, u32[]{:S(2)}) async-start(f32[64,1,64]{2,1,0:T(1,128)} %broadcast_in_dim.80), calls=%async_computation.13 | async-start | bytes 65536 | tf_op jit(solution)/shard_map/all_to_all | solution.py:36
  138.5 58.7 %copy-start.7 = (f32[64,1,64]{2,1,0:T(1,128)}, f32[64,1,64]{2,1,0:T(1,128)S(1)}, u32[]{:S(2)}) copy-start(f32[64,1,64]{2,1,0:T(1,128)S(1)} %all-to-all-done.12) | copy-start | bytes 49156
  138.5 65.8 %all-to-all-start.1 = ((f32[64,2,1280]{2,1,0:T(2,128)}), f32[64,2,1280]{2,1,0:T(2,128)}, u32[]{:S(2)}, u32[]{:S(2)}) async-start(f32[64,2,1280]{2,1,0:T(2,128)} %copy.121), calls=%async_computation.1 | async-start | bytes 1310720 | tf_op jit(solution)/shard_map/all_to_all | solution.py:51
  198.0 13.8 %copy-start.1 = (bf16[2,2048,1,256]{3,1,2,0:T(8,128)(2,1)S(1)}, bf16[2,2048,1,256]{3,1,2,0:T(8,128)(2,1)}, u32[]{:S(2)}) copy-start(bf16[2,2048,1,256]{3,1,2,0:T(8,128)(2,1)} %param.16) | copy-start | bytes 6291460
  205.1 14.5 %all-to-all-start.4 = ((bf16[4,64,1,1024]{3,1,2,0:T(8,128)(2,1)}), bf16[4,64,1,1024]{3,1,2,0:T(8,128)(2,1)}, u32[]{:S(2)}, u32[]{:S(2)}) async-start(bf16[4,64,1,1024]{3,1,2,0:T(8,128)(2,1)} %broadcast_in_dim.74), calls=%async_computation.4 | async-start | bytes 1048576 | tf_op jit(solution)/shard_map/all_to_all | solution.py:36
  211.3 0.5 copy-start.10
  217.1 24.9 %copy-start.6 = (bf16[1,1024,64]{1,2,0:T(8,128)(2,1)S(1)}, bf16[1,1024,64]{1,2,0:T(8,128)(2,1)}, u32[]{:S(2)}) copy-start(bf16[1,1024,64]{1,2,0:T(8,128)(2,1)} %param.18) | copy-start | bytes 393220
  218.1 0.6 copy-start.9
  221.1 20.8 %all-to-all-start.2 = ((bf16[64,2,1024]{2,1,0:T(2,128)(2,1)}), bf16[64,2,1024]{2,1,0:T(2,128)(2,1)}, u32[]{:S(2)}, u32[]{:S(2)}) async-start(bf16[64,2,1024]{2,1,0:T(2,128)(2,1)} %broadcast_in_dim.73), calls=%async_computation.2 | async-start | bytes 524288 | tf_op jit(solution)/shard_map/all_to_all | solution.py:36
  243.9 15.0 %all-to-all-start.3 = ((f32[64,1,128]{2,1,0:T(1,128)}), f32[64,1,128]{2,1,0:T(1,128)S(1)}, u32[]{:S(2)}, u32[]{:S(2)}) async-start(f32[64,1,128]{2,1,0:T(1,128)} %reshape.180), calls=%async_computation.3 | async-start | bytes 65536 | tf_op jit(solution)/shard_map/all_to_all | solution.py:148
  261.9 10.5 %all-to-all-start.5 = ((f32[4,2,4096]{2,1,0:T(2,128)}), f32[4,2,4096]{2,1,0:T(2,128)S(1)}, u32[]{:S(2)}, u32[]{:S(2)}) async-start(f32[4,2,4096]{2,1,0:T(2,128)} %broadcast_in_dim.75), calls=%async_computation.5 | async-start | bytes 262144 | tf_op jit(solution)/shard_map/all_to_all | solution.py:36
  272.4 1.8 copy-start.3
  274.2 12.5 %all-to-all-start.11 = ((f32[4,512,64]{1,2,0:T(8,128)}), f32[4,512,64]{1,2,0:T(8,128)}, u32[]{:S(2)}, u32[]{:S(2)}) async-start(f32[4,512,64]{1,2,0:T(8,128)} %broadcast_in_dim.78), calls=%async_computation.12 | async-start | bytes 1048576 | tf_op jit(solution)/shard_map/all_to_all | solution.py:36
  286.7 14.0 %all-to-all-start.6 = ((f32[64,1,128]{2,1,0:T(1,128)}), f32[64,1,128]{2,1,0:T(1,128)S(1)}, u32[]{:S(2)}, u32[]{:S(2)}) async-start(f32[64,1,128]{2,1,0:T(1,128)} %reshape.182), calls=%async_computation.6 | async-start | bytes 65536 | tf_op jit(solution)/shard_map/all_to_all | solution.py:134
  302.5 14.0 %all-to-all-start.13 = ((f32[4,512,64]{1,2,0:T(8,128)}), f32[4,512,64]{1,2,0:T(8,128)}, u32[]{:S(2)}, u32[]{:S(2)}) async-start(f32[4,512,64]{1,2,0:T(8,128)} %broadcast_in_dim.83), calls=%async_computation.14 | async-start | bytes 1048576 | tf_op jit(solution)/shard_map/all_to_all | solution.py:36
  307.5 16.4 %copy-start.12 = (f32[512]{0:T(512)S(1)}, f32[512]{0:T(512)}, u32[]{:S(2)}) copy-start(f32[512]{0:T(512)} %fusion.61) | copy-start | bytes 6148
  316.5 25.5 %all-to-all-start.7 = ((f32[64,2,1280]{2,1,0:T(2,128)}), f32[64,2,1280]{2,1,0:T(2,128)}, u32[]{:S(2)}, u32[]{:S(2)}) async-start(f32[64,2,1280]{2,1,0:T(2,128)} %copy.131), calls=%async_computation.7 | async-start | bytes 1310720 | tf_op jit(solution)/shard_map/all_to_all | solution.py:51
  331.7 19.0 %copy-start.11 = (f32[2,128]{1,0:T(2,128)S(1)}, f32[2,128]{1,0:T(2,128)}, u32[]{:S(2)}) copy-start(f32[2,128]{1,0:T(2,128)} %copy-done.10) | copy-start | bytes 3076
  331.7 19.2 %copy-start.8 = (pred[2,2048]{1,0:T(4,128)(4,1)S(1)}, pred[2,2048]{1,0:T(4,128)(4,1)}, u32[]{:S(2)}) copy-start(pred[2,2048]{1,0:T(4,128)(4,1)} %iota_compare_fusion) | copy-start | bytes 12292
  342.0 23.9 %all-to-all-start.14 = ((f32[64,128,1,16]{1,3,2,0:T(8,128)}), f32[64,128,1,16]{1,3,2,0:T(8,128)}, u32[]{:S(2)}, u32[]{:S(2)}) async-start(f32[64,128,1,16]{1,3,2,0:T(8,128)} %maximum_bitcast_fusion), calls=%async_computation.15 | async-start | bytes 1048576 | tf_op jit(solution)/shard_map/all_to_all | solution.py:51
  366.8 18.5 %all-to-all-start.8 = ((bf16[64,2,1024]{2,1,0:T(2,128)(2,1)}), bf16[64,2,1024]{2,1,0:T(2,128)(2,1)S(1)}, u32[]{:S(2)}, u32[]{:S(2)}) async-start(bf16[64,2,1024]{2,1,0:T(2,128)(2,1)} %broadcast_in_dim.76), calls=%async_computation.8 | async-start | bytes 524288 | tf_op jit(solution)/shard_map/all_to_all | solution.py:36
  387.2 15.0 %all-to-all-start.9 = ((f32[64,1,128]{2,1,0:T(1,128)}), f32[64,1,128]{2,1,0:T(1,128)S(1)}, u32[]{:S(2)}, u32[]{:S(2)}) async-start(f32[64,1,128]{2,1,0:T(1,128)} %reshape.184), calls=%async_computation.9 | async-start | bytes 65536 | tf_op jit(solution)/shard_map/all_to_all | solution.py:148
  405.1 9.3 %all-to-all-start.10 = ((f32[4,2,4096]{2,1,0:T(2,128)}), f32[4,2,4096]{2,1,0:T(2,128)S(1)}, u32[]{:S(2)}, u32[]{:S(2)}) async-start(f32[4,2,4096]{2,1,0:T(2,128)} %broadcast_in_dim.77), calls=%async_computation.10 | async-start | bytes 262144 | tf_op jit(solution)/shard_map/all_to_all | solution.py:36
Sparse Core Ops, SparseCore 0:
  10.8 84.6 all-gather.1
  105.8 81.5 reduce-scatter.1
where the time goes:
time: 428 us; the launch traced here: 425 us
  waiting for transfers between devices  180 us (42%)
  starting transfers between devices  88.3 us (21%)
  blocking collectives  51.7 us (12%)
  matrix products  33.9 us (8%)
  local copies, waits for them, and re-layouts  32.1 us (8%)
  other arithmetic  24.7 us (6%)
  between operations  14.5 us (3%)
    all_gather x1, waiting for transfers between devices, shards(): lax.all_gather(output_weight_frozen, 'dp', axis=2, tiled=True)[0]  87.5 us
    all_gather x1, blocking collectives, turned_gather(): out, at, finished = (lax.all_gather(both, axis, axis=0, tiled=True), 0, [])  51.7 us
    all_to_all x8, waiting for transfers between devices, sent_to_all(): return lax.all_to_all(copies, axis, split_axis=0, concat_axis=0, tiled=True)  43.4 us
    all_to_all x8, starting transfers between devices, sent_to_all(): return lax.all_to_all(copies, axis, split_axis=0, concat_axis=0, tiled=True)  42.1 us
    all_to_all x3, starting transfers between devices, sent_and_summed(): lax.all_to_all(tiles, axis, split_axis=0, concat_axis=0, tiled=True)  19.9 us
    all_to_all x3, waiting for transfers between devices, sent_and_summed(): lax.all_to_all(tiles, axis, split_axis=0, concat_axis=0, tiled=True)  18.8 us
    all_to_all x2, waiting for transfers between devices, shards(): lax.all_to_all(columns, 'dp', split_axis=0, concat_axis=1, tiled=True)  15.5 us
    all_to_all x2, waiting for transfers between devices, shards(): lax.all_to_all(normed, 'dp', split_axis=1, concat_axis=0, tiled=True)  14.3 us
  transfers between devices with their start and end apart: 17, of which 15 were waited for; matrix products, arithmetic and copies ran while one was open for 18% of the time, Pallas kernels for 0%

commit v1 on v0

v1 whole, which is shorter than its diff:
```python
import math

import jax
import jax.numpy as jnp
from jax import lax
from jax.experimental import pallas as pl
from jax.experimental.pallas import tpu as pltpu
from jax.sharding import Mesh
from jax.sharding import PartitionSpec as P

HD = 128
HEADS_TP = 8
GROUP = 4
COMP = 256
QUERY = HEADS_TP * HD

adapter_scale = 2.0
f32 = jnp.float32
bf16 = jnp.bfloat16
CHIPS = ("y", "z")
DP = ("y", "z", "c")
HIGH = lax.Precision.HIGHEST


def nt_dot(a, b, precision=None):
    return lax.dot_general(
        a, b, (((1,), (1,)), ((), ())), preferred_element_type=f32, precision=precision
    )


def tn_dot(a, b):
    return lax.dot_general(a, b, (((0,), (0,)), ((), ())), preferred_element_type=f32)


def swapped(x):
    return lax.ppermute(x, "c", [(0, 1), (1, 0)])


def in_core_order(own, other, axis):
    first = lax.axis_index("c") == 0
    return jnp.where(
        first,
        jnp.concatenate([own, other], axis=axis),
        jnp.concatenate([other, own], axis=axis),
    )


def shift(x, by, n):
    return lax.ppermute(x, "t", [(i, (i + by) % n) for i in range(n)])


def exchange(x, axes):
    return lax.all_to_all(x, axes, split_axis=0, concat_axis=0, tiled=True)


def to_all(x, axes):
    return exchange(jnp.broadcast_to(x, (lax.axis_size(axes), *x.shape)), axes)


def summed_over_t(x):
    n = lax.axis_size("t")
    out = x
    for by in range(1, n):
        out = out + shift(x, by, n)
    return out


def attend(query, cache, lengths, new_keys, new_values):
    head = query.shape[-1]
    slots = cache.shape[1]
    factor = 1.0 / math.sqrt(head)
    keys = cache[:, :, :head].astype(f32)
    values = cache[:, :, head:]
    scores = jnp.einsum("bhd,bcd->bhc", query, keys, precision=HIGH) * factor
    valid = jnp.arange(slots, dtype=jnp.int32)[None, None, :] < lengths[:, None, None]
    scores = jnp.where(valid, scores, -1e30)
    extra = jnp.einsum("bhd,bed->bhe", query, new_keys, precision=HIGH) * factor
    joined = jnp.concatenate([scores, extra], axis=-1)
    top = jnp.max(joined, axis=-1, keepdims=True)
    expo = jnp.exp(joined - top)
    probs = (expo / jnp.sum(expo, axis=-1, keepdims=True)).astype(bf16)
    out = jnp.einsum("bhc,bcd->bhd", probs[..., :slots], values, preferred_element_type=f32)
    out = out + jnp.einsum(
        "bhe,bed->bhd", probs[..., slots:].astype(f32), new_values, precision=HIGH
    )
    return out.astype(bf16).reshape(query.shape[0], -1)


def rows_kernel(n, where_ref, own, left, right, far_a, far_b, w_ref, low, b_ref, out):
    half = far_a.shape[0]
    acc = adapter_scale * nt_dot(low[...], b_ref[...])
    acc = acc + nt_dot(own[...], w_ref[where_ref[0]])
    acc = acc + nt_dot(left[...], w_ref[where_ref[1]])
    acc = acc + nt_dot(right[...], w_ref[where_ref[3]])
    out[...] = acc
    far = w_ref[where_ref[2]]
    out[:half, :] += nt_dot(far_a[...], far)
    out[half:, :] += nt_dot(far_b[...], far)


def output_rows(where, own, left, right, far_a, far_b, w, low, b):
    n, width, depth = w.shape
    rows = own.shape[0]
    tile = 256
    whole = lambda a: pl.BlockSpec(a.shape, lambda j, s: (0, 0))
    return pl.pallas_call(
        lambda *refs: rows_kernel(n, *refs),
        out_shape=jax.ShapeDtypeStruct((rows, width), f32),
        grid_spec=pltpu.PrefetchScalarGridSpec(
            num_scalar_prefetch=1,
            grid=(width // tile,),
            in_specs=[
                whole(own),
                whole(left),
                whole(right),
                whole(far_a),
                whole(far_b),
                pl.BlockSpec((n, tile, depth), lambda j, s: (0, j, 0)),
                whole(low),
                pl.BlockSpec((tile, b.shape[1]), lambda j, s: (j, 0)),
            ],
            out_specs=pl.BlockSpec((rows, tile), lambda j, s: (0, j)),
        ),
        compiler_params=pltpu.CompilerParams(vmem_limit_bytes=40 << 20),
        cost_estimate=pl.CostEstimate(
            flops=2 * rows * width * depth * n,
            bytes_accessed=2 * (n * width * depth + n * rows * depth) + 4 * rows * width,
            transcendentals=0,
        ),
    )(where, own, left, right, far_a, far_b, w, low, b)


def shards(
    hidden,
    attention_norm_gain,
    query_key_value_weight,
    key_value_cache,
    cache_fill_lengths,
    output_weight_frozen,
    adapter_down_transposed,
    adapter_up_matrix,
    attention_rows,
    upstream,
    rewards,
    prompt_group_index,
    completion_live_lengths,
):
    nt = lax.axis_size("t")
    chips = lax.axis_size(CHIPS)
    t = lax.axis_index("t")
    y = lax.axis_index("y")
    z = lax.axis_index("z")
    m = lax.axis_index(CHIPS)
    rolls, width = hidden.shape
    shard_width = width // nt
    rank = adapter_up_matrix.shape[0]
    cols = width // chips
    cache = key_value_cache[:, :, 0, :]

    w_cols = output_weight_frozen[0].T
    ny = lax.axis_size("y")
    turned = lax.ppermute(
        w_cols, ("y", "t"), [(a * nt + b, b * nt + a) for a in range(ny) for b in range(nt)]
    )
    w_block = lax.all_gather(turned, DP, axis=0, tiled=True)
    w_block = w_block.reshape(nt, shard_width, w_cols.shape[1])

    half = attention_rows.shape[0] // 2
    left = shift(attention_rows, 1, nt)
    right = shift(attention_rows, nt - 1, nt)
    far_a = shift(left[:half], 1, nt)
    far_b = shift(right[half:], nt - 1, nt)

    w_rows = query_key_value_weight[:, 0, :]
    w_rows = in_core_order(w_rows, swapped(w_rows), 0).astype(f32)
    w_pair = in_core_order(w_cols, swapped(w_cols), 0)

    pieces = jnp.concatenate(
        [adapter_down_transposed[:, 0, :].T, adapter_up_matrix[:, 0, :].T], axis=1
    )
    high = lax.reduce_precision(rewards, 8, 7)
    mid = lax.reduce_precision(rewards - high, 8, 7)
    low_part = rewards - high - mid
    stats = jnp.concatenate([high, mid, low_part, prompt_group_index.astype(f32)]).astype(bf16)
    tail = jnp.pad(stats[None, :], ((0, 5), (0, 128 - stats.shape[0])))
    depth = pieces.shape[0]
    hid = hidden.reshape(rolls, chips, cols).transpose(1, 0, 2)
    message = jnp.concatenate(
        [
            jnp.broadcast_to(pieces, (chips, *pieces.shape)),
            hid,
            jnp.broadcast_to(tail, (chips, *tail.shape)),
        ],
        axis=1,
    )
    arrived = exchange(message, CHIPS)
    state = arrived[:, depth : depth + rolls, :].reshape(chips * rolls, cols).astype(f32)
    common = jnp.concatenate([arrived[:, :depth], arrived[:, depth + rolls :]], axis=1)
    common_other = swapped(common)
    own_pieces, other_pieces = common[:, None, :depth], common_other[:, None, :depth]
    both = in_core_order(own_pieces, other_pieces, 1).reshape(-1, 2 * rank)
    a_t = both[:, :rank]
    b_t = both[:, rank:]

    everyone = jnp.concatenate([common[:, depth], common_other[:, depth]], axis=0).astype(f32)
    values = (
        everyone[:, :rolls] + everyone[:, rolls : 2 * rolls] + everyone[:, 2 * rolls : 3 * rolls]
    )
    prompts = everyone[:, 3 * rolls : 4 * rolls]
    mine = (
        prompt_group_index.astype(f32)[:, None, None] == prompts[None, :, :]
    ).astype(f32)
    totals = jnp.sum(mine * values[None], axis=(1, 2))
    squares = jnp.sum(mine * (values * values)[None], axis=(1, 2))
    mean = totals / GROUP
    std = jnp.sqrt(jnp.maximum(squares / GROUP - mean * mean, 0.09))
    per_roll = (rewards - mean) / std / completion_live_lengths.astype(f32)
    rows = attention_rows.shape[0]
    index = lax.broadcasted_iota(jnp.int32, (rows, 1), 0)
    weight = jnp.zeros((rows, 1), f32)
    for r in range(rolls):
        slot = index - r * COMP
        inside = (slot >= 0) & (slot < COMP) & (slot < completion_live_lengths[r])
        weight = jnp.where(inside, per_roll[r], weight)
    weighted = (weight * upstream.astype(f32)).astype(bf16)

    low_part = jnp.dot(attention_rows, a_t, preferred_element_type=f32)
    back_part = jnp.dot(weighted, b_t, preferred_element_type=f32)
    b_slice = lax.dynamic_slice_in_dim(b_t, z * cols, cols, 0).astype(f32)
    b_slice = jnp.pad(b_slice, ((0, 0), (0, rank)))
    part = jnp.concatenate([low_part, back_part], axis=1)
    part = jnp.concatenate([part, b_slice], axis=0)
    by_shift = [part] + [shift(part, by, nt) for by in range(1, nt)]
    low_back = sum(p[:rows] for p in by_shift).astype(bf16)
    from_y = lax.rem(t - y + nt, nt)
    b_cols = by_shift[0][rows:, :rank]
    for by in range(1, nt):
        b_cols = jnp.where(from_y == by, by_shift[by][rows:, :rank], b_cols)
    low_rows = low_back[:, :rank]
    back_rows = low_back[:, rank:]
    grads = adapter_scale * jnp.concatenate(
        [tn_dot(back_rows, attention_rows), tn_dot(low_rows, weighted)], axis=0
    )

    gain = lax.dynamic_slice_in_dim(attention_norm_gain, m * cols, cols, 0).astype(f32)
    owned = hidden.astype(f32)
    keys_new = []
    values_new = []
    for step in range(2):
        partial_value = jnp.dot(state * gain[None, :], w_rows, precision=HIGH)
        partial_value = partial_value.reshape(chips, rolls, -1)
        if step:
            partial_value = jnp.concatenate(
                [partial_value, state.reshape(chips, rolls, cols)], axis=2
            )
        came = exchange(partial_value, CHIPS)
        qkv = came[:, :, : w_rows.shape[1]].sum(axis=0)
        if step:
            owned = came[:, :, w_rows.shape[1] :].transpose(1, 0, 2).reshape(rolls, width)
        scale = lax.rsqrt(jnp.mean(owned * owned, axis=-1, keepdims=True) + 1e-05)
        qkv = qkv * scale
        query = qkv[:, :QUERY].reshape(rolls, HEADS_TP, HD)
        keys_new.append(qkv[:, QUERY : QUERY + HD])
        values_new.append(qkv[:, QUERY + HD :])
        attended = attend(
            query,
            cache,
            cache_fill_lengths,
            jnp.stack(keys_new, axis=1),
            jnp.stack(values_new, axis=1),
        )
        if step == 0:
            everyones = to_all(attended, CHIPS).reshape(chips * rolls, -1)
            share = jnp.concatenate(
                [nt_dot(everyones, w_pair), jnp.dot(everyones, a_t, preferred_element_type=f32)],
                axis=1,
            )
            share = summed_over_t(share)
            state = (
                state
                + share[:, :cols]
                + adapter_scale * nt_dot(share[:, cols:], b_cols, precision=HIGH)
            )
        else:
            low_decode = jnp.dot(attended, a_t, preferred_element_type=f32)
            groups = to_all(jnp.concatenate([attended.astype(f32), low_decode], axis=1), "t")
            low_decode = groups[:, :, shard_width:].sum(axis=0)
            heads = groups[:, :, :shard_width].astype(bf16)
            update = adapter_scale * nt_dot(low_decode, b_t.astype(f32), precision=HIGH)
            for g in range(nt):
                update = update + nt_dot(heads[g], w_block[g])
            own_cols = lax.dynamic_slice_in_dim(owned, t * shard_width, shard_width, 1) + update
            decoded = to_all(own_cols, "t").transpose(1, 0, 2).reshape(rolls, width)

    tiles = grads.reshape(2 * rank, chips, 2, depth).transpose(2, 1, 0, 3)
    c = lax.axis_index("c")
    kept = lax.dynamic_index_in_dim(tiles, c, 0, keepdims=False)
    given = lax.dynamic_index_in_dim(tiles, 1 - c, 0, keepdims=False)
    kept = kept + swapped(given)
    kept = kept.reshape(chips, -1, 128)
    summed = exchange(kept, CHIPS).sum(axis=0).reshape(2 * rank, depth)

    where = lax.rem(t - jnp.arange(nt, dtype=jnp.int32) + nt, nt)
    adapted = output_rows(
        where, attention_rows, left, right, far_a, far_b, w_block, low_rows, b_t
    )
    return (decoded, adapted, summed[:rank, None, :], summed[rank:, None, :])


def solution(mesh):
    split = Mesh(mesh.devices.reshape(4, 8, 2, 4), ("y", "z", "c", "t"))
    placed = (
        P(DP, None),
        P(),
        P(DP, "t", None),
        P(DP, None, "t", None),
        P(DP),
        P("t", None, DP),
        P(None, "t", DP),
        P(None, "t", DP),
        P(DP, "t"),
        P(DP, "t"),
        P(DP),
        P(DP),
        P(DP),
    )
    return jax.shard_map(
        shards,
        mesh=split,
        in_specs=placed,
        out_specs=(P(DP, None), P(DP, "t"), P(None, "t", DP), P(None, "t", DP)),
        check_vma=False,
    )
```

time: 428 us -> 223 us (0.52)
  waiting for transfers between devices: 180 us -> 34 us
  blocking collectives: 51.7 us -> 0 us
  starting transfers between devices: 88.3 us -> 69 us
  Pallas kernels: 0 us -> 8.36 us
  other arithmetic: 24.7 us -> 30 us
    all_gather x1, waiting for transfers between devices: 87.5 us -> 0.01 us  [shards(): w_block = lax.all_gather(turned, DP, axis=0, tiled=True)]
    all_to_all x15 -> x7, waiting for transfers between devices: 92 us -> 18.8 us  [exchange(): return lax.all_to_all(x, axes, split_axis=0, concat_axis=0, tiled=True)]
    all_gather x1 -> x0, blocking collectives: 51.7 us -> none  [turned_gather(): out, at, finished = (lax.all_gather(both, axis, axis=0, tiled=True), 0, [])]
    all_to_all x15 -> x7, starting transfers between devices: 88.3 us -> 54.4 us  [exchange(): return lax.all_to_all(x, axes, split_axis=0, concat_axis=0, tiled=True)]
    ppermute x0 -> x15, waiting for transfers between devices: none -> 15.2 us  [the longest x10 8.98 us: shift(): return lax.ppermute(x, 't', [(i, (i + by) % n) for i in range(n)])]
    ppermute x0 -> x15, starting transfers between devices: none -> 14.6 us  [the longest x10 11 us: shift(): return lax.ppermute(x, 't', [(i, (i + by) % n) for i in range(n)])]
    pallas_call x0 -> x1, Pallas kernels: none -> 8.36 us  [output_rows(): pl.pallas_call(lambda *refs: rows_kernel(n, *refs), out_shape=jax.ShapeDt...]
    reshape x0 -> x4, local copies, waits for them, and re-layouts: none -> 7.12 us  [the longest x1 2.24 us: shards(): kept = kept.reshape(chips, -1, 128)]
  transfers between devices with their start and end apart: 17 -> 23, of which waited for: 15 -> 7; matrix products, arithmetic and copies ran while one was open for 18% -> 39% of each run, Pallas kernels for 0% -> 4%
where the time goes in v1:
time: 223 us; the launch traced here: 220 us
  starting transfers between devices  69 us (31%)
  waiting for transfers between devices  34 us (15%)
  local copies, waits for them, and re-layouts  32.3 us (14%)
  matrix products  31.4 us (14%)
  other arithmetic  30 us (13%)
  between operations  14.6 us (7%)
  Pallas kernels  8.36 us (4%)
    all_to_all x7, starting transfers between devices, exchange(): return lax.all_to_all(x, axes, split_axis=0, concat_axis=0, tiled=True)  54.4 us
    all_to_all x7, waiting for transfers between devices, exchange(): return lax.all_to_all(x, axes, split_axis=0, concat_axis=0, tiled=True)  18.8 us
    dot_general x7, matrix products, nt_dot(): lax.dot_general(a, b, (((1,), (1,)), ((), ())), preferred_element_type=f3...  12.8 us
    ppermute x10, starting transfers between devices, shift(): return lax.ppermute(x, 't', [(i, (i + by) % n) for i in range(n)])  11 us
    unnamed x45, local copies, waits for them, and re-layouts  10.5 us
    ppermute x10, waiting for transfers between devices, shift(): return lax.ppermute(x, 't', [(i, (i + by) % n) for i in range(n)])  8.98 us
    pallas_call x1, Pallas kernels, output_rows(): pl.pallas_call(lambda *refs: rows_kernel(n, *refs), out_shape=jax.ShapeDt...  8.36 us
    dot_general x2, matrix products, attend(): scores = jnp.einsum('bhd,bcd->bhc', query, keys, precision=HIGH) * factor  5.06 us
  transfers between devices with their start and end apart: 23, of which 7 were waited for; matrix products, arithmetic and copies ran while one was open for 39% of the time, Pallas kernels for 4%

profile of v1, /device:TPU:8, one launch (start us, length us, event | category | flops | bytes accessed | tf_op | source)
XLA Modules:
  0.0 219.7 jit_solution(13727168130452309977)
XLA Ops:
  7.2 3.3 %collective-permute-start.9 = (bf16[64,1024]{1,0:T(8,128)(2,1)}, bf16[64,1024]{1,0:T(8,128)(2,1)S(1)}, u32[]{:S(2)}, u32[]{:S(2)}) collective-permute-start(bf16[64,1024]{1,0:T(8,128)(2,1)} %bitcast.165), channel_id=1, source_target_pairs={{0,0},{1,64},{2,128},{3,192},{64,1},{65,65},{66,129},{67,193},{128... | collective-permute-start | bytes 393224 | tf_op jit(solution)/shard_map/ppermute | solution.py:162
  10.5 4.9 %collective-permute-done.9 = bf16[64,1024]{1,0:T(8,128)(2,1)S(1)} collective-permute-done((bf16[64,1024]{1,0:T(8,128)(2,1)}, bf16[64,1024]{1,0:T(8,128)(2,1)S(1)}, u32[]{:S(2)}, u32[]{:S(2)}) %collective-permute-start.9) | collective-permute-done | bytes 131104 | tf_op jit(solution)/shard_map/ppermute | solution.py:162
  18.5 1.5 pad_maximum_fusion.1
  20.0 16.8 %all-to-all-start = ((bf16[32,24,128]{2,1,0:T(8,128)(2,1)}), bf16[32,24,128]{2,1,0:T(8,128)(2,1)S(1)}, u32[]{:S(2)}, u32[]{:S(2)}) async-start(bf16[32,24,128]{2,1,0:T(8,128)(2,1)} %pad_maximum_fusion.1), calls=%async_computation | async-start | bytes 393216 | tf_op jit(solution)/shard_map/all_to_all | solution.py:53
  40.7 7.6 %all-to-all-done = bf16[32,24,128]{2,1,0:T(8,128)(2,1)S(1)} async-done(((bf16[32,24,128]{2,1,0:T(8,128)(2,1)}), bf16[32,24,128]{2,1,0:T(8,128)(2,1)S(1)}, u32[]{:S(2)}, u32[]{:S(2)}) %all-to-all-start) | async-done | bytes 196640 | tf_op jit(solution)/shard_map/all_to_all | solution.py:53
  51.3 2.6 %select_select_fusion = f32[512]{0:T(512)S(1)} fusion(f32[]{:T(128)} %bitcast.33, s32[]{:T(128)} %bitcast.32, f32[]{:T(128)} %bitcast.31, s32[]{:T(128)} %bitcast.28), kind=kLoop, calls=%fused_computation.154 | loop fusion | flops 5632 | bytes 2064 | tf_op jit(solution)/shard_map/jit(_where)/select_n | solution.py:224
  54.4 1.9 fusion.35
  59.1 2.0 collective-permute-start.6
  62.4 6.0 %all-to-all-start.1 = ((f32[32,2,1280]{2,1,0:T(2,128)}), f32[32,2,1280]{2,1,0:T(2,128)}, u32[]{:S(2)}, u32[]{:S(2)}) async-start(f32[32,2,1280]{2,1,0:T(2,128)} %copy.151), calls=%async_computation.1 | async-start | bytes 655360 | tf_op jit(solution)/shard_map/all_to_all | solution.py:53
  69.1 9.0 %collective-permute-done.8 = f32[640,128]{1,0:T(8,128)} collective-permute-done((f32[640,128]{1,0:T(8,128)}, f32[640,128]{1,0:T(8,128)}, u32[]{:S(2)}, u32[]{:S(2)}) %collective-permute-start.8) | collective-permute-done | bytes 327712 | tf_op jit(solution)/shard_map/ppermute | solution.py:49
  78.0 1.5 fusion.38
  79.5 2.7 %fusion.34 = f32[64,1024]{0,1:T(8,128)} fusion(bf16[512,1024]{1,0:T(8,128)(2,1)} %param.22, f32[512]{0:T(512)S(1)} %select_select_fusion, bf16[512,128]{1,0:T(8,128)(2,1)S(1)} %fusion.38), kind=kOutput, calls=%fused_computation.34 | convolution fusion | flops 68681728 | bytes 1443840 | tf_op jit(solution)/shard_map/dot_general | solution.py:32
  82.2 1.7 reduce_sum.90
  85.4 2.8 %fusion.134 = (f32[2,8]{1,0:T(2,128)S(1)}, f32[2,8,2048]{2,1,0:T(8,128)}) fusion(bf16[2,2048,256]{2,1,0:T(8,128)(2,1)} %bitcast.135, f32[1,2,8,128]{3,1,2,0:T(2,128)S(1)} %slice_bitcast_fusion.3, pred[2,2048]{1,0:T(4,128)(4,1)S(1)} %iota_compare_fusion.1), kind=kOutput, calls=%fused_computation.200 | convolution fusion | flops 50429936 | bytes 1192000 | tf_op jit(solution)/shard_map/bhd,bcd->bhc/dot_general | solution.py:74
  91.1 1.5 fusion.28
  93.4 9.8 %all-to-all-start.2 = ((bf16[32,2,1024]{2,1,0:T(2,128)(2,1)}), bf16[32,2,1024]{2,1,0:T(2,128)(2,1)}, u32[]{:S(2)}, u32[]{:S(2)}) async-start(bf16[32,2,1024]{2,1,0:T(2,128)(2,1)} %broadcast_in_dim.74), calls=%async_computation.2 | async-start | bytes 262144 | tf_op jit(solution)/shard_map/all_to_all | solution.py:53
  106.6 5.7 %all-to-all-done.2 = bf16[32,2,1024]{2,1,0:T(2,128)(2,1)} async-done(((bf16[32,2,1024]{2,1,0:T(2,128)(2,1)}), bf16[32,2,1024]{2,1,0:T(2,128)(2,1)}, u32[]{:S(2)}, u32[]{:S(2)}) %all-to-all-start.2) | async-done | bytes 131104 | tf_op jit(solution)/shard_map/all_to_all | solution.py:53
  112.3 1.6 reshape.233
  115.1 1.4 fusion.39
  117.2 4.3 %collective-permute-start.4 = (f32[64,192]{1,0:T(8,128)}, f32[64,192]{1,0:T(8,128)}, u32[]{:S(2)}, u32[]{:S(2)}) collective-permute-start(f32[64,192]{1,0:T(8,128)} %pad_maximum_fusion.3), channel_id=1, source_target_pairs={{0,2},{1,3},{2,0},{3,1},{4,6},{5,7},{6,4},{7,5},{8,10},{9,11},{10,... | collective-permute-start | bytes 147464 | tf_op jit(solution)/shard_map/ppermute | solution.py:49
  121.5 1.8 bitcast_add_fusion
  123.3 2.3 %copy.172 = f32[32,128,16]{0,2,1:T(8,128)} copy(f32[32,128,16]{1,2,0:T(8,128)} %bitcast_add_fusion) | data formatting | bytes 524288 | tf_op jit(solution)/shard_map/add | solution.py:299
  125.6 2.2 %copy.173 = f32[32,16,128]{2,1,0:T(8,128)} copy(f32[32,16,128]{0,2,1:T(8,128)} %bitcast.145) | data formatting | bytes 524288 | tf_op jit(solution)/shard_map/reshape | solution.py:300
  127.9 5.6 %all-to-all-start.6 = ((f32[32,16,128]{2,1,0:T(8,128)}), f32[32,16,128]{2,1,0:T(8,128)}, u32[]{:S(2)}, u32[]{:S(2)}) async-start(f32[32,16,128]{2,1,0:T(8,128)} %copy.173), calls=%async_computation.6 | async-start | bytes 524288 | tf_op jit(solution)/shard_map/all_to_all | solution.py:53
  136.3 2.2 fusion.64
  138.4 1.9 reshape.234
  140.3 1.9 pad_maximum_fusion
  142.2 1.4 all-to-all-done.6
  143.6 8.5 %all-to-all-start.3 = ((f32[32,2,1408]{2,1,0:T(2,128)}), f32[32,2,1408]{2,1,0:T(2,128)}, u32[]{:S(2)}, u32[]{:S(2)}) async-start(f32[32,2,1408]{2,1,0:T(2,128)} %pad_maximum_fusion), calls=%async_computation.3 | async-start | bytes 720896 | tf_op jit(solution)/shard_map/all_to_all | solution.py:53
  153.8 3.2 %collective-permute-start.13 = (bf16[256,1024]{1,0:T(8,128)(2,1)}, bf16[256,1024]{1,0:T(8,128)(2,1)}, u32[]{:S(2)}, u32[]{:S(2)}) collective-permute-start(bf16[256,1024]{1,0:T(8,128)(2,1)} %slice.265), channel_id=1, source_target_pairs={{0,3},{1,0},{2,1},{3,2},{4,7},{5,4},{6,5},{7,6},{8,11},{9,8},{10,9... | collective-permute-start | bytes 1572872 | tf_op jit(solution)/shard_map/ppermute | solution.py:49
  157.1 1.6 reduce_sum.99
  160.0 1.4 broadcast_in_dim.82
  161.3 1.4 copy.174
  163.4 1.4 copy.175
  167.8 2.2 %fusion.135 = (f32[2,8]{1,0:T(2,128)S(1)}, f32[2,8,2048]{2,1,0:T(8,128)S(1)}) fusion(bf16[2,2048,256]{2,1,0:T(8,128)(2,1)} %bitcast.137, f32[1,2,8,128]{3,1,2,0:T(2,128)S(1)} %slice_bitcast_fusion.2, pred[2,2048]{1,0:T(4,128)(4,1)S(1)} %iota_compare_fusion.1), kind=kOutput, calls=%fused_computation.201 | convolution fusion | flops 50429936 | bytes 1192000 | tf_op jit(solution)/shard_map/bhd,bcd->bhc/dot_general | solution.py:74
  171.0 1.5 fusion.29
  173.4 3.9 %all-to-all-start.4 = ((f32[4,2,1088]{2,1,0:T(2,128)}), f32[4,2,1088]{2,1,0:T(2,128)}, u32[]{:S(2)}, u32[]{:S(2)}) async-start(f32[4,2,1088]{2,1,0:T(2,128)} %broadcast_in_dim.80), calls=%async_computation.4 | async-start | bytes 73728 | tf_op jit(solution)/shard_map/all_to_all | solution.py:53
  177.3 1.4 slice_bitcast_fusion.1
  178.7 4.2 %all-to-all-done.4 = f32[4,2,1088]{2,1,0:T(2,128)} async-done(((f32[4,2,1088]{2,1,0:T(2,128)}), f32[4,2,1088]{2,1,0:T(2,128)}, u32[]{:S(2)}, u32[]{:S(2)}) %all-to-all-start.4) | async-done | bytes 34848 | tf_op jit(solution)/shard_map/all_to_all | solution.py:53
  182.8 1.4 convert.30
  186.2 2.3 %fusion.2 = f32[2,1024]{1,0:T(2,128)S(1)} fusion(bf16[4096,1024]{1,0:T(8,128)(2,1)} %all-gather.2.cloned.1.call-done, bf16[4,2,1088]{2,1,0:T(2,128)(2,1)} %convert.30), kind=kOutput, calls=%fused_computation.4 | convolution fusion | flops 4194304 | bytes 2109440 | tf_op jit(solution)/shard_map/dot_general | solution.py:26
  188.5 2.2 %fusion.4 = f32[2,1024]{1,0:T(2,128)S(1)} fusion(bf16[4096,1024]{1,0:T(8,128)(2,1)} %all-gather.2.cloned.1.call-done, bf16[4,2,1088]{2,1,0:T(2,128)(2,1)S(1)} %copy-done.11), kind=kOutput, calls=%fused_computation.6 | convolution fusion | flops 4194304 | bytes 2109440 | tf_op jit(solution)/shard_map/dot_general | solution.py:26
  190.7 2.2 %fusion.6 = f32[2,1024]{1,0:T(2,128)S(1)} fusion(bf16[4096,1024]{1,0:T(8,128)(2,1)} %all-gather.2.cloned.1.call-done, bf16[4,2,1088]{2,1,0:T(2,128)(2,1)S(1)} %copy-done.11), kind=kOutput, calls=%fused_computation.8 | convolution fusion | flops 4194304 | bytes 2109440 | tf_op jit(solution)/shard_map/dot_general | solution.py:26
  193.0 2.3 %fusion.22 = f32[2,1024]{1,0:T(2,128)S(1)} fusion(f32[2,1024]{1,0:T(2,128)S(1)} %fusion.2, f32[2,1024]{1,0:T(2,128)S(1)} %fusion.4, f32[2,1024]{1,0:T(2,128)S(1)} %fusion.6, f32[2,1024]{1,0:T(2,128)S(1)} %convolution_multiply_fusion.3, bf16[4096,1024]{1,0:T(8,128)(2,1)} %all-gather.2.cloned.1.call-done, f32[2,4096]{1,0:T(2,128)} %slice_bitcast_fusion.1, ...), kind=kOutput, calls=%fused_computation.19 | convolution fusion | flops 4204544 | bytes 2150404 | tf_op jit(solution)/shard_map/dot_general | solution.py:26
  195.9 3.9 %all-to-all-start.5 = ((f32[4,2,1024]{2,1,0:T(2,128)}), f32[4,2,1024]{2,1,0:T(2,128)}, u32[]{:S(2)}, u32[]{:S(2)}) async-start(f32[4,2,1024]{2,1,0:T(2,128)} %broadcast_in_dim.81), calls=%async_computation.5 | async-start | bytes 65536 | tf_op jit(solution)/shard_map/all_to_all | solution.py:53
  199.8 3.4 %copy-done = bf16[4096,1024]{1,0:T(8,128)(2,1)S(1)} copy-done((bf16[4096,1024]{1,0:T(8,128)(2,1)S(1)}, bf16[4096,1024]{1,0:T(8,128)(2,1)}, u32[]{:S(2)}) %copy-start) | copy-done | bytes 8388632
  203.1 8.4 %shard_map.156 = f32[512,1024]{1,0:T(8,128)} custom-call(s32[4]{0:T(128)S(1)} %compare_select_fusion.2.refs_0_, bf16[512,1024]{1,0:T(8,128)(2,1)S(1)} %copy-done.1, bf16[512,1024]{1,0:T(8,128)(2,1)S(1)} %collective-permute-done.10.refs_2_, bf16[512,1024]{1,0:T(8,128)(2,1)S(1)} %collective-permute-done.11.refs_3_, ...), custom_call_target="tpu_custom_call" | custom-call | flops 4294967296 | bytes 14680064 | tf_op jit(solution)/shard_map/pallas_call | solution.py:106
  211.5 1.4 copy.227
  (145 shorter events, 39.2 us)
Async XLA Ops:
  7.2 179.0 %all-gather.2.cloned.1.call-start = ((), (), s32[]{:S(2)}) async-start(), calls=%async_computation.7 | async-start | bytes 8519680 | tf_op jit(solution)/shard_map/all_gather | solution.py:165
  7.2 8.2 %collective-permute-start.9 = (bf16[64,1024]{1,0:T(8,128)(2,1)}, bf16[64,1024]{1,0:T(8,128)(2,1)S(1)}, u32[]{:S(2)}, u32[]{:S(2)}) collective-permute-start(bf16[64,1024]{1,0:T(8,128)(2,1)} %bitcast.165), channel_id=1, source_target_pairs={{0,0},{1,64},{2,128},{3,192},{64,1},{65,65},{66,129},{67,193},{128... | collective-permute-start | bytes 393224 | tf_op jit(solution)/shard_map/ppermute | solution.py:162
  15.5 0.6 copy-start.9
  16.1 99.0 %collective-permute-start.1 = (bf16[64,1024]{1,0:T(8,128)(2,1)}, bf16[64,1024]{1,0:T(8,128)(2,1)}, u32[]{:S(2)}, u32[]{:S(2)}) collective-permute-start(bf16[64,1024]{1,0:T(8,128)(2,1)} %bitcast.166), channel_id=1, source_target_pairs={{0,4},{4,0},{1,5},{5,1},{2,6},{6,2},{3,7},{7,3},{8,12},{12,8},{9,1... | collective-permute-start | bytes 393224 | tf_op jit(solution)/shard_map/ppermute | solution.py:36
  18.4 32.3 %copy-start.13 = (s32[2]{0:T(128)S(1)}, s32[2]{0:T(128)}, u32[]{:S(2)}) copy-start(s32[2]{0:T(128)} %param.25) | copy-start | bytes 28
  18.4 32.3 %copy-start.14 = (f32[2]{0:T(128)S(1)}, f32[2]{0:T(128)}, u32[]{:S(2)}) copy-start(f32[2]{0:T(128)} %param.23) | copy-start | bytes 28
  18.4 35.5 %copy-start.1 = (bf16[512,1024]{1,0:T(8,128)(2,1)S(1)}, bf16[512,1024]{1,0:T(8,128)(2,1)}, u32[]{:S(2)}) copy-start(bf16[512,1024]{1,0:T(8,128)(2,1)} %refs_1_.1) | copy-start | bytes 3145732
  20.0 28.3 %all-to-all-start = ((bf16[32,24,128]{2,1,0:T(8,128)(2,1)}), bf16[32,24,128]{2,1,0:T(8,128)(2,1)S(1)}, u32[]{:S(2)}, u32[]{:S(2)}) async-start(bf16[32,24,128]{2,1,0:T(8,128)(2,1)} %pad_maximum_fusion.1), calls=%async_computation | async-start | bytes 393216 | tf_op jit(solution)/shard_map/all_to_all | solution.py:53
  36.8 22.4 %collective-permute-start = (bf16[64,1280]{1,0:T(8,128)(2,1)}, bf16[64,1280]{1,0:T(8,128)(2,1)S(1)}, u32[]{:S(2)}, u32[]{:S(2)}) collective-permute-start(bf16[64,1280]{1,0:T(8,128)(2,1)} %bitcast.162), channel_id=1, source_target_pairs={{0,4},{4,0},{1,5},{5,1},{2,6},{6,2},{3,7},{7,3},{8,12},{12,8},{9,1... | collective-permute-start | bytes 491528 | tf_op jit(solution)/shard_map/ppermute | solution.py:36
  36.9 115.3 %collective-permute-start.10 = (bf16[512,1024]{1,0:T(8,128)(2,1)}, bf16[512,1024]{1,0:T(8,128)(2,1)S(1)}, u32[]{:S(2)}, u32[]{:S(2)}) collective-permute-start(bf16[512,1024]{1,0:T(8,128)(2,1)} %refs_1_.1), channel_id=1, source_target_pairs={{0,1},{1,2},{2,3},{3,0},{4,5},{5,6},{6,7},{7,4},{8,9},{9,10},{10,1... | collective-permute-start | bytes 3145736 | tf_op jit(solution)/shard_map/ppermute | solution.py:49
  37.7 12.3 %copy-start.15 = (f32[128]{0:T(128)}, f32[128]{0:T(128)S(1)}, u32[]{:S(2)}) copy-start(f32[128]{0:T(128)S(1)} %dynamic-slice_convert_fusion.2) | copy-start | bytes 1540
  48.5 1.5 collective-permute-start.2
  50.1 6.2 %copy-start.2 = (bf16[32,2,16,128]{3,2,1,0:T(8,128)(2,1)}, bf16[32,2,16,128]{3,2,1,0:T(8,128)(2,1)S(1)}, u32[]{:S(2)}) copy-start(bf16[32,2,16,128]{3,2,1,0:T(8,128)(2,1)S(1)} %maximum_select_fusion.3) | copy-start | bytes 786436
  53.9 7.2 %copy-start.17 = (bf16[64,1,1280]{2,0,1:T(8,128)(2,1)S(1)}, bf16[64,1,1280]{2,0,1:T(8,128)(2,1)}, u32[]{:S(2)}) copy-start(bf16[64,1,1280]{2,0,1:T(8,128)(2,1)} %param.15) | copy-start | bytes 491524
  54.4 7.1 %copy-start.4 = (f32[512,64]{1,0:T(8,128)}, f32[512,64]{1,0:T(8,128)S(1)}, u32[]{:S(2)}) copy-start(f32[512,64]{1,0:T(8,128)S(1)} %convolution_bitcast_fusion) | copy-start | bytes 393220
  56.2 0.7 copy-start.6
  57.8 20.2 %collective-permute-start.8 = (f32[640,128]{1,0:T(8,128)}, f32[640,128]{1,0:T(8,128)}, u32[]{:S(2)}, u32[]{:S(2)}) collective-permute-start(f32[640,128]{1,0:T(8,128)} %select_maximum_fusion), channel_id=1, source_target_pairs={{0,1},{1,2},{2,3},{3,0},{4,5},{5,6},{6,7},{7,4},{8,9},{9,10},{10,1... | collective-permute-start | bytes 983048 | tf_op jit(solution)/shard_map/ppermute | solution.py:49
  57.8 20.2 %collective-permute-start.7 = (f32[640,128]{1,0:T(8,128)}, f32[640,128]{1,0:T(8,128)}, u32[]{:S(2)}, u32[]{:S(2)}) collective-permute-start(f32[640,128]{1,0:T(8,128)} %select_maximum_fusion), channel_id=1, source_target_pairs={{0,2},{1,3},{2,0},{3,1},{4,6},{5,7},{6,4},{7,5},{8,10},{9,11},{10,... | collective-permute-start | bytes 983048 | tf_op jit(solution)/shard_map/ppermute | solution.py:49
  59.1 9.9 %copy-start.18 = (bf16[64,1280]{1,0:T(8,128)(2,1)}, bf16[64,1280]{1,0:T(8,128)(2,1)S(1)}, u32[]{:S(2)}) copy-start(bf16[64,1280]{1,0:T(8,128)(2,1)S(1)} %collective-permute-done) | copy-start | bytes 491524
  59.1 18.9 %collective-permute-start.6 = (f32[640,128]{1,0:T(8,128)}, f32[640,128]{1,0:T(8,128)}, u32[]{:S(2)}, u32[]{:S(2)}) collective-permute-start(f32[640,128]{1,0:T(8,128)} %select_maximum_fusion), channel_id=1, source_target_pairs={{0,3},{1,0},{2,1},{3,2},{4,7},{5,4},{6,5},{7,6},{8,11},{9,8},{10,9... | collective-permute-start | bytes 983048 | tf_op jit(solution)/shard_map/ppermute | solution.py:49
  62.4 19.8 %all-to-all-start.1 = ((f32[32,2,1280]{2,1,0:T(2,128)}), f32[32,2,1280]{2,1,0:T(2,128)}, u32[]{:S(2)}, u32[]{:S(2)}) async-start(f32[32,2,1280]{2,1,0:T(2,128)} %copy.151), calls=%async_computation.1 | async-start | bytes 655360 | tf_op jit(solution)/shard_map/all_to_all | solution.py:53
  78.0 75.0 %collective-permute-start.11 = (bf16[512,1024]{1,0:T(8,128)(2,1)S(1)}, bf16[512,1024]{1,0:T(8,128)(2,1)S(1)}, u32[]{:S(2)}, u32[]{:S(2)}) collective-permute-start(bf16[512,1024]{1,0:T(8,128)(2,1)S(1)} %copy-done.1), channel_id=1, source_target_pairs={{0,3},{1,0},{2,1},{3,2},{4,7},{5,4},{6,5},{7,6},{8,11},{9,8},{10,9... | collective-permute-start | bytes 3145736 | tf_op jit(solution)/shard_map/ppermute | solution.py:49
  85.2 3.0 %copy-start.12 = (f32[2,128]{1,0:T(2,128)}, f32[2,128]{1,0:T(2,128)S(1)}, u32[]{:S(2)}) copy-start(f32[2,128]{1,0:T(2,128)S(1)} %get-tuple-element.40) | copy-start | bytes 3076
  93.4 18.9 %all-to-all-start.2 = ((bf16[32,2,1024]{2,1,0:T(2,128)(2,1)}), bf16[32,2,1024]{2,1,0:T(2,128)(2,1)}, u32[]{:S(2)}, u32[]{:S(2)}) async-start(bf16[32,2,1024]{2,1,0:T(2,128)(2,1)} %broadcast_in_dim.74), calls=%async_computation.2 | async-start | bytes 262144 | tf_op jit(solution)/shard_map/all_to_all | solution.py:53
  105.1 0.8 copy-start.5
  106.6 14.9 %collective-permute-start.14 = (f32[32,128,16]{1,2,0:T(8,128)}, f32[32,128,16]{1,2,0:T(8,128)}, u32[]{:S(2)}, u32[]{:S(2)}) collective-permute-start(f32[32,128,16]{1,2,0:T(8,128)} %dynamic-slice_bitcast_fusion), channel_id=1, source_target_pairs={{0,4},{4,0},{1,5},{5,1},{2,6},{6,2},{3,7},{7,3},{8,12},{12,8},{9,1... | collective-permute-start | bytes 786440 | tf_op jit(solution)/shard_map/ppermute | solution.py:36
  115.1 1.4 copy-start.7
  116.5 0.6 copy-start.10
  117.2 16.3 %collective-permute-start.5 = (f32[64,192]{1,0:T(8,128)}, f32[64,192]{1,0:T(8,128)}, u32[]{:S(2)}, u32[]{:S(2)}) collective-permute-start(f32[64,192]{1,0:T(8,128)} %pad_maximum_fusion.3), channel_id=1, source_target_pairs={{0,3},{1,0},{2,1},{3,2},{4,7},{5,4},{6,5},{7,6},{8,11},{9,8},{10,9... | collective-permute-start | bytes 147464 | tf_op jit(solution)/shard_map/ppermute | solution.py:49
  117.2 16.3 %collective-permute-start.4 = (f32[64,192]{1,0:T(8,128)}, f32[64,192]{1,0:T(8,128)}, u32[]{:S(2)}, u32[]{:S(2)}) collective-permute-start(f32[64,192]{1,0:T(8,128)} %pad_maximum_fusion.3), channel_id=1, source_target_pairs={{0,2},{1,3},{2,0},{3,1},{4,6},{5,7},{6,4},{7,5},{8,10},{9,11},{10,... | collective-permute-start | bytes 147464 | tf_op jit(solution)/shard_map/ppermute | solution.py:49
  121.5 12.0 %collective-permute-start.3 = (f32[64,192]{1,0:T(8,128)}, f32[64,192]{1,0:T(8,128)}, u32[]{:S(2)}, u32[]{:S(2)}) collective-permute-start(f32[64,192]{1,0:T(8,128)} %pad_maximum_fusion.3), channel_id=1, source_target_pairs={{0,1},{1,2},{2,3},{3,0},{4,5},{5,6},{6,7},{7,4},{8,9},{9,10},{10,1... | collective-permute-start | bytes 147464 | tf_op jit(solution)/shard_map/ppermute | solution.py:49
  123.3 13.0 %copy-start.16 = (f32[128]{0:T(128)S(1)}, f32[128]{0:T(128)}, u32[]{:S(2)}) copy-start(f32[128]{0:T(128)} %copy-done.15) | copy-start | bytes 1540
  127.9 15.7 %all-to-all-start.6 = ((f32[32,16,128]{2,1,0:T(8,128)}), f32[32,16,128]{2,1,0:T(8,128)}, u32[]{:S(2)}, u32[]{:S(2)}) async-start(f32[32,16,128]{2,1,0:T(8,128)} %copy.173), calls=%async_computation.6 | async-start | bytes 524288 | tf_op jit(solution)/shard_map/all_to_all | solution.py:53
  135.6 0.6 copy-start.8
  143.6 21.3 %all-to-all-start.3 = ((f32[32,2,1408]{2,1,0:T(2,128)}), f32[32,2,1408]{2,1,0:T(2,128)}, u32[]{:S(2)}, u32[]{:S(2)}) async-start(f32[32,2,1408]{2,1,0:T(2,128)} %pad_maximum_fusion), calls=%async_computation.3 | async-start | bytes 720896 | tf_op jit(solution)/shard_map/all_to_all | solution.py:53
  153.0 46.7 %collective-permute-start.12 = (bf16[256,1024]{1,0:T(8,128)(2,1)}, bf16[256,1024]{1,0:T(8,128)(2,1)}, u32[]{:S(2)}, u32[]{:S(2)}) collective-permute-start(bf16[256,1024]{1,0:T(8,128)(2,1)} %slice.264), channel_id=1, source_target_pairs={{0,1},{1,2},{2,3},{3,0},{4,5},{5,6},{6,7},{7,4},{8,9},{9,10},{10,1... | collective-permute-start | bytes 1572872 | tf_op jit(solution)/shard_map/ppermute | solution.py:49
  153.8 45.9 %collective-permute-start.13 = (bf16[256,1024]{1,0:T(8,128)(2,1)}, bf16[256,1024]{1,0:T(8,128)(2,1)}, u32[]{:S(2)}, u32[]{:S(2)}) collective-permute-start(bf16[256,1024]{1,0:T(8,128)(2,1)} %slice.265), channel_id=1, source_target_pairs={{0,3},{1,0},{2,1},{3,2},{4,7},{5,4},{6,5},{7,6},{8,11},{9,8},{10,9... | collective-permute-start | bytes 1572872 | tf_op jit(solution)/shard_map/ppermute | solution.py:49
  164.9 7.7 %copy-start.3 = (bf16[32,2,16,128]{3,2,1,0:T(8,128)(2,1)S(1)}, bf16[32,2,16,128]{3,2,1,0:T(8,128)(2,1)}, u32[]{:S(2)}) copy-start(bf16[32,2,16,128]{3,2,1,0:T(8,128)(2,1)} %copy-done.2) | copy-start | bytes 786436
  173.4 9.4 %all-to-all-start.4 = ((f32[4,2,1088]{2,1,0:T(2,128)}), f32[4,2,1088]{2,1,0:T(2,128)}, u32[]{:S(2)}, u32[]{:S(2)}) async-start(f32[4,2,1088]{2,1,0:T(2,128)} %broadcast_in_dim.80), calls=%async_computation.4 | async-start | bytes 73728 | tf_op jit(solution)/shard_map/all_to_all | solution.py:53
  186.2 2.3 %copy-start.11 = (bf16[4,2,1088]{2,1,0:T(2,128)(2,1)S(1)}, bf16[4,2,1088]{2,1,0:T(2,128)(2,1)}, u32[]{:S(2)}) copy-start(bf16[4,2,1088]{2,1,0:T(2,128)(2,1)} %convert.30) | copy-start | bytes 52228
  195.9 15.6 %all-to-all-start.5 = ((f32[4,2,1024]{2,1,0:T(2,128)}), f32[4,2,1024]{2,1,0:T(2,128)}, u32[]{:S(2)}, u32[]{:S(2)}) async-start(f32[4,2,1024]{2,1,0:T(2,128)} %broadcast_in_dim.81), calls=%async_computation.5 | async-start | bytes 65536 | tf_op jit(solution)/shard_map/all_to_all | solution.py:53
  199.8 3.4 %copy-start = (bf16[4096,1024]{1,0:T(8,128)(2,1)S(1)}, bf16[4096,1024]{1,0:T(8,128)(2,1)}, u32[]{:S(2)}) copy-start(bf16[4096,1024]{1,0:T(8,128)(2,1)} %all-gather.2.cloned.1.call-done) | copy-start | bytes 25165828
Sparse Core Ops, SparseCore 0:
  16.2 89.5 all-gather.1

commit v2 on v1

v2 whole, which is shorter than its diff:
```python
import math

import jax
import jax.numpy as jnp
from jax import lax
from jax.experimental import pallas as pl
from jax.experimental.pallas import tpu as pltpu
from jax.sharding import Mesh
from jax.sharding import PartitionSpec as P

HD = 128
HEADS_TP = 8
GROUP = 4
COMP = 256
RANK = 64
LANES = 128
ROLLS = 2
CHIP_COUNT = 32
PIECE = 16
FIRST_ROWS = 24
QKV_ROWS = 24
KEY_ROW = ROLLS * HEADS_TP
STATE_ROW = KEY_ROW + 2 * ROLLS

adapter_scale = 2.0
f32 = jnp.float32
bf16 = jnp.bfloat16
CHIPS = ("y", "z")
DP = ("y", "z", "c")
HIGH = lax.Precision.HIGHEST
VMEM = pl.BlockSpec(memory_space=pltpu.VMEM)
SMEM = pl.BlockSpec(memory_space=pltpu.SMEM)


def nn_dot(a, b):
    return jnp.dot(a, b, preferred_element_type=f32)


def nt_dot(a, b, precision=None):
    return lax.dot_general(
        a, b, (((1,), (1,)), ((), ())), preferred_element_type=f32, precision=precision
    )


def tn_dot(a, b):
    return lax.dot_general(a, b, (((0,), (0,)), ((), ())), preferred_element_type=f32)


def swapped(x):
    return lax.ppermute(x, "c", [(0, 1), (1, 0)])


def shift(x, by, n):
    return lax.ppermute(x, "t", [(i, (i + by) % n) for i in range(n)])


def shifts(x, n):
    return [x] + [shift(x, by, n) for by in range(1, n)]


def exchange(x, axes):
    return lax.all_to_all(x, axes, split_axis=0, concat_axis=0, tiled=True)


def to_all(x, axes):
    return exchange(jnp.broadcast_to(x, (lax.axis_size(axes), *x.shape)), axes)


def together(*xs):
    return lax.optimization_barrier(xs)


def lane_iota(shape):
    return lax.broadcasted_iota(jnp.int32, shape, len(shape) - 1)


def call(kernel, out, specs, args, scratch=(), flops=0, vmem=32):
    moved = sum(a.size * a.dtype.itemsize for a in args)
    outs = out if isinstance(out, tuple) else (out,)
    moved += sum(math.prod(o.shape) * o.dtype.itemsize for o in outs)
    return pl.pallas_call(
        kernel,
        out_shape=out,
        in_specs=specs,
        out_specs=tuple(VMEM for _ in outs) if isinstance(out, tuple) else VMEM,
        scratch_shapes=list(scratch),
        compiler_params=pltpu.CompilerParams(vmem_limit_bytes=vmem << 20),
        cost_estimate=pl.CostEstimate(flops=flops, bytes_accessed=moved, transcendentals=0),
    )(*args)


def shape(*dims, dtype=f32):
    return jax.ShapeDtypeStruct(dims, dtype)


def message_kernel(rewards, prompts, a_ref, b_ref, hidden, out):
    pieces = jnp.concatenate([a_ref[...], b_ref[...]], axis=1)
    out[:, :PIECE, :] = jnp.broadcast_to(pieces, (CHIP_COUNT, PIECE, LANES))
    lane = lane_iota((1, LANES))
    value = jnp.where(lane == 0, rewards[0], jnp.where(lane == 1, rewards[1], 0.0))
    prompt = jnp.where(lane == 0, prompts[0], jnp.where(lane == 1, prompts[1], 0)).astype(f32)
    high = value.astype(bf16).astype(f32)
    mid = (value - high).astype(bf16).astype(f32)
    low = value - high - mid
    tail = jnp.concatenate([high, mid, low, prompt, jnp.zeros((2, LANES), f32)], axis=0)
    for m in range(CHIP_COUNT):
        cut = hidden[:, m * LANES : (m + 1) * LANES].astype(f32)
        out[m, PIECE:, :] = jnp.concatenate([cut, tail], axis=0).astype(bf16)


def spread_qkv(state, gain, first, w_own, w_other, out):
    w_even = jnp.where(first, w_own[...], w_other[...])
    w_odd = jnp.where(first, w_other[...], w_own[...])
    w = jnp.concatenate([w_even, w_odd], axis=0)
    x = state * gain
    x1 = x.astype(bf16)
    rest = x - x1.astype(f32)
    x2 = rest.astype(bf16)
    x3 = (rest - x2.astype(f32)).astype(bf16)
    count = x.shape[0]
    parts = nn_dot(jnp.concatenate([x1, x2, x3], axis=0), w)
    qkv = parts[:count] + parts[count : 2 * count] + parts[2 * count :]

    def put(row, block):
        out[pl.ds(row, CHIP_COUNT, stride=QKV_ROWS), :] = block

    for b in range(ROLLS):
        mine = qkv[b * CHIP_COUNT : (b + 1) * CHIP_COUNT]
        for h in range(HEADS_TP):
            put(b * HEADS_TP + h, mine[:, h * HD : (h + 1) * HD])
        put(KEY_ROW + 2 * b, mine[:, HEADS_TP * HD : (HEADS_TP + 1) * HD])
        put(KEY_ROW + 2 * b + 1, mine[:, (HEADS_TP + 1) * HD :])
        put(STATE_ROW + b, state[b * CHIP_COUNT : (b + 1) * CHIP_COUNT])
    for row in range(STATE_ROW + ROLLS, QKV_ROWS):
        put(row, jnp.zeros((CHIP_COUNT, LANES), f32))


def qkv_first_kernel(place, arrived, gain, w_own, w_other, out, state_out, held):
    held[...] = arrived[...].astype(f32).reshape(CHIP_COUNT * FIRST_ROWS, LANES)
    state = jnp.concatenate(
        [held[pl.ds(PIECE + b, CHIP_COUNT, stride=FIRST_ROWS), :] for b in range(ROLLS)], axis=0
    )
    state_out[...] = state
    spread_qkv(state, gain[...], place[0] == 0, w_own, w_other, out)


def qkv_later_kernel(place, state, gain, w_own, w_other, b_cols, s0, s1, s2, s3, out):
    share = s0[...] + s1[...] + s2[...] + s3[...]
    low = share[:, LANES:]
    now = (
        state[...]
        + share[:, :LANES]
        + adapter_scale * nt_dot(low, b_cols[...], precision=HIGH)
    )
    spread_qkv(now, gain[...], place[0] == 0, w_own, w_other, out)


def attend_kernel(last, lengths, came, cache, before, ab, attended, kv_out, owned_out, held):
    sums = jnp.sum(came[...].reshape(CHIP_COUNT, QKV_ROWS, LANES), axis=0)
    factor = 1.0 / math.sqrt(HD)
    width = CHIP_COUNT * LANES
    rows = []
    lows = []
    kvs = []
    for b in range(ROLLS):
        owned = came[pl.ds(STATE_ROW + b, CHIP_COUNT, stride=QKV_ROWS), :]
        owned_out[b * CHIP_COUNT : (b + 1) * CHIP_COUNT, :] = owned
        total = jnp.sum(jnp.sum(owned * owned, axis=0, keepdims=True), axis=1, keepdims=True)
        scale = lax.rsqrt(total * (1.0 / width) + 1e-05)
        query = sums[b * HEADS_TP : (b + 1) * HEADS_TP] * scale
        fresh = sums[KEY_ROW + 2 * b : KEY_ROW + 2 * b + 2] * scale
        kvs.append(fresh)
        q1 = query.astype(bf16)
        rest = query - q1.astype(f32)
        q2 = rest.astype(bf16)
        q3 = (rest - q2.astype(f32)).astype(bf16)
        keys = cache[b, :, :HD]
        parts = nt_dot(jnp.concatenate([q1, q2, q3], axis=0), keys)
        scores = (parts[:HEADS_TP] + parts[HEADS_TP : 2 * HEADS_TP] + parts[2 * HEADS_TP :]) * factor
        scores = jnp.where(lane_iota(scores.shape) < lengths[b], scores, -1e30)
        newest = [(fresh[0:1], fresh[1:2])]
        if last:
            newest = [(before[2 * b : 2 * b + 1], before[2 * b + 1 : 2 * b + 2])] + newest
        extra = [jnp.sum(query * k, axis=1, keepdims=True) * factor for k, _ in newest]
        top = jnp.max(scores, axis=1, keepdims=True)
        for e in extra:
            top = jnp.maximum(top, e)
        expo = jnp.exp(scores - top)
        total = jnp.sum(expo, axis=1, keepdims=True)
        more = [jnp.exp(e - top) for e in extra]
        for e in more:
            total = total + e
        out = nn_dot((expo / total).astype(bf16), cache[b, :, HD:])
        for e, (_, v) in zip(more, newest):
            out = out + (e / total).astype(bf16).astype(f32) * v
        out = out.astype(bf16)
        rows.append(out)
        if last:
            flat = out.astype(f32)
            lows.append(
                jnp.concatenate([flat[h : h + 1] for h in range(HEADS_TP)], axis=1)
            )
    both = jnp.concatenate([r.astype(f32) for r in rows], axis=0)
    if last:
        low = jnp.concatenate(lows + [jnp.zeros((8 - ROLLS, HEADS_TP * HD), f32)], axis=0)
        low = nn_dot(low.astype(bf16), ab[...])
        attended[...] = jnp.concatenate([both, low], axis=0)
    else:
        attended[...] = both.astype(bf16)
    kv_out[...] = jnp.concatenate(kvs + [jnp.zeros((8 - 2 * ROLLS, LANES), f32)], axis=0)


def attend(last, lengths, came, cache, before, ab):
    att = shape(24, LANES) if last else shape(ROLLS * HEADS_TP, LANES, dtype=bf16)
    return call(
        lambda *refs: attend_kernel(last, *refs),
        (att, shape(8, LANES), shape(ROLLS * CHIP_COUNT, LANES)),
        [SMEM, VMEM, VMEM, VMEM, VMEM],
        (lengths, came, cache, before, ab),
        scratch=[pltpu.VMEM((8, LANES), f32)],
        flops=2 * 32 * 2 * cache.shape[0] * cache.shape[1] * HD,
    )


def close_kernel(place, came, w_own, w_other, ab, out, held):
    rows = ROLLS * HEADS_TP
    held[...] = came[...].astype(f32).reshape(CHIP_COUNT * rows, LANES)
    blocks = []
    for b in range(ROLLS):
        heads = [
            held[pl.ds(b * HEADS_TP + h, CHIP_COUNT, stride=rows), :] for h in range(HEADS_TP)
        ]
        blocks.append(jnp.concatenate(heads, axis=1))
    everyone = jnp.concatenate(blocks, axis=0).astype(bf16)
    first = place[0] == 0
    w_even = jnp.where(first, w_own[...], w_other[...])
    w_odd = jnp.where(first, w_other[...], w_own[...])
    w = jnp.concatenate([w_even, w_odd], axis=0)
    out[:, :LANES] = nt_dot(everyone, w)
    out[:, LANES:] = nn_dot(everyone, ab[...])


def adapter_kernel(
    place, rewards, prompts, live, own, other, rows, upstream, weighted_out, ab_out, part
):
    first = place[0] == 0
    even = jnp.where(first, own[...], other[...])
    odd = jnp.where(first, other[...], own[...])
    ab_out[:, :PIECE, :] = even[:, :PIECE]
    ab_out[:, PIECE:, :] = odd[:, :PIECE]
    lane = lane_iota((CHIP_COUNT, LANES))
    seen = []
    for side in (own, other):
        tail = side[:, PIECE:, :].astype(f32)
        seen.append((tail[:, 2, :] + tail[:, 3, :] + tail[:, 4, :], tail[:, 5, :]))
    count = rows.shape[0]
    index = lax.broadcasted_iota(jnp.int32, (count, 1), 0)
    weight = jnp.zeros((count, 1), f32)
    for b in range(ROLLS):
        total = jnp.zeros((1, 1), f32)
        squares = jnp.zeros((1, 1), f32)
        for value, prompt in seen:
            hit = (prompt == prompts[b].astype(f32)) & (lane < ROLLS)
            value = jnp.where(hit, value, 0.0)
            total = total + jnp.sum(jnp.sum(value, axis=0, keepdims=True), axis=1, keepdims=True)
            value = value * value
            squares = squares + jnp.sum(
                jnp.sum(value, axis=0, keepdims=True), axis=1, keepdims=True
            )
        mean = total / GROUP
        std = jnp.sqrt(jnp.maximum(squares / GROUP - mean * mean, 0.09))
        per_roll = (rewards[b] - mean) / std / live[b].astype(f32)
        slot = index - b * COMP
        inside = (slot >= 0) & (slot < COMP) & (slot < live[b])
        weight = jnp.where(inside, per_roll, weight)
    weighted = (weight * upstream[...].astype(f32)).astype(bf16)
    weighted_out[...] = weighted
    ab = ab_out[...].reshape(2 * CHIP_COUNT * PIECE, LANES)
    low = nn_dot(rows[...], ab)
    back = nn_dot(weighted, ab)
    part[:count, :] = jnp.where(lane_iota((count, LANES)) < RANK, low, back)
    z = place[2]
    each = LANES // (2 * PIECE)
    piece = ab_out[pl.ds(z * each, each), :, :].reshape(LANES, LANES).astype(f32)
    piece = pltpu.roll(piece, RANK, 1)
    part[count:, :] = jnp.where(lane_iota((LANES, LANES)) < RANK, piece, 0.0)


def gradient_kernel(
    place, p0, p1, p2, p3, rows, weighted, low_back, b_cols, kept, given
):
    count = rows.shape[0]
    total = p0[:count, :] + p1[:count, :] + p2[:count, :] + p3[:count, :]
    low_back[...] = total.astype(bf16)
    turned = pltpu.roll(total, RANK, 1).astype(bf16)
    from_y = place[3]
    piece = p0[count:, :]
    for by, p in ((1, p1), (2, p2), (3, p3)):
        piece = jnp.where(from_y == by, p[count:, :], piece)
    b_cols[...] = piece
    a_side = tn_dot(rows[...], turned)
    b_side = tn_dot(weighted[...], turned)
    both = adapter_scale * jnp.where(lane_iota(a_side.shape) < RANK, a_side, b_side)
    both = both.reshape(CHIP_COUNT, 2 * PIECE, LANES)
    even, odd = both[:, :PIECE], both[:, PIECE:]
    first = place[0] == 0
    kept[...] = jnp.where(first, even, odd)
    given[...] = jnp.where(first, odd, even)


def rows_kernel(
    where_ref, own, left, right, far_a, far_b, w_ref, low, b_ref, s0, s1, s2, s3, owned, out, cols
):
    half = far_a.shape[0]
    b_tile = b_ref[...]
    mine = lane_iota(b_tile.shape) >= RANK
    b_tile = jnp.where(mine, b_tile, jnp.zeros_like(b_tile))
    b_turned = pltpu.roll(b_tile.astype(f32), RANK, 1)
    acc = adapter_scale * nt_dot(low[...], b_turned.astype(bf16))
    acc = acc + nt_dot(own[...], w_ref[where_ref[0]])
    acc = acc + nt_dot(left[...], w_ref[where_ref[1]])
    acc = acc + nt_dot(right[...], w_ref[where_ref[3]])
    out[...] = acc
    far = w_ref[where_ref[2]]
    out[:half, :] += nt_dot(far_a[...], far)
    out[half:, :] += nt_dot(far_b[...], far)
    top = ROLLS * HEADS_TP
    low_sum = s0[top:, :] + s1[top:, :] + s2[top:, :] + s3[top:, :]
    got = adapter_scale * nt_dot(low_sum, b_turned, precision=HIGH)
    for k, s in enumerate((s0, s1, s2, s3)):
        flat = [
            jnp.concatenate(
                [s[b * HEADS_TP + h : b * HEADS_TP + h + 1, :] for h in range(HEADS_TP)], axis=1
            )
            for b in range(ROLLS)
        ]
        flat.append(jnp.zeros((8 - ROLLS, HEADS_TP * HD), f32))
        heads = jnp.concatenate(flat, axis=0).astype(bf16)
        got = got + nt_dot(heads, w_ref[where_ref[k]])
    cols[...] = got[:ROLLS, :] + owned[...]


def output_rows(where, own, left, right, far_a, far_b, w, low, b, sent, owned):
    n, width, depth = w.shape
    rows = own.shape[0]
    tile = 256
    tiles = width // tile
    whole = lambda a: pl.BlockSpec(a.shape, lambda j, s: (0, 0))
    return pl.pallas_call(
        rows_kernel,
        out_shape=(shape(rows, width), shape(ROLLS, width)),
        grid_spec=pltpu.PrefetchScalarGridSpec(
            num_scalar_prefetch=1,
            grid=(tiles,),
            in_specs=[
                whole(own),
                whole(left),
                whole(right),
                whole(far_a),
                whole(far_b),
                pl.BlockSpec((n, tile, depth), lambda j, s: (0, j, 0)),
                whole(low),
                pl.BlockSpec((tile, b.shape[1]), lambda j, s: (j, 0)),
                *(whole(s) for s in sent),
                pl.BlockSpec((ROLLS, tile), lambda j, s: (0, s[0] * tiles + j)),
            ],
            out_specs=(
                pl.BlockSpec((rows, tile), lambda j, s: (0, j)),
                pl.BlockSpec((ROLLS, tile), lambda j, s: (0, j)),
            ),
        ),
        compiler_params=pltpu.CompilerParams(vmem_limit_bytes=40 << 20),
        cost_estimate=pl.CostEstimate(
            flops=2 * rows * width * depth * n,
            bytes_accessed=2 * (n * width * depth + n * rows * depth) + 4 * rows * width,
            transcendentals=0,
        ),
    )(where, own, left, right, far_a, far_b, w, low, b, *sent, owned)


def shards(
    hidden,
    attention_norm_gain,
    query_key_value_weight,
    key_value_cache,
    cache_fill_lengths,
    output_weight_frozen,
    adapter_down_transposed,
    adapter_up_matrix,
    attention_rows,
    upstream,
    rewards,
    prompt_group_index,
    completion_live_lengths,
):
    nt = lax.axis_size("t")
    t = lax.axis_index("t")
    y = lax.axis_index("y")
    z = lax.axis_index("z")
    c = lax.axis_index("c")
    m = lax.axis_index(CHIPS)
    width = hidden.shape[1]
    shard_width = width // nt
    cache = key_value_cache[:, :, 0, :]
    place = jnp.stack([c, y, z, lax.rem(t - y + nt, nt)]).astype(jnp.int32)
    where = lax.rem(t - jnp.arange(nt, dtype=jnp.int32) + nt, nt)

    message = call(
        message_kernel,
        shape(CHIP_COUNT, FIRST_ROWS, LANES, dtype=bf16),
        [SMEM, SMEM, VMEM, VMEM, VMEM],
        (
            rewards,
            prompt_group_index,
            adapter_down_transposed[:, 0, :].T,
            adapter_up_matrix[:, 0, :].T,
            hidden,
        ),
    )

    w_cols = output_weight_frozen[0].T
    ny = lax.axis_size("y")
    turned = lax.ppermute(
        w_cols, ("y", "t"), [(a * nt + b, b * nt + a) for a in range(ny) for b in range(nt)]
    )
    w_block = lax.all_gather(turned, DP, axis=0, tiled=True)
    w_block = w_block.reshape(nt, shard_width, w_cols.shape[1])

    left = shift(attention_rows, 1, nt)
    right = shift(attention_rows, nt - 1, nt)
    w_rows = query_key_value_weight[:, 0, :]
    w_rows_other = swapped(w_rows)
    w_cols_other = swapped(w_cols)

    arrived = exchange(message, CHIPS)
    gain = lax.dynamic_slice_in_dim(attention_norm_gain, m * LANES, LANES, 0).astype(f32)[None, :]
    sent, state = call(
        qkv_first_kernel,
        (shape(CHIP_COUNT * QKV_ROWS, LANES), shape(ROLLS * CHIP_COUNT, LANES)),
        [SMEM] + [VMEM] * 4,
        (place, arrived, gain, w_rows, w_rows_other),
        scratch=[pltpu.VMEM((CHIP_COUNT * FIRST_ROWS, LANES), f32)],
    )
    arrived_other = swapped(arrived)
    sent, arrived, arrived_other = together(sent, arrived, arrived_other)
    came = exchange(sent.reshape(CHIP_COUNT, QKV_ROWS, LANES), CHIPS)

    rows = attention_rows.shape[0]
    weighted, ab, part = call(
        adapter_kernel,
        (
            shape(rows, shard_width, dtype=bf16),
            shape(CHIP_COUNT, 2 * PIECE, LANES, dtype=bf16),
            shape(rows + LANES, LANES),
        ),
        [SMEM] * 4 + [VMEM] * 4,
        (
            place,
            rewards,
            prompt_group_index,
            completion_live_lengths,
            arrived,
            arrived_other,
            attention_rows,
            upstream,
        ),
        flops=4 * rows * shard_width * LANES,
    )
    ab = ab.reshape(shard_width, LANES)
    parts = shifts(part, nt)

    nothing = jnp.zeros((8, LANES), f32)
    attended, kv, _ = attend(
        False, cache_fill_lengths, came.reshape(-1, LANES), cache, nothing, ab
    )
    attended, *parts = together(attended, *parts)
    everyone = to_all(attended, CHIPS)

    low_back, b_cols, kept, given = call(
        gradient_kernel,
        (
            shape(rows, LANES, dtype=bf16),
            shape(LANES, LANES),
            shape(CHIP_COUNT, PIECE, LANES),
            shape(CHIP_COUNT, PIECE, LANES),
        ),
        [SMEM] + [VMEM] * 6,
        (place, *parts, attention_rows, weighted),
        flops=4 * rows * shard_width * LANES,
    )

    share = call(
        close_kernel,
        shape(ROLLS * CHIP_COUNT, 2 * LANES),
        [SMEM] + [VMEM] * 4,
        (place, everyone, w_cols, w_cols_other, ab),
        scratch=[pltpu.VMEM((CHIP_COUNT * ROLLS * HEADS_TP, LANES), f32)],
    )
    share, given, kept = together(share, given, kept)
    shares = shifts(share, nt)
    kept = kept + swapped(given)
    summed = exchange(kept, CHIPS)

    sent = call(
        qkv_later_kernel,
        shape(CHIP_COUNT * QKV_ROWS, LANES),
        [SMEM] + [VMEM] * 9,
        (place, state, gain, w_rows, w_rows_other, b_cols, *shares),
    )
    sent, left, right = together(sent, left, right)
    came = exchange(sent.reshape(CHIP_COUNT, QKV_ROWS, LANES), CHIPS)
    half = rows // 2
    far_a = shift(left[:half], 1, nt)
    far_b = shift(right[half:], nt - 1, nt)
    summed = summed.sum(axis=0)

    attended, _, owned = attend(True, cache_fill_lengths, came.reshape(-1, LANES), cache, kv, ab)
    adapted, own_cols = output_rows(
        where,
        attention_rows,
        left,
        right,
        far_a,
        far_b,
        w_block,
        low_back,
        ab,
        shifts(attended, nt),
        owned.reshape(ROLLS, width),
    )
    decoded = to_all(own_cols, "t").transpose(1, 0, 2).reshape(ROLLS, width)
    grad_a = summed[:, :RANK].T[:, None, :]
    grad_b = summed[:, RANK:].T[:, None, :]
    return (decoded, adapted, grad_a, grad_b)


def solution(mesh):
    split = Mesh(mesh.devices.reshape(4, 8, 2, 4), ("y", "z", "c", "t"))
    placed = (
        P(DP, None),
        P(),
        P(DP, "t", None),
        P(DP, None, "t", None),
        P(DP),
        P("t", None, DP),
        P(None, "t", DP),
        P(None, "t", DP),
        P(DP, "t"),
        P(DP, "t"),
        P(DP),
        P(DP),
        P(DP),
    )
    return jax.shard_map(
        shards,
        mesh=split,
        in_specs=placed,
        out_specs=(P(DP, None), P(DP, "t"), P(None, "t", DP), P(None, "t", DP)),
        check_vma=False,
    )
```

time: 223 us -> 210 us (0.942)
  waiting for transfers between devices: 34 us -> 66.2 us
  matrix products: 31.4 us -> 0 us
  other arithmetic: 30 us -> 2.57 us
  Pallas kernels: 8.36 us -> 25.2 us
    dot_general x22 -> x0, matrix products: 31.4 us -> none  [the longest x7 12.8 us: nt_dot(): lax.dot_general(a, b, (((1,), (1,)), ((), ())), preferred_element_type=f3...]
    ppermute x10 -> x13, waiting for transfers between devices: 8.98 us -> 29.8 us  [shift(): return lax.ppermute(x, 't', [(i, (i + by) % n) for i in range(n)])]
    pallas_call x1 -> x9, Pallas kernels: 8.36 us -> 25.2 us  [the longest x8 13.6 us: call(): pl.pallas_call(kernel, out_shape=out, in_specs=specs, out_specs=tuple((VM...]
    unnamed x45 -> x73, local copies, waits for them, and re-layouts: 10.5 us -> 26.8 us
    all_to_all x7 -> x6, waiting for transfers between devices: 18.8 us -> 31.4 us  [exchange(): return lax.all_to_all(x, axes, split_axis=0, concat_axis=0, tiled=True)]
    reduce_sum x9 -> x1, other arithmetic: 8.28 us -> 0.99 us  [shards(): summed = summed.sum(axis=0)]
    reshape x4 -> x1, local copies, waits for them, and re-layouts: 7.12 us -> 0.02 us  [shards(): owned.reshape(ROLLS, width)]
    concatenate x9 -> x0, other arithmetic: 6.46 us -> none  [the longest x1 1.9 us: shards(): jnp.concatenate([partial_value, state.reshape(chips, rolls, cols)], axis=2)]
  transfers between devices with their start and end apart: 23 -> 25, of which waited for: 7 -> 12; matrix products, arithmetic and copies ran while one was open for 39% -> 4% of each run, Pallas kernels for 4% -> 7%
where the time goes in v2:
time: 210 us; the launch traced here: 208 us
  starting transfers between devices  67.4 us (32%)
  waiting for transfers between devices  66.2 us (32%)
  local copies, waits for them, and re-layouts  32.5 us (15%)
  Pallas kernels  25.2 us (12%)
  between operations  14.3 us (7%)
  other arithmetic  2.57 us (1%)
    all_to_all x6, starting transfers between devices, exchange(): return lax.all_to_all(x, axes, split_axis=0, concat_axis=0, tiled=True)  50.2 us
    all_to_all x6, waiting for transfers between devices, exchange(): return lax.all_to_all(x, axes, split_axis=0, concat_axis=0, tiled=True)  31.4 us
    ppermute x13, waiting for transfers between devices, shift(): return lax.ppermute(x, 't', [(i, (i + by) % n) for i in range(n)])  29.8 us
    unnamed x73, local copies, waits for them, and re-layouts  26.8 us
    pallas_call x8, Pallas kernels, call(): pl.pallas_call(kernel, out_shape=out, in_specs=specs, out_specs=tuple((VM...  13.6 us
    ppermute x13, starting transfers between devices, shift(): return lax.ppermute(x, 't', [(i, (i + by) % n) for i in range(n)])  13.5 us
    pallas_call x1, Pallas kernels, output_rows(): pl.pallas_call(rows_kernel, out_shape=(shape(rows, width), shape(ROLLS, w...  11.6 us
    ppermute x1, waiting for transfers between devices, shards(): lax.ppermute(w_cols, ('y', 't'), [(a * nt + b, b * nt + a) for a in range...  4.95 us
  transfers between devices with their start and end apart: 25, of which 12 were waited for; matrix products, arithmetic and copies ran while one was open for 4% of the time, Pallas kernels for 7%

profile of v2, /device:TPU:8, one launch (start us, length us, event | category | flops | bytes accessed | tf_op | source)
XLA Modules:
  0.0 208.2 jit_solution(65980260475616504)
XLA Ops:
  7.2 3.4 %collective-permute-start.13 = (bf16[64,1024]{1,0:T(8,128)(2,1)}, bf16[64,1024]{1,0:T(8,128)(2,1)S(1)}, u32[]{:S(2)}, u32[]{:S(2)}) collective-permute-start(bf16[64,1024]{1,0:T(8,128)(2,1)} %bitcast.46), channel_id=1, source_target_pairs={{0,0},{1,64},{2,128},{3,192},{64,1},{65,65},{66,129},{67,193},{128... | collective-permute-start | bytes 393224 | tf_op jit(solution)/shard_map/ppermute | solution.py:423
  10.6 4.9 %collective-permute-done.13 = bf16[64,1024]{1,0:T(8,128)(2,1)S(1)} collective-permute-done((bf16[64,1024]{1,0:T(8,128)(2,1)}, bf16[64,1024]{1,0:T(8,128)(2,1)S(1)}, u32[]{:S(2)}, u32[]{:S(2)}) %collective-permute-start.13) | collective-permute-done | bytes 131104 | tf_op jit(solution)/shard_map/ppermute | solution.py:423
  19.7 1.3 shard_map.156
  21.0 16.9 %all-to-all-start = ((bf16[32,24,128]{2,1,0:T(8,128)(2,1)}), bf16[32,24,128]{2,1,0:T(8,128)(2,1)S(1)}, u32[]{:S(2)}, u32[]{:S(2)}) async-start(bf16[32,24,128]{2,1,0:T(8,128)(2,1)} %shard_map.156), calls=%async_computation | async-start | bytes 393216 | tf_op jit(solution)/shard_map/all_to_all | solution.py:62
  38.0 10.6 %all-to-all-done.arrived.own = bf16[32,24,128]{2,1,0:T(8,128)(2,1)S(1)} async-done(((bf16[32,24,128]{2,1,0:T(8,128)(2,1)}), bf16[32,24,128]{2,1,0:T(8,128)(2,1)S(1)}, u32[]{:S(2)}, u32[]{:S(2)}) %all-to-all-start) | async-done | bytes 196640 | tf_op jit(solution)/shard_map/all_to_all | solution.py:62
  49.4 0.9 copy-done.8
  50.3 0.8 shard_map.157
  52.5 5.8 %all-to-all-start.1 = ((f32[32,24,128]{2,1,0:T(8,128)}), f32[32,24,128]{2,1,0:T(8,128)}, u32[]{:S(2)}, u32[]{:S(2)}) async-start(f32[32,24,128]{2,1,0:T(8,128)} %bitcast.45), calls=%async_computation.1 | async-start | bytes 786432 | tf_op jit(solution)/shard_map/all_to_all | solution.py:62
  58.4 3.2 %collective-permute-start.10 = (bf16[512,1024]{1,0:T(8,128)(2,1)S(1)}, bf16[512,1024]{1,0:T(8,128)(2,1)}, u32[]{:S(2)}, u32[]{:S(2)}) collective-permute-start(bf16[512,1024]{1,0:T(8,128)(2,1)S(1)} %copy-done.1), channel_id=1, source_target_pairs={{0,3},{1,0},{2,1},{3,2},{4,7},{5,4},{6,5},{7,6},{8,11},{9,8},{10,9... | collective-permute-start | bytes 3145736 | tf_op jit(solution)/shard_map/ppermute | solution.py:54
  61.6 0.9 copy-done.3
  62.6 1.2 copy-done.5
  65.7 2.6 %shard_map.158 = (bf16[512,1024]{1,0:T(8,128)(2,1)S(1)}, bf16[32,32,128]{2,1,0:T(8,128)(2,1)S(1)}, f32[640,128]{1,0:T(8,128)}) custom-call(s32[4]{0:T(128)S(1)} %pad_add_fusion.place, f32[2]{0:T(128)S(1)} %copy-done.27, s32[2]{0:T(128)S(1)} %copy-done.29, s32[2]{0:T(128)S(1)} %copy-done.30, bf16[32,24,128]{2,1,0:T(8,128)(2,1)S(1)} %copy-done.3, ...), custom_call_target="tpu_custom_call" | custom-call | flops 268435456 | bytes 4128808 | tf_op jit(solution)/shard_map/pallas_call | solution.py:81
  68.4 1.0 copy-done.6
  69.4 1.0 collective-permute-start.3
  70.3 1.1 collective-permute-start.2
  71.4 0.8 all-to-all-done.1
  72.2 2.3 %shard_map.159 = (bf16[16,128]{1,0:T(8,128)(2,1)S(1)}, f32[8,128]{1,0:T(8,128)S(1)}, f32[64,128]{1,0:T(8,128)}) custom-call(s32[2]{0:T(128)S(1)} %copy-done.25, f32[768,128]{1,0:T(8,128)} %bitcast.11.refs_1_, bf16[2,2048,256]{2,1,0:T(8,128)(2,1)S(1)} %bitcast.35, f32[8,128]{1,0:T(8,128)S(1)} %broadcast_in_dim.22.refs_3_, bf16[1024,128]{1,0:T(8,128)(2,1)S(1)} %bitcast.37), custom_call_target="tpu_custom_call" | custom-call | flops 67108864 | bytes 2797576 | tf_op jit(solution)/shard_map/pallas_call | solution.py:81
  74.5 23.8 %collective-permute-done.4.p3 = f32[640,128]{1,0:T(8,128)} collective-permute-done((f32[640,128]{1,0:T(8,128)}, f32[640,128]{1,0:T(8,128)}, u32[]{:S(2)}, u32[]{:S(2)}) %collective-permute-start.4) | collective-permute-done | bytes 327712 | tf_op jit(solution)/shard_map/ppermute | solution.py:54
  99.7 9.9 %all-to-all-start.2 = ((bf16[32,16,128]{2,1,0:T(8,128)(2,1)}), bf16[32,16,128]{2,1,0:T(8,128)(2,1)S(1)}, u32[]{:S(2)}, u32[]{:S(2)}) async-start(bf16[32,16,128]{2,1,0:T(8,128)(2,1)} %broadcast_in_dim.23), calls=%async_computation.2 | async-start | bytes 262144 | tf_op jit(solution)/shard_map/all_to_all | solution.py:62
  109.7 1.2 copy-done.7
  110.9 2.1 %shard_map.160 = (bf16[512,128]{1,0:T(8,128)(2,1)S(1)}, f32[128,128]{1,0:T(8,128)S(1)}, f32[32,16,128]{2,1,0:T(8,128)S(1)}, f32[32,16,128]{2,1,0:T(8,128)S(1)}) custom-call(s32[4]{0:T(128)S(1)} %pad_add_fusion.place, f32[640,128]{1,0:T(8,128)} %get-tuple-element.41.p0, f32[640,128]{1,0:T(8,128)} %collective-permute-done.2.p1, ...), custom_call_target="tpu_custom_call" | custom-call | flops 268435456 | bytes 4128784 | tf_op jit(solution)/shard_map/pallas_call | solution.py:81
  116.4 2.4 %all-to-all-done.2.came = bf16[32,16,128]{2,1,0:T(8,128)(2,1)S(1)} async-done(((bf16[32,16,128]{2,1,0:T(8,128)(2,1)}), bf16[32,16,128]{2,1,0:T(8,128)(2,1)S(1)}, u32[]{:S(2)}, u32[]{:S(2)}) %all-to-all-start.2) | async-done | bytes 131104 | tf_op jit(solution)/shard_map/all_to_all | solution.py:62
  118.8 0.9 copy-done.15
  119.7 0.9 copy-done.17
  121.4 3.1 %collective-permute-start.8 = (f32[64,256]{1,0:T(8,128)S(1)}, f32[64,256]{1,0:T(8,128)S(1)}, u32[]{:S(2)}, u32[]{:S(2)}) collective-permute-start(f32[64,256]{1,0:T(8,128)S(1)} %shard_map.161.s0), channel_id=1, source_target_pairs={{0,3},{1,0},{2,1},{3,2},{4,7},{5,4},{6,5},{7,6},{8,11},{9,8},{10,9... | collective-permute-start | bytes 196616 | tf_op jit(solution)/shard_map/ppermute | solution.py:54
  124.5 1.0 collective-permute-start.6
  125.4 1.6 collective-permute-done.8.s3
  127.0 3.4 %collective-permute-done.7.s2 = f32[64,256]{1,0:T(8,128)S(1)} collective-permute-done((f32[64,256]{1,0:T(8,128)S(1)}, f32[64,256]{1,0:T(8,128)S(1)}, u32[]{:S(2)}, u32[]{:S(2)}) %collective-permute-start.7) | collective-permute-done | bytes 65568 | tf_op jit(solution)/shard_map/ppermute | solution.py:54
  130.7 0.9 copy-done.9
  131.6 0.9 copy-done.11
  132.5 0.8 copy-done.19
  134.1 1.2 shard_map.162
  136.1 8.0 %all-to-all-start.3 = ((f32[32,24,128]{2,1,0:T(8,128)}), f32[32,24,128]{2,1,0:T(8,128)}, u32[]{:S(2)}, u32[]{:S(2)}) async-start(f32[32,24,128]{2,1,0:T(8,128)} %bitcast.41), calls=%async_computation.3 | async-start | bytes 786432 | tf_op jit(solution)/shard_map/all_to_all | solution.py:62
  144.2 1.9 slice.12
  146.1 1.9 slice.13
  148.0 0.9 collective-permute-start.12
  148.8 1.2 collective-permute-start.11
  150.8 6.7 %all-to-all-done.3 = f32[32,24,128]{2,1,0:T(8,128)} async-done(((f32[32,24,128]{2,1,0:T(8,128)}), f32[32,24,128]{2,1,0:T(8,128)}, u32[]{:S(2)}, u32[]{:S(2)}) %all-to-all-start.3) | async-done | bytes 393248 | tf_op jit(solution)/shard_map/all_to_all | solution.py:62
  157.5 6.3 %all-to-all-start.5 = ((f32[32,16,128]{2,1,0:T(8,128)}), f32[32,16,128]{2,1,0:T(8,128)}, u32[]{:S(2)}, u32[]{:S(2)}) async-start(f32[32,16,128]{2,1,0:T(8,128)} %add.19), calls=%async_computation.5 | async-start | bytes 524288 | tf_op jit(solution)/shard_map/all_to_all | solution.py:62
  163.8 2.4 %shard_map.163 = (f32[24,128]{1,0:T(8,128)S(1)}, f32[8,128]{1,0:T(8,128)}, f32[64,128]{1,0:T(8,128)S(1)}) custom-call(s32[2]{0:T(128)S(1)} %copy-done.25, f32[768,128]{1,0:T(8,128)} %bitcast.19.refs_1_, bf16[2,2048,256]{2,1,0:T(8,128)(2,1)S(1)} %bitcast.36, f32[8,128]{1,0:T(8,128)S(1)} %get-tuple-element.55.refs_3_, bf16[1024,128]{1,0:T(8,128)(2,1)S(1)} %bitcast.39), custom_call_target="tpu_custom_call" | custom-call | flops 67108864 | bytes 2805768 | tf_op jit(solution)/shard_map/pallas_call | solution.py:81
  167.3 0.9 collective-permute-start.14
  168.3 6.2 %all-to-all-done.5 = f32[32,16,128]{2,1,0:T(8,128)} async-done(((f32[32,16,128]{2,1,0:T(8,128)}), f32[32,16,128]{2,1,0:T(8,128)}, u32[]{:S(2)}, u32[]{:S(2)}) %all-to-all-start.5) | async-done | bytes 262176 | tf_op jit(solution)/shard_map/all_to_all | solution.py:62
  174.5 1.0 reduce_sum.9
  175.6 3.4 %copy-done.31 = bf16[4096,1024]{1,0:T(8,128)(2,1)S(1)} copy-done((bf16[4096,1024]{1,0:T(8,128)(2,1)S(1)}, bf16[4096,1024]{1,0:T(8,128)(2,1)}, u32[]{:S(2)}) %copy-start.31) | copy-done | bytes 8388632
  178.9 0.9 copy-done.34
  179.8 11.6 %shard_map.164 = (f32[512,1024]{1,0:T(8,128)}, f32[2,1024]{1,0:T(2,128)S(1)}) custom-call(s32[4]{0:T(128)S(1)} %compare_select_fusion.where_ref, bf16[512,1024]{1,0:T(8,128)(2,1)S(1)} %copy-done.1, bf16[512,1024]{1,0:T(8,128)(2,1)} %collective-permute-done.9.left, bf16[512,1024]{1,0:T(8,128)(2,1)} %collective-permute-done.10.right, ...), custom_call_target="tpu_custom_call" | custom-call | flops 4294967296 | bytes 14680064 | tf_op jit(solution)/shard_map/pallas_call | solution.py:349
  192.1 3.3 %all-to-all-start.4 = ((f32[4,2,1024]{2,1,0:T(2,128)}), f32[4,2,1024]{2,1,0:T(2,128)S(1)}, u32[]{:S(2)}, u32[]{:S(2)}) async-start(f32[4,2,1024]{2,1,0:T(2,128)} %broadcast_in_dim.24), calls=%async_computation.4 | async-start | bytes 65536 | tf_op jit(solution)/shard_map/all_to_all | solution.py:62
  196.0 4.7 %all-to-all-done.4 = f32[4,2,1024]{2,1,0:T(2,128)S(1)} async-done(((f32[4,2,1024]{2,1,0:T(2,128)}), f32[4,2,1024]{2,1,0:T(2,128)S(1)}, u32[]{:S(2)}, u32[]{:S(2)}) %all-to-all-start.4) | async-done | bytes 32800 | tf_op jit(solution)/shard_map/all_to_all | solution.py:62
  (97 shorter events, 19.8 us)
Async XLA Ops:
  7.2 51.1 %copy-start.1 = (bf16[512,1024]{1,0:T(8,128)(2,1)S(1)}, bf16[512,1024]{1,0:T(8,128)(2,1)}, u32[]{:S(2)}) copy-start(bf16[512,1024]{1,0:T(8,128)(2,1)} %own.1) | copy-start | bytes 3145732
  7.2 168.4 %all-gather.2.cloned.1.call-start = ((), (), s32[]{:S(2)}) async-start(), calls=%async_computation.6 | async-start | bytes 8519680 | tf_op jit(solution)/shard_map/all_gather | solution.py:426
  7.2 8.4 %collective-permute-start.13 = (bf16[64,1024]{1,0:T(8,128)(2,1)}, bf16[64,1024]{1,0:T(8,128)(2,1)S(1)}, u32[]{:S(2)}, u32[]{:S(2)}) collective-permute-start(bf16[64,1024]{1,0:T(8,128)(2,1)} %bitcast.46), channel_id=1, source_target_pairs={{0,0},{1,64},{2,128},{3,192},{64,1},{65,65},{66,129},{67,193},{128... | collective-permute-start | bytes 393224 | tf_op jit(solution)/shard_map/ppermute | solution.py:423
  16.3 0.7 copy-start.22
  21.0 51.3 %copy-start = (bf16[2,2048,1,256]{3,1,2,0:T(8,128)(2,1)S(1)}, bf16[2,2048,1,256]{3,1,2,0:T(8,128)(2,1)}, u32[]{:S(2)}) copy-start(bf16[2,2048,1,256]{3,1,2,0:T(8,128)(2,1)} %param.16) | copy-start | bytes 6291460
  21.0 27.6 %all-to-all-start = ((bf16[32,24,128]{2,1,0:T(8,128)(2,1)}), bf16[32,24,128]{2,1,0:T(8,128)(2,1)S(1)}, u32[]{:S(2)}, u32[]{:S(2)}) async-start(bf16[32,24,128]{2,1,0:T(8,128)(2,1)} %shard_map.156), calls=%async_computation | async-start | bytes 393216 | tf_op jit(solution)/shard_map/all_to_all | solution.py:62
  37.9 11.5 %collective-permute-start = (bf16[64,1280]{1,0:T(8,128)(2,1)}, bf16[64,1280]{1,0:T(8,128)(2,1)S(1)}, u32[]{:S(2)}, u32[]{:S(2)}) collective-permute-start(bf16[64,1280]{1,0:T(8,128)(2,1)} %bitcast.42), channel_id=1, source_target_pairs={{0,4},{4,0},{1,5},{5,1},{2,6},{6,2},{3,7},{7,3},{8,12},{12,8},{9,1... | collective-permute-start | bytes 491528 | tf_op jit(solution)/shard_map/ppermute | solution.py:50
  48.5 9.9 %copy-start.2 = (bf16[32,24,128]{2,1,0:T(8,128)(2,1)}, bf16[32,24,128]{2,1,0:T(8,128)(2,1)S(1)}, u32[]{:S(2)}) copy-start(bf16[32,24,128]{2,1,0:T(8,128)(2,1)S(1)} %all-to-all-done.arrived.own) | copy-start | bytes 589828
  48.5 3.9 %collective-permute-start.1 = (bf16[32,24,128]{2,1,0:T(8,128)(2,1)S(1)}, bf16[32,24,128]{2,1,0:T(8,128)(2,1)}, u32[]{:S(2)}, u32[]{:S(2)}) collective-permute-start(bf16[32,24,128]{2,1,0:T(8,128)(2,1)S(1)} %all-to-all-done.arrived.own), channel_id=1, source_target_pairs={{0,4},{4,0},{1,5},{5,1},{2,6},{6,2},{3,7},{7,3},{8,12},{12,8},{9,1... | collective-permute-start | bytes 589832 | tf_op jit(solution)/shard_map/ppermute | solution.py:50
  49.4 0.9 copy-start.8
  50.3 8.1 %copy-start.10 = (bf16[64,1280]{1,0:T(8,128)(2,1)}, bf16[64,1280]{1,0:T(8,128)(2,1)S(1)}, u32[]{:S(2)}) copy-start(bf16[64,1280]{1,0:T(8,128)(2,1)S(1)} %collective-permute-done.w_other) | copy-start | bytes 491524
  51.1 0.7 copy-start.12
  52.5 19.8 %all-to-all-start.1 = ((f32[32,24,128]{2,1,0:T(8,128)}), f32[32,24,128]{2,1,0:T(8,128)}, u32[]{:S(2)}, u32[]{:S(2)}) async-start(f32[32,24,128]{2,1,0:T(8,128)} %bitcast.45), calls=%async_computation.1 | async-start | bytes 786432 | tf_op jit(solution)/shard_map/all_to_all | solution.py:62
  58.3 77.8 %collective-permute-start.9 = (bf16[512,1024]{1,0:T(8,128)(2,1)S(1)}, bf16[512,1024]{1,0:T(8,128)(2,1)}, u32[]{:S(2)}, u32[]{:S(2)}) collective-permute-start(bf16[512,1024]{1,0:T(8,128)(2,1)S(1)} %copy-done.1), channel_id=1, source_target_pairs={{0,1},{1,2},{2,3},{3,0},{4,5},{5,6},{6,7},{7,4},{8,9},{9,10},{10,1... | collective-permute-start | bytes 3145736 | tf_op jit(solution)/shard_map/ppermute | solution.py:54
  58.4 77.6 %collective-permute-start.10 = (bf16[512,1024]{1,0:T(8,128)(2,1)S(1)}, bf16[512,1024]{1,0:T(8,128)(2,1)}, u32[]{:S(2)}, u32[]{:S(2)}) collective-permute-start(bf16[512,1024]{1,0:T(8,128)(2,1)S(1)} %copy-done.1), channel_id=1, source_target_pairs={{0,3},{1,0},{2,1},{3,2},{4,7},{5,4},{6,5},{7,6},{8,11},{9,8},{10,9... | collective-permute-start | bytes 3145736 | tf_op jit(solution)/shard_map/ppermute | solution.py:54
  61.6 0.9 copy-start.3
  62.6 1.2 copy-start.5
  65.7 6.5 %copy-start.25 = (s32[2]{0:T(128)S(1)}, s32[2]{0:T(128)}, u32[]{:S(2)}) copy-start(s32[2]{0:T(128)} %refs_0_.3) | copy-start | bytes 28
  68.4 1.0 copy-start.6
  69.4 28.9 %collective-permute-start.4 = (f32[640,128]{1,0:T(8,128)}, f32[640,128]{1,0:T(8,128)}, u32[]{:S(2)}, u32[]{:S(2)}) collective-permute-start(f32[640,128]{1,0:T(8,128)} %get-tuple-element.41.p0), channel_id=1, source_target_pairs={{0,3},{1,0},{2,1},{3,2},{4,7},{5,4},{6,5},{7,6},{8,11},{9,8},{10,9... | collective-permute-start | bytes 983048 | tf_op jit(solution)/shard_map/ppermute | solution.py:54
  69.4 28.9 %collective-permute-start.3 = (f32[640,128]{1,0:T(8,128)}, f32[640,128]{1,0:T(8,128)}, u32[]{:S(2)}, u32[]{:S(2)}) collective-permute-start(f32[640,128]{1,0:T(8,128)} %get-tuple-element.41.p0), channel_id=1, source_target_pairs={{0,2},{1,3},{2,0},{3,1},{4,6},{5,7},{6,4},{7,5},{8,10},{9,11},{10,... | collective-permute-start | bytes 983048 | tf_op jit(solution)/shard_map/ppermute | solution.py:54
  70.3 28.7 %collective-permute-start.2 = (f32[640,128]{1,0:T(8,128)}, f32[640,128]{1,0:T(8,128)}, u32[]{:S(2)}, u32[]{:S(2)}) collective-permute-start(f32[640,128]{1,0:T(8,128)} %get-tuple-element.41.p0), channel_id=1, source_target_pairs={{0,1},{1,2},{2,3},{3,0},{4,5},{5,6},{6,7},{7,4},{8,9},{9,10},{10,1... | collective-permute-start | bytes 983048 | tf_op jit(solution)/shard_map/ppermute | solution.py:54
  99.7 19.1 %all-to-all-start.2 = ((bf16[32,16,128]{2,1,0:T(8,128)(2,1)}), bf16[32,16,128]{2,1,0:T(8,128)(2,1)S(1)}, u32[]{:S(2)}, u32[]{:S(2)}) async-start(bf16[32,16,128]{2,1,0:T(8,128)(2,1)} %broadcast_in_dim.23), calls=%async_computation.2 | async-start | bytes 262144 | tf_op jit(solution)/shard_map/all_to_all | solution.py:62
  109.6 6.1 %collective-permute-start.5 = (bf16[64,1024]{1,0:T(8,128)(2,1)}, bf16[64,1024]{1,0:T(8,128)(2,1)S(1)}, u32[]{:S(2)}, u32[]{:S(2)}) collective-permute-start(bf16[64,1024]{1,0:T(8,128)(2,1)} %bitcast.47), channel_id=1, source_target_pairs={{0,4},{4,0},{1,5},{5,1},{2,6},{6,2},{3,7},{7,3},{8,12},{12,8},{9,1... | collective-permute-start | bytes 393224 | tf_op jit(solution)/shard_map/ppermute | solution.py:50
  109.7 1.2 copy-start.7
  113.0 0.7 copy-start.13
  118.8 0.9 copy-start.15
  119.7 0.9 copy-start.17
  121.4 5.6 %collective-permute-start.8 = (f32[64,256]{1,0:T(8,128)S(1)}, f32[64,256]{1,0:T(8,128)S(1)}, u32[]{:S(2)}, u32[]{:S(2)}) collective-permute-start(f32[64,256]{1,0:T(8,128)S(1)} %shard_map.161.s0), channel_id=1, source_target_pairs={{0,3},{1,0},{2,1},{3,2},{4,7},{5,4},{6,5},{7,6},{8,11},{9,8},{10,9... | collective-permute-start | bytes 196616 | tf_op jit(solution)/shard_map/ppermute | solution.py:54
  124.5 5.9 %collective-permute-start.7 = (f32[64,256]{1,0:T(8,128)S(1)}, f32[64,256]{1,0:T(8,128)S(1)}, u32[]{:S(2)}, u32[]{:S(2)}) collective-permute-start(f32[64,256]{1,0:T(8,128)S(1)} %shard_map.161.s0), channel_id=1, source_target_pairs={{0,2},{1,3},{2,0},{3,1},{4,6},{5,7},{6,4},{7,5},{8,10},{9,11},{10,... | collective-permute-start | bytes 196616 | tf_op jit(solution)/shard_map/ppermute | solution.py:54
  124.5 6.2 %collective-permute-start.6 = (f32[64,256]{1,0:T(8,128)S(1)}, f32[64,256]{1,0:T(8,128)S(1)}, u32[]{:S(2)}, u32[]{:S(2)}) collective-permute-start(f32[64,256]{1,0:T(8,128)S(1)} %shard_map.161.s0), channel_id=1, source_target_pairs={{0,1},{1,2},{2,3},{3,0},{4,5},{5,6},{6,7},{7,4},{8,9},{9,10},{10,1... | collective-permute-start | bytes 196616 | tf_op jit(solution)/shard_map/ppermute | solution.py:54
  130.7 0.9 copy-start.9
  131.6 0.9 copy-start.11
  132.5 0.8 copy-start.19
  133.3 0.8 copy-start.21
  135.3 0.7 copy-start.4
  136.1 21.4 %all-to-all-start.3 = ((f32[32,24,128]{2,1,0:T(8,128)}), f32[32,24,128]{2,1,0:T(8,128)}, u32[]{:S(2)}, u32[]{:S(2)}) async-start(f32[32,24,128]{2,1,0:T(8,128)} %bitcast.41), calls=%async_computation.3 | async-start | bytes 786432 | tf_op jit(solution)/shard_map/all_to_all | solution.py:62
  144.1 5.9 %copy-start.14 = (f32[32,16,128]{2,1,0:T(8,128)S(1)}, f32[32,16,128]{2,1,0:T(8,128)}, u32[]{:S(2)}) copy-start(f32[32,16,128]{2,1,0:T(8,128)} %copy-done.13) | copy-start | bytes 786436
  144.1 5.9 %collective-permute-start.17 = (f32[32,16,128]{2,1,0:T(8,128)}, f32[32,16,128]{2,1,0:T(8,128)S(1)}, u32[]{:S(2)}, u32[]{:S(2)}) collective-permute-start(f32[32,16,128]{2,1,0:T(8,128)} %copy-done.32), channel_id=1, source_target_pairs={{0,4},{4,0},{1,5},{5,1},{2,6},{6,2},{3,7},{7,3},{8,12},{12,8},{9,1... | collective-permute-start | bytes 786440 | tf_op jit(solution)/shard_map/ppermute | solution.py:50
  148.0 27.5 %collective-permute-start.12 = (bf16[256,1024]{1,0:T(8,128)(2,1)}, bf16[256,1024]{1,0:T(8,128)(2,1)}, u32[]{:S(2)}, u32[]{:S(2)}) collective-permute-start(bf16[256,1024]{1,0:T(8,128)(2,1)} %slice.13), channel_id=1, source_target_pairs={{0,3},{1,0},{2,1},{3,2},{4,7},{5,4},{6,5},{7,6},{8,11},{9,8},{10,9... | collective-permute-start | bytes 1572872 | tf_op jit(solution)/shard_map/ppermute | solution.py:54
  148.8 26.6 %collective-permute-start.11 = (bf16[256,1024]{1,0:T(8,128)(2,1)}, bf16[256,1024]{1,0:T(8,128)(2,1)}, u32[]{:S(2)}, u32[]{:S(2)}) collective-permute-start(bf16[256,1024]{1,0:T(8,128)(2,1)} %slice.12), channel_id=1, source_target_pairs={{0,1},{1,2},{2,3},{3,0},{4,5},{5,6},{6,7},{7,4},{8,9},{9,10},{10,1... | collective-permute-start | bytes 1572872 | tf_op jit(solution)/shard_map/ppermute | solution.py:54
  157.5 17.0 %all-to-all-start.5 = ((f32[32,16,128]{2,1,0:T(8,128)}), f32[32,16,128]{2,1,0:T(8,128)}, u32[]{:S(2)}, u32[]{:S(2)}) async-start(f32[32,16,128]{2,1,0:T(8,128)} %add.19), calls=%async_computation.5 | async-start | bytes 524288 | tf_op jit(solution)/shard_map/all_to_all | solution.py:62
  166.2 9.3 %collective-permute-start.16 = (f32[24,128]{1,0:T(8,128)S(1)}, f32[24,128]{1,0:T(8,128)S(1)}, u32[]{:S(2)}, u32[]{:S(2)}) collective-permute-start(f32[24,128]{1,0:T(8,128)S(1)} %get-tuple-element.56.s0), channel_id=1, source_target_pairs={{0,3},{1,0},{2,1},{3,2},{4,7},{5,4},{6,5},{7,6},{8,11},{9,8},{10,9... | collective-permute-start | bytes 36872 | tf_op jit(solution)/shard_map/ppermute | solution.py:54
  166.8 8.8 %collective-permute-start.15 = (f32[24,128]{1,0:T(8,128)S(1)}, f32[24,128]{1,0:T(8,128)S(1)}, u32[]{:S(2)}, u32[]{:S(2)}) collective-permute-start(f32[24,128]{1,0:T(8,128)S(1)} %get-tuple-element.56.s0), channel_id=1, source_target_pairs={{0,2},{1,3},{2,0},{3,1},{4,6},{5,7},{6,4},{7,5},{8,10},{9,11},{10,... | collective-permute-start | bytes 36872 | tf_op jit(solution)/shard_map/ppermute | solution.py:54
  167.3 8.2 %collective-permute-start.14 = (f32[24,128]{1,0:T(8,128)S(1)}, f32[24,128]{1,0:T(8,128)S(1)}, u32[]{:S(2)}, u32[]{:S(2)}) collective-permute-start(f32[24,128]{1,0:T(8,128)S(1)} %get-tuple-element.56.s0), channel_id=1, source_target_pairs={{0,1},{1,2},{2,3},{3,0},{4,5},{5,6},{6,7},{7,4},{8,9},{9,10},{10,1... | collective-permute-start | bytes 36872 | tf_op jit(solution)/shard_map/ppermute | solution.py:54
  175.6 3.4 %copy-start.31 = (bf16[4096,1024]{1,0:T(8,128)(2,1)S(1)}, bf16[4096,1024]{1,0:T(8,128)(2,1)}, u32[]{:S(2)}) copy-start(bf16[4096,1024]{1,0:T(8,128)(2,1)} %all-gather.2.cloned.1.call-done) | copy-start | bytes 25165828
  178.9 0.9 copy-start.34
  192.1 8.7 %all-to-all-start.4 = ((f32[4,2,1024]{2,1,0:T(2,128)}), f32[4,2,1024]{2,1,0:T(2,128)S(1)}, u32[]{:S(2)}, u32[]{:S(2)}) async-start(f32[4,2,1024]{2,1,0:T(2,128)} %broadcast_in_dim.24), calls=%async_computation.4 | async-start | bytes 65536 | tf_op jit(solution)/shard_map/all_to_all | solution.py:62
  (13 other events, 8.5 us)
Sparse Core Ops, SparseCore 0:
  16.4 88.0 all-gather.1

commit v3 on v2

--- a/solution.py
+++ b/solution.py
@@ -28,7 +28,7 @@
 CHIPS = ("y", "z")
 DP = ("y", "z", "c")
 HIGH = lax.Precision.HIGHEST
-VMEM = pl.BlockSpec(memory_space=pltpu.VMEM)
+VMEM = pl.BlockSpec()
 SMEM = pl.BlockSpec(memory_space=pltpu.SMEM)
 
 
@@ -309,35 +309,43 @@
 
 
 def rows_kernel(
-    where_ref, own, left, right, far_a, far_b, w_ref, low, b_ref, s0, s1, s2, s3, owned, out, cols
+    where_ref, own, left, right, far_a, far_b, w_ref, low, b_ref, s0, s1, s2, s3, owned, out, cols, x
 ):
+    rows = own.shape[0]
     half = far_a.shape[0]
+    sent = (s0, s1, s2, s3)
+
+    @pl.when(pl.program_id(0) == 0)
+    def _():
+        x[0, :rows, :] = own[...]
+        x[1, :rows, :] = left[...]
+        x[2, :half, :] = far_a[...]
+        x[2, half:rows, :] = far_b[...]
+        x[3, :rows, :] = right[...]
+        for k, s in enumerate(sent):
+            flat = [
+                jnp.concatenate(
+                    [s[b * HEADS_TP + h : b * HEADS_TP + h + 1, :] for h in range(HEADS_TP)],
+                    axis=1,
+                )
+                for b in range(ROLLS)
+            ]
+            flat.append(jnp.zeros((16 - ROLLS, HEADS_TP * HD), f32))
+            x[k, rows:, :] = jnp.concatenate(flat, axis=0).astype(bf16)
+
     b_tile = b_ref[...]
     mine = lane_iota(b_tile.shape) >= RANK
     b_tile = jnp.where(mine, b_tile, jnp.zeros_like(b_tile))
     b_turned = pltpu.roll(b_tile.astype(f32), RANK, 1)
-    acc = adapter_scale * nt_dot(low[...], b_turned.astype(bf16))
-    acc = acc + nt_dot(own[...], w_ref[where_ref[0]])
-    acc = acc + nt_dot(left[...], w_ref[where_ref[1]])
-    acc = acc + nt_dot(right[...], w_ref[where_ref[3]])
-    out[...] = acc
-    far = w_ref[where_ref[2]]
-    out[:half, :] += nt_dot(far_a[...], far)
-    out[half:, :] += nt_dot(far_b[...], far)
+    acc = nt_dot(x[0], w_ref[where_ref[0]])
+    for k in range(1, len(sent)):
+        acc = acc + nt_dot(x[k], w_ref[where_ref[k]])
+    out[...] = acc[:rows] + adapter_scale * nt_dot(low[...], b_turned.astype(bf16))
     top = ROLLS * HEADS_TP
     low_sum = s0[top:, :] + s1[top:, :] + s2[top:, :] + s3[top:, :]
     got = adapter_scale * nt_dot(low_sum, b_turned, precision=HIGH)
-    for k, s in enumerate((s0, s1, s2, s3)):
-        flat = [
-            jnp.concatenate(
-                [s[b * HEADS_TP + h : b * HEADS_TP + h + 1, :] for h in range(HEADS_TP)], axis=1
-            )
-            for b in range(ROLLS)
-        ]
-        flat.append(jnp.zeros((8 - ROLLS, HEADS_TP * HD), f32))
-        heads = jnp.concatenate(flat, axis=0).astype(bf16)
-        got = got + nt_dot(heads, w_ref[where_ref[k]])
-    cols[...] = got[:ROLLS, :] + owned[...]
+    got = got[:ROLLS, :] + acc[rows : rows + ROLLS] + owned[...]
+    cols[...] = jnp.broadcast_to(got, cols.shape)
 
 
 def output_rows(where, own, left, right, far_a, far_b, w, low, b, sent, owned):
@@ -348,7 +356,7 @@
     whole = lambda a: pl.BlockSpec(a.shape, lambda j, s: (0, 0))
     return pl.pallas_call(
         rows_kernel,
-        out_shape=(shape(rows, width), shape(ROLLS, width)),
+        out_shape=(shape(rows, width), shape(n, ROLLS, width)),
         grid_spec=pltpu.PrefetchScalarGridSpec(
             num_scalar_prefetch=1,
             grid=(tiles,),
@@ -366,8 +374,9 @@
             ],
             out_specs=(
                 pl.BlockSpec((rows, tile), lambda j, s: (0, j)),
-                pl.BlockSpec((ROLLS, tile), lambda j, s: (0, j)),
+                pl.BlockSpec((n, ROLLS, tile), lambda j, s: (0, 0, j)),
             ),
+            scratch_shapes=[pltpu.VMEM((n, rows + 16, depth), bf16)],
         ),
         compiler_params=pltpu.CompilerParams(vmem_limit_bytes=40 << 20),
         cost_estimate=pl.CostEstimate(
@@ -418,19 +427,21 @@
         ),
     )
 
+    w_rows = query_key_value_weight[:, 0, :]
+    w_rows_other = swapped(w_rows)
     w_cols = output_weight_frozen[0].T
+    w_cols_other = swapped(w_cols)
+
     ny = lax.axis_size("y")
     turned = lax.ppermute(
         w_cols, ("y", "t"), [(a * nt + b, b * nt + a) for a in range(ny) for b in range(nt)]
     )
+    turned, message = together(turned, message)
     w_block = lax.all_gather(turned, DP, axis=0, tiled=True)
     w_block = w_block.reshape(nt, shard_width, w_cols.shape[1])
 
     left = shift(attention_rows, 1, nt)
     right = shift(attention_rows, nt - 1, nt)
-    w_rows = query_key_value_weight[:, 0, :]
-    w_rows_other = swapped(w_rows)
-    w_cols_other = swapped(w_cols)
 
     arrived = exchange(message, CHIPS)
     gain = lax.dynamic_slice_in_dim(attention_norm_gain, m * LANES, LANES, 0).astype(f32)[None, :]
@@ -442,7 +453,9 @@
         scratch=[pltpu.VMEM((CHIP_COUNT * FIRST_ROWS, LANES), f32)],
     )
     arrived_other = swapped(arrived)
-    sent, arrived, arrived_other = together(sent, arrived, arrived_other)
+    sent, arrived, arrived_other, left, right = together(
+        sent, arrived, arrived_other, left, right
+    )
     came = exchange(sent.reshape(CHIP_COUNT, QKV_ROWS, LANES), CHIPS)
 
     rows = attention_rows.shape[0]
@@ -473,7 +486,10 @@
     attended, kv, _ = attend(
         False, cache_fill_lengths, came.reshape(-1, LANES), cache, nothing, ab
     )
-    attended, *parts = together(attended, *parts)
+    attended, weighted, left, right = together(attended, weighted, left, right)
+    half = rows // 2
+    far_a = shift(left[:half], 1, nt)
+    far_b = shift(right[half:], nt - 1, nt)
     everyone = to_all(attended, CHIPS)
 
     low_back, b_cols, kept, given = call(
@@ -499,7 +515,6 @@
     share, given, kept = together(share, given, kept)
     shares = shifts(share, nt)
     kept = kept + swapped(given)
-    summed = exchange(kept, CHIPS)
 
     sent = call(
         qkv_later_kernel,
@@ -507,14 +522,11 @@
         [SMEM] + [VMEM] * 9,
         (place, state, gain, w_rows, w_rows_other, b_cols, *shares),
     )
-    sent, left, right = together(sent, left, right)
     came = exchange(sent.reshape(CHIP_COUNT, QKV_ROWS, LANES), CHIPS)
-    half = rows // 2
-    far_a = shift(left[:half], 1, nt)
-    far_b = shift(right[half:], nt - 1, nt)
-    summed = summed.sum(axis=0)
 
     attended, _, owned = attend(True, cache_fill_lengths, came.reshape(-1, LANES), cache, kv, ab)
+    attended, kept = together(attended, kept)
+    summed = exchange(kept, CHIPS)
     adapted, own_cols = output_rows(
         where,
         attention_rows,
@@ -528,7 +540,9 @@
         shifts(attended, nt),
         owned.reshape(ROLLS, width),
     )
-    decoded = to_all(own_cols, "t").transpose(1, 0, 2).reshape(ROLLS, width)
+    own_cols, summed = together(own_cols, summed)
+    summed = summed.sum(axis=0)
+    decoded = exchange(own_cols, "t").transpose(1, 0, 2).reshape(ROLLS, width)
     grad_a = summed[:, :RANK].T[:, None, :]
     grad_b = summed[:, RANK:].T[:, None, :]
     return (decoded, adapted, grad_a, grad_b)

time: 210 us -> 176 us (0.84)
  waiting for transfers between devices: 66.2 us -> 31.6 us
  starting transfers between devices: 67.4 us -> 71.5 us
    ppermute x13, waiting for transfers between devices: 29.8 us -> 6.27 us  [shift(): return lax.ppermute(x, 't', [(i, (i + by) % n) for i in range(n)])]
    all_to_all x6, waiting for transfers between devices: 31.4 us -> 23.3 us  [exchange(): return lax.all_to_all(x, axes, split_axis=0, concat_axis=0, tiled=True)]
    ppermute x13, starting transfers between devices: 13.5 us -> 18.6 us  [shift(): return lax.ppermute(x, 't', [(i, (i + by) % n) for i in range(n)])]
    ppermute x1, waiting for transfers between devices: 4.95 us -> 0.24 us  [shards(): lax.ppermute(w_cols, ('y', 't'), [(a * nt + b, b * nt + a) for a in range...]
  transfers between devices with their start and end apart: 25 -> 25, of which waited for: 12 -> 11; matrix products, arithmetic and copies ran while one was open for 4% -> 4% of each run, Pallas kernels for 7% -> 14%
where the time goes in v3:
time: 176 us; the launch traced here: 175 us
  starting transfers between devices  71.5 us (41%)
  local copies, waits for them, and re-layouts  32 us (18%)
  waiting for transfers between devices  31.6 us (18%)
  Pallas kernels  23.7 us (13%)
  between operations  14.4 us (8%)
    all_to_all x6, starting transfers between devices, exchange(): return lax.all_to_all(x, axes, split_axis=0, concat_axis=0, tiled=True)  49.3 us
    unnamed x73, local copies, waits for them, and re-layouts  26.8 us
    all_to_all x6, waiting for transfers between devices, exchange(): return lax.all_to_all(x, axes, split_axis=0, concat_axis=0, tiled=True)  23.3 us
    ppermute x13, starting transfers between devices, shift(): return lax.ppermute(x, 't', [(i, (i + by) % n) for i in range(n)])  18.6 us
    pallas_call x8, Pallas kernels, call(): pl.pallas_call(kernel, out_shape=out, in_specs=specs, out_specs=tuple((VM...  13.7 us
    pallas_call x1, Pallas kernels, output_rows(): pl.pallas_call(rows_kernel, out_shape=(shape(rows, width), shape(n, ROLLS...  10 us
    ppermute x13, waiting for transfers between devices, shift(): return lax.ppermute(x, 't', [(i, (i + by) % n) for i in range(n)])  6.27 us
  transfers between devices with their start and end apart: 25, of which 11 were waited for; matrix products, arithmetic and copies ran while one was open for 4% of the time, Pallas kernels for 14%

profile of v3, /device:TPU:8, one launch (start us, length us, event | category | flops | bytes accessed | tf_op | source)
XLA Modules:
  0.0 174.8 jit_solution(12617028393010735998)
XLA Ops:
  7.2 3.4 %collective-permute-start = (bf16[64,1024]{1,0:T(8,128)(2,1)}, bf16[64,1024]{1,0:T(8,128)(2,1)S(1)}, u32[]{:S(2)}, u32[]{:S(2)}) collective-permute-start(bf16[64,1024]{1,0:T(8,128)(2,1)} %bitcast.46), channel_id=1, source_target_pairs={{0,0},{1,64},{2,128},{3,192},{64,1},{65,65},{66,129},{67,193},{128... | collective-permute-start | bytes 393224 | tf_op jit(solution)/shard_map/ppermute | solution.py:436
  14.1 1.3 shard_map.156
  16.3 6.7 %collective-permute-start.4 = (bf16[512,1024]{1,0:T(8,128)(2,1)}, bf16[512,1024]{1,0:T(8,128)(2,1)}, u32[]{:S(2)}, u32[]{:S(2)}) collective-permute-start(bf16[512,1024]{1,0:T(8,128)(2,1)} %own.1), channel_id=1, source_target_pairs={{0,3},{1,0},{2,1},{3,2},{4,7},{5,4},{6,5},{7,6},{8,11},{9,8},{10,9... | collective-permute-start | bytes 3145736 | tf_op jit(solution)/shard_map/ppermute | solution.py:54
  22.9 12.2 %all-to-all-start = ((bf16[32,24,128]{2,1,0:T(8,128)(2,1)}), bf16[32,24,128]{2,1,0:T(8,128)(2,1)S(1)}, u32[]{:S(2)}, u32[]{:S(2)}) async-start(bf16[32,24,128]{2,1,0:T(8,128)(2,1)} %shard_map.156), calls=%async_computation | async-start | bytes 393216 | tf_op jit(solution)/shard_map/all_to_all | solution.py:62
  35.2 9.8 %all-to-all-done.arrived.own = bf16[32,24,128]{2,1,0:T(8,128)(2,1)S(1)} async-done(((bf16[32,24,128]{2,1,0:T(8,128)(2,1)}), bf16[32,24,128]{2,1,0:T(8,128)(2,1)S(1)}, u32[]{:S(2)}, u32[]{:S(2)}) %all-to-all-start) | async-done | bytes 196640 | tf_op jit(solution)/shard_map/all_to_all | solution.py:62
  45.1 0.8 bitcast_convert_fusion.gain
  45.9 0.9 copy-done.8
  46.9 0.8 shard_map.157
  49.1 10.3 %all-to-all-start.1 = ((f32[32,24,128]{2,1,0:T(8,128)}), f32[32,24,128]{2,1,0:T(8,128)}, u32[]{:S(2)}, u32[]{:S(2)}) async-start(f32[32,24,128]{2,1,0:T(8,128)} %bitcast.45), calls=%async_computation.1 | async-start | bytes 786432 | tf_op jit(solution)/shard_map/all_to_all | solution.py:62
  59.4 0.9 copy-done.3
  60.3 1.2 copy-done.5
  63.5 2.6 %shard_map.158 = (bf16[512,1024]{1,0:T(8,128)(2,1)S(1)}, bf16[32,32,128]{2,1,0:T(8,128)(2,1)S(1)}, f32[640,128]{1,0:T(8,128)}) custom-call(s32[4]{0:T(128)S(1)} %pad_add_fusion.place, f32[2]{0:T(128)S(1)} %copy-done.27, s32[2]{0:T(128)S(1)} %copy-done.29, s32[2]{0:T(128)S(1)} %copy-done.30, bf16[32,24,128]{2,1,0:T(8,128)(2,1)S(1)} %copy-done.3, ...), custom_call_target="tpu_custom_call" | custom-call | flops 268435456 | bytes 4128808 | tf_op jit(solution)/shard_map/pallas_call | solution.py:81
  66.2 1.0 copy-done.6
  67.3 2.3 %collective-permute-start.8 = (f32[640,128]{1,0:T(8,128)}, f32[640,128]{1,0:T(8,128)}, u32[]{:S(2)}, u32[]{:S(2)}) collective-permute-start(f32[640,128]{1,0:T(8,128)} %get-tuple-element.50.p0), channel_id=1, source_target_pairs={{0,2},{1,3},{2,0},{3,1},{4,6},{5,7},{6,4},{7,5},{8,10},{9,11},{10,... | collective-permute-start | bytes 983048 | tf_op jit(solution)/shard_map/ppermute | solution.py:54
  69.6 1.9 %all-to-all-done.1 = f32[32,24,128]{2,1,0:T(8,128)} async-done(((f32[32,24,128]{2,1,0:T(8,128)}), f32[32,24,128]{2,1,0:T(8,128)}, u32[]{:S(2)}, u32[]{:S(2)}) %all-to-all-start.1) | async-done | bytes 393248 | tf_op jit(solution)/shard_map/all_to_all | solution.py:62
  71.5 2.3 %shard_map.159 = (bf16[16,128]{1,0:T(8,128)(2,1)S(1)}, f32[8,128]{1,0:T(8,128)S(1)}, f32[64,128]{1,0:T(8,128)}) custom-call(s32[2]{0:T(128)S(1)} %copy-done.25, f32[768,128]{1,0:T(8,128)} %bitcast.13.refs_1_, bf16[2,2048,256]{2,1,0:T(8,128)(2,1)S(1)} %bitcast.35, f32[8,128]{1,0:T(8,128)S(1)} %broadcast_in_dim.19.refs_3_, bf16[1024,128]{1,0:T(8,128)(2,1)S(1)} %bitcast.37), custom_call_target="tpu_custom_call" | custom-call | flops 67108864 | bytes 2797576 | tf_op jit(solution)/shard_map/pallas_call | solution.py:81
  74.6 7.8 %all-to-all-start.2 = ((bf16[32,16,128]{2,1,0:T(8,128)(2,1)}), bf16[32,16,128]{2,1,0:T(8,128)(2,1)S(1)}, u32[]{:S(2)}, u32[]{:S(2)}) async-start(bf16[32,16,128]{2,1,0:T(8,128)(2,1)} %broadcast_in_dim.20), calls=%async_computation.2 | async-start | bytes 262144 | tf_op jit(solution)/shard_map/all_to_all | solution.py:62
  82.5 1.4 collective-permute-done.7.p1
  83.9 1.2 copy-done.7
  85.1 2.2 %shard_map.160 = (bf16[512,128]{1,0:T(8,128)(2,1)S(1)}, f32[128,128]{1,0:T(8,128)S(1)}, f32[32,16,128]{2,1,0:T(8,128)S(1)}, f32[32,16,128]{2,1,0:T(8,128)S(1)}) custom-call(s32[4]{0:T(128)S(1)} %pad_add_fusion.place, f32[640,128]{1,0:T(8,128)} %get-tuple-element.50.p0, f32[640,128]{1,0:T(8,128)} %collective-permute-done.7.p1, ...), custom_call_target="tpu_custom_call" | custom-call | flops 268435456 | bytes 4128784 | tf_op jit(solution)/shard_map/pallas_call | solution.py:81
  90.6 1.7 all-to-all-done.2.came
  92.3 0.9 copy-done.15
  93.2 0.9 copy-done.17
  94.1 0.8 shard_map.161.s0
  94.9 3.6 %collective-permute-start.13 = (f32[64,256]{1,0:T(8,128)S(1)}, f32[64,256]{1,0:T(8,128)S(1)}, u32[]{:S(2)}, u32[]{:S(2)}) collective-permute-start(f32[64,256]{1,0:T(8,128)S(1)} %shard_map.161.s0), channel_id=1, source_target_pairs={{0,3},{1,0},{2,1},{3,2},{4,7},{5,4},{6,5},{7,6},{8,11},{9,8},{10,9... | collective-permute-start | bytes 196616 | tf_op jit(solution)/shard_map/ppermute | solution.py:54
  98.7 1.3 collective-permute-start.11
  100.3 4.0 %collective-permute-done.12.s2 = f32[64,256]{1,0:T(8,128)S(1)} collective-permute-done((f32[64,256]{1,0:T(8,128)S(1)}, f32[64,256]{1,0:T(8,128)S(1)}, u32[]{:S(2)}, u32[]{:S(2)}) %collective-permute-start.12) | collective-permute-done | bytes 65568 | tf_op jit(solution)/shard_map/ppermute | solution.py:54
  104.9 0.9 copy-done.9
  105.8 0.9 copy-done.11
  106.7 0.8 copy-done.19
  107.6 0.8 copy-done.21
  108.3 1.2 shard_map.162
  110.3 7.3 %all-to-all-start.3 = ((f32[32,24,128]{2,1,0:T(8,128)}), f32[32,24,128]{2,1,0:T(8,128)}, u32[]{:S(2)}, u32[]{:S(2)}) async-start(f32[32,24,128]{2,1,0:T(8,128)} %bitcast.41), calls=%async_computation.3 | async-start | bytes 786432 | tf_op jit(solution)/shard_map/all_to_all | solution.py:62
  117.6 1.9 %slice.12 = bf16[256,1024]{1,0:T(8,128)(2,1)} slice(bf16[512,1024]{1,0:T(8,128)(2,1)} %collective-permute-done.3.left), slice={[0:256], [0:1024]} | slice | bytes 1048576 | tf_op jit(solution)/shard_map/slice | solution.py:491
  119.5 1.9 %slice.13 = bf16[256,1024]{1,0:T(8,128)(2,1)} slice(bf16[512,1024]{1,0:T(8,128)(2,1)} %collective-permute-done.4.right), slice={[256:512], [0:1024]} | slice | bytes 1048576 | tf_op jit(solution)/shard_map/slice | solution.py:492
  122.0 1.5 collective-permute-start.5
  123.4 1.7 collective-permute-done.14
  125.2 0.7 add.19
  125.9 5.1 %all-to-all-done.3 = f32[32,24,128]{2,1,0:T(8,128)} async-done(((f32[32,24,128]{2,1,0:T(8,128)}), f32[32,24,128]{2,1,0:T(8,128)}, u32[]{:S(2)}, u32[]{:S(2)}) %all-to-all-start.3) | async-done | bytes 393248 | tf_op jit(solution)/shard_map/all_to_all | solution.py:62
  131.1 2.4 %shard_map.163 = (f32[24,128]{1,0:T(8,128)S(1)}, f32[8,128]{1,0:T(8,128)}, f32[64,128]{1,0:T(8,128)S(1)}) custom-call(s32[2]{0:T(128)S(1)} %copy-done.25, f32[768,128]{1,0:T(8,128)} %bitcast.20.refs_1_, bf16[2,2048,256]{2,1,0:T(8,128)(2,1)S(1)} %bitcast.36, f32[8,128]{1,0:T(8,128)S(1)} %get-tuple-element.59.refs_3_, bf16[1024,128]{1,0:T(8,128)(2,1)S(1)} %bitcast.39), custom_call_target="tpu_custom_call" | custom-call | flops 67108864 | bytes 2805768 | tf_op jit(solution)/shard_map/pallas_call | solution.py:81
  133.7 1.1 collective-permute-start.16
  134.8 0.8 collective-permute-start.15
  135.6 6.4 %all-to-all-start.4 = ((f32[32,16,128]{2,1,0:T(8,128)}), f32[32,16,128]{2,1,0:T(8,128)S(1)}, u32[]{:S(2)}, u32[]{:S(2)}) async-start(f32[32,16,128]{2,1,0:T(8,128)} %add.19), calls=%async_computation.4 | async-start | bytes 524288 | tf_op jit(solution)/shard_map/all_to_all | solution.py:62
  142.1 3.4 %copy-done.31 = bf16[4096,1024]{1,0:T(8,128)(2,1)S(1)} copy-done((bf16[4096,1024]{1,0:T(8,128)(2,1)S(1)}, bf16[4096,1024]{1,0:T(8,128)(2,1)}, u32[]{:S(2)}) %copy-start.31) | copy-done | bytes 8388632
  145.5 0.9 copy-done.34
  146.4 10.0 %shard_map.164 = (f32[512,1024]{1,0:T(8,128)}, f32[4,2,1024]{2,1,0:T(2,128)}) custom-call(s32[4]{0:T(128)S(1)} %compare_select_fusion.where_ref, bf16[512,1024]{1,0:T(8,128)(2,1)S(1)} %copy-done.1, bf16[512,1024]{1,0:T(8,128)(2,1)} %collective-permute-done.3.left, bf16[512,1024]{1,0:T(8,128)(2,1)} %collective-permute-done.4.right, ...), custom_call_target="tpu_custom_call" | custom-call | flops 4294967296 | bytes 14680064 | tf_op jit(solution)/shard_map/pallas_call | solution.py:357
  156.5 5.4 %all-to-all-start.5 = ((f32[4,2,1024]{2,1,0:T(2,128)}), f32[4,2,1024]{2,1,0:T(2,128)S(1)}, u32[]{:S(2)}, u32[]{:S(2)}) async-start(f32[4,2,1024]{2,1,0:T(2,128)} %get-tuple-element.67), calls=%async_computation.5 | async-start | bytes 65536 | tf_op jit(solution)/shard_map/all_to_all | solution.py:62
  162.5 4.8 %all-to-all-done.5 = f32[4,2,1024]{2,1,0:T(2,128)S(1)} async-done(((f32[4,2,1024]{2,1,0:T(2,128)}), f32[4,2,1024]{2,1,0:T(2,128)S(1)}, u32[]{:S(2)}, u32[]{:S(2)}) %all-to-all-start.5) | async-done | bytes 32800 | tf_op jit(solution)/shard_map/all_to_all | solution.py:62
  (96 shorter events, 16.3 us)
Async XLA Ops:
  7.2 52.2 %copy-start.1 = (bf16[512,1024]{1,0:T(8,128)(2,1)S(1)}, bf16[512,1024]{1,0:T(8,128)(2,1)}, u32[]{:S(2)}) copy-start(bf16[512,1024]{1,0:T(8,128)(2,1)} %own.1) | copy-start | bytes 3145732
  7.2 134.9 %all-gather.2.cloned.1.call-start = ((), (), s32[]{:S(2)}) async-start(), calls=%async_computation.6 | async-start | bytes 8519680 | tf_op jit(solution)/shard_map/all_gather | solution.py:440
  7.2 8.4 %collective-permute-start = (bf16[64,1024]{1,0:T(8,128)(2,1)}, bf16[64,1024]{1,0:T(8,128)(2,1)S(1)}, u32[]{:S(2)}, u32[]{:S(2)}) collective-permute-start(bf16[64,1024]{1,0:T(8,128)(2,1)} %bitcast.46), channel_id=1, source_target_pairs={{0,0},{1,64},{2,128},{3,192},{64,1},{65,65},{66,129},{67,193},{128... | collective-permute-start | bytes 393224 | tf_op jit(solution)/shard_map/ppermute | solution.py:436
  10.6 0.7 copy-start.22
  16.3 55.3 %copy-start = (bf16[2,2048,1,256]{3,1,2,0:T(8,128)(2,1)S(1)}, bf16[2,2048,1,256]{3,1,2,0:T(8,128)(2,1)}, u32[]{:S(2)}) copy-start(bf16[2,2048,1,256]{3,1,2,0:T(8,128)(2,1)} %param.16) | copy-start | bytes 6291460
  16.3 32.8 %collective-permute-start.4 = (bf16[512,1024]{1,0:T(8,128)(2,1)}, bf16[512,1024]{1,0:T(8,128)(2,1)}, u32[]{:S(2)}, u32[]{:S(2)}) collective-permute-start(bf16[512,1024]{1,0:T(8,128)(2,1)} %own.1), channel_id=1, source_target_pairs={{0,3},{1,0},{2,1},{3,2},{4,7},{5,4},{6,5},{7,6},{8,11},{9,8},{10,9... | collective-permute-start | bytes 3145736 | tf_op jit(solution)/shard_map/ppermute | solution.py:54
  22.9 26.1 %collective-permute-start.3 = (bf16[512,1024]{1,0:T(8,128)(2,1)}, bf16[512,1024]{1,0:T(8,128)(2,1)}, u32[]{:S(2)}, u32[]{:S(2)}) collective-permute-start(bf16[512,1024]{1,0:T(8,128)(2,1)} %own.1), channel_id=1, source_target_pairs={{0,1},{1,2},{2,3},{3,0},{4,5},{5,6},{6,7},{7,4},{8,9},{9,10},{10,1... | collective-permute-start | bytes 3145736 | tf_op jit(solution)/shard_map/ppermute | solution.py:54
  22.9 22.2 %all-to-all-start = ((bf16[32,24,128]{2,1,0:T(8,128)(2,1)}), bf16[32,24,128]{2,1,0:T(8,128)(2,1)S(1)}, u32[]{:S(2)}, u32[]{:S(2)}) async-start(bf16[32,24,128]{2,1,0:T(8,128)(2,1)} %shard_map.156), calls=%async_computation | async-start | bytes 393216 | tf_op jit(solution)/shard_map/all_to_all | solution.py:62
  35.1 10.8 %collective-permute-start.1 = (bf16[64,1280]{1,0:T(8,128)(2,1)}, bf16[64,1280]{1,0:T(8,128)(2,1)S(1)}, u32[]{:S(2)}, u32[]{:S(2)}) collective-permute-start(bf16[64,1280]{1,0:T(8,128)(2,1)} %bitcast.42), channel_id=1, source_target_pairs={{0,4},{4,0},{1,5},{5,1},{2,6},{6,2},{3,7},{7,3},{8,12},{12,8},{9,1... | collective-permute-start | bytes 491528 | tf_op jit(solution)/shard_map/ppermute | solution.py:50
  45.1 4.0 %copy-start.2 = (bf16[32,24,128]{2,1,0:T(8,128)(2,1)}, bf16[32,24,128]{2,1,0:T(8,128)(2,1)S(1)}, u32[]{:S(2)}) copy-start(bf16[32,24,128]{2,1,0:T(8,128)(2,1)S(1)} %all-to-all-done.arrived.own) | copy-start | bytes 589828
  45.1 3.9 %collective-permute-start.2 = (bf16[32,24,128]{2,1,0:T(8,128)(2,1)S(1)}, bf16[32,24,128]{2,1,0:T(8,128)(2,1)}, u32[]{:S(2)}, u32[]{:S(2)}) collective-permute-start(bf16[32,24,128]{2,1,0:T(8,128)(2,1)S(1)} %all-to-all-done.arrived.own), channel_id=1, source_target_pairs={{0,4},{4,0},{1,5},{5,1},{2,6},{6,2},{3,7},{7,3},{8,12},{12,8},{9,1... | collective-permute-start | bytes 589832 | tf_op jit(solution)/shard_map/ppermute | solution.py:50
  45.9 0.9 copy-start.8
  46.8 2.2 %copy-start.10 = (bf16[64,1280]{1,0:T(8,128)(2,1)}, bf16[64,1280]{1,0:T(8,128)(2,1)S(1)}, u32[]{:S(2)}) copy-start(bf16[64,1280]{1,0:T(8,128)(2,1)S(1)} %collective-permute-done.1.w_other) | copy-start | bytes 491524
  47.7 0.7 copy-start.12
  49.1 22.5 %all-to-all-start.1 = ((f32[32,24,128]{2,1,0:T(8,128)}), f32[32,24,128]{2,1,0:T(8,128)}, u32[]{:S(2)}, u32[]{:S(2)}) async-start(f32[32,24,128]{2,1,0:T(8,128)} %bitcast.45), calls=%async_computation.1 | async-start | bytes 786432 | tf_op jit(solution)/shard_map/all_to_all | solution.py:62
  59.4 0.9 copy-start.3
  60.3 1.2 copy-start.5
  63.5 8.0 %copy-start.25 = (s32[2]{0:T(128)S(1)}, s32[2]{0:T(128)}, u32[]{:S(2)}) copy-start(s32[2]{0:T(128)} %refs_0_.3) | copy-start | bytes 28
  66.2 1.0 copy-start.6
  67.1 15.3 %collective-permute-start.9 = (f32[640,128]{1,0:T(8,128)}, f32[640,128]{1,0:T(8,128)}, u32[]{:S(2)}, u32[]{:S(2)}) collective-permute-start(f32[640,128]{1,0:T(8,128)} %get-tuple-element.50.p0), channel_id=1, source_target_pairs={{0,3},{1,0},{2,1},{3,2},{4,7},{5,4},{6,5},{7,6},{8,11},{9,8},{10,9... | collective-permute-start | bytes 983048 | tf_op jit(solution)/shard_map/ppermute | solution.py:54
  67.3 15.1 %collective-permute-start.8 = (f32[640,128]{1,0:T(8,128)}, f32[640,128]{1,0:T(8,128)}, u32[]{:S(2)}, u32[]{:S(2)}) collective-permute-start(f32[640,128]{1,0:T(8,128)} %get-tuple-element.50.p0), channel_id=1, source_target_pairs={{0,2},{1,3},{2,0},{3,1},{4,6},{5,7},{6,4},{7,5},{8,10},{9,11},{10,... | collective-permute-start | bytes 983048 | tf_op jit(solution)/shard_map/ppermute | solution.py:54
  69.6 14.2 %collective-permute-start.7 = (f32[640,128]{1,0:T(8,128)}, f32[640,128]{1,0:T(8,128)}, u32[]{:S(2)}, u32[]{:S(2)}) collective-permute-start(f32[640,128]{1,0:T(8,128)} %get-tuple-element.50.p0), channel_id=1, source_target_pairs={{0,1},{1,2},{2,3},{3,0},{4,5},{5,6},{6,7},{7,4},{8,9},{9,10},{10,1... | collective-permute-start | bytes 983048 | tf_op jit(solution)/shard_map/ppermute | solution.py:54
  74.6 17.7 %all-to-all-start.2 = ((bf16[32,16,128]{2,1,0:T(8,128)(2,1)}), bf16[32,16,128]{2,1,0:T(8,128)(2,1)S(1)}, u32[]{:S(2)}, u32[]{:S(2)}) async-start(bf16[32,16,128]{2,1,0:T(8,128)(2,1)} %broadcast_in_dim.20), calls=%async_computation.2 | async-start | bytes 262144 | tf_op jit(solution)/shard_map/all_to_all | solution.py:62
  82.4 7.6 %collective-permute-start.10 = (bf16[64,1024]{1,0:T(8,128)(2,1)}, bf16[64,1024]{1,0:T(8,128)(2,1)S(1)}, u32[]{:S(2)}, u32[]{:S(2)}) collective-permute-start(bf16[64,1024]{1,0:T(8,128)(2,1)} %bitcast.47), channel_id=1, source_target_pairs={{0,4},{4,0},{1,5},{5,1},{2,6},{6,2},{3,7},{7,3},{8,12},{12,8},{9,1... | collective-permute-start | bytes 393224 | tf_op jit(solution)/shard_map/ppermute | solution.py:50
  83.9 1.2 copy-start.7
  87.3 0.7 copy-start.13
  92.3 0.9 copy-start.15
  93.2 0.9 copy-start.17
  94.9 5.5 %collective-permute-start.13 = (f32[64,256]{1,0:T(8,128)S(1)}, f32[64,256]{1,0:T(8,128)S(1)}, u32[]{:S(2)}, u32[]{:S(2)}) collective-permute-start(f32[64,256]{1,0:T(8,128)S(1)} %shard_map.161.s0), channel_id=1, source_target_pairs={{0,3},{1,0},{2,1},{3,2},{4,7},{5,4},{6,5},{7,6},{8,11},{9,8},{10,9... | collective-permute-start | bytes 196616 | tf_op jit(solution)/shard_map/ppermute | solution.py:54
  98.4 5.9 %collective-permute-start.12 = (f32[64,256]{1,0:T(8,128)S(1)}, f32[64,256]{1,0:T(8,128)S(1)}, u32[]{:S(2)}, u32[]{:S(2)}) collective-permute-start(f32[64,256]{1,0:T(8,128)S(1)} %shard_map.161.s0), channel_id=1, source_target_pairs={{0,2},{1,3},{2,0},{3,1},{4,6},{5,7},{6,4},{7,5},{8,10},{9,11},{10,... | collective-permute-start | bytes 196616 | tf_op jit(solution)/shard_map/ppermute | solution.py:54
  98.7 6.2 %collective-permute-start.11 = (f32[64,256]{1,0:T(8,128)S(1)}, f32[64,256]{1,0:T(8,128)S(1)}, u32[]{:S(2)}, u32[]{:S(2)}) collective-permute-start(f32[64,256]{1,0:T(8,128)S(1)} %shard_map.161.s0), channel_id=1, source_target_pairs={{0,1},{1,2},{2,3},{3,0},{4,5},{5,6},{6,7},{7,4},{8,9},{9,10},{10,1... | collective-permute-start | bytes 196616 | tf_op jit(solution)/shard_map/ppermute | solution.py:54
  104.9 0.9 copy-start.9
  105.8 0.9 copy-start.11
  106.7 0.8 copy-start.19
  107.6 0.8 copy-start.21
  109.6 0.7 copy-start.4
  110.3 20.7 %all-to-all-start.3 = ((f32[32,24,128]{2,1,0:T(8,128)}), f32[32,24,128]{2,1,0:T(8,128)}, u32[]{:S(2)}, u32[]{:S(2)}) async-start(f32[32,24,128]{2,1,0:T(8,128)} %bitcast.41), calls=%async_computation.3 | async-start | bytes 786432 | tf_op jit(solution)/shard_map/all_to_all | solution.py:62
  117.6 7.6 %copy-start.14 = (f32[32,16,128]{2,1,0:T(8,128)S(1)}, f32[32,16,128]{2,1,0:T(8,128)}, u32[]{:S(2)}) copy-start(f32[32,16,128]{2,1,0:T(8,128)} %copy-done.13) | copy-start | bytes 786436
  121.4 20.6 %collective-permute-start.6 = (bf16[256,1024]{1,0:T(8,128)(2,1)}, bf16[256,1024]{1,0:T(8,128)(2,1)}, u32[]{:S(2)}, u32[]{:S(2)}) collective-permute-start(bf16[256,1024]{1,0:T(8,128)(2,1)} %slice.13), channel_id=1, source_target_pairs={{0,3},{1,0},{2,1},{3,2},{4,7},{5,4},{6,5},{7,6},{8,11},{9,8},{10,9... | collective-permute-start | bytes 1572872 | tf_op jit(solution)/shard_map/ppermute | solution.py:54
  122.0 20.1 %collective-permute-start.5 = (bf16[256,1024]{1,0:T(8,128)(2,1)}, bf16[256,1024]{1,0:T(8,128)(2,1)}, u32[]{:S(2)}, u32[]{:S(2)}) collective-permute-start(bf16[256,1024]{1,0:T(8,128)(2,1)} %slice.12), channel_id=1, source_target_pairs={{0,1},{1,2},{2,3},{3,0},{4,5},{5,6},{6,7},{7,4},{8,9},{9,10},{10,1... | collective-permute-start | bytes 1572872 | tf_op jit(solution)/shard_map/ppermute | solution.py:54
  123.4 1.7 collective-permute-start.14
  133.4 8.6 %collective-permute-start.17 = (f32[24,128]{1,0:T(8,128)S(1)}, f32[24,128]{1,0:T(8,128)S(1)}, u32[]{:S(2)}, u32[]{:S(2)}) collective-permute-start(f32[24,128]{1,0:T(8,128)S(1)} %get-tuple-element.63.s0), channel_id=1, source_target_pairs={{0,3},{1,0},{2,1},{3,2},{4,7},{5,4},{6,5},{7,6},{8,11},{9,8},{10,9... | collective-permute-start | bytes 36872 | tf_op jit(solution)/shard_map/ppermute | solution.py:54
  133.7 8.4 %collective-permute-start.16 = (f32[24,128]{1,0:T(8,128)S(1)}, f32[24,128]{1,0:T(8,128)S(1)}, u32[]{:S(2)}, u32[]{:S(2)}) collective-permute-start(f32[24,128]{1,0:T(8,128)S(1)} %get-tuple-element.63.s0), channel_id=1, source_target_pairs={{0,2},{1,3},{2,0},{3,1},{4,6},{5,7},{6,4},{7,5},{8,10},{9,11},{10,... | collective-permute-start | bytes 36872 | tf_op jit(solution)/shard_map/ppermute | solution.py:54
  134.8 7.2 %collective-permute-start.15 = (f32[24,128]{1,0:T(8,128)S(1)}, f32[24,128]{1,0:T(8,128)S(1)}, u32[]{:S(2)}, u32[]{:S(2)}) collective-permute-start(f32[24,128]{1,0:T(8,128)S(1)} %get-tuple-element.63.s0), channel_id=1, source_target_pairs={{0,1},{1,2},{2,3},{3,0},{4,5},{5,6},{6,7},{7,4},{8,9},{9,10},{10,1... | collective-permute-start | bytes 36872 | tf_op jit(solution)/shard_map/ppermute | solution.py:54
  135.6 20.8 %all-to-all-start.4 = ((f32[32,16,128]{2,1,0:T(8,128)}), f32[32,16,128]{2,1,0:T(8,128)S(1)}, u32[]{:S(2)}, u32[]{:S(2)}) async-start(f32[32,16,128]{2,1,0:T(8,128)} %add.19), calls=%async_computation.4 | async-start | bytes 524288 | tf_op jit(solution)/shard_map/all_to_all | solution.py:62
  142.1 3.4 %copy-start.31 = (bf16[4096,1024]{1,0:T(8,128)(2,1)S(1)}, bf16[4096,1024]{1,0:T(8,128)(2,1)}, u32[]{:S(2)}) copy-start(bf16[4096,1024]{1,0:T(8,128)(2,1)} %all-gather.2.cloned.1.call-done) | copy-start | bytes 25165828
  145.5 0.9 copy-start.34
  156.5 10.9 %all-to-all-start.5 = ((f32[4,2,1024]{2,1,0:T(2,128)}), f32[4,2,1024]{2,1,0:T(2,128)S(1)}, u32[]{:S(2)}, u32[]{:S(2)}) async-start(f32[4,2,1024]{2,1,0:T(2,128)} %get-tuple-element.67), calls=%async_computation.5 | async-start | bytes 65536 | tf_op jit(solution)/shard_map/all_to_all | solution.py:62
  (13 other events, 8.5 us)
Sparse Core Ops, SparseCore 0:
  16.4 88.8 all-gather.1

commit v4 on v2

--- a/solution.py
+++ b/solution.py
@@ -21,6 +21,10 @@
 QKV_ROWS = 24
 KEY_ROW = ROLLS * HEADS_TP
 STATE_ROW = KEY_ROW + 2 * ROLLS
+GRANT = 56
+SMALL_GRANT = 24
+MID_GRANT = 60
+DECODE_HINT = 1
 
 adapter_scale = 2.0
 f32 = jnp.float32
@@ -28,8 +32,9 @@
 CHIPS = ("y", "z")
 DP = ("y", "z", "c")
 HIGH = lax.Precision.HIGHEST
-VMEM = pl.BlockSpec(memory_space=pltpu.VMEM)
-SMEM = pl.BlockSpec(memory_space=pltpu.SMEM)
+HBM = pltpu.HBM
+SMEM = pltpu.SMEM
+ANY = pl.ANY
 
 
 def nn_dot(a, b):
@@ -74,18 +79,51 @@
     return lax.broadcasted_iota(jnp.int32, shape, len(shape) - 1)
 
 
-def call(kernel, out, specs, args, scratch=(), flops=0, vmem=32):
+def call(kernel, out, specs, args, scratch=(), flops=0, grant=GRANT):
     moved = sum(a.size * a.dtype.itemsize for a in args)
     outs = out if isinstance(out, tuple) else (out,)
     moved += sum(math.prod(o.shape) * o.dtype.itemsize for o in outs)
+    in_hbm = [i for i, kind in enumerate(specs) if kind != SMEM]
+    n_in, n_out = len(specs), len(outs)
+    buffers = [pltpu.VMEM(args[i].shape, args[i].dtype) for i in in_hbm]
+    buffers += [pltpu.VMEM(o.shape, o.dtype) for o in outs]
+
+    def body(*refs):
+        ins, results, rest = refs[:n_in], refs[n_in : n_in + n_out], refs[n_in + n_out :]
+        held, rest = rest[: len(buffers)], rest[len(buffers) :]
+        sem, rest = rest[0], rest[1:]
+        copies = [
+            pltpu.make_async_copy(ins[i], held[k], sem.at[k]) for k, i in enumerate(in_hbm)
+        ]
+        for copy in copies:
+            copy.start()
+        for copy in copies:
+            copy.wait()
+        given = list(ins)
+        for k, i in enumerate(in_hbm):
+            given[i] = held[k]
+        made = held[len(in_hbm) :]
+        kernel(*given, *made, *rest)
+        copies = [
+            pltpu.make_async_copy(made[k], results[k], sem.at[len(in_hbm) + k])
+            for k in range(n_out)
+        ]
+        for copy in copies:
+            copy.start()
+        for copy in copies:
+            copy.wait()
+
+    hbm = pl.BlockSpec(memory_space=HBM)
     return pl.pallas_call(
-        kernel,
+        body,
         out_shape=out,
-        in_specs=specs,
-        out_specs=tuple(VMEM for _ in outs) if isinstance(out, tuple) else VMEM,
-        scratch_shapes=list(scratch),
-        compiler_params=pltpu.CompilerParams(vmem_limit_bytes=vmem << 20),
-        cost_estimate=pl.CostEstimate(flops=flops, bytes_accessed=moved, transcendentals=0),
+        in_specs=[pl.BlockSpec(memory_space=kind) for kind in specs],
+        out_specs=tuple(hbm for _ in outs) if isinstance(out, tuple) else hbm,
+        scratch_shapes=[*buffers, pltpu.SemaphoreType.DMA((len(buffers),)), *scratch],
+        compiler_params=pltpu.CompilerParams(vmem_limit_bytes=grant << 20),
+        cost_estimate=pl.CostEstimate(
+            flops=flops, bytes_accessed=moved, transcendentals=0
+        ),
     )(*args)
 
 
@@ -135,13 +173,18 @@
         put(row, jnp.zeros((CHIP_COUNT, LANES), f32))
 
 
+def gain_of(place, gain):
+    start = pl.multiple_of(place[4] * LANES, LANES)
+    return gain[:, pl.ds(start, LANES)].astype(f32)
+
+
 def qkv_first_kernel(place, arrived, gain, w_own, w_other, out, state_out, held):
     held[...] = arrived[...].astype(f32).reshape(CHIP_COUNT * FIRST_ROWS, LANES)
     state = jnp.concatenate(
         [held[pl.ds(PIECE + b, CHIP_COUNT, stride=FIRST_ROWS), :] for b in range(ROLLS)], axis=0
     )
     state_out[...] = state
-    spread_qkv(state, gain[...], place[0] == 0, w_own, w_other, out)
+    spread_qkv(state, gain_of(place, gain), place[0] == 0, w_own, w_other, out)
 
 
 def qkv_later_kernel(place, state, gain, w_own, w_other, b_cols, s0, s1, s2, s3, out):
@@ -152,7 +195,7 @@
         + share[:, :LANES]
         + adapter_scale * nt_dot(low, b_cols[...], precision=HIGH)
     )
-    spread_qkv(now, gain[...], place[0] == 0, w_own, w_other, out)
+    spread_qkv(now, gain_of(place, gain), place[0] == 0, w_own, w_other, out)
 
 
 def attend_kernel(last, lengths, came, cache, before, ab, attended, kv_out, owned_out, held):
@@ -206,16 +249,20 @@
         low = nn_dot(low.astype(bf16), ab[...])
         attended[...] = jnp.concatenate([both, low], axis=0)
     else:
-        attended[...] = both.astype(bf16)
+        attended[...] = jnp.broadcast_to(both.astype(bf16), attended.shape)
     kv_out[...] = jnp.concatenate(kvs + [jnp.zeros((8 - 2 * ROLLS, LANES), f32)], axis=0)
 
 
 def attend(last, lengths, came, cache, before, ab):
-    att = shape(24, LANES) if last else shape(ROLLS * HEADS_TP, LANES, dtype=bf16)
+    att = (
+        shape(24, LANES)
+        if last
+        else shape(CHIP_COUNT, ROLLS * HEADS_TP, LANES, dtype=bf16)
+    )
     return call(
         lambda *refs: attend_kernel(last, *refs),
         (att, shape(8, LANES), shape(ROLLS * CHIP_COUNT, LANES)),
-        [SMEM, VMEM, VMEM, VMEM, VMEM],
+        [SMEM, ANY, HBM, HBM, HBM],
         (lengths, came, cache, before, ab),
         scratch=[pltpu.VMEM((8, LANES), f32)],
         flops=2 * 32 * 2 * cache.shape[0] * cache.shape[1] * HD,
@@ -308,50 +355,33 @@
     given[...] = jnp.where(first, odd, even)
 
 
-def rows_kernel(
-    where_ref, own, left, right, far_a, far_b, w_ref, low, b_ref, s0, s1, s2, s3, owned, out, cols
-):
+def turned_up(b_ref):
+    b = b_ref[...]
+    b = jnp.where(lane_iota(b.shape) >= RANK, b, jnp.zeros_like(b))
+    return pltpu.roll(b.astype(f32), RANK, 1)
+
+
+def rows_kernel(where_ref, own, left, right, far_a, far_b, w_ref, low, b_ref, out):
     half = far_a.shape[0]
-    b_tile = b_ref[...]
-    mine = lane_iota(b_tile.shape) >= RANK
-    b_tile = jnp.where(mine, b_tile, jnp.zeros_like(b_tile))
-    b_turned = pltpu.roll(b_tile.astype(f32), RANK, 1)
-    acc = adapter_scale * nt_dot(low[...], b_turned.astype(bf16))
-    acc = acc + nt_dot(own[...], w_ref[where_ref[0]])
+    acc = nt_dot(own[...], w_ref[where_ref[0]])
     acc = acc + nt_dot(left[...], w_ref[where_ref[1]])
     acc = acc + nt_dot(right[...], w_ref[where_ref[3]])
-    out[...] = acc
-    far = w_ref[where_ref[2]]
-    out[:half, :] += nt_dot(far_a[...], far)
-    out[half:, :] += nt_dot(far_b[...], far)
-    top = ROLLS * HEADS_TP
-    low_sum = s0[top:, :] + s1[top:, :] + s2[top:, :] + s3[top:, :]
-    got = adapter_scale * nt_dot(low_sum, b_turned, precision=HIGH)
-    for k, s in enumerate((s0, s1, s2, s3)):
-        flat = [
-            jnp.concatenate(
-                [s[b * HEADS_TP + h : b * HEADS_TP + h + 1, :] for h in range(HEADS_TP)], axis=1
-            )
-            for b in range(ROLLS)
-        ]
-        flat.append(jnp.zeros((8 - ROLLS, HEADS_TP * HD), f32))
-        heads = jnp.concatenate(flat, axis=0).astype(bf16)
-        got = got + nt_dot(heads, w_ref[where_ref[k]])
-    cols[...] = got[:ROLLS, :] + owned[...]
-
-
-def output_rows(where, own, left, right, far_a, far_b, w, low, b, sent, owned):
+    far = jnp.concatenate([far_a[...], far_b[...]], axis=0)
+    acc = acc + nt_dot(far, w_ref[where_ref[2]])
+    out[...] = acc + adapter_scale * nt_dot(low[...], turned_up(b_ref).astype(bf16))
+
+
+def output_rows(where, own, left, right, far_a, far_b, w, low, b):
     n, width, depth = w.shape
     rows = own.shape[0]
     tile = 256
-    tiles = width // tile
     whole = lambda a: pl.BlockSpec(a.shape, lambda j, s: (0, 0))
     return pl.pallas_call(
         rows_kernel,
-        out_shape=(shape(rows, width), shape(ROLLS, width)),
+        out_shape=shape(rows, width),
         grid_spec=pltpu.PrefetchScalarGridSpec(
             num_scalar_prefetch=1,
-            grid=(tiles,),
+            grid=(width // tile,),
             in_specs=[
                 whole(own),
                 whole(left),
@@ -361,21 +391,95 @@
                 pl.BlockSpec((n, tile, depth), lambda j, s: (0, j, 0)),
                 whole(low),
                 pl.BlockSpec((tile, b.shape[1]), lambda j, s: (j, 0)),
-                *(whole(s) for s in sent),
-                pl.BlockSpec((ROLLS, tile), lambda j, s: (0, s[0] * tiles + j)),
             ],
-            out_specs=(
-                pl.BlockSpec((rows, tile), lambda j, s: (0, j)),
-                pl.BlockSpec((ROLLS, tile), lambda j, s: (0, j)),
-            ),
-        ),
-        compiler_params=pltpu.CompilerParams(vmem_limit_bytes=40 << 20),
+            out_specs=pl.BlockSpec((rows, tile), lambda j, s: (0, j)),
+        ),
+        compiler_params=pltpu.CompilerParams(vmem_limit_bytes=GRANT << 20),
         cost_estimate=pl.CostEstimate(
             flops=2 * rows * width * depth * n,
             bytes_accessed=2 * (n * width * depth + n * rows * depth) + 4 * rows * width,
             transcendentals=0,
         ),
-    )(where, own, left, right, far_a, far_b, w, low, b, *sent, owned)
+    )(where, own, left, right, far_a, far_b, w, low, b)
+
+
+def decode_kernel(where_ref, p0, p1, p2, p3, w_ref, b_ref, owned, out, heads, held, sem):
+    k = pl.program_id(1)
+
+    @pl.when((pl.program_id(0) == 0) & (k == 0))
+    def _():
+        copies = [
+            pltpu.make_async_copy(p, held.at[i], sem.at[i]) for i, p in enumerate((p0, p1, p2, p3))
+        ]
+        for copy in copies:
+            copy.start()
+        for copy in copies:
+            copy.wait()
+        for i in range(len(copies)):
+            s = held[i]
+            flat = [
+                jnp.concatenate(
+                    [s[b * HEADS_TP + h : b * HEADS_TP + h + 1] for h in range(HEADS_TP)],
+                    axis=1,
+                )
+                for b in range(ROLLS)
+            ]
+            flat.append(jnp.zeros((16 - ROLLS, HEADS_TP * HD), f32))
+            heads[i] = jnp.concatenate(flat, axis=0).astype(bf16)
+
+    got = nt_dot(heads[k], w_ref[0])[:8]
+
+    @pl.when(k == 0)
+    def _():
+        top = ROLLS * HEADS_TP
+        low = held[0, top:, :] + held[1, top:, :] + held[2, top:, :] + held[3, top:, :]
+        start = adapter_scale * nt_dot(low, turned_up(b_ref), precision=HIGH)
+        base = jnp.concatenate([owned[...], jnp.zeros((8 - ROLLS, owned.shape[1]), f32)], axis=0)
+        out[...] = base + start + got
+
+    @pl.when(k > 0)
+    def _():
+        out[...] += got
+
+
+def decode_columns(where, sent, w, b, owned):
+    n, width, depth = w.shape
+    tile = 512
+    tiles = width // tile
+    whole = lambda a: pl.BlockSpec(a.shape, lambda j, k, s: (0, 0))
+    return pl.pallas_call(
+        decode_kernel,
+        out_shape=shape(8, width),
+        grid_spec=pltpu.PrefetchScalarGridSpec(
+            num_scalar_prefetch=1,
+            grid=(tiles, n),
+            in_specs=[
+                *(pl.BlockSpec(memory_space=ANY) for s in sent),
+                pl.BlockSpec((1, tile, depth), lambda j, k, s: (s[k], j, 0)),
+                pl.BlockSpec((tile, b.shape[1]), lambda j, k, s: (j, 0)),
+                pl.BlockSpec((ROLLS, tile), lambda j, k, s: (0, s[0] * tiles + j)),
+            ],
+            out_specs=pl.BlockSpec((8, tile), lambda j, k, s: (0, j)),
+            scratch_shapes=[
+                pltpu.VMEM((n, 16, depth), bf16),
+                pltpu.VMEM((n, *sent[0].shape), f32),
+                pltpu.SemaphoreType.DMA((n,)),
+            ],
+        ),
+        compiler_params=pltpu.CompilerParams(vmem_limit_bytes=MID_GRANT << 20),
+        cost_estimate=pl.CostEstimate(
+            flops=2 * 16 * width * depth * n,
+            bytes_accessed=DECODE_HINT * 2 * n * width * depth,
+            transcendentals=0,
+        ),
+    )(where, *sent, w, b, owned)
+
+
+def place_kernel(where_ref, c0, c1, c2, c3, out):
+    width = c0.shape[1]
+    for k, part in enumerate((c0, c1, c2, c3)):
+        start = pl.multiple_of(where_ref[k] * width, width)
+        out[:, pl.ds(start, width)] = part[:ROLLS, :]
 
 
 def shards(
@@ -402,13 +506,13 @@
     width = hidden.shape[1]
     shard_width = width // nt
     cache = key_value_cache[:, :, 0, :]
-    place = jnp.stack([c, y, z, lax.rem(t - y + nt, nt)]).astype(jnp.int32)
+    place = jnp.stack([c, y, z, lax.rem(t - y + nt, nt), m]).astype(jnp.int32)
     where = lax.rem(t - jnp.arange(nt, dtype=jnp.int32) + nt, nt)
 
     message = call(
         message_kernel,
         shape(CHIP_COUNT, FIRST_ROWS, LANES, dtype=bf16),
-        [SMEM, SMEM, VMEM, VMEM, VMEM],
+        [SMEM, SMEM, HBM, HBM, HBM],
         (
             rewards,
             prompt_group_index,
@@ -418,32 +522,39 @@
         ),
     )
 
+    w_rows = query_key_value_weight[:, 0, :]
+    w_rows_other = swapped(w_rows)
     w_cols = output_weight_frozen[0].T
+    w_cols_other = swapped(w_cols)
+
     ny = lax.axis_size("y")
     turned = lax.ppermute(
         w_cols, ("y", "t"), [(a * nt + b, b * nt + a) for a in range(ny) for b in range(nt)]
     )
+    turned, message, place, where = together(turned, message, place, where)
     w_block = lax.all_gather(turned, DP, axis=0, tiled=True)
     w_block = w_block.reshape(nt, shard_width, w_cols.shape[1])
 
     left = shift(attention_rows, 1, nt)
     right = shift(attention_rows, nt - 1, nt)
-    w_rows = query_key_value_weight[:, 0, :]
-    w_rows_other = swapped(w_rows)
-    w_cols_other = swapped(w_cols)
 
     arrived = exchange(message, CHIPS)
-    gain = lax.dynamic_slice_in_dim(attention_norm_gain, m * LANES, LANES, 0).astype(f32)[None, :]
+    gain = attention_norm_gain[None, :]
     sent, state = call(
         qkv_first_kernel,
         (shape(CHIP_COUNT * QKV_ROWS, LANES), shape(ROLLS * CHIP_COUNT, LANES)),
-        [SMEM] + [VMEM] * 4,
+        [SMEM, ANY, HBM, HBM, ANY],
         (place, arrived, gain, w_rows, w_rows_other),
         scratch=[pltpu.VMEM((CHIP_COUNT * FIRST_ROWS, LANES), f32)],
     )
     arrived_other = swapped(arrived)
-    sent, arrived, arrived_other = together(sent, arrived, arrived_other)
+    sent, arrived, arrived_other, left, right = together(
+        sent, arrived, arrived_other, left, right
+    )
     came = exchange(sent.reshape(CHIP_COUNT, QKV_ROWS, LANES), CHIPS)
+    half = attention_rows.shape[0] // 2
+    far_a = shift(left[:half], 1, nt)
+    far_b = shift(right[half:], nt - 1, nt)
 
     rows = attention_rows.shape[0]
     weighted, ab, part = call(
@@ -453,7 +564,7 @@
             shape(CHIP_COUNT, 2 * PIECE, LANES, dtype=bf16),
             shape(rows + LANES, LANES),
         ),
-        [SMEM] * 4 + [VMEM] * 4,
+        [SMEM] * 4 + [ANY, ANY, HBM, HBM],
         (
             place,
             rewards,
@@ -473,8 +584,8 @@
     attended, kv, _ = attend(
         False, cache_fill_lengths, came.reshape(-1, LANES), cache, nothing, ab
     )
-    attended, *parts = together(attended, *parts)
-    everyone = to_all(attended, CHIPS)
+    attended, weighted, far_a, far_b = together(attended, weighted, far_a, far_b)
+    everyone = exchange(attended, CHIPS)
 
     low_back, b_cols, kept, given = call(
         gradient_kernel,
@@ -484,7 +595,7 @@
             shape(CHIP_COUNT, PIECE, LANES),
             shape(CHIP_COUNT, PIECE, LANES),
         ),
-        [SMEM] + [VMEM] * 6,
+        [SMEM] + [ANY] * 4 + [HBM] * 2,
         (place, *parts, attention_rows, weighted),
         flops=4 * rows * shard_width * LANES,
     )
@@ -492,43 +603,42 @@
     share = call(
         close_kernel,
         shape(ROLLS * CHIP_COUNT, 2 * LANES),
-        [SMEM] + [VMEM] * 4,
+        [SMEM, ANY, HBM, ANY, HBM],
         (place, everyone, w_cols, w_cols_other, ab),
         scratch=[pltpu.VMEM((CHIP_COUNT * ROLLS * HEADS_TP, LANES), f32)],
     )
-    share, given, kept = together(share, given, kept)
     shares = shifts(share, nt)
-    kept = kept + swapped(given)
-    summed = exchange(kept, CHIPS)
 
     sent = call(
         qkv_later_kernel,
         shape(CHIP_COUNT * QKV_ROWS, LANES),
-        [SMEM] + [VMEM] * 9,
+        [SMEM, HBM, HBM, HBM, ANY, HBM] + [ANY] * 4,
         (place, state, gain, w_rows, w_rows_other, b_cols, *shares),
     )
-    sent, left, right = together(sent, left, right)
+    sent, low_back, given = together(sent, low_back, given)
+    kept = kept + swapped(given)
     came = exchange(sent.reshape(CHIP_COUNT, QKV_ROWS, LANES), CHIPS)
-    half = rows // 2
-    far_a = shift(left[:half], 1, nt)
-    far_b = shift(right[half:], nt - 1, nt)
+
+    adapted = output_rows(
+        where, attention_rows, left, right, far_a, far_b, w_block, low_back, ab
+    )
+
+    came, adapted = together(came, adapted)
+
+    attended, _, owned = attend(True, cache_fill_lengths, came.reshape(-1, LANES), cache, kv, ab)
+    attended, kept = together(attended, kept)
+    summed = exchange(kept, CHIPS)
+    cols = decode_columns(where, shifts(attended, nt), w_block, ab, owned.reshape(ROLLS, width))
+    arriving = shifts(cols, nt)
+    arriving[1], summed = together(arriving[1], summed)
     summed = summed.sum(axis=0)
-
-    attended, _, owned = attend(True, cache_fill_lengths, came.reshape(-1, LANES), cache, kv, ab)
-    adapted, own_cols = output_rows(
-        where,
-        attention_rows,
-        left,
-        right,
-        far_a,
-        far_b,
-        w_block,
-        low_back,
-        ab,
-        shifts(attended, nt),
-        owned.reshape(ROLLS, width),
-    )
-    decoded = to_all(own_cols, "t").transpose(1, 0, 2).reshape(ROLLS, width)
+    decoded = call(
+        place_kernel,
+        shape(ROLLS, width),
+        [SMEM] + [ANY] * nt,
+        (where, *arriving),
+        grant=SMALL_GRANT,
+    )
     grad_a = summed[:, :RANK].T[:, None, :]
     grad_b = summed[:, RANK:].T[:, None, :]
     return (decoded, adapted, grad_a, grad_b)

time: 210 us -> 192 us (0.914)
  waiting for transfers between devices: 66.2 us -> 22.9 us
  Pallas kernels: 25.2 us -> 50.3 us
  blocking collectives: 0 us -> 24.5 us
  local copies, waits for them, and re-layouts: 32.5 us -> 12.8 us
  starting transfers between devices: 67.4 us -> 63.7 us
    pallas_call x9 -> x11, Pallas kernels: 25.2 us -> 50.3 us  [the longest x9 29.9 us: call(): pl.pallas_call(body, out_shape=out, in_specs=[pl.BlockSpec(memory_space=k...]
    all_to_all x0 -> x1, blocking collectives: none -> 24.5 us  [exchange(): return lax.all_to_all(x, axes, split_axis=0, concat_axis=0, tiled=True)]
    all_to_all x6 -> x4, waiting for transfers between devices: 31.4 us -> 8.34 us  [exchange(): return lax.all_to_all(x, axes, split_axis=0, concat_axis=0, tiled=True)]
    ppermute x13 -> x16, waiting for transfers between devices: 29.8 us -> 9.98 us  [shift(): return lax.ppermute(x, 't', [(i, (i + by) % n) for i in range(n)])]
    unnamed x73 -> x44, local copies, waits for them, and re-layouts: 26.8 us -> 7.04 us
    all_to_all x6 -> x4, starting transfers between devices: 50.2 us -> 31.4 us  [exchange(): return lax.all_to_all(x, axes, split_axis=0, concat_axis=0, tiled=True)]
    ppermute x13 -> x16, starting transfers between devices: 13.5 us -> 28.3 us  [shift(): return lax.ppermute(x, 't', [(i, (i + by) % n) for i in range(n)])]
    ppermute x1, waiting for transfers between devices: 4.95 us -> 1.44 us  [shards(): lax.ppermute(w_cols, ('y', 't'), [(a * nt + b, b * nt + a) for a in range...]
  transfers between devices with their start and end apart: 25 -> 26, of which waited for: 12 -> 9; matrix products, arithmetic and copies ran while one was open for 4% -> 4% of each run, Pallas kernels for 7% -> 23%
where the time goes in v4:
time: 192 us; the launch traced here: 191 us
  starting transfers between devices  63.7 us (33%)
  Pallas kernels  50.3 us (26%)
  blocking collectives  24.5 us (13%)
  waiting for transfers between devices  22.9 us (12%)
  between operations  14.4 us (8%)
  local copies, waits for them, and re-layouts  12.8 us (7%)
  other arithmetic  2.32 us (1%)
    all_to_all x4, starting transfers between devices, exchange(): return lax.all_to_all(x, axes, split_axis=0, concat_axis=0, tiled=True)  31.4 us
    pallas_call x9, Pallas kernels, call(): pl.pallas_call(body, out_shape=out, in_specs=[pl.BlockSpec(memory_space=k...  29.9 us
    ppermute x16, starting transfers between devices, shift(): return lax.ppermute(x, 't', [(i, (i + by) % n) for i in range(n)])  28.3 us
    all_to_all x1, blocking collectives, exchange(): return lax.all_to_all(x, axes, split_axis=0, concat_axis=0, tiled=True)  24.5 us
    pallas_call x1, Pallas kernels, output_rows(): pl.pallas_call(rows_kernel, out_shape=shape(rows, width), grid_spec=pltpu...  10.3 us
    pallas_call x1, Pallas kernels, decode_columns(): pl.pallas_call(decode_kernel, out_shape=shape(8, width), grid_spec=pltpu....  10.1 us
    ppermute x16, waiting for transfers between devices, shift(): return lax.ppermute(x, 't', [(i, (i + by) % n) for i in range(n)])  9.98 us
    all_to_all x4, waiting for transfers between devices, exchange(): return lax.all_to_all(x, axes, split_axis=0, concat_axis=0, tiled=True)  8.34 us
  transfers between devices with their start and end apart: 26, of which 9 were waited for; matrix products, arithmetic and copies ran while one was open for 4% of the time, Pallas kernels for 23%

profile of v4, /device:TPU:8, one launch (start us, length us, event | category | flops | bytes accessed | tf_op | source)
XLA Modules:
  0.0 190.9 jit_solution(11791381090522646104)
XLA Ops:
  7.2 3.3 %collective-permute-start = (bf16[64,1024]{1,0:T(8,128)(2,1)}, bf16[64,1024]{1,0:T(8,128)(2,1)S(1)}, u32[]{:S(2)}, u32[]{:S(2)}) collective-permute-start(bf16[64,1024]{1,0:T(8,128)(2,1)} %bitcast.46), channel_id=1, source_target_pairs={{0,0},{1,64},{2,128},{3,192},{64,1},{65,65},{66,129},{67,193},{128... | collective-permute-start | bytes 393224 | tf_op jit(solution)/shard_map/ppermute | solution.py:531
  10.5 0.7 stack.23.refs_0_
  11.2 2.2 %shard_map.156 = bf16[32,24,128]{2,1,0:T(8,128)(2,1)} custom-call(f32[2]{0:T(128)} %refs_1_.3, s32[2]{0:T(128)} %refs_2_.1, bf16[16,64]{1,0:T(8,128)(2,1)} %bitcast.49, bf16[16,64]{1,0:T(8,128)(2,1)} %bitcast.50, bf16[2,4096]{1,0:T(2,128)(2,1)} %refs_4_.1), custom_call_target="tpu_custom_call" | custom-call | bytes 217104 | tf_op jit(solution)/shard_map/pallas_call | solution.py:117
  14.0 1.4 collective-permute-done
  15.5 0.7 copy-done.14
  16.2 6.7 %collective-permute-start.4 = (bf16[512,1024]{1,0:T(8,128)(2,1)}, bf16[512,1024]{1,0:T(8,128)(2,1)}, u32[]{:S(2)}, u32[]{:S(2)}) collective-permute-start(bf16[512,1024]{1,0:T(8,128)(2,1)} %own.1), channel_id=1, source_target_pairs={{0,3},{1,0},{2,1},{3,2},{4,7},{5,4},{6,5},{7,6},{8,11},{9,8},{10,9... | collective-permute-start | bytes 3145736 | tf_op jit(solution)/shard_map/ppermute | solution.py:59
  22.9 24.5 %all_to_all.25.refs_1_.refs_4_ = bf16[32,24,128]{2,1,0:T(8,128)(2,1)S(1)} all-to-all(bf16[32,24,128]{2,1,0:T(8,128)(2,1)} %shard_map.156), channel_id=1, replica_groups=mesh['y'=4,'z'=8,'c'=2,'t'=4] {'y','z'}, dimensions={0} | all-to-all | bytes 393216 | tf_op jit(solution)/shard_map/all_to_all | solution.py:67
  47.9 1.3 broadcast_in_dim.12.refs_2_
  49.2 0.6 copy-done.5
  49.9 2.9 %shard_map.157 = (f32[768,128]{1,0:T(8,128)}, f32[64,128]{1,0:T(8,128)}) custom-call(s32[5]{0:T(128)} %stack.23.refs_0_, bf16[32,24,128]{2,1,0:T(8,128)(2,1)} %copy-done.2, bf16[1,4096]{1,0:T(2,128)(2,1)} %broadcast_in_dim.12.refs_2_, bf16[64,1280]{1,0:T(8,128)(2,1)} %bitcast.43, bf16[64,1280]{1,0:T(8,128)(2,1)} %copy-done.5), custom_call_target="tpu_custom_call" | custom-call | bytes 958484 | tf_op jit(solution)/shard_map/pallas_call | solution.py:117
  52.8 6.2 %all-to-all-start.1 = ((f32[32,24,128]{2,1,0:T(8,128)}), f32[32,24,128]{2,1,0:T(8,128)S(1)}, u32[]{:S(2)}, u32[]{:S(2)}) async-start(f32[32,24,128]{2,1,0:T(8,128)} %bitcast.45), calls=%async_computation.1 | async-start | bytes 786432 | tf_op jit(solution)/shard_map/all_to_all | solution.py:67
  59.1 1.1 slice.13
  60.2 3.3 %collective-permute-start.9 = (bf16[256,1024]{1,0:T(8,128)(2,1)S(1)}, bf16[256,1024]{1,0:T(8,128)(2,1)}, u32[]{:S(2)}, u32[]{:S(2)}) collective-permute-start(bf16[256,1024]{1,0:T(8,128)(2,1)S(1)} %slice.13), channel_id=1, source_target_pairs={{0,3},{1,0},{2,1},{3,2},{4,7},{5,4},{6,5},{7,6},{8,11},{9,8},{10,9... | collective-permute-start | bytes 1572872 | tf_op jit(solution)/shard_map/ppermute | solution.py:59
  63.5 4.2 %shard_map.158 = (bf16[512,1024]{1,0:T(8,128)(2,1)}, bf16[32,32,128]{2,1,0:T(8,128)(2,1)}, f32[640,128]{1,0:T(8,128)}) custom-call(s32[5]{0:T(128)} %stack.23.refs_0_, f32[2]{0:T(128)} %refs_1_.3, s32[2]{0:T(128)} %refs_2_.1, s32[2]{0:T(128)} %refs_3_.1, bf16[32,24,128]{2,1,0:T(8,128)(2,1)} %copy-done.2, bf16[32,24,128]{2,1,0:T(8,128)(2,1)} %copy-done.11, ...), custom_call_target="tpu_custom_call" | custom-call | flops 268435456 | bytes 4128812 | tf_op jit(solution)/shard_map/pallas_call | solution.py:117
  67.8 3.3 %collective-permute-start.6 = (f32[640,128]{1,0:T(8,128)}, f32[640,128]{1,0:T(8,128)S(1)}, u32[]{:S(2)}, u32[]{:S(2)}) collective-permute-start(f32[640,128]{1,0:T(8,128)} %get-tuple-element.46.refs_1_), channel_id=1, source_target_pairs={{0,2},{1,3},{2,0},{3,1},{4,6},{5,7},{6,4},{7,5},{8,10},{9,11},{10,... | collective-permute-start | bytes 983048 | tf_op jit(solution)/shard_map/ppermute | solution.py:59
  71.1 0.6 collective-permute-start.7
  71.8 0.6 broadcast_in_dim.13.refs_3_
  72.5 4.3 %shard_map.159 = (bf16[32,16,128]{2,1,0:T(8,128)(2,1)}, f32[8,128]{1,0:T(8,128)}, f32[64,128]{1,0:T(8,128)}) custom-call(s32[2]{0:T(128)} %refs_0_.5, f32[768,128]{1,0:T(8,128)} %bitcast.39, bf16[2,2048,256]{2,1,0:T(8,128)(2,1)} %bitcast.32, f32[8,128]{1,0:T(8,128)} %broadcast_in_dim.13.refs_3_, bf16[1024,128]{1,0:T(8,128)(2,1)} %bitcast.34), custom_call_target="tpu_custom_call" | custom-call | flops 67108864 | bytes 2924552 | tf_op jit(solution)/shard_map/pallas_call | solution.py:117
  76.9 6.0 %collective-permute-done.9.far_b = bf16[256,1024]{1,0:T(8,128)(2,1)} collective-permute-done((bf16[256,1024]{1,0:T(8,128)(2,1)S(1)}, bf16[256,1024]{1,0:T(8,128)(2,1)}, u32[]{:S(2)}, u32[]{:S(2)}) %collective-permute-start.9) | collective-permute-done | bytes 524320 | tf_op jit(solution)/shard_map/ppermute | solution.py:59
  82.9 9.8 %all-to-all-start.2 = ((bf16[32,16,128]{2,1,0:T(8,128)(2,1)}), bf16[32,16,128]{2,1,0:T(8,128)(2,1)S(1)}, u32[]{:S(2)}, u32[]{:S(2)}) async-start(bf16[32,16,128]{2,1,0:T(8,128)(2,1)} %get-tuple-element.55), calls=%async_computation.2 | async-start | bytes 262144 | tf_op jit(solution)/shard_map/all_to_all | solution.py:67
  92.8 1.3 collective-permute-done.10.refs_3_
  94.2 8.3 %all-to-all-done.2.refs_1_ = bf16[32,16,128]{2,1,0:T(8,128)(2,1)S(1)} async-done(((bf16[32,16,128]{2,1,0:T(8,128)(2,1)}), bf16[32,16,128]{2,1,0:T(8,128)(2,1)S(1)}, u32[]{:S(2)}, u32[]{:S(2)}) %all-to-all-start.2) | async-done | bytes 131104 | tf_op jit(solution)/shard_map/all_to_all | solution.py:67
  102.5 0.6 copy-done.6
  103.1 2.7 %shard_map.161.refs_6_ = f32[64,256]{1,0:T(8,128)} custom-call(s32[5]{0:T(128)} %stack.23.refs_0_, bf16[32,16,128]{2,1,0:T(8,128)(2,1)} %copy-done.6, bf16[64,1024]{1,0:T(8,128)(2,1)} %bitcast.47, bf16[64,1024]{1,0:T(8,128)(2,1)} %copy-done.13, bf16[1024,128]{1,0:T(8,128)(2,1)} %bitcast.35), custom_call_target="tpu_custom_call" | custom-call | bytes 720916 | tf_op jit(solution)/shard_map/pallas_call | solution.py:117
  106.0 5.2 %collective-permute-start.12 = (f32[64,256]{1,0:T(8,128)}, f32[64,256]{1,0:T(8,128)S(1)}, u32[]{:S(2)}, u32[]{:S(2)}) collective-permute-start(f32[64,256]{1,0:T(8,128)} %shard_map.161.refs_6_), channel_id=1, source_target_pairs={{0,2},{1,3},{2,0},{3,1},{4,6},{5,7},{6,4},{7,5},{8,10},{9,11},{10,... | collective-permute-start | bytes 196616 | tf_op jit(solution)/shard_map/ppermute | solution.py:59
  111.2 0.7 copy-done.7
  112.0 0.7 copy-done.9
  112.8 4.4 %shard_map.160 = (bf16[512,128]{1,0:T(8,128)(2,1)}, f32[128,128]{1,0:T(8,128)}, f32[32,16,128]{2,1,0:T(8,128)}, f32[32,16,128]{2,1,0:T(8,128)}) custom-call(s32[5]{0:T(128)} %stack.23.refs_0_, f32[640,128]{1,0:T(8,128)} %get-tuple-element.46.refs_1_, f32[640,128]{1,0:T(8,128)} %copy-done.7, f32[640,128]{1,0:T(8,128)} %copy-done.8, f32[640,128]{1,0:T(8,128)} %copy-done.9, ...), custom_call_target="tpu_custom_call" | custom-call | flops 268435456 | bytes 4128788 | tf_op jit(solution)/shard_map/pallas_call | solution.py:117
  117.8 3.3 %shard_map.162 = f32[768,128]{1,0:T(8,128)} custom-call(s32[5]{0:T(128)} %stack.23.refs_0_, f32[64,128]{1,0:T(8,128)} %get-tuple-element.42.refs_1_, bf16[1,4096]{1,0:T(2,128)(2,1)} %broadcast_in_dim.12.refs_2_, bf16[64,1280]{1,0:T(8,128)(2,1)} %bitcast.44, bf16[64,1280]{1,0:T(8,128)(2,1)} %copy-done.5, f32[128,128]{1,0:T(8,128)} %get-tuple-element.54.refs_5_, ...), custom_call_target="tpu_custom_call" | custom-call | bytes 1089556 | tf_op jit(solution)/shard_map/pallas_call | solution.py:117
  121.1 5.7 %all-to-all-start.3 = ((f32[32,24,128]{2,1,0:T(8,128)}), f32[32,24,128]{2,1,0:T(8,128)S(1)}, u32[]{:S(2)}, u32[]{:S(2)}) async-start(f32[32,24,128]{2,1,0:T(8,128)} %bitcast.41), calls=%async_computation.3 | async-start | bytes 786432 | tf_op jit(solution)/shard_map/all_to_all | solution.py:67
  126.9 1.7 collective-permute-done.14
  128.6 1.7 add.15
  130.3 10.3 %shard_map.163 = f32[512,1024]{1,0:T(8,128)} custom-call(s32[4]{0:T(128)} %compare_select_fusion.where_ref.refs_0_, bf16[512,1024]{1,0:T(8,128)(2,1)} %own.1, bf16[512,1024]{1,0:T(8,128)(2,1)} %copy-done.10, bf16[512,1024]{1,0:T(8,128)(2,1)} %collective-permute-done.4.right, bf16[256,1024]{1,0:T(8,128)(2,1)} %copy-done.21, ...), custom_call_target="tpu_custom_call" | custom-call | flops 4294967296 | bytes 14680064 | tf_op jit(solution)/shard_map/pallas_call | solution.py:379
  140.7 0.8 copy-done.4
  141.4 4.4 %shard_map.164 = (f32[24,128]{1,0:T(8,128)}, f32[8,128]{1,0:T(8,128)}, f32[64,128]{1,0:T(8,128)}) custom-call(s32[2]{0:T(128)} %refs_0_.5, f32[768,128]{1,0:T(8,128)} %bitcast.40, bf16[2,2048,256]{2,1,0:T(8,128)(2,1)} %bitcast.33, f32[8,128]{1,0:T(8,128)} %get-tuple-element.64.refs_3_, bf16[1024,128]{1,0:T(8,128)(2,1)} %bitcast.37), custom_call_target="tpu_custom_call" | custom-call | flops 67108864 | bytes 2805768 | tf_op jit(solution)/shard_map/pallas_call | solution.py:117
  145.9 9.8 %all-to-all-start.4 = ((f32[32,16,128]{2,1,0:T(8,128)}), f32[32,16,128]{2,1,0:T(8,128)S(1)}, u32[]{:S(2)}, u32[]{:S(2)}) async-start(f32[32,16,128]{2,1,0:T(8,128)} %add.15), calls=%async_computation.4 | async-start | bytes 524288 | tf_op jit(solution)/shard_map/all_to_all | solution.py:67
  155.7 2.0 %collective-permute-start.15 = (f32[24,128]{1,0:T(8,128)}, f32[24,128]{1,0:T(8,128)S(1)}, u32[]{:S(2)}, u32[]{:S(2)}) collective-permute-start(f32[24,128]{1,0:T(8,128)} %get-tuple-element.68.p0), channel_id=1, source_target_pairs={{0,1},{1,2},{2,3},{3,0},{4,5},{5,6},{6,7},{7,4},{8,9},{9,10},{10,1... | collective-permute-start | bytes 36872 | tf_op jit(solution)/shard_map/ppermute | solution.py:59
  157.9 2.5 %collective-permute-start.17 = (f32[24,128]{1,0:T(8,128)}, f32[24,128]{1,0:T(8,128)S(1)}, u32[]{:S(2)}, u32[]{:S(2)}) collective-permute-start(f32[24,128]{1,0:T(8,128)} %get-tuple-element.68.p0), channel_id=1, source_target_pairs={{0,3},{1,0},{2,1},{3,2},{4,7},{5,4},{6,5},{7,6},{8,11},{9,8},{10,9... | collective-permute-start | bytes 36872 | tf_op jit(solution)/shard_map/ppermute | solution.py:59
  160.4 1.4 reshape.35.owned
  161.8 1.2 collective-permute-done.16.p2
  164.3 10.1 %shard_map.165.refs_1_ = f32[8,1024]{1,0:T(8,128)} custom-call(s32[4]{0:T(128)} %compare_select_fusion.where_ref.refs_0_, f32[24,128]{1,0:T(8,128)} %get-tuple-element.68.p0, f32[24,128]{1,0:T(8,128)} %copy-done.18, f32[24,128]{1,0:T(8,128)} %copy-done.19, f32[24,128]{1,0:T(8,128)} %copy-done.20, bf16[4,1024,1024]{2,1,0:T(8,128)(2,1)} %bitcast.31, ...), custom_call_target="tpu_custom_call" | custom-call | flops 134217728 | bytes 8388608 | tf_op jit(solution)/shard_map/pallas_call | solution.py:450
  174.5 3.2 %collective-permute-start.19 = (f32[8,1024]{1,0:T(8,128)}, f32[8,1024]{1,0:T(8,128)S(1)}, u32[]{:S(2)}, u32[]{:S(2)}) collective-permute-start(f32[8,1024]{1,0:T(8,128)} %shard_map.165.refs_1_), channel_id=1, source_target_pairs={{0,2},{1,3},{2,0},{3,1},{4,6},{5,7},{6,4},{7,5},{8,10},{9,11},{10,... | collective-permute-start | bytes 98312 | tf_op jit(solution)/shard_map/ppermute | solution.py:59
  177.8 0.7 collective-permute-start.20
  178.5 1.3 collective-permute-done.18.refs_2_
  179.8 0.7 slice_bitcast_fusion
  180.5 1.4 collective-permute-done.20.refs_4_
  181.9 0.8 copy-done
  182.7 1.4 shard_map.166
  (71 shorter events, 4.4 us)
Async XLA Ops:
  7.2 123.2 %all-gather.2.cloned.1.call-start = ((), (), s32[]{:S(2)}) async-start(), calls=%async_computation.5 | async-start | bytes 8519680 | tf_op jit(solution)/shard_map/all_gather | solution.py:535
  7.2 8.2 %collective-permute-start = (bf16[64,1024]{1,0:T(8,128)(2,1)}, bf16[64,1024]{1,0:T(8,128)(2,1)S(1)}, u32[]{:S(2)}, u32[]{:S(2)}) collective-permute-start(bf16[64,1024]{1,0:T(8,128)(2,1)} %bitcast.46), channel_id=1, source_target_pairs={{0,0},{1,64},{2,128},{3,192},{64,1},{65,65},{66,129},{67,193},{128... | collective-permute-start | bytes 393224 | tf_op jit(solution)/shard_map/ppermute | solution.py:531
  15.5 0.7 copy-start.14
  16.1 36.6 %collective-permute-start.3 = (bf16[512,1024]{1,0:T(8,128)(2,1)}, bf16[512,1024]{1,0:T(8,128)(2,1)S(1)}, u32[]{:S(2)}, u32[]{:S(2)}) collective-permute-start(bf16[512,1024]{1,0:T(8,128)(2,1)} %own.1), channel_id=1, source_target_pairs={{0,1},{1,2},{2,3},{3,0},{4,5},{5,6},{6,7},{7,4},{8,9},{9,10},{10,1... | collective-permute-start | bytes 3145736 | tf_op jit(solution)/shard_map/ppermute | solution.py:59
  16.2 36.6 %collective-permute-start.4 = (bf16[512,1024]{1,0:T(8,128)(2,1)}, bf16[512,1024]{1,0:T(8,128)(2,1)}, u32[]{:S(2)}, u32[]{:S(2)}) collective-permute-start(bf16[512,1024]{1,0:T(8,128)(2,1)} %own.1), channel_id=1, source_target_pairs={{0,3},{1,0},{2,1},{3,2},{4,7},{5,4},{6,5},{7,6},{8,11},{9,8},{10,9... | collective-permute-start | bytes 3145736 | tf_op jit(solution)/shard_map/ppermute | solution.py:59
  47.4 1.9 copy-start.2
  47.4 5.4 %collective-permute-start.2 = (bf16[32,24,128]{2,1,0:T(8,128)(2,1)S(1)}, bf16[32,24,128]{2,1,0:T(8,128)(2,1)S(1)}, u32[]{:S(2)}, u32[]{:S(2)}) collective-permute-start(bf16[32,24,128]{2,1,0:T(8,128)(2,1)S(1)} %all_to_all.25.refs_1_.refs_4_), channel_id=1, source_target_pairs={{0,4},{4,0},{1,5},{5,1},{2,6},{6,2},{3,7},{7,3},{8,12},{12,8},{9,1... | collective-permute-start | bytes 589832 | tf_op jit(solution)/shard_map/ppermute | solution.py:55
  47.4 1.9 collective-permute-start.1
  49.2 0.7 copy-start.5
  52.8 10.7 %copy-start.11 = (bf16[32,24,128]{2,1,0:T(8,128)(2,1)}, bf16[32,24,128]{2,1,0:T(8,128)(2,1)S(1)}, u32[]{:S(2)}) copy-start(bf16[32,24,128]{2,1,0:T(8,128)(2,1)S(1)} %collective-permute-done.2.refs_5_) | copy-start | bytes 589828
  52.8 14.9 %copy-start.10 = (bf16[512,1024]{1,0:T(8,128)(2,1)}, bf16[512,1024]{1,0:T(8,128)(2,1)S(1)}, u32[]{:S(2)}) copy-start(bf16[512,1024]{1,0:T(8,128)(2,1)S(1)} %collective-permute-done.3.left) | copy-start | bytes 3145732
  52.8 19.0 %all-to-all-start.1 = ((f32[32,24,128]{2,1,0:T(8,128)}), f32[32,24,128]{2,1,0:T(8,128)S(1)}, u32[]{:S(2)}, u32[]{:S(2)}) async-start(f32[32,24,128]{2,1,0:T(8,128)} %bitcast.45), calls=%async_computation.1 | async-start | bytes 786432 | tf_op jit(solution)/shard_map/all_to_all | solution.py:67
  59.0 17.8 %collective-permute-start.8 = (bf16[256,1024]{1,0:T(8,128)(2,1)S(1)}, bf16[256,1024]{1,0:T(8,128)(2,1)S(1)}, u32[]{:S(2)}, u32[]{:S(2)}) collective-permute-start(bf16[256,1024]{1,0:T(8,128)(2,1)S(1)} %slice.12), channel_id=1, source_target_pairs={{0,1},{1,2},{2,3},{3,0},{4,5},{5,6},{6,7},{7,4},{8,9},{9,10},{10,1... | collective-permute-start | bytes 1572872 | tf_op jit(solution)/shard_map/ppermute | solution.py:59
  60.2 22.7 %collective-permute-start.9 = (bf16[256,1024]{1,0:T(8,128)(2,1)S(1)}, bf16[256,1024]{1,0:T(8,128)(2,1)}, u32[]{:S(2)}, u32[]{:S(2)}) collective-permute-start(bf16[256,1024]{1,0:T(8,128)(2,1)S(1)} %slice.13), channel_id=1, source_target_pairs={{0,3},{1,0},{2,1},{3,2},{4,7},{5,4},{6,5},{7,6},{8,11},{9,8},{10,9... | collective-permute-start | bytes 1572872 | tf_op jit(solution)/shard_map/ppermute | solution.py:59
  67.7 25.0 %copy-start.12 = (bf16[1,1024,64]{1,2,0:T(8,128)(2,1)S(1)}, bf16[1,1024,64]{1,2,0:T(8,128)(2,1)}, u32[]{:S(2)}) copy-start(bf16[1,1024,64]{1,2,0:T(8,128)(2,1)} %param.18) | copy-start | bytes 393220
  67.8 43.4 %collective-permute-start.5 = (f32[640,128]{1,0:T(8,128)}, f32[640,128]{1,0:T(8,128)S(1)}, u32[]{:S(2)}, u32[]{:S(2)}) collective-permute-start(f32[640,128]{1,0:T(8,128)} %get-tuple-element.46.refs_1_), channel_id=1, source_target_pairs={{0,1},{1,2},{2,3},{3,0},{4,5},{5,6},{6,7},{7,4},{8,9},{9,10},{10,1... | collective-permute-start | bytes 983048 | tf_op jit(solution)/shard_map/ppermute | solution.py:59
  67.8 43.3 %collective-permute-start.6 = (f32[640,128]{1,0:T(8,128)}, f32[640,128]{1,0:T(8,128)S(1)}, u32[]{:S(2)}, u32[]{:S(2)}) collective-permute-start(f32[640,128]{1,0:T(8,128)} %get-tuple-element.46.refs_1_), channel_id=1, source_target_pairs={{0,2},{1,3},{2,0},{3,1},{4,6},{5,7},{6,4},{7,5},{8,10},{9,11},{10,... | collective-permute-start | bytes 983048 | tf_op jit(solution)/shard_map/ppermute | solution.py:59
  71.1 40.0 %collective-permute-start.7 = (f32[640,128]{1,0:T(8,128)}, f32[640,128]{1,0:T(8,128)S(1)}, u32[]{:S(2)}, u32[]{:S(2)}) collective-permute-start(f32[640,128]{1,0:T(8,128)} %get-tuple-element.46.refs_1_), channel_id=1, source_target_pairs={{0,3},{1,0},{2,1},{3,2},{4,7},{5,4},{6,5},{7,6},{8,11},{9,8},{10,9... | collective-permute-start | bytes 983048 | tf_op jit(solution)/shard_map/ppermute | solution.py:59
  71.8 0.8 copy-start.3
  76.9 53.5 %copy-start.21 = (bf16[256,1024]{1,0:T(8,128)(2,1)}, bf16[256,1024]{1,0:T(8,128)(2,1)S(1)}, u32[]{:S(2)}) copy-start(bf16[256,1024]{1,0:T(8,128)(2,1)S(1)} %collective-permute-done.8.far_a) | copy-start | bytes 1572868
  82.9 19.6 %all-to-all-start.2 = ((bf16[32,16,128]{2,1,0:T(8,128)(2,1)}), bf16[32,16,128]{2,1,0:T(8,128)(2,1)S(1)}, u32[]{:S(2)}, u32[]{:S(2)}) async-start(bf16[32,16,128]{2,1,0:T(8,128)(2,1)} %get-tuple-element.55), calls=%async_computation.2 | async-start | bytes 262144 | tf_op jit(solution)/shard_map/all_to_all | solution.py:67
  92.7 1.4 collective-permute-start.10
  94.1 8.3 %copy-start.13 = (bf16[64,1024]{1,0:T(8,128)(2,1)}, bf16[64,1024]{1,0:T(8,128)(2,1)S(1)}, u32[]{:S(2)}) copy-start(bf16[64,1024]{1,0:T(8,128)(2,1)S(1)} %collective-permute-done.10.refs_3_) | copy-start | bytes 393220
  102.5 0.6 copy-start.6
  105.9 11.3 %collective-permute-start.11 = (f32[64,256]{1,0:T(8,128)}, f32[64,256]{1,0:T(8,128)S(1)}, u32[]{:S(2)}, u32[]{:S(2)}) collective-permute-start(f32[64,256]{1,0:T(8,128)} %shard_map.161.refs_6_), channel_id=1, source_target_pairs={{0,1},{1,2},{2,3},{3,0},{4,5},{5,6},{6,7},{7,4},{8,9},{9,10},{10,1... | collective-permute-start | bytes 196616 | tf_op jit(solution)/shard_map/ppermute | solution.py:59
  106.0 11.2 %collective-permute-start.12 = (f32[64,256]{1,0:T(8,128)}, f32[64,256]{1,0:T(8,128)S(1)}, u32[]{:S(2)}, u32[]{:S(2)}) collective-permute-start(f32[64,256]{1,0:T(8,128)} %shard_map.161.refs_6_), channel_id=1, source_target_pairs={{0,2},{1,3},{2,0},{3,1},{4,6},{5,7},{6,4},{7,5},{8,10},{9,11},{10,... | collective-permute-start | bytes 196616 | tf_op jit(solution)/shard_map/ppermute | solution.py:59
  111.1 0.7 copy-start.7
  111.1 6.0 %collective-permute-start.13 = (f32[64,256]{1,0:T(8,128)}, f32[64,256]{1,0:T(8,128)S(1)}, u32[]{:S(2)}, u32[]{:S(2)}) collective-permute-start(f32[64,256]{1,0:T(8,128)} %shard_map.161.refs_6_), channel_id=1, source_target_pairs={{0,3},{1,0},{2,1},{3,2},{4,7},{5,4},{6,5},{7,6},{8,11},{9,8},{10,9... | collective-permute-start | bytes 196616 | tf_op jit(solution)/shard_map/ppermute | solution.py:59
  111.1 0.9 copy-start.8
  112.0 0.7 copy-start.9
  117.1 0.6 copy-start.15
  117.2 0.6 copy-start.16
  117.2 0.6 copy-start.17
  121.1 19.5 %all-to-all-start.3 = ((f32[32,24,128]{2,1,0:T(8,128)}), f32[32,24,128]{2,1,0:T(8,128)S(1)}, u32[]{:S(2)}, u32[]{:S(2)}) async-start(f32[32,24,128]{2,1,0:T(8,128)} %bitcast.41), calls=%async_computation.3 | async-start | bytes 786432 | tf_op jit(solution)/shard_map/all_to_all | solution.py:67
  126.8 1.8 collective-permute-start.14
  140.6 0.8 copy-start.4
  145.9 33.9 %all-to-all-start.4 = ((f32[32,16,128]{2,1,0:T(8,128)}), f32[32,16,128]{2,1,0:T(8,128)S(1)}, u32[]{:S(2)}, u32[]{:S(2)}) async-start(f32[32,16,128]{2,1,0:T(8,128)} %add.15), calls=%async_computation.4 | async-start | bytes 524288 | tf_op jit(solution)/shard_map/all_to_all | solution.py:67
  155.7 6.1 %collective-permute-start.15 = (f32[24,128]{1,0:T(8,128)}, f32[24,128]{1,0:T(8,128)S(1)}, u32[]{:S(2)}, u32[]{:S(2)}) collective-permute-start(f32[24,128]{1,0:T(8,128)} %get-tuple-element.68.p0), channel_id=1, source_target_pairs={{0,1},{1,2},{2,3},{3,0},{4,5},{5,6},{6,7},{7,4},{8,9},{9,10},{10,1... | collective-permute-start | bytes 36872 | tf_op jit(solution)/shard_map/ppermute | solution.py:59
  157.7 5.4 %collective-permute-start.16 = (f32[24,128]{1,0:T(8,128)}, f32[24,128]{1,0:T(8,128)S(1)}, u32[]{:S(2)}, u32[]{:S(2)}) collective-permute-start(f32[24,128]{1,0:T(8,128)} %get-tuple-element.68.p0), channel_id=1, source_target_pairs={{0,2},{1,3},{2,0},{3,1},{4,6},{5,7},{6,4},{7,5},{8,10},{9,11},{10,... | collective-permute-start | bytes 36872 | tf_op jit(solution)/shard_map/ppermute | solution.py:59
  157.9 5.2 %collective-permute-start.17 = (f32[24,128]{1,0:T(8,128)}, f32[24,128]{1,0:T(8,128)S(1)}, u32[]{:S(2)}, u32[]{:S(2)}) collective-permute-start(f32[24,128]{1,0:T(8,128)} %get-tuple-element.68.p0), channel_id=1, source_target_pairs={{0,3},{1,0},{2,1},{3,2},{4,7},{5,4},{6,5},{7,6},{8,11},{9,8},{10,9... | collective-permute-start | bytes 36872 | tf_op jit(solution)/shard_map/ppermute | solution.py:59
  161.8 20.1 %copy-start.1 = (s32[4]{0:T(128)S(1)}, s32[4]{0:T(128)}, u32[]{:S(2)}) copy-start(s32[4]{0:T(128)} %compare_select_fusion.where_ref.refs_0_) | copy-start | bytes 52
  161.8 1.3 copy-start.18
  163.1 0.6 copy-start.19
  163.7 0.6 copy-start.20
  174.3 5.4 %collective-permute-start.18 = (f32[8,1024]{1,0:T(8,128)}, f32[8,1024]{1,0:T(8,128)S(1)}, u32[]{:S(2)}, u32[]{:S(2)}) collective-permute-start(f32[8,1024]{1,0:T(8,128)} %shard_map.165.refs_1_), channel_id=1, source_target_pairs={{0,1},{1,2},{2,3},{3,0},{4,5},{5,6},{6,7},{7,4},{8,9},{9,10},{10,1... | collective-permute-start | bytes 98312 | tf_op jit(solution)/shard_map/ppermute | solution.py:59
  174.5 5.9 %collective-permute-start.19 = (f32[8,1024]{1,0:T(8,128)}, f32[8,1024]{1,0:T(8,128)S(1)}, u32[]{:S(2)}, u32[]{:S(2)}) collective-permute-start(f32[8,1024]{1,0:T(8,128)} %shard_map.165.refs_1_), channel_id=1, source_target_pairs={{0,2},{1,3},{2,0},{3,1},{4,6},{5,7},{6,4},{7,5},{8,10},{9,11},{10,... | collective-permute-start | bytes 98312 | tf_op jit(solution)/shard_map/ppermute | solution.py:59
  177.8 4.1 %collective-permute-start.20 = (f32[8,1024]{1,0:T(8,128)}, f32[8,1024]{1,0:T(8,128)S(1)}, u32[]{:S(2)}, u32[]{:S(2)}) collective-permute-start(f32[8,1024]{1,0:T(8,128)} %shard_map.165.refs_1_), channel_id=1, source_target_pairs={{0,3},{1,0},{2,1},{3,2},{4,7},{5,4},{6,5},{7,6},{8,11},{9,8},{10,9... | collective-permute-start | bytes 98312 | tf_op jit(solution)/shard_map/ppermute | solution.py:59
  181.9 0.8 copy-start
Sparse Core Ops, SparseCore 0:
  16.3 90.1 all-gather.1

commit v5 on v4

--- a/solution.py
+++ b/solution.py
@@ -24,7 +24,7 @@
 GRANT = 56
 SMALL_GRANT = 24
 MID_GRANT = 60
-DECODE_HINT = 1
+DECODE_HINT = 128
 
 adapter_scale = 2.0
 f32 = jnp.float32
@@ -32,9 +32,8 @@
 CHIPS = ("y", "z")
 DP = ("y", "z", "c")
 HIGH = lax.Precision.HIGHEST
-HBM = pltpu.HBM
 SMEM = pltpu.SMEM
-ANY = pl.ANY
+VMEM = None
 
 
 def nn_dot(a, b):
@@ -79,51 +78,19 @@
     return lax.broadcasted_iota(jnp.int32, shape, len(shape) - 1)
 
 
-def call(kernel, out, specs, args, scratch=(), flops=0, grant=GRANT):
+def call(kernel, out, specs, args, scratch=(), flops=0, grant=SMALL_GRANT):
     moved = sum(a.size * a.dtype.itemsize for a in args)
     outs = out if isinstance(out, tuple) else (out,)
     moved += sum(math.prod(o.shape) * o.dtype.itemsize for o in outs)
-    in_hbm = [i for i, kind in enumerate(specs) if kind != SMEM]
-    n_in, n_out = len(specs), len(outs)
-    buffers = [pltpu.VMEM(args[i].shape, args[i].dtype) for i in in_hbm]
-    buffers += [pltpu.VMEM(o.shape, o.dtype) for o in outs]
-
-    def body(*refs):
-        ins, results, rest = refs[:n_in], refs[n_in : n_in + n_out], refs[n_in + n_out :]
-        held, rest = rest[: len(buffers)], rest[len(buffers) :]
-        sem, rest = rest[0], rest[1:]
-        copies = [
-            pltpu.make_async_copy(ins[i], held[k], sem.at[k]) for k, i in enumerate(in_hbm)
-        ]
-        for copy in copies:
-            copy.start()
-        for copy in copies:
-            copy.wait()
-        given = list(ins)
-        for k, i in enumerate(in_hbm):
-            given[i] = held[k]
-        made = held[len(in_hbm) :]
-        kernel(*given, *made, *rest)
-        copies = [
-            pltpu.make_async_copy(made[k], results[k], sem.at[len(in_hbm) + k])
-            for k in range(n_out)
-        ]
-        for copy in copies:
-            copy.start()
-        for copy in copies:
-            copy.wait()
-
-    hbm = pl.BlockSpec(memory_space=HBM)
+    whole = pl.BlockSpec()
     return pl.pallas_call(
-        body,
+        kernel,
         out_shape=out,
-        in_specs=[pl.BlockSpec(memory_space=kind) for kind in specs],
-        out_specs=tuple(hbm for _ in outs) if isinstance(out, tuple) else hbm,
-        scratch_shapes=[*buffers, pltpu.SemaphoreType.DMA((len(buffers),)), *scratch],
+        in_specs=[pl.BlockSpec(memory_space=k) if k == SMEM else whole for k in specs],
+        out_specs=tuple(whole for _ in outs) if isinstance(out, tuple) else whole,
+        scratch_shapes=list(scratch),
         compiler_params=pltpu.CompilerParams(vmem_limit_bytes=grant << 20),
-        cost_estimate=pl.CostEstimate(
-            flops=flops, bytes_accessed=moved, transcendentals=0
-        ),
+        cost_estimate=pl.CostEstimate(flops=flops, bytes_accessed=moved, transcendentals=0),
     )(*args)
 
 
@@ -173,21 +140,26 @@
         put(row, jnp.zeros((CHIP_COUNT, LANES), f32))
 
 
-def gain_of(place, gain):
-    start = pl.multiple_of(place[4] * LANES, LANES)
+def first_core():
+    return lax.axis_index("c") == 0
+
+
+def gain_of(gain):
+    m = lax.axis_index("y") * lax.axis_size("z") + lax.axis_index("z")
+    start = pl.multiple_of(m * LANES, LANES)
     return gain[:, pl.ds(start, LANES)].astype(f32)
 
 
-def qkv_first_kernel(place, arrived, gain, w_own, w_other, out, state_out, held):
+def qkv_first_kernel(arrived, gain, w_own, w_other, out, state_out, held):
     held[...] = arrived[...].astype(f32).reshape(CHIP_COUNT * FIRST_ROWS, LANES)
     state = jnp.concatenate(
         [held[pl.ds(PIECE + b, CHIP_COUNT, stride=FIRST_ROWS), :] for b in range(ROLLS)], axis=0
     )
     state_out[...] = state
-    spread_qkv(state, gain_of(place, gain), place[0] == 0, w_own, w_other, out)
-
-
-def qkv_later_kernel(place, state, gain, w_own, w_other, b_cols, s0, s1, s2, s3, out):
+    spread_qkv(state, gain_of(gain), first_core(), w_own, w_other, out)
+
+
+def qkv_later_kernel(state, gain, w_own, w_other, b_cols, s0, s1, s2, s3, out):
     share = s0[...] + s1[...] + s2[...] + s3[...]
     low = share[:, LANES:]
     now = (
@@ -195,7 +167,7 @@
         + share[:, :LANES]
         + adapter_scale * nt_dot(low, b_cols[...], precision=HIGH)
     )
-    spread_qkv(now, gain_of(place, gain), place[0] == 0, w_own, w_other, out)
+    spread_qkv(now, gain_of(gain), first_core(), w_own, w_other, out)
 
 
 def attend_kernel(last, lengths, came, cache, before, ab, attended, kv_out, owned_out, held):
@@ -262,14 +234,14 @@
     return call(
         lambda *refs: attend_kernel(last, *refs),
         (att, shape(8, LANES), shape(ROLLS * CHIP_COUNT, LANES)),
-        [SMEM, ANY, HBM, HBM, HBM],
+        [SMEM, VMEM, VMEM, VMEM, VMEM],
         (lengths, came, cache, before, ab),
         scratch=[pltpu.VMEM((8, LANES), f32)],
         flops=2 * 32 * 2 * cache.shape[0] * cache.shape[1] * HD,
     )
 
 
-def close_kernel(place, came, w_own, w_other, ab, out, held):
+def close_kernel(came, w_own, w_other, ab, out, held):
     rows = ROLLS * HEADS_TP
     held[...] = came[...].astype(f32).reshape(CHIP_COUNT * rows, LANES)
     blocks = []
@@ -279,7 +251,7 @@
         ]
         blocks.append(jnp.concatenate(heads, axis=1))
     everyone = jnp.concatenate(blocks, axis=0).astype(bf16)
-    first = place[0] == 0
+    first = first_core()
     w_even = jnp.where(first, w_own[...], w_other[...])
     w_odd = jnp.where(first, w_other[...], w_own[...])
     w = jnp.concatenate([w_even, w_odd], axis=0)
@@ -288,9 +260,9 @@
 
 
 def adapter_kernel(
-    place, rewards, prompts, live, own, other, rows, upstream, weighted_out, ab_out, part
+    rewards, prompts, live, own, other, rows, upstream, weighted_out, ab_out, part
 ):
-    first = place[0] == 0
+    first = first_core()
     even = jnp.where(first, own[...], other[...])
     odd = jnp.where(first, other[...], own[...])
     ab_out[:, :PIECE, :] = even[:, :PIECE]
@@ -326,7 +298,7 @@
     low = nn_dot(rows[...], ab)
     back = nn_dot(weighted, ab)
     part[:count, :] = jnp.where(lane_iota((count, LANES)) < RANK, low, back)
-    z = place[2]
+    z = lax.axis_index("z")
     each = LANES // (2 * PIECE)
     piece = ab_out[pl.ds(z * each, each), :, :].reshape(LANES, LANES).astype(f32)
     piece = pltpu.roll(piece, RANK, 1)
@@ -334,13 +306,14 @@
 
 
 def gradient_kernel(
-    place, p0, p1, p2, p3, rows, weighted, low_back, b_cols, kept, given
+    p0, p1, p2, p3, rows, weighted, low_back, b_cols, kept, given
 ):
     count = rows.shape[0]
     total = p0[:count, :] + p1[:count, :] + p2[:count, :] + p3[:count, :]
     low_back[...] = total.astype(bf16)
     turned = pltpu.roll(total, RANK, 1).astype(bf16)
-    from_y = place[3]
+    nt = lax.axis_size("t")
+    from_y = lax.rem(lax.axis_index("t") - lax.axis_index("y") + nt, nt)
     piece = p0[count:, :]
     for by, p in ((1, p1), (2, p2), (3, p3)):
         piece = jnp.where(from_y == by, p[count:, :], piece)
@@ -350,7 +323,7 @@
     both = adapter_scale * jnp.where(lane_iota(a_side.shape) < RANK, a_side, b_side)
     both = both.reshape(CHIP_COUNT, 2 * PIECE, LANES)
     even, odd = both[:, :PIECE], both[:, PIECE:]
-    first = place[0] == 0
+    first = first_core()
     kept[...] = jnp.where(first, even, odd)
     given[...] = jnp.where(first, odd, even)
 
@@ -403,82 +376,71 @@
     )(where, own, left, right, far_a, far_b, w, low, b)
 
 
-def decode_kernel(where_ref, p0, p1, p2, p3, w_ref, b_ref, owned, out, heads, held, sem):
-    k = pl.program_id(1)
-
-    @pl.when((pl.program_id(0) == 0) & (k == 0))
+def decode_kernel(where_ref, s0, s1, s2, s3, w_ref, b_ref, owned, out, heads, acc):
+    sent = (s0, s1, s2, s3)
+    k = pl.program_id(0)
+
+    @pl.when(k == 0)
     def _():
-        copies = [
-            pltpu.make_async_copy(p, held.at[i], sem.at[i]) for i, p in enumerate((p0, p1, p2, p3))
-        ]
-        for copy in copies:
-            copy.start()
-        for copy in copies:
-            copy.wait()
-        for i in range(len(copies)):
-            s = held[i]
+        for i, s in enumerate(sent):
             flat = [
                 jnp.concatenate(
-                    [s[b * HEADS_TP + h : b * HEADS_TP + h + 1] for h in range(HEADS_TP)],
+                    [s[b * HEADS_TP + h : b * HEADS_TP + h + 1, :] for h in range(HEADS_TP)],
                     axis=1,
                 )
                 for b in range(ROLLS)
             ]
             flat.append(jnp.zeros((16 - ROLLS, HEADS_TP * HD), f32))
             heads[i] = jnp.concatenate(flat, axis=0).astype(bf16)
-
-    got = nt_dot(heads[k], w_ref[0])[:8]
-
-    @pl.when(k == 0)
+        acc[...] = jnp.zeros_like(acc)
+
+    acc[...] += nt_dot(w_ref[0], heads[k])
+
+    @pl.when(k == pl.num_programs(0) - 1)
     def _():
         top = ROLLS * HEADS_TP
-        low = held[0, top:, :] + held[1, top:, :] + held[2, top:, :] + held[3, top:, :]
-        start = adapter_scale * nt_dot(low, turned_up(b_ref), precision=HIGH)
-        base = jnp.concatenate([owned[...], jnp.zeros((8 - ROLLS, owned.shape[1]), f32)], axis=0)
-        out[...] = base + start + got
-
-    @pl.when(k > 0)
-    def _():
-        out[...] += got
+        low = s0[top:, :] + s1[top:, :] + s2[top:, :] + s3[top:, :]
+        got = acc[...].T[:8] + adapter_scale * nt_dot(low, turned_up(b_ref), precision=HIGH)
+        out[...] = got
+        out[:ROLLS, :] += owned[...]
 
 
 def decode_columns(where, sent, w, b, owned):
     n, width, depth = w.shape
-    tile = 512
-    tiles = width // tile
-    whole = lambda a: pl.BlockSpec(a.shape, lambda j, k, s: (0, 0))
+    whole = lambda a: pl.BlockSpec(a.shape, lambda k, s: (0, 0))
     return pl.pallas_call(
         decode_kernel,
         out_shape=shape(8, width),
         grid_spec=pltpu.PrefetchScalarGridSpec(
             num_scalar_prefetch=1,
-            grid=(tiles, n),
+            grid=(n,),
             in_specs=[
-                *(pl.BlockSpec(memory_space=ANY) for s in sent),
-                pl.BlockSpec((1, tile, depth), lambda j, k, s: (s[k], j, 0)),
-                pl.BlockSpec((tile, b.shape[1]), lambda j, k, s: (j, 0)),
-                pl.BlockSpec((ROLLS, tile), lambda j, k, s: (0, s[0] * tiles + j)),
+                *(whole(s) for s in sent),
+                pl.BlockSpec((1, width, depth), lambda k, s: (s[k], 0, 0)),
+                whole(b),
+                pl.BlockSpec((ROLLS, width), lambda k, s: (0, s[0])),
             ],
-            out_specs=pl.BlockSpec((8, tile), lambda j, k, s: (0, j)),
+            out_specs=pl.BlockSpec((8, width), lambda k, s: (0, 0)),
             scratch_shapes=[
                 pltpu.VMEM((n, 16, depth), bf16),
-                pltpu.VMEM((n, *sent[0].shape), f32),
-                pltpu.SemaphoreType.DMA((n,)),
+                pltpu.VMEM((width, 16), f32),
             ],
         ),
         compiler_params=pltpu.CompilerParams(vmem_limit_bytes=MID_GRANT << 20),
         cost_estimate=pl.CostEstimate(
-            flops=2 * 16 * width * depth * n,
-            bytes_accessed=DECODE_HINT * 2 * n * width * depth,
+            flops=DECODE_HINT * 2 * 16 * width * depth * n,
+            bytes_accessed=2 * n * width * depth,
             transcendentals=0,
         ),
     )(where, *sent, w, b, owned)
 
 
-def place_kernel(where_ref, c0, c1, c2, c3, out):
+def place_kernel(c0, c1, c2, c3, out):
     width = c0.shape[1]
+    nt = lax.axis_size("t")
     for k, part in enumerate((c0, c1, c2, c3)):
-        start = pl.multiple_of(where_ref[k] * width, width)
+        block = lax.rem(lax.axis_index("t") - k + nt, nt)
+        start = pl.multiple_of(block * width, width)
         out[:, pl.ds(start, width)] = part[:ROLLS, :]
 
 
@@ -499,20 +461,15 @@
 ):
     nt = lax.axis_size("t")
     t = lax.axis_index("t")
-    y = lax.axis_index("y")
-    z = lax.axis_index("z")
-    c = lax.axis_index("c")
-    m = lax.axis_index(CHIPS)
     width = hidden.shape[1]
     shard_width = width // nt
     cache = key_value_cache[:, :, 0, :]
-    place = jnp.stack([c, y, z, lax.rem(t - y + nt, nt), m]).astype(jnp.int32)
     where = lax.rem(t - jnp.arange(nt, dtype=jnp.int32) + nt, nt)
 
     message = call(
         message_kernel,
         shape(CHIP_COUNT, FIRST_ROWS, LANES, dtype=bf16),
-        [SMEM, SMEM, HBM, HBM, HBM],
+        [SMEM, SMEM, VMEM, VMEM, VMEM],
         (
             rewards,
             prompt_group_index,
@@ -531,20 +488,20 @@
     turned = lax.ppermute(
         w_cols, ("y", "t"), [(a * nt + b, b * nt + a) for a in range(ny) for b in range(nt)]
     )
-    turned, message, place, where = together(turned, message, place, where)
+    turned, message, where = together(turned, message, where)
     w_block = lax.all_gather(turned, DP, axis=0, tiled=True)
     w_block = w_block.reshape(nt, shard_width, w_cols.shape[1])
 
+
     left = shift(attention_rows, 1, nt)
     right = shift(attention_rows, nt - 1, nt)
-
     arrived = exchange(message, CHIPS)
     gain = attention_norm_gain[None, :]
     sent, state = call(
         qkv_first_kernel,
         (shape(CHIP_COUNT * QKV_ROWS, LANES), shape(ROLLS * CHIP_COUNT, LANES)),
-        [SMEM, ANY, HBM, HBM, ANY],
-        (place, arrived, gain, w_rows, w_rows_other),
+        [VMEM] * 4,
+        (arrived, gain, w_rows, w_rows_other),
         scratch=[pltpu.VMEM((CHIP_COUNT * FIRST_ROWS, LANES), f32)],
     )
     arrived_other = swapped(arrived)
@@ -553,8 +510,7 @@
     )
     came = exchange(sent.reshape(CHIP_COUNT, QKV_ROWS, LANES), CHIPS)
     half = attention_rows.shape[0] // 2
-    far_a = shift(left[:half], 1, nt)
-    far_b = shift(right[half:], nt - 1, nt)
+    came, left_half, right_half = together(came, left[:half], right[half:])
 
     rows = attention_rows.shape[0]
     weighted, ab, part = call(
@@ -564,9 +520,8 @@
             shape(CHIP_COUNT, 2 * PIECE, LANES, dtype=bf16),
             shape(rows + LANES, LANES),
         ),
-        [SMEM] * 4 + [ANY, ANY, HBM, HBM],
+        [SMEM] * 3 + [VMEM] * 4,
         (
-            place,
             rewards,
             prompt_group_index,
             completion_live_lengths,
@@ -584,7 +539,7 @@
     attended, kv, _ = attend(
         False, cache_fill_lengths, came.reshape(-1, LANES), cache, nothing, ab
     )
-    attended, weighted, far_a, far_b = together(attended, weighted, far_a, far_b)
+    attended, weighted = together(attended, weighted)
     everyone = exchange(attended, CHIPS)
 
     low_back, b_cols, kept, given = call(
@@ -595,16 +550,18 @@
             shape(CHIP_COUNT, PIECE, LANES),
             shape(CHIP_COUNT, PIECE, LANES),
         ),
-        [SMEM] + [ANY] * 4 + [HBM] * 2,
-        (place, *parts, attention_rows, weighted),
+        [VMEM] * 6,
+        (*parts, attention_rows, weighted),
         flops=4 * rows * shard_width * LANES,
     )
+
+    everyone, b_cols = together(everyone, b_cols)
 
     share = call(
         close_kernel,
         shape(ROLLS * CHIP_COUNT, 2 * LANES),
-        [SMEM, ANY, HBM, ANY, HBM],
-        (place, everyone, w_cols, w_cols_other, ab),
+        [VMEM] * 4,
+        (everyone, w_cols, w_cols_other, ab),
         scratch=[pltpu.VMEM((CHIP_COUNT * ROLLS * HEADS_TP, LANES), f32)],
     )
     shares = shifts(share, nt)
@@ -612,11 +569,14 @@
     sent = call(
         qkv_later_kernel,
         shape(CHIP_COUNT * QKV_ROWS, LANES),
-        [SMEM, HBM, HBM, HBM, ANY, HBM] + [ANY] * 4,
-        (place, state, gain, w_rows, w_rows_other, b_cols, *shares),
+        [VMEM] * 9,
+        (state, gain, w_rows, w_rows_other, b_cols, *shares),
     )
     sent, low_back, given = together(sent, low_back, given)
-    kept = kept + swapped(given)
+    given, left_half, right_half = together(swapped(given), left_half, right_half)
+    kept = kept + given
+    far_a = shift(left_half, 1, nt)
+    far_b = shift(right_half, nt - 1, nt)
     came = exchange(sent.reshape(CHIP_COUNT, QKV_ROWS, LANES), CHIPS)
 
     adapted = output_rows(
@@ -635,8 +595,8 @@
     decoded = call(
         place_kernel,
         shape(ROLLS, width),
-        [SMEM] + [ANY] * nt,
-        (where, *arriving),
+        [VMEM] * nt,
+        tuple(arriving),
         grant=SMALL_GRANT,
     )
     grad_a = summed[:, :RANK].T[:, None, :]

time: 192 us -> 183 us (0.953)
  Pallas kernels: 50.3 us -> 31.3 us
  local copies, waits for them, and re-layouts: 12.8 us -> 31 us
  waiting for transfers between devices: 22.9 us -> 19.1 us
  starting transfers between devices: 63.7 us -> 60.1 us
    unnamed x44 -> x92, local copies, waits for them, and re-layouts: 7.04 us -> 26.3 us
    pallas_call x9, Pallas kernels: 29.9 us -> 13.5 us  [call(): pl.pallas_call(kernel, out_shape=out, in_specs=[pl.BlockSpec(memory_space...]
    all_to_all x4, waiting for transfers between devices: 8.34 us -> 3.62 us  [exchange(): return lax.all_to_all(x, axes, split_axis=0, concat_axis=0, tiled=True)]
    all_to_all x4, starting transfers between devices: 31.4 us -> 28.4 us  [exchange(): return lax.all_to_all(x, axes, split_axis=0, concat_axis=0, tiled=True)]
    ppermute x16, waiting for transfers between devices: 9.98 us -> 12.7 us  [shift(): return lax.ppermute(x, 't', [(i, (i + by) % n) for i in range(n)])]
    pallas_call x1, Pallas kernels: 10.1 us -> 7.43 us  [decode_columns(): pl.pallas_call(decode_kernel, out_shape=shape(8, width), grid_spec=pltpu....]
  transfers between devices with their start and end apart: 26 -> 26, of which waited for: 9 -> 10; matrix products, arithmetic and copies ran while one was open for 4% -> 3% of each run, Pallas kernels for 23% -> 16%
where the time goes in v5:
time: 183 us; the launch traced here: 181 us
  starting transfers between devices  60.1 us (33%)
  Pallas kernels  31.3 us (17%)
  local copies, waits for them, and re-layouts  31 us (17%)
  blocking collectives  24.1 us (13%)
  waiting for transfers between devices  19.1 us (10%)
  between operations  14.4 us (8%)
    all_to_all x4, starting transfers between devices, exchange(): return lax.all_to_all(x, axes, split_axis=0, concat_axis=0, tiled=True)  28.4 us
    ppermute x16, starting transfers between devices, shift(): return lax.ppermute(x, 't', [(i, (i + by) % n) for i in range(n)])  27.7 us
    unnamed x92, local copies, waits for them, and re-layouts  26.3 us
    all_to_all x1, blocking collectives, exchange(): return lax.all_to_all(x, axes, split_axis=0, concat_axis=0, tiled=True)  24.1 us
    pallas_call x9, Pallas kernels, call(): pl.pallas_call(kernel, out_shape=out, in_specs=[pl.BlockSpec(memory_space...  13.5 us
    ppermute x16, waiting for transfers between devices, shift(): return lax.ppermute(x, 't', [(i, (i + by) % n) for i in range(n)])  12.7 us
    pallas_call x1, Pallas kernels, output_rows(): pl.pallas_call(rows_kernel, out_shape=shape(rows, width), grid_spec=pltpu...  10.4 us
    pallas_call x1, Pallas kernels, decode_columns(): pl.pallas_call(decode_kernel, out_shape=shape(8, width), grid_spec=pltpu....  7.43 us
  transfers between devices with their start and end apart: 26, of which 10 were waited for; matrix products, arithmetic and copies ran while one was open for 3% of the time, Pallas kernels for 16%

profile of v5, /device:TPU:8, one launch (start us, length us, event | category | flops | bytes accessed | tf_op | source)
XLA Modules:
  0.0 181.4 jit_solution(16429268857223003964)
XLA Ops:
  7.2 3.4 %collective-permute-start = (bf16[64,1024]{1,0:T(8,128)(2,1)}, bf16[64,1024]{1,0:T(8,128)(2,1)S(1)}, u32[]{:S(2)}, u32[]{:S(2)}) collective-permute-start(bf16[64,1024]{1,0:T(8,128)(2,1)} %bitcast.36), channel_id=1, source_target_pairs={{0,0},{1,64},{2,128},{3,192},{64,1},{65,65},{66,129},{67,193},{128... | collective-permute-start | bytes 393224 | tf_op jit(solution)/shard_map/ppermute | solution.py:488
  10.7 0.7 copy-done.24
  16.4 6.7 %collective-permute-start.4 = (bf16[512,1024]{1,0:T(8,128)(2,1)}, bf16[512,1024]{1,0:T(8,128)(2,1)S(1)}, u32[]{:S(2)}, u32[]{:S(2)}) collective-permute-start(bf16[512,1024]{1,0:T(8,128)(2,1)} %own.1), channel_id=1, source_target_pairs={{0,3},{1,0},{2,1},{3,2},{4,7},{5,4},{6,5},{7,6},{8,11},{9,8},{10,9... | collective-permute-start | bytes 3145736 | tf_op jit(solution)/shard_map/ppermute | solution.py:58
  23.0 24.1 %all_to_all.25.arrived.own = bf16[32,24,128]{2,1,0:T(8,128)(2,1)S(1)} all-to-all(bf16[32,24,128]{2,1,0:T(8,128)(2,1)S(1)} %shard_map.156), channel_id=1, replica_groups=mesh['y'=4,'z'=8,'c'=2,'t'=4] {'y','z'}, dimensions={0} | all-to-all | bytes 393216 | tf_op jit(solution)/shard_map/all_to_all | solution.py:66
  49.0 0.9 copy-done.9
  49.9 1.1 shard_map.157
  52.9 1.0 copy-done.39
  53.9 1.0 copy-done.40
  54.9 6.2 %all-to-all-start.1 = ((f32[32,24,128]{2,1,0:T(8,128)}), f32[32,24,128]{2,1,0:T(8,128)}, u32[]{:S(2)}, u32[]{:S(2)}) async-start(f32[32,24,128]{2,1,0:T(8,128)} %bitcast.7), calls=%async_computation.1 | async-start | bytes 786432 | tf_op jit(solution)/shard_map/all_to_all | solution.py:66
  61.1 0.9 copy-done.5
  62.1 1.2 copy-done.6
  63.3 0.9 copy-done.16
  66.2 2.2 %shard_map.158 = (bf16[512,1024]{1,0:T(8,128)(2,1)S(1)}, bf16[32,32,128]{2,1,0:T(8,128)(2,1)S(1)}, f32[640,128]{1,0:T(8,128)}) custom-call(f32[2]{0:T(128)S(1)} %copy-done.30, s32[2]{0:T(128)S(1)} %copy-done.32, s32[2]{0:T(128)S(1)} %copy-done.35, bf16[32,24,128]{2,1,0:T(8,128)(2,1)S(1)} %copy-done.5, bf16[32,24,128]{2,1,0:T(8,128)(2,1)S(1)} %copy-done.16, ...), custom_call_target="tpu_custom_call" | custom-call | flops 268435456 | bytes 4128792 | tf_op jit(solution)/shard_map/pallas_call | solution.py:86
  68.4 1.0 copy-done.7
  69.4 3.4 %collective-permute-start.6 = (f32[640,128]{1,0:T(8,128)}, f32[640,128]{1,0:T(8,128)}, u32[]{:S(2)}, u32[]{:S(2)}) collective-permute-start(f32[640,128]{1,0:T(8,128)} %get-tuple-element.58.p0), channel_id=1, source_target_pairs={{0,2},{1,3},{2,0},{3,1},{4,6},{5,7},{6,4},{7,5},{8,10},{9,11},{10,... | collective-permute-start | bytes 983048 | tf_op jit(solution)/shard_map/ppermute | solution.py:58
  72.8 1.9 %slice.12 = bf16[256,1024]{1,0:T(8,128)(2,1)} slice(bf16[512,1024]{1,0:T(8,128)(2,1)} %copy-done.39), slice={[0:256], [0:1024]} | slice | bytes 1048576 | tf_op jit(solution)/shard_map/slice | solution.py:513
  74.7 0.8 slice.13
  75.6 2.2 %shard_map.159 = (bf16[32,16,128]{2,1,0:T(8,128)(2,1)S(1)}, f32[8,128]{1,0:T(8,128)S(1)}, f32[64,128]{1,0:T(8,128)}) custom-call(s32[2]{0:T(128)S(1)} %copy-done.33, f32[768,128]{1,0:T(8,128)} %bitcast.8.refs_1_, bf16[2,2048,256]{2,1,0:T(8,128)(2,1)S(1)} %bitcast.25, f32[8,128]{1,0:T(8,128)S(1)} %broadcast_in_dim.13.refs_3_, bf16[1024,128]{1,0:T(8,128)(2,1)S(1)} %bitcast.27), custom_call_target="tpu_custom_call" | custom-call | flops 67108864 | bytes 2924552 | tf_op jit(solution)/shard_map/pallas_call | solution.py:86
  79.1 9.8 %all-to-all-start.2 = ((bf16[32,16,128]{2,1,0:T(8,128)(2,1)}), bf16[32,16,128]{2,1,0:T(8,128)(2,1)S(1)}, u32[]{:S(2)}, u32[]{:S(2)}) async-start(bf16[32,16,128]{2,1,0:T(8,128)(2,1)} %copy-done.17), calls=%async_computation.2 | async-start | bytes 262144 | tf_op jit(solution)/shard_map/all_to_all | solution.py:66
  89.0 1.2 copy-done.8
  90.3 2.2 %shard_map.160 = (bf16[512,128]{1,0:T(8,128)(2,1)S(1)}, f32[128,128]{1,0:T(8,128)S(1)}, f32[32,16,128]{2,1,0:T(8,128)S(1)}, f32[32,16,128]{2,1,0:T(8,128)S(1)}) custom-call(f32[640,128]{1,0:T(8,128)} %get-tuple-element.58.p0, f32[640,128]{1,0:T(8,128)} %collective-permute-done.5.p1, f32[640,128]{1,0:T(8,128)} %collective-permute-done.6.p2, ...), custom_call_target="tpu_custom_call" | custom-call | flops 268435456 | bytes 4128768 | tf_op jit(solution)/shard_map/pallas_call | solution.py:86
  95.1 3.6 %all-to-all-done.2.came = bf16[32,16,128]{2,1,0:T(8,128)(2,1)S(1)} async-done(((bf16[32,16,128]{2,1,0:T(8,128)(2,1)}), bf16[32,16,128]{2,1,0:T(8,128)(2,1)S(1)}, u32[]{:S(2)}, u32[]{:S(2)}) %all-to-all-start.2) | async-done | bytes 131104 | tf_op jit(solution)/shard_map/all_to_all | solution.py:66
  98.7 0.9 copy-done.18
  99.6 1.2 shard_map.161.s0
  100.8 3.0 %collective-permute-start.10 = (f32[64,256]{1,0:T(8,128)S(1)}, f32[64,256]{1,0:T(8,128)S(1)}, u32[]{:S(2)}, u32[]{:S(2)}) collective-permute-start(f32[64,256]{1,0:T(8,128)S(1)} %shard_map.161.s0), channel_id=1, source_target_pairs={{0,2},{1,3},{2,0},{3,1},{4,6},{5,7},{6,4},{7,5},{8,10},{9,11},{10,... | collective-permute-start | bytes 196616 | tf_op jit(solution)/shard_map/ppermute | solution.py:58
  103.8 1.7 collective-permute-start.11
  105.8 0.9 collective-permute-done.10.s2
  106.8 1.3 collective-permute-done.11.s3
  108.1 2.9 %collective-permute-done.9.s1 = f32[64,256]{1,0:T(8,128)S(1)} collective-permute-done((f32[64,256]{1,0:T(8,128)S(1)}, f32[64,256]{1,0:T(8,128)S(1)}, u32[]{:S(2)}, u32[]{:S(2)}) %collective-permute-start.9) | collective-permute-done | bytes 65568 | tf_op jit(solution)/shard_map/ppermute | solution.py:58
  111.0 0.9 copy-done.10
  111.9 0.9 copy-done.12
  112.8 0.8 copy-done.20
  113.7 0.8 copy-done.22
  114.4 1.4 shard_map.162
  115.9 1.7 collective-permute-done.12
  117.6 3.2 %collective-permute-start.14 = (bf16[256,1024]{1,0:T(8,128)(2,1)}, bf16[256,1024]{1,0:T(8,128)(2,1)}, u32[]{:S(2)}, u32[]{:S(2)}) collective-permute-start(bf16[256,1024]{1,0:T(8,128)(2,1)} %slice.13), channel_id=1, source_target_pairs={{0,3},{1,0},{2,1},{3,2},{4,7},{5,4},{6,5},{7,6},{8,11},{9,8},{10,9... | collective-permute-start | bytes 1572872 | tf_op jit(solution)/shard_map/ppermute | solution.py:58
  120.9 6.2 %all-to-all-start.3 = ((f32[32,24,128]{2,1,0:T(8,128)}), f32[32,24,128]{2,1,0:T(8,128)S(1)}, u32[]{:S(2)}, u32[]{:S(2)}) async-start(f32[32,24,128]{2,1,0:T(8,128)} %bitcast.12), calls=%async_computation.3 | async-start | bytes 786432 | tf_op jit(solution)/shard_map/all_to_all | solution.py:66
  127.1 0.7 add.7
  127.8 5.3 %collective-permute-done.13.far_a = bf16[256,1024]{1,0:T(8,128)(2,1)} collective-permute-done((bf16[256,1024]{1,0:T(8,128)(2,1)}, bf16[256,1024]{1,0:T(8,128)(2,1)}, u32[]{:S(2)}, u32[]{:S(2)}) %collective-permute-start.13) | collective-permute-done | bytes 524320 | tf_op jit(solution)/shard_map/ppermute | solution.py:58
  133.1 10.4 %shard_map.163 = f32[512,1024]{1,0:T(8,128)} custom-call(s32[4]{0:T(128)} %compare_select_fusion.where_ref, bf16[512,1024]{1,0:T(8,128)(2,1)} %own.1, bf16[512,1024]{1,0:T(8,128)(2,1)} %copy-done.39, bf16[512,1024]{1,0:T(8,128)(2,1)} %copy-done.40, bf16[256,1024]{1,0:T(8,128)(2,1)} %collective-permute-done.13.far_a, ...), custom_call_target="tpu_custom_call" | custom-call | flops 4294967296 | bytes 14680064 | tf_op jit(solution)/shard_map/pallas_call | solution.py:352
  143.6 1.9 %shard_map.164 = (f32[24,128]{1,0:T(8,128)S(1)}, f32[8,128]{1,0:T(8,128)}, f32[64,128]{1,0:T(8,128)S(1)}) custom-call(s32[2]{0:T(128)S(1)} %copy-done.34, f32[768,128]{1,0:T(8,128)S(1)} %bitcast.32, bf16[2,2048,256]{2,1,0:T(8,128)(2,1)S(1)} %bitcast.26, f32[8,128]{1,0:T(8,128)S(1)} %copy-done.28, bf16[1024,128]{1,0:T(8,128)(2,1)S(1)} %bitcast.31), custom_call_target="tpu_custom_call" | custom-call | flops 67108864 | bytes 2805768 | tf_op jit(solution)/shard_map/pallas_call | solution.py:86
  145.6 4.4 %collective-permute-start.16 = (f32[24,128]{1,0:T(8,128)S(1)}, f32[24,128]{1,0:T(8,128)S(1)}, u32[]{:S(2)}, u32[]{:S(2)}) collective-permute-start(f32[24,128]{1,0:T(8,128)S(1)} %get-tuple-element.78.s0), channel_id=1, source_target_pairs={{0,2},{1,3},{2,0},{3,1},{4,6},{5,7},{6,4},{7,5},{8,10},{9,11},{10,... | collective-permute-start | bytes 36872 | tf_op jit(solution)/shard_map/ppermute | solution.py:58
  150.6 6.2 %all-to-all-start.4 = ((f32[32,16,128]{2,1,0:T(8,128)}), f32[32,16,128]{2,1,0:T(8,128)S(1)}, u32[]{:S(2)}, u32[]{:S(2)}) async-start(f32[32,16,128]{2,1,0:T(8,128)} %add.7), calls=%async_computation.4 | async-start | bytes 524288 | tf_op jit(solution)/shard_map/all_to_all | solution.py:66
  158.1 7.4 %shard_map.165.c0 = f32[8,1024]{1,0:T(8,128)} custom-call(s32[4]{0:T(128)} %compare_select_fusion.where_ref, f32[24,128]{1,0:T(8,128)} %copy-done.38, f32[24,128]{1,0:T(8,128)} %copy-done.43, f32[24,128]{1,0:T(8,128)} %copy-done.44, f32[24,128]{1,0:T(8,128)} %copy-done.45, bf16[4,1024,1024]{2,1,0:T(8,128)(2,1)} %bitcast.42, bf16[1024,128]{1,0:T(8,128)(2,1)} %bitcast.30, ...), custom_call_target="tpu_custom_call" | custom-call | flops 17179869184 | bytes 8388608 | tf_op jit(solution)/shard_map/pallas_call | solution.py:411
  165.5 2.0 %collective-permute-start.18 = (f32[8,1024]{1,0:T(8,128)}, f32[8,1024]{1,0:T(8,128)S(1)}, u32[]{:S(2)}, u32[]{:S(2)}) collective-permute-start(f32[8,1024]{1,0:T(8,128)} %shard_map.165.c0), channel_id=1, source_target_pairs={{0,1},{1,2},{2,3},{3,0},{4,5},{5,6},{6,7},{7,4},{8,9},{9,10},{10,1... | collective-permute-start | bytes 98312 | tf_op jit(solution)/shard_map/ppermute | solution.py:58
  167.5 2.7 %collective-permute-start.20 = (f32[8,1024]{1,0:T(8,128)}, f32[8,1024]{1,0:T(8,128)S(1)}, u32[]{:S(2)}, u32[]{:S(2)}) collective-permute-start(f32[8,1024]{1,0:T(8,128)} %shard_map.165.c0), channel_id=1, source_target_pairs={{0,3},{1,0},{2,1},{3,2},{4,7},{5,4},{6,5},{7,6},{8,11},{9,8},{10,9... | collective-permute-start | bytes 98312 | tf_op jit(solution)/shard_map/ppermute | solution.py:58
  171.5 1.6 collective-permute-done.19.c2
  173.2 0.8 copy-done.23
  (118 shorter events, 19.1 us)
Async XLA Ops:
  7.2 54.0 %copy-start.1 = (bf16[512,1024]{1,0:T(8,128)(2,1)S(1)}, bf16[512,1024]{1,0:T(8,128)(2,1)}, u32[]{:S(2)}) copy-start(bf16[512,1024]{1,0:T(8,128)(2,1)} %own.1) | copy-start | bytes 3145732
  7.2 125.9 %all-gather.2.cloned.1.call-start = ((), (), s32[]{:S(2)}) async-start(), calls=%async_computation.5 | async-start | bytes 8519680 | tf_op jit(solution)/shard_map/all_gather | solution.py:492
  7.2 8.4 %collective-permute-start = (bf16[64,1024]{1,0:T(8,128)(2,1)}, bf16[64,1024]{1,0:T(8,128)(2,1)S(1)}, u32[]{:S(2)}, u32[]{:S(2)}) collective-permute-start(bf16[64,1024]{1,0:T(8,128)(2,1)} %bitcast.36), channel_id=1, source_target_pairs={{0,0},{1,64},{2,128},{3,192},{64,1},{65,65},{66,129},{67,193},{128... | collective-permute-start | bytes 393224 | tf_op jit(solution)/shard_map/ppermute | solution.py:488
  16.3 36.7 %collective-permute-start.3 = (bf16[512,1024]{1,0:T(8,128)(2,1)}, bf16[512,1024]{1,0:T(8,128)(2,1)S(1)}, u32[]{:S(2)}, u32[]{:S(2)}) collective-permute-start(bf16[512,1024]{1,0:T(8,128)(2,1)} %own.1), channel_id=1, source_target_pairs={{0,1},{1,2},{2,3},{3,0},{4,5},{5,6},{6,7},{7,4},{8,9},{9,10},{10,1... | collective-permute-start | bytes 3145736 | tf_op jit(solution)/shard_map/ppermute | solution.py:58
  16.4 37.6 %collective-permute-start.4 = (bf16[512,1024]{1,0:T(8,128)(2,1)}, bf16[512,1024]{1,0:T(8,128)(2,1)S(1)}, u32[]{:S(2)}, u32[]{:S(2)}) collective-permute-start(bf16[512,1024]{1,0:T(8,128)(2,1)} %own.1), channel_id=1, source_target_pairs={{0,3},{1,0},{2,1},{3,2},{4,7},{5,4},{6,5},{7,6},{8,11},{9,8},{10,9... | collective-permute-start | bytes 3145736 | tf_op jit(solution)/shard_map/ppermute | solution.py:58
  47.1 5.2 %collective-permute-start.2 = (bf16[32,24,128]{2,1,0:T(8,128)(2,1)S(1)}, bf16[32,24,128]{2,1,0:T(8,128)(2,1)S(1)}, u32[]{:S(2)}, u32[]{:S(2)}) collective-permute-start(bf16[32,24,128]{2,1,0:T(8,128)(2,1)S(1)} %all_to_all.25.arrived.own), channel_id=1, source_target_pairs={{0,4},{4,0},{1,5},{5,1},{2,6},{6,2},{3,7},{7,3},{8,12},{12,8},{9,1... | collective-permute-start | bytes 589832 | tf_op jit(solution)/shard_map/ppermute | solution.py:54
  47.1 1.9 %collective-permute-start.1 = (bf16[64,1280]{1,0:T(8,128)(2,1)}, bf16[64,1280]{1,0:T(8,128)(2,1)S(1)}, u32[]{:S(2)}, u32[]{:S(2)}) collective-permute-start(bf16[64,1280]{1,0:T(8,128)(2,1)} %bitcast.33), channel_id=1, source_target_pairs={{0,4},{4,0},{1,5},{5,1},{2,6},{6,2},{3,7},{7,3},{8,12},{12,8},{9,1... | collective-permute-start | bytes 491528 | tf_op jit(solution)/shard_map/ppermute | solution.py:54
  49.0 0.9 copy-start.9
  49.9 2.4 %copy-start.11 = (bf16[64,1280]{1,0:T(8,128)(2,1)}, bf16[64,1280]{1,0:T(8,128)(2,1)S(1)}, u32[]{:S(2)}) copy-start(bf16[64,1280]{1,0:T(8,128)(2,1)S(1)} %collective-permute-done.1.w_other) | copy-start | bytes 491524
  52.9 1.0 copy-start.39
  53.9 1.0 copy-start.40
  54.9 20.7 %all-to-all-start.1 = ((f32[32,24,128]{2,1,0:T(8,128)}), f32[32,24,128]{2,1,0:T(8,128)}, u32[]{:S(2)}, u32[]{:S(2)}) async-start(f32[32,24,128]{2,1,0:T(8,128)} %bitcast.7), calls=%async_computation.1 | async-start | bytes 786432 | tf_op jit(solution)/shard_map/all_to_all | solution.py:66
  61.1 0.9 copy-start.5
  62.1 1.2 copy-start.6
  63.3 0.9 copy-start.16
  66.2 8.6 %copy-start.41 = (bf16[512,1024]{1,0:T(8,128)(2,1)S(1)}, bf16[512,1024]{1,0:T(8,128)(2,1)}, u32[]{:S(2)}) copy-start(bf16[512,1024]{1,0:T(8,128)(2,1)} %copy-done.40) | copy-start | bytes 3145732
  66.2 9.4 %copy-start = (bf16[2,2048,1,256]{3,1,2,0:T(8,128)(2,1)S(1)}, bf16[2,2048,1,256]{3,1,2,0:T(8,128)(2,1)}, u32[]{:S(2)}) copy-start(bf16[2,2048,1,256]{3,1,2,0:T(8,128)(2,1)} %param.16) | copy-start | bytes 6291460
  66.2 9.4 %copy-start.33 = (s32[2]{0:T(128)S(1)}, s32[2]{0:T(128)}, u32[]{:S(2)}) copy-start(s32[2]{0:T(128)} %refs_0_.3) | copy-start | bytes 28
  68.4 1.0 copy-start.7
  69.4 29.3 %copy-start.2 = (bf16[32,32,128]{2,1,0:T(8,128)(2,1)}, bf16[32,32,128]{2,1,0:T(8,128)(2,1)S(1)}, u32[]{:S(2)}) copy-start(bf16[32,32,128]{2,1,0:T(8,128)(2,1)S(1)} %get-tuple-element.54) | copy-start | bytes 786436
  69.4 19.6 %collective-permute-start.5 = (f32[640,128]{1,0:T(8,128)}, f32[640,128]{1,0:T(8,128)}, u32[]{:S(2)}, u32[]{:S(2)}) collective-permute-start(f32[640,128]{1,0:T(8,128)} %get-tuple-element.58.p0), channel_id=1, source_target_pairs={{0,1},{1,2},{2,3},{3,0},{4,5},{5,6},{6,7},{7,4},{8,9},{9,10},{10,1... | collective-permute-start | bytes 983048 | tf_op jit(solution)/shard_map/ppermute | solution.py:58
  69.4 19.6 %collective-permute-start.6 = (f32[640,128]{1,0:T(8,128)}, f32[640,128]{1,0:T(8,128)}, u32[]{:S(2)}, u32[]{:S(2)}) collective-permute-start(f32[640,128]{1,0:T(8,128)} %get-tuple-element.58.p0), channel_id=1, source_target_pairs={{0,2},{1,3},{2,0},{3,1},{4,6},{5,7},{6,4},{7,5},{8,10},{9,11},{10,... | collective-permute-start | bytes 983048 | tf_op jit(solution)/shard_map/ppermute | solution.py:58
  72.8 16.2 %collective-permute-start.7 = (f32[640,128]{1,0:T(8,128)}, f32[640,128]{1,0:T(8,128)}, u32[]{:S(2)}, u32[]{:S(2)}) collective-permute-start(f32[640,128]{1,0:T(8,128)} %get-tuple-element.58.p0), channel_id=1, source_target_pairs={{0,3},{1,0},{2,1},{3,2},{4,7},{5,4},{6,5},{7,6},{8,11},{9,8},{10,9... | collective-permute-start | bytes 983048 | tf_op jit(solution)/shard_map/ppermute | solution.py:58
  79.1 19.6 %all-to-all-start.2 = ((bf16[32,16,128]{2,1,0:T(8,128)(2,1)}), bf16[32,16,128]{2,1,0:T(8,128)(2,1)S(1)}, u32[]{:S(2)}, u32[]{:S(2)}) async-start(bf16[32,16,128]{2,1,0:T(8,128)(2,1)} %copy-done.17), calls=%async_computation.2 | async-start | bytes 262144 | tf_op jit(solution)/shard_map/all_to_all | solution.py:66
  88.9 9.8 %collective-permute-start.8 = (bf16[64,1024]{1,0:T(8,128)(2,1)}, bf16[64,1024]{1,0:T(8,128)(2,1)}, u32[]{:S(2)}, u32[]{:S(2)}) collective-permute-start(bf16[64,1024]{1,0:T(8,128)(2,1)} %bitcast.37), channel_id=1, source_target_pairs={{0,4},{4,0},{1,5},{5,1},{2,6},{6,2},{3,7},{7,3},{8,12},{12,8},{9,1... | collective-permute-start | bytes 393224 | tf_op jit(solution)/shard_map/ppermute | solution.py:54
  89.0 1.2 copy-start.8
  98.7 28.4 %copy-start.14 = (f32[32,16,128]{2,1,0:T(8,128)S(1)}, f32[32,16,128]{2,1,0:T(8,128)}, u32[]{:S(2)}) copy-start(f32[32,16,128]{2,1,0:T(8,128)} %copy-done.13) | copy-start | bytes 786436
  98.7 1.0 copy-start.18
  100.8 6.0 %collective-permute-start.10 = (f32[64,256]{1,0:T(8,128)S(1)}, f32[64,256]{1,0:T(8,128)S(1)}, u32[]{:S(2)}, u32[]{:S(2)}) collective-permute-start(f32[64,256]{1,0:T(8,128)S(1)} %shard_map.161.s0), channel_id=1, source_target_pairs={{0,2},{1,3},{2,0},{3,1},{4,6},{5,7},{6,4},{7,5},{8,10},{9,11},{10,... | collective-permute-start | bytes 196616 | tf_op jit(solution)/shard_map/ppermute | solution.py:58
  103.8 4.3 %collective-permute-start.11 = (f32[64,256]{1,0:T(8,128)S(1)}, f32[64,256]{1,0:T(8,128)S(1)}, u32[]{:S(2)}, u32[]{:S(2)}) collective-permute-start(f32[64,256]{1,0:T(8,128)S(1)} %shard_map.161.s0), channel_id=1, source_target_pairs={{0,3},{1,0},{2,1},{3,2},{4,7},{5,4},{6,5},{7,6},{8,11},{9,8},{10,9... | collective-permute-start | bytes 196616 | tf_op jit(solution)/shard_map/ppermute | solution.py:58
  105.5 5.5 %collective-permute-start.9 = (f32[64,256]{1,0:T(8,128)S(1)}, f32[64,256]{1,0:T(8,128)S(1)}, u32[]{:S(2)}, u32[]{:S(2)}) collective-permute-start(f32[64,256]{1,0:T(8,128)S(1)} %shard_map.161.s0), channel_id=1, source_target_pairs={{0,1},{1,2},{2,3},{3,0},{4,5},{5,6},{6,7},{7,4},{8,9},{9,10},{10,1... | collective-permute-start | bytes 196616 | tf_op jit(solution)/shard_map/ppermute | solution.py:58
  111.0 0.9 copy-start.10
  111.9 0.9 copy-start.12
  115.9 1.7 collective-permute-start.12
  117.6 15.5 %collective-permute-start.13 = (bf16[256,1024]{1,0:T(8,128)(2,1)}, bf16[256,1024]{1,0:T(8,128)(2,1)}, u32[]{:S(2)}, u32[]{:S(2)}) collective-permute-start(bf16[256,1024]{1,0:T(8,128)(2,1)} %slice.12), channel_id=1, source_target_pairs={{0,1},{1,2},{2,3},{3,0},{4,5},{5,6},{6,7},{7,4},{8,9},{9,10},{10,1... | collective-permute-start | bytes 1572872 | tf_op jit(solution)/shard_map/ppermute | solution.py:58
  117.6 15.5 %collective-permute-start.14 = (bf16[256,1024]{1,0:T(8,128)(2,1)}, bf16[256,1024]{1,0:T(8,128)(2,1)}, u32[]{:S(2)}, u32[]{:S(2)}) collective-permute-start(bf16[256,1024]{1,0:T(8,128)(2,1)} %slice.13), channel_id=1, source_target_pairs={{0,3},{1,0},{2,1},{3,2},{4,7},{5,4},{6,5},{7,6},{8,11},{9,8},{10,9... | collective-permute-start | bytes 1572872 | tf_op jit(solution)/shard_map/ppermute | solution.py:58
  120.9 22.7 %all-to-all-start.3 = ((f32[32,24,128]{2,1,0:T(8,128)}), f32[32,24,128]{2,1,0:T(8,128)S(1)}, u32[]{:S(2)}, u32[]{:S(2)}) async-start(f32[32,24,128]{2,1,0:T(8,128)} %bitcast.12), calls=%async_computation.3 | async-start | bytes 786432 | tf_op jit(solution)/shard_map/all_to_all | solution.py:66
  133.1 10.5 %copy-start.3 = (bf16[32,32,128]{2,1,0:T(8,128)(2,1)S(1)}, bf16[32,32,128]{2,1,0:T(8,128)(2,1)}, u32[]{:S(2)}) copy-start(bf16[32,32,128]{2,1,0:T(8,128)(2,1)} %copy-done.2) | copy-start | bytes 786436
  133.1 10.5 %copy-start.28 = (f32[8,128]{1,0:T(8,128)S(1)}, f32[8,128]{1,0:T(8,128)}, u32[]{:S(2)}) copy-start(f32[8,128]{1,0:T(8,128)} %copy-done.27) | copy-start | bytes 12292
  133.1 10.5 %copy-start.34 = (s32[2]{0:T(128)S(1)}, s32[2]{0:T(128)}, u32[]{:S(2)}) copy-start(s32[2]{0:T(128)} %refs_0_.3) | copy-start | bytes 28
  145.5 11.4 %copy-start.38 = (f32[24,128]{1,0:T(8,128)}, f32[24,128]{1,0:T(8,128)S(1)}, u32[]{:S(2)}) copy-start(f32[24,128]{1,0:T(8,128)S(1)} %get-tuple-element.78.s0) | copy-start | bytes 36868
  145.5 11.3 %collective-permute-start.15 = (f32[24,128]{1,0:T(8,128)S(1)}, f32[24,128]{1,0:T(8,128)S(1)}, u32[]{:S(2)}, u32[]{:S(2)}) collective-permute-start(f32[24,128]{1,0:T(8,128)S(1)} %get-tuple-element.78.s0), channel_id=1, source_target_pairs={{0,1},{1,2},{2,3},{3,0},{4,5},{5,6},{6,7},{7,4},{8,9},{9,10},{10,1... | collective-permute-start | bytes 36872 | tf_op jit(solution)/shard_map/ppermute | solution.py:58
  145.6 11.3 %collective-permute-start.16 = (f32[24,128]{1,0:T(8,128)S(1)}, f32[24,128]{1,0:T(8,128)S(1)}, u32[]{:S(2)}, u32[]{:S(2)}) collective-permute-start(f32[24,128]{1,0:T(8,128)S(1)} %get-tuple-element.78.s0), channel_id=1, source_target_pairs={{0,2},{1,3},{2,0},{3,1},{4,6},{5,7},{6,4},{7,5},{8,10},{9,11},{10,... | collective-permute-start | bytes 36872 | tf_op jit(solution)/shard_map/ppermute | solution.py:58
  150.0 6.9 %collective-permute-start.17 = (f32[24,128]{1,0:T(8,128)S(1)}, f32[24,128]{1,0:T(8,128)S(1)}, u32[]{:S(2)}, u32[]{:S(2)}) collective-permute-start(f32[24,128]{1,0:T(8,128)S(1)} %get-tuple-element.78.s0), channel_id=1, source_target_pairs={{0,3},{1,0},{2,1},{3,2},{4,7},{5,4},{6,5},{7,6},{8,11},{9,8},{10,9... | collective-permute-start | bytes 36872 | tf_op jit(solution)/shard_map/ppermute | solution.py:58
  150.6 20.2 %all-to-all-start.4 = ((f32[32,16,128]{2,1,0:T(8,128)}), f32[32,16,128]{2,1,0:T(8,128)S(1)}, u32[]{:S(2)}, u32[]{:S(2)}) async-start(f32[32,16,128]{2,1,0:T(8,128)} %add.7), calls=%async_computation.4 | async-start | bytes 524288 | tf_op jit(solution)/shard_map/all_to_all | solution.py:66
  165.5 5.3 %collective-permute-start.18 = (f32[8,1024]{1,0:T(8,128)}, f32[8,1024]{1,0:T(8,128)S(1)}, u32[]{:S(2)}, u32[]{:S(2)}) collective-permute-start(f32[8,1024]{1,0:T(8,128)} %shard_map.165.c0), channel_id=1, source_target_pairs={{0,1},{1,2},{2,3},{3,0},{4,5},{5,6},{6,7},{7,4},{8,9},{9,10},{10,1... | collective-permute-start | bytes 98312 | tf_op jit(solution)/shard_map/ppermute | solution.py:58
  167.5 5.6 %collective-permute-start.19 = (f32[8,1024]{1,0:T(8,128)}, f32[8,1024]{1,0:T(8,128)S(1)}, u32[]{:S(2)}, u32[]{:S(2)}) collective-permute-start(f32[8,1024]{1,0:T(8,128)} %shard_map.165.c0), channel_id=1, source_target_pairs={{0,2},{1,3},{2,0},{3,1},{4,6},{5,7},{6,4},{7,5},{8,10},{9,11},{10,... | collective-permute-start | bytes 98312 | tf_op jit(solution)/shard_map/ppermute | solution.py:58
  167.5 5.6 %collective-permute-start.20 = (f32[8,1024]{1,0:T(8,128)}, f32[8,1024]{1,0:T(8,128)S(1)}, u32[]{:S(2)}, u32[]{:S(2)}) collective-permute-start(f32[8,1024]{1,0:T(8,128)} %shard_map.165.c0), channel_id=1, source_target_pairs={{0,3},{1,0},{2,1},{3,2},{4,7},{5,4},{6,5},{7,6},{8,11},{9,8},{10,9... | collective-permute-start | bytes 98312 | tf_op jit(solution)/shard_map/ppermute | solution.py:58
  (24 other events, 16.0 us)
Sparse Core Ops, SparseCore 0:
  16.4 90.2 all-gather.1

commit v6 on v5

--- a/solution.py
+++ b/solution.py
@@ -21,9 +21,8 @@
 QKV_ROWS = 24
 KEY_ROW = ROLLS * HEADS_TP
 STATE_ROW = KEY_ROW + 2 * ROLLS
-GRANT = 56
+GRANT = 40
 SMALL_GRANT = 24
-MID_GRANT = 60
 DECODE_HINT = 128
 
 adapter_scale = 2.0
@@ -113,10 +112,7 @@
         out[m, PIECE:, :] = jnp.concatenate([cut, tail], axis=0).astype(bf16)
 
 
-def spread_qkv(state, gain, first, w_own, w_other, out):
-    w_even = jnp.where(first, w_own[...], w_other[...])
-    w_odd = jnp.where(first, w_other[...], w_own[...])
-    w = jnp.concatenate([w_even, w_odd], axis=0)
+def spread_qkv(state, gain, w, out):
     x = state * gain
     x1 = x.astype(bf16)
     rest = x - x1.astype(f32)
@@ -150,27 +146,36 @@
     return gain[:, pl.ds(start, LANES)].astype(f32)
 
 
-def qkv_first_kernel(arrived, gain, w_own, w_other, out, state_out, held):
+def qkv_first_kernel(arrived, gain, w_own, w_other, out, state_out, w_out, held):
     held[...] = arrived[...].astype(f32).reshape(CHIP_COUNT * FIRST_ROWS, LANES)
     state = jnp.concatenate(
         [held[pl.ds(PIECE + b, CHIP_COUNT, stride=FIRST_ROWS), :] for b in range(ROLLS)], axis=0
     )
     state_out[...] = state
-    spread_qkv(state, gain_of(gain), first_core(), w_own, w_other, out)
-
-
-def qkv_later_kernel(state, gain, w_own, w_other, b_cols, s0, s1, s2, s3, out):
+    first = first_core()
+    rows = w_own.shape[0]
+    w_out[:rows, :] = jnp.where(first, w_own[...], w_other[...])
+    w_out[rows:, :] = jnp.where(first, w_other[...], w_own[...])
+    spread_qkv(state, gain_of(gain), w_out[...], out)
+
+
+def qkv_later_kernel(held, gain, w, s0, s1, s2, s3, out):
     share = s0[...] + s1[...] + s2[...] + s3[...]
     low = share[:, LANES:]
+    count = share.shape[0]
     now = (
-        state[...]
+        held[:count, :]
         + share[:, :LANES]
-        + adapter_scale * nt_dot(low, b_cols[...], precision=HIGH)
-    )
-    spread_qkv(now, gain_of(gain), first_core(), w_own, w_other, out)
-
-
-def attend_kernel(last, lengths, came, cache, before, ab, attended, kv_out, owned_out, held):
+        + adapter_scale * nt_dot(low, held[count:, :], precision=HIGH)
+    )
+    spread_qkv(now, gain_of(gain), w[...], out)
+
+
+def attend_kernel(last, lengths, came, cache, *refs):
+    if last:
+        before, ab, attended, owned_out = refs
+    else:
+        attended, kv_out = refs
     sums = jnp.sum(came[...].reshape(CHIP_COUNT, QKV_ROWS, LANES), axis=0)
     factor = 1.0 / math.sqrt(HD)
     width = CHIP_COUNT * LANES
@@ -179,7 +184,8 @@
     kvs = []
     for b in range(ROLLS):
         owned = came[pl.ds(STATE_ROW + b, CHIP_COUNT, stride=QKV_ROWS), :]
-        owned_out[b * CHIP_COUNT : (b + 1) * CHIP_COUNT, :] = owned
+        if last:
+            owned_out[b * CHIP_COUNT : (b + 1) * CHIP_COUNT, :] = owned
         total = jnp.sum(jnp.sum(owned * owned, axis=0, keepdims=True), axis=1, keepdims=True)
         scale = lax.rsqrt(total * (1.0 / width) + 1e-05)
         query = sums[b * HEADS_TP : (b + 1) * HEADS_TP] * scale
@@ -222,21 +228,20 @@
         attended[...] = jnp.concatenate([both, low], axis=0)
     else:
         attended[...] = jnp.broadcast_to(both.astype(bf16), attended.shape)
-    kv_out[...] = jnp.concatenate(kvs + [jnp.zeros((8 - 2 * ROLLS, LANES), f32)], axis=0)
-
-
-def attend(last, lengths, came, cache, before, ab):
-    att = (
-        shape(24, LANES)
-        if last
-        else shape(CHIP_COUNT, ROLLS * HEADS_TP, LANES, dtype=bf16)
-    )
+        kv_out[...] = jnp.concatenate(kvs + [jnp.zeros((8 - 2 * ROLLS, LANES), f32)], axis=0)
+
+
+def attend(last, lengths, came, cache, *more):
+    if last:
+        out = (shape(24, LANES), shape(ROLLS * CHIP_COUNT, LANES))
+    else:
+        out = (shape(CHIP_COUNT, ROLLS * HEADS_TP, LANES, dtype=bf16), shape(8, LANES))
+    args = (lengths, came, cache, *more)
     return call(
         lambda *refs: attend_kernel(last, *refs),
-        (att, shape(8, LANES), shape(ROLLS * CHIP_COUNT, LANES)),
-        [SMEM, VMEM, VMEM, VMEM, VMEM],
-        (lengths, came, cache, before, ab),
-        scratch=[pltpu.VMEM((8, LANES), f32)],
+        out,
+        [SMEM] + [VMEM] * (len(args) - 1),
+        args,
         flops=2 * 32 * 2 * cache.shape[0] * cache.shape[1] * HD,
     )
 
@@ -306,7 +311,7 @@
 
 
 def gradient_kernel(
-    p0, p1, p2, p3, rows, weighted, low_back, b_cols, kept, given
+    p0, p1, p2, p3, rows, weighted, state, low_back, joined, kept, given
 ):
     count = rows.shape[0]
     total = p0[:count, :] + p1[:count, :] + p2[:count, :] + p3[:count, :]
@@ -317,7 +322,8 @@
     piece = p0[count:, :]
     for by, p in ((1, p1), (2, p2), (3, p3)):
         piece = jnp.where(from_y == by, p[count:, :], piece)
-    b_cols[...] = piece
+    joined[: state.shape[0], :] = state[...]
+    joined[state.shape[0] :, :] = piece
     a_side = tn_dot(rows[...], turned)
     b_side = tn_dot(weighted[...], turned)
     both = adapter_scale * jnp.where(lane_iota(a_side.shape) < RANK, a_side, b_side)
@@ -334,23 +340,20 @@
     return pltpu.roll(b.astype(f32), RANK, 1)
 
 
-def rows_kernel(where_ref, own, left, right, far_a, far_b, w_ref, low, b_ref, out):
-    half = far_a.shape[0]
+def near_kernel(where_ref, own, left, right, w_ref, low, b_ref, out):
     acc = nt_dot(own[...], w_ref[where_ref[0]])
     acc = acc + nt_dot(left[...], w_ref[where_ref[1]])
     acc = acc + nt_dot(right[...], w_ref[where_ref[3]])
-    far = jnp.concatenate([far_a[...], far_b[...]], axis=0)
-    acc = acc + nt_dot(far, w_ref[where_ref[2]])
     out[...] = acc + adapter_scale * nt_dot(low[...], turned_up(b_ref).astype(bf16))
 
 
-def output_rows(where, own, left, right, far_a, far_b, w, low, b):
+def near_rows(where, own, left, right, w, low, b):
     n, width, depth = w.shape
     rows = own.shape[0]
     tile = 256
     whole = lambda a: pl.BlockSpec(a.shape, lambda j, s: (0, 0))
     return pl.pallas_call(
-        rows_kernel,
+        near_kernel,
         out_shape=shape(rows, width),
         grid_spec=pltpu.PrefetchScalarGridSpec(
             num_scalar_prefetch=1,
@@ -359,8 +362,6 @@
                 whole(own),
                 whole(left),
                 whole(right),
-                whole(far_a),
-                whole(far_b),
                 pl.BlockSpec((n, tile, depth), lambda j, s: (0, j, 0)),
                 whole(low),
                 pl.BlockSpec((tile, b.shape[1]), lambda j, s: (j, 0)),
@@ -369,16 +370,20 @@
         ),
         compiler_params=pltpu.CompilerParams(vmem_limit_bytes=GRANT << 20),
         cost_estimate=pl.CostEstimate(
-            flops=2 * rows * width * depth * n,
+            flops=2 * rows * width * depth * (n - 1),
             bytes_accessed=2 * (n * width * depth + n * rows * depth) + 4 * rows * width,
             transcendentals=0,
         ),
-    )(where, own, left, right, far_a, far_b, w, low, b)
-
-
-def decode_kernel(where_ref, s0, s1, s2, s3, w_ref, b_ref, owned, out, heads, acc):
+    )(where, own, left, right, w, low, b)
+
+
+def last_kernel(
+    where_ref, s0, s1, s2, s3, w_ref, b_ref, owned, near, far_a, far_b, out, rows_out, heads, acc
+):
     sent = (s0, s1, s2, s3)
     k = pl.program_id(0)
+    half = far_a.shape[0]
+    mid = len(sent) // 2
 
     @pl.when(k == 0)
     def _():
@@ -394,7 +399,16 @@
             heads[i] = jnp.concatenate(flat, axis=0).astype(bf16)
         acc[...] = jnp.zeros_like(acc)
 
-    acc[...] += nt_dot(w_ref[0], heads[k])
+    @pl.when(k != mid)
+    def _():
+        acc[...] += nt_dot(w_ref[0], heads[k])
+
+    @pl.when(k == mid)
+    def _():
+        w = w_ref[0]
+        acc[...] += nt_dot(w, heads[k])
+        rows_out[:half, :] = near[:half, :] + nt_dot(far_a[...], w)
+        rows_out[half:, :] = near[half:, :] + nt_dot(far_b[...], w)
 
     @pl.when(k == pl.num_programs(0) - 1)
     def _():
@@ -405,12 +419,12 @@
         out[:ROLLS, :] += owned[...]
 
 
-def decode_columns(where, sent, w, b, owned):
+def last_products(where, sent, w, b, owned, near, far_a, far_b):
     n, width, depth = w.shape
     whole = lambda a: pl.BlockSpec(a.shape, lambda k, s: (0, 0))
     return pl.pallas_call(
-        decode_kernel,
-        out_shape=shape(8, width),
+        last_kernel,
+        out_shape=(shape(8, width), shape(*near.shape)),
         grid_spec=pltpu.PrefetchScalarGridSpec(
             num_scalar_prefetch=1,
             grid=(n,),
@@ -419,20 +433,26 @@
                 pl.BlockSpec((1, width, depth), lambda k, s: (s[k], 0, 0)),
                 whole(b),
                 pl.BlockSpec((ROLLS, width), lambda k, s: (0, s[0])),
+                whole(near),
+                whole(far_a),
+                whole(far_b),
             ],
-            out_specs=pl.BlockSpec((8, width), lambda k, s: (0, 0)),
+            out_specs=(
+                pl.BlockSpec((8, width), lambda k, s: (0, 0)),
+                whole(near),
+            ),
             scratch_shapes=[
                 pltpu.VMEM((n, 16, depth), bf16),
                 pltpu.VMEM((width, 16), f32),
             ],
         ),
-        compiler_params=pltpu.CompilerParams(vmem_limit_bytes=MID_GRANT << 20),
+        compiler_params=pltpu.CompilerParams(vmem_limit_bytes=GRANT << 20),
         cost_estimate=pl.CostEstimate(
             flops=DECODE_HINT * 2 * 16 * width * depth * n,
             bytes_accessed=2 * n * width * depth,
             transcendentals=0,
         ),
-    )(where, *sent, w, b, owned)
+    )(where, *sent, w, b, owned, near, far_a, far_b)
 
 
 def place_kernel(c0, c1, c2, c3, out):
@@ -493,26 +513,29 @@
     w_block = w_block.reshape(nt, shard_width, w_cols.shape[1])
 
 
-    left = shift(attention_rows, 1, nt)
-    right = shift(attention_rows, nt - 1, nt)
     arrived = exchange(message, CHIPS)
     gain = attention_norm_gain[None, :]
-    sent, state = call(
+    sent, state, w_both = call(
         qkv_first_kernel,
-        (shape(CHIP_COUNT * QKV_ROWS, LANES), shape(ROLLS * CHIP_COUNT, LANES)),
+        (
+            shape(CHIP_COUNT * QKV_ROWS, LANES),
+            shape(ROLLS * CHIP_COUNT, LANES),
+            shape(2 * w_rows.shape[0], w_rows.shape[1], dtype=bf16),
+        ),
         [VMEM] * 4,
         (arrived, gain, w_rows, w_rows_other),
         scratch=[pltpu.VMEM((CHIP_COUNT * FIRST_ROWS, LANES), f32)],
     )
     arrived_other = swapped(arrived)
-    sent, arrived, arrived_other, left, right = together(
-        sent, arrived, arrived_other, left, right
+    sent, arrived, arrived_other, own_rows = together(
+        sent, arrived, arrived_other, attention_rows
     )
     came = exchange(sent.reshape(CHIP_COUNT, QKV_ROWS, LANES), CHIPS)
-    half = attention_rows.shape[0] // 2
-    came, left_half, right_half = together(came, left[:half], right[half:])
-
+
+    left = shift(own_rows, 1, nt)
+    right = shift(own_rows, nt - 1, nt)
     rows = attention_rows.shape[0]
+    half = rows // 2
     weighted, ab, part = call(
         adapter_kernel,
         (
@@ -535,27 +558,8 @@
     ab = ab.reshape(shard_width, LANES)
     parts = shifts(part, nt)
 
-    nothing = jnp.zeros((8, LANES), f32)
-    attended, kv, _ = attend(
-        False, cache_fill_lengths, came.reshape(-1, LANES), cache, nothing, ab
-    )
-    attended, weighted = together(attended, weighted)
+    attended, kv = attend(False, cache_fill_lengths, came.reshape(-1, LANES), cache)
     everyone = exchange(attended, CHIPS)
-
-    low_back, b_cols, kept, given = call(
-        gradient_kernel,
-        (
-            shape(rows, LANES, dtype=bf16),
-            shape(LANES, LANES),
-            shape(CHIP_COUNT, PIECE, LANES),
-            shape(CHIP_COUNT, PIECE, LANES),
-        ),
-        [VMEM] * 6,
-        (*parts, attention_rows, weighted),
-        flops=4 * rows * shard_width * LANES,
-    )
-
-    everyone, b_cols = together(everyone, b_cols)
 
     share = call(
         close_kernel,
@@ -564,41 +568,47 @@
         (everyone, w_cols, w_cols_other, ab),
         scratch=[pltpu.VMEM((CHIP_COUNT * ROLLS * HEADS_TP, LANES), f32)],
     )
+    share, weighted = together(share, weighted)
     shares = shifts(share, nt)
+
+    low_back, joined, kept, given = call(
+        gradient_kernel,
+        (
+            shape(rows, LANES, dtype=bf16),
+            shape(ROLLS * CHIP_COUNT + LANES, LANES),
+            shape(CHIP_COUNT, PIECE, LANES),
+            shape(CHIP_COUNT, PIECE, LANES),
+        ),
+        [VMEM] * 7,
+        (*parts, attention_rows, weighted, state),
+        flops=4 * rows * shard_width * LANES,
+    )
 
     sent = call(
         qkv_later_kernel,
         shape(CHIP_COUNT * QKV_ROWS, LANES),
-        [VMEM] * 9,
-        (state, gain, w_rows, w_rows_other, b_cols, *shares),
-    )
-    sent, low_back, given = together(sent, low_back, given)
-    given, left_half, right_half = together(swapped(given), left_half, right_half)
-    kept = kept + given
-    far_a = shift(left_half, 1, nt)
-    far_b = shift(right_half, nt - 1, nt)
+        [VMEM] * 7,
+        (joined, gain, w_both, *shares),
+    )
+    sent, low_back, left_far, right_far = together(sent, low_back, left, right)
     came = exchange(sent.reshape(CHIP_COUNT, QKV_ROWS, LANES), CHIPS)
 
-    adapted = output_rows(
-        where, attention_rows, left, right, far_a, far_b, w_block, low_back, ab
-    )
-
-    came, adapted = together(came, adapted)
-
-    attended, _, owned = attend(True, cache_fill_lengths, came.reshape(-1, LANES), cache, kv, ab)
+    far_a = shift(left_far[:half], 1, nt)
+    far_b = shift(right_far[half:], nt - 1, nt)
+    kept = kept + swapped(given)
+    near = near_rows(where, attention_rows, left, right, w_block, low_back, ab)
+    came, near = together(came, near)
+
+    attended, owned = attend(True, cache_fill_lengths, came.reshape(-1, LANES), cache, kv, ab)
     attended, kept = together(attended, kept)
     summed = exchange(kept, CHIPS)
-    cols = decode_columns(where, shifts(attended, nt), w_block, ab, owned.reshape(ROLLS, width))
+    cols, adapted = last_products(
+        where, shifts(attended, nt), w_block, ab, owned.reshape(ROLLS, width), near, far_a, far_b
+    )
     arriving = shifts(cols, nt)
     arriving[1], summed = together(arriving[1], summed)
     summed = summed.sum(axis=0)
-    decoded = call(
-        place_kernel,
-        shape(ROLLS, width),
-        [VMEM] * nt,
-        tuple(arriving),
-        grant=SMALL_GRANT,
-    )
+    decoded = call(place_kernel, shape(ROLLS, width), [VMEM] * nt, tuple(arriving))
     grad_a = summed[:, :RANK].T[:, None, :]
     grad_b = summed[:, RANK:].T[:, None, :]
     return (decoded, adapted, grad_a, grad_b)

time: 183 us -> 179 us (0.978)
  blocking collectives: 24.1 us -> 46.6 us
  waiting for transfers between devices: 19.1 us -> 1.83 us
  starting transfers between devices: 60.1 us -> 53.3 us
  Pallas kernels: 31.3 us -> 26.2 us
    all_to_all x1 -> x2, blocking collectives: 24.1 us -> 46.6 us  [exchange(): return lax.all_to_all(x, axes, split_axis=0, concat_axis=0, tiled=True)]
    ppermute x16, waiting for transfers between devices: 12.7 us -> 1.14 us  [shift(): return lax.ppermute(x, 't', [(i, (i + by) % n) for i in range(n)])]
    ppermute x16, starting transfers between devices: 27.7 us -> 23.2 us  [shift(): return lax.ppermute(x, 't', [(i, (i + by) % n) for i in range(n)])]
    all_to_all x4 -> x3, waiting for transfers between devices: 3.62 us -> 0.01 us  [exchange(): return lax.all_to_all(x, axes, split_axis=0, concat_axis=0, tiled=True)]
    pallas_call x2, Pallas kernels: 17.9 us -> 14.7 us  [the longest x1 7.65 us: last_products(): pl.pallas_call(last_kernel, out_shape=(shape(8, width), shape(*near.shape...]
    all_to_all x4 -> x3, starting transfers between devices: 28.4 us -> 26 us  [exchange(): return lax.all_to_all(x, axes, split_axis=0, concat_axis=0, tiled=True)]
    pallas_call x9, Pallas kernels: 13.5 us -> 11.5 us  [call(): pl.pallas_call(kernel, out_shape=out, in_specs=[pl.BlockSpec(memory_space...]
    unnamed x92 -> x84, local copies, waits for them, and re-layouts: 26.3 us -> 27.5 us
  transfers between devices with their start and end apart: 26 -> 25, of which waited for: 10 -> 3; matrix products, arithmetic and copies ran while one was open for 3% -> 4% of each run, Pallas kernels for 16% -> 14%
where the time goes in v6:
time: 179 us; the launch traced here: 177 us
  starting transfers between devices  53.3 us (30%)
  blocking collectives  46.6 us (26%)
  local copies, waits for them, and re-layouts  32.7 us (18%)
  Pallas kernels  26.2 us (15%)
  between operations  14.4 us (8%)
  other arithmetic  2.25 us (1%)
  waiting for transfers between devices  1.83 us (1%)
    all_to_all x2, blocking collectives, exchange(): return lax.all_to_all(x, axes, split_axis=0, concat_axis=0, tiled=True)  46.6 us
    unnamed x84, local copies, waits for them, and re-layouts  27.5 us
    all_to_all x3, starting transfers between devices, exchange(): return lax.all_to_all(x, axes, split_axis=0, concat_axis=0, tiled=True)  26 us
    ppermute x16, starting transfers between devices, shift(): return lax.ppermute(x, 't', [(i, (i + by) % n) for i in range(n)])  23.2 us
    pallas_call x9, Pallas kernels, call(): pl.pallas_call(kernel, out_shape=out, in_specs=[pl.BlockSpec(memory_space...  11.5 us
    pallas_call x1, Pallas kernels, last_products(): pl.pallas_call(last_kernel, out_shape=(shape(8, width), shape(*near.shape...  7.65 us
    pallas_call x1, Pallas kernels, near_rows(): pl.pallas_call(near_kernel, out_shape=shape(rows, width), grid_spec=pltpu...  7.05 us
  transfers between devices with their start and end apart: 25, of which 3 were waited for; matrix products, arithmetic and copies ran while one was open for 4% of the time, Pallas kernels for 14%

profile of v6, /device:TPU:8, one launch (start us, length us, event | category | flops | bytes accessed | tf_op | source)
XLA Modules:
  0.0 177.3 jit_solution(13191169397041311612)
XLA Ops:
  7.2 3.4 %collective-permute-start = (bf16[64,1024]{1,0:T(8,128)(2,1)}, bf16[64,1024]{1,0:T(8,128)(2,1)S(1)}, u32[]{:S(2)}, u32[]{:S(2)}) collective-permute-start(bf16[64,1024]{1,0:T(8,128)(2,1)} %bitcast.37), channel_id=1, source_target_pairs={{0,0},{1,64},{2,128},{3,192},{64,1},{65,65},{66,129},{67,193},{128... | collective-permute-start | bytes 393224 | tf_op jit(solution)/shard_map/ppermute | solution.py:508
  10.7 0.7 copy-done.26
  11.4 0.7 copy-done.27
  12.1 0.7 copy-done.28
  16.6 26.5 %all_to_all.25.arrived.own = bf16[32,24,128]{2,1,0:T(8,128)(2,1)S(1)} all-to-all(bf16[32,24,128]{2,1,0:T(8,128)(2,1)} %copy-done.12), channel_id=1, replica_groups=mesh['y'=4,'z'=8,'c'=2,'t'=4] {'y','z'}, dimensions={0} | all-to-all | bytes 393216 | tf_op jit(solution)/shard_map/all_to_all | solution.py:65
  43.6 0.7 broadcast_in_dim.9.gain
  44.9 0.9 copy-done.20
  46.8 0.7 copy-done.13
  47.6 0.7 copy-done.14
  48.9 0.7 copy-done.18
  49.6 6.2 %all-to-all-start.1 = ((f32[32,24,128]{2,1,0:T(8,128)}), f32[32,24,128]{2,1,0:T(8,128)}, u32[]{:S(2)}, u32[]{:S(2)}) async-start(f32[32,24,128]{2,1,0:T(8,128)} %bitcast.34), calls=%async_computation.1 | async-start | bytes 786432 | tf_op jit(solution)/shard_map/all_to_all | solution.py:65
  55.9 3.2 %collective-permute-start.11 = (bf16[512,1024]{1,0:T(8,128)(2,1)S(1)}, bf16[512,1024]{1,0:T(8,128)(2,1)}, u32[]{:S(2)}, u32[]{:S(2)}) collective-permute-start(bf16[512,1024]{1,0:T(8,128)(2,1)S(1)} %copy-done), channel_id=1, source_target_pairs={{0,3},{1,0},{2,1},{3,2},{4,7},{5,4},{6,5},{7,6},{8,11},{9,8},{10,9... | collective-permute-start | bytes 3145736 | tf_op jit(solution)/shard_map/ppermute | solution.py:57
  59.1 0.9 copy-done.7
  60.1 1.2 copy-done.9
  61.3 0.9 copy-done.19
  64.2 2.3 %shard_map.158 = (bf16[512,1024]{1,0:T(8,128)(2,1)S(1)}, bf16[32,32,128]{2,1,0:T(8,128)(2,1)S(1)}, f32[640,128]{1,0:T(8,128)}) custom-call(f32[2]{0:T(128)S(1)} %copy-done.32, s32[2]{0:T(128)S(1)} %copy-done.34, s32[2]{0:T(128)S(1)} %copy-done.37, bf16[32,24,128]{2,1,0:T(8,128)(2,1)S(1)} %copy-done.7, bf16[32,24,128]{2,1,0:T(8,128)(2,1)S(1)} %copy-done.19, ...), custom_call_target="tpu_custom_call" | custom-call | flops 268435456 | bytes 4128792 | tf_op jit(solution)/shard_map/pallas_call | solution.py:85
  66.5 1.0 copy-done.10
  67.4 1.5 collective-permute-start.4
  69.6 1.8 collective-permute-start.5
  71.4 0.7 copy-done.35
  72.1 2.2 %shard_map.159 = (bf16[32,16,128]{2,1,0:T(8,128)(2,1)S(1)}, f32[8,128]{1,0:T(8,128)S(1)}) custom-call(s32[2]{0:T(128)S(1)} %copy-done.35, f32[768,128]{1,0:T(8,128)} %bitcast.8.refs_1_, bf16[2,2048,256]{2,1,0:T(8,128)(2,1)S(1)} %bitcast.27), custom_call_target="tpu_custom_call" | custom-call | flops 67108864 | bytes 2625544 | tf_op jit(solution)/shard_map/pallas_call | solution.py:85
  75.0 20.1 %all_to_all.26.came = bf16[32,16,128]{2,1,0:T(8,128)(2,1)S(1)} all-to-all(bf16[32,16,128]{2,1,0:T(8,128)(2,1)S(1)} %get-tuple-element.46), channel_id=1, replica_groups=mesh['y'=4,'z'=8,'c'=2,'t'=4] {'y','z'}, dimensions={0} | all-to-all | bytes 262144 | tf_op jit(solution)/shard_map/all_to_all | solution.py:65
  95.4 0.9 collective-permute-done.3.p1
  96.5 1.9 %collective-permute-start.8 = (f32[64,256]{1,0:T(8,128)S(1)}, f32[64,256]{1,0:T(8,128)S(1)}, u32[]{:S(2)}, u32[]{:S(2)}) collective-permute-start(f32[64,256]{1,0:T(8,128)S(1)} %shard_map.160.s0), channel_id=1, source_target_pairs={{0,2},{1,3},{2,0},{3,1},{4,6},{5,7},{6,4},{7,5},{8,10},{9,11},{10,... | collective-permute-start | bytes 196616 | tf_op jit(solution)/shard_map/ppermute | solution.py:57
  98.4 2.5 %collective-permute-start.9 = (f32[64,256]{1,0:T(8,128)S(1)}, f32[64,256]{1,0:T(8,128)S(1)}, u32[]{:S(2)}, u32[]{:S(2)}) collective-permute-start(f32[64,256]{1,0:T(8,128)S(1)} %shard_map.160.s0), channel_id=1, source_target_pairs={{0,3},{1,0},{2,1},{3,2},{4,7},{5,4},{6,5},{7,6},{8,11},{9,8},{10,9... | collective-permute-start | bytes 196616 | tf_op jit(solution)/shard_map/ppermute | solution.py:57
  101.0 2.1 %shard_map.161 = (bf16[512,128]{1,0:T(8,128)(2,1)S(1)}, f32[192,128]{1,0:T(8,128)S(1)}, f32[32,16,128]{2,1,0:T(8,128)S(1)}, f32[32,16,128]{2,1,0:T(8,128)S(1)}) custom-call(f32[640,128]{1,0:T(8,128)} %get-tuple-element.44.p0, f32[640,128]{1,0:T(8,128)} %collective-permute-done.3.p1, f32[640,128]{1,0:T(8,128)} %collective-permute-done.4.p2, ...), custom_call_target="tpu_custom_call" | custom-call | flops 268435456 | bytes 4194304 | tf_op jit(solution)/shard_map/pallas_call | solution.py:85
  103.3 0.7 shard_map.162
  104.0 0.7 copy-done.8
  104.8 9.9 %all-to-all-start.3 = ((f32[32,24,128]{2,1,0:T(8,128)}), f32[32,24,128]{2,1,0:T(8,128)}, u32[]{:S(2)}, u32[]{:S(2)}) async-start(f32[32,24,128]{2,1,0:T(8,128)} %bitcast.33), calls=%async_computation.3 | async-start | bytes 786432 | tf_op jit(solution)/shard_map/all_to_all | solution.py:65
  114.8 1.9 %slice.12 = bf16[256,1024]{1,0:T(8,128)(2,1)} slice(bf16[512,1024]{1,0:T(8,128)(2,1)} %collective-permute-done.10.left), slice={[0:256], [0:1024]} | slice | bytes 1048576 | tf_op jit(solution)/shard_map/slice | solution.py:596
  116.7 1.3 collective-permute-start.16
  118.1 1.9 %slice.13 = bf16[256,1024]{1,0:T(8,128)(2,1)} slice(bf16[512,1024]{1,0:T(8,128)(2,1)} %collective-permute-done.11.right), slice={[256:512], [0:1024]} | slice | bytes 1048576 | tf_op jit(solution)/shard_map/slice | solution.py:597
  120.0 1.9 %collective-permute-start.17 = (bf16[256,1024]{1,0:T(8,128)(2,1)}, bf16[256,1024]{1,0:T(8,128)(2,1)}, u32[]{:S(2)}, u32[]{:S(2)}) collective-permute-start(bf16[256,1024]{1,0:T(8,128)(2,1)} %slice.13), channel_id=1, source_target_pairs={{0,3},{1,0},{2,1},{3,2},{4,7},{5,4},{6,5},{7,6},{8,11},{9,8},{10,9... | collective-permute-start | bytes 1572872 | tf_op jit(solution)/shard_map/ppermute | solution.py:57
  121.9 0.7 add.7
  122.6 3.4 %copy-done.1 = bf16[4096,1024]{1,0:T(8,128)(2,1)S(1)} copy-done((bf16[4096,1024]{1,0:T(8,128)(2,1)S(1)}, bf16[4096,1024]{1,0:T(8,128)(2,1)}, u32[]{:S(2)}) %copy-start.1) | copy-done | bytes 8388632
  126.0 7.0 %shard_map.163.near = f32[512,1024]{1,0:T(8,128)S(1)} custom-call(s32[4]{0:T(128)S(1)} %copy-done.38, bf16[512,1024]{1,0:T(8,128)(2,1)S(1)} %copy-done, bf16[512,1024]{1,0:T(8,128)(2,1)} %collective-permute-done.10.left, bf16[512,1024]{1,0:T(8,128)(2,1)} %collective-permute-done.11.right, bf16[4,1024,1024]{2,1,0:T(8,128)(2,1)S(1)} %bitcast.25, ...), custom_call_target="tpu_custom_call" | custom-call | flops 3221225472 | bytes 14680064 | tf_op jit(solution)/shard_map/pallas_call | solution.py:355
  133.1 1.3 copy-done.4
  134.4 2.4 %shard_map.164 = (f32[24,128]{1,0:T(8,128)S(1)}, f32[64,128]{1,0:T(8,128)S(1)}) custom-call(s32[2]{0:T(128)S(1)} %copy-done.36, f32[768,128]{1,0:T(8,128)} %bitcast.14.refs_1_, bf16[2,2048,256]{2,1,0:T(8,128)(2,1)S(1)} %bitcast.28, f32[8,128]{1,0:T(8,128)S(1)} %copy-done.30, bf16[1024,128]{1,0:T(8,128)(2,1)S(1)} %bitcast.31), custom_call_target="tpu_custom_call" | custom-call | flops 67108864 | bytes 2801672 | tf_op jit(solution)/shard_map/pallas_call | solution.py:85
  136.9 2.8 %collective-permute-start.14 = (f32[24,128]{1,0:T(8,128)S(1)}, f32[24,128]{1,0:T(8,128)S(1)}, u32[]{:S(2)}, u32[]{:S(2)}) collective-permute-start(f32[24,128]{1,0:T(8,128)S(1)} %get-tuple-element.64.s0), channel_id=1, source_target_pairs={{0,2},{1,3},{2,0},{3,1},{4,6},{5,7},{6,4},{7,5},{8,10},{9,11},{10,... | collective-permute-start | bytes 36872 | tf_op jit(solution)/shard_map/ppermute | solution.py:57
  140.3 9.9 %all-to-all-start.4 = ((f32[32,16,128]{2,1,0:T(8,128)}), f32[32,16,128]{2,1,0:T(8,128)}, u32[]{:S(2)}, u32[]{:S(2)}) async-start(f32[32,16,128]{2,1,0:T(8,128)} %add.7), calls=%async_computation.4 | async-start | bytes 524288 | tf_op jit(solution)/shard_map/all_to_all | solution.py:65
  150.2 3.4 %copy-done.2 = bf16[4096,1024]{1,0:T(8,128)(2,1)S(1)} copy-done((bf16[4096,1024]{1,0:T(8,128)(2,1)S(1)}, bf16[4096,1024]{1,0:T(8,128)(2,1)}, u32[]{:S(2)}) %copy-start.2) | copy-done | bytes 8388632
  153.6 1.6 copy-done.5
  155.2 7.6 %shard_map.165 = (f32[8,1024]{1,0:T(8,128)S(1)}, f32[512,1024]{1,0:T(8,128)}) custom-call(s32[4]{0:T(128)S(1)} %copy-done.39, f32[24,128]{1,0:T(8,128)S(1)} %get-tuple-element.64.s0, f32[24,128]{1,0:T(8,128)S(1)} %collective-permute-done.13.s1, f32[24,128]{1,0:T(8,128)S(1)} %collective-permute-done.14.s2, f32[24,128]{1,0:T(8,128)S(1)} %collective-permute-done.15.s3, ...), custom_call_target="tpu_custom_call" | custom-call | flops 17179869184 | bytes 8388608 | tf_op jit(solution)/shard_map/pallas_call | solution.py:425
  162.8 1.4 collective-permute-start.18
  164.3 1.2 collective-permute-start.19
  165.5 2.6 %collective-permute-start.20 = (f32[8,1024]{1,0:T(8,128)S(1)}, f32[8,1024]{1,0:T(8,128)S(1)}, u32[]{:S(2)}, u32[]{:S(2)}) collective-permute-start(f32[8,1024]{1,0:T(8,128)S(1)} %get-tuple-element.69.c0), channel_id=1, source_target_pairs={{0,3},{1,0},{2,1},{3,2},{4,7},{5,4},{6,5},{7,6},{8,11},{9,8},{10,9... | collective-permute-start | bytes 98312 | tf_op jit(solution)/shard_map/ppermute | solution.py:57
  168.1 1.0 reduce_sum.9
  169.1 0.7 slice_bitcast_fusion
  (108 shorter events, 12.1 us)
Async XLA Ops:
  7.2 48.7 %copy-start = (bf16[512,1024]{1,0:T(8,128)(2,1)S(1)}, bf16[512,1024]{1,0:T(8,128)(2,1)}, u32[]{:S(2)}) copy-start(bf16[512,1024]{1,0:T(8,128)(2,1)} %own.1) | copy-start | bytes 3145732
  7.2 115.4 %all-gather.2.cloned.1.call-start = ((), (), s32[]{:S(2)}) async-start(), calls=%async_computation.5 | async-start | bytes 8519680 | tf_op jit(solution)/shard_map/all_gather | solution.py:512
  7.2 8.7 %collective-permute-start = (bf16[64,1024]{1,0:T(8,128)(2,1)}, bf16[64,1024]{1,0:T(8,128)(2,1)S(1)}, u32[]{:S(2)}, u32[]{:S(2)}) collective-permute-start(bf16[64,1024]{1,0:T(8,128)(2,1)} %bitcast.37), channel_id=1, source_target_pairs={{0,0},{1,64},{2,128},{3,192},{64,1},{65,65},{66,129},{67,193},{128... | collective-permute-start | bytes 393224 | tf_op jit(solution)/shard_map/ppermute | solution.py:508
  16.6 54.8 %copy-start.3 = (bf16[2,2048,1,256]{3,1,2,0:T(8,128)(2,1)S(1)}, bf16[2,2048,1,256]{3,1,2,0:T(8,128)(2,1)}, u32[]{:S(2)}) copy-start(bf16[2,2048,1,256]{3,1,2,0:T(8,128)(2,1)} %param.16) | copy-start | bytes 6291460
  43.1 5.9 %collective-permute-start.2 = (bf16[32,24,128]{2,1,0:T(8,128)(2,1)S(1)}, bf16[32,24,128]{2,1,0:T(8,128)(2,1)S(1)}, u32[]{:S(2)}, u32[]{:S(2)}) collective-permute-start(bf16[32,24,128]{2,1,0:T(8,128)(2,1)S(1)} %all_to_all.25.arrived.own), channel_id=1, source_target_pairs={{0,4},{4,0},{1,5},{5,1},{2,6},{6,2},{3,7},{7,3},{8,12},{12,8},{9,1... | collective-permute-start | bytes 589832 | tf_op jit(solution)/shard_map/ppermute | solution.py:53
  43.1 1.9 %collective-permute-start.1 = (bf16[64,1280]{1,0:T(8,128)(2,1)}, bf16[64,1280]{1,0:T(8,128)(2,1)S(1)}, u32[]{:S(2)}, u32[]{:S(2)}) collective-permute-start(bf16[64,1280]{1,0:T(8,128)(2,1)} %bitcast.35), channel_id=1, source_target_pairs={{0,4},{4,0},{1,5},{5,1},{2,6},{6,2},{3,7},{7,3},{8,12},{12,8},{9,1... | collective-permute-start | bytes 491528 | tf_op jit(solution)/shard_map/ppermute | solution.py:53
  44.9 0.9 copy-start.20
  49.6 21.8 %all-to-all-start.1 = ((f32[32,24,128]{2,1,0:T(8,128)}), f32[32,24,128]{2,1,0:T(8,128)}, u32[]{:S(2)}, u32[]{:S(2)}) async-start(f32[32,24,128]{2,1,0:T(8,128)} %bitcast.34), calls=%async_computation.1 | async-start | bytes 786432 | tf_op jit(solution)/shard_map/all_to_all | solution.py:65
  55.8 48.9 %collective-permute-start.10 = (bf16[512,1024]{1,0:T(8,128)(2,1)S(1)}, bf16[512,1024]{1,0:T(8,128)(2,1)}, u32[]{:S(2)}, u32[]{:S(2)}) collective-permute-start(bf16[512,1024]{1,0:T(8,128)(2,1)S(1)} %copy-done), channel_id=1, source_target_pairs={{0,1},{1,2},{2,3},{3,0},{4,5},{5,6},{6,7},{7,4},{8,9},{9,10},{10,1... | collective-permute-start | bytes 3145736 | tf_op jit(solution)/shard_map/ppermute | solution.py:57
  55.9 48.9 %collective-permute-start.11 = (bf16[512,1024]{1,0:T(8,128)(2,1)S(1)}, bf16[512,1024]{1,0:T(8,128)(2,1)}, u32[]{:S(2)}, u32[]{:S(2)}) collective-permute-start(bf16[512,1024]{1,0:T(8,128)(2,1)S(1)} %copy-done), channel_id=1, source_target_pairs={{0,3},{1,0},{2,1},{3,2},{4,7},{5,4},{6,5},{7,6},{8,11},{9,8},{10,9... | collective-permute-start | bytes 3145736 | tf_op jit(solution)/shard_map/ppermute | solution.py:57
  59.1 9.8 %collective-permute-start.6 = (bf16[64,1024]{1,0:T(8,128)(2,1)}, bf16[64,1024]{1,0:T(8,128)(2,1)S(1)}, u32[]{:S(2)}, u32[]{:S(2)}) collective-permute-start(bf16[64,1024]{1,0:T(8,128)(2,1)} %bitcast.38), channel_id=1, source_target_pairs={{0,4},{4,0},{1,5},{5,1},{2,6},{6,2},{3,7},{7,3},{8,12},{12,8},{9,1... | collective-permute-start | bytes 393224 | tf_op jit(solution)/shard_map/ppermute | solution.py:53
  59.1 0.9 copy-start.7
  60.1 1.2 copy-start.9
  61.3 0.9 copy-start.19
  64.2 30.9 %copy-start.21 = (bf16[1,1024,64]{1,2,0:T(8,128)(2,1)S(1)}, bf16[1,1024,64]{1,2,0:T(8,128)(2,1)}, u32[]{:S(2)}) copy-start(bf16[1,1024,64]{1,2,0:T(8,128)(2,1)} %param.18) | copy-start | bytes 393220
  66.5 1.0 copy-start.10
  67.4 28.9 %collective-permute-start.3 = (f32[640,128]{1,0:T(8,128)}, f32[640,128]{1,0:T(8,128)}, u32[]{:S(2)}, u32[]{:S(2)}) collective-permute-start(f32[640,128]{1,0:T(8,128)} %get-tuple-element.44.p0), channel_id=1, source_target_pairs={{0,1},{1,2},{2,3},{3,0},{4,5},{5,6},{6,7},{7,4},{8,9},{9,10},{10,1... | collective-permute-start | bytes 983048 | tf_op jit(solution)/shard_map/ppermute | solution.py:57
  67.4 29.1 %collective-permute-start.4 = (f32[640,128]{1,0:T(8,128)}, f32[640,128]{1,0:T(8,128)}, u32[]{:S(2)}, u32[]{:S(2)}) collective-permute-start(f32[640,128]{1,0:T(8,128)} %get-tuple-element.44.p0), channel_id=1, source_target_pairs={{0,2},{1,3},{2,0},{3,1},{4,6},{5,7},{6,4},{7,5},{8,10},{9,11},{10,... | collective-permute-start | bytes 983048 | tf_op jit(solution)/shard_map/ppermute | solution.py:57
  69.6 28.9 %collective-permute-start.5 = (f32[640,128]{1,0:T(8,128)}, f32[640,128]{1,0:T(8,128)}, u32[]{:S(2)}, u32[]{:S(2)}) collective-permute-start(f32[640,128]{1,0:T(8,128)} %get-tuple-element.44.p0), channel_id=1, source_target_pairs={{0,3},{1,0},{2,1},{3,2},{4,7},{5,4},{6,5},{7,6},{8,11},{9,8},{10,9... | collective-permute-start | bytes 983048 | tf_op jit(solution)/shard_map/ppermute | solution.py:57
  71.3 23.8 %copy-start.23 = (bf16[64,1024]{1,0:T(8,128)(2,1)S(1)}, bf16[64,1024]{1,0:T(8,128)(2,1)}, u32[]{:S(2)}) copy-start(bf16[64,1024]{1,0:T(8,128)(2,1)} %copy-done.22) | copy-start | bytes 393220
  71.3 29.6 %copy-start.11 = (bf16[512,1024]{1,0:T(8,128)(2,1)S(1)}, bf16[512,1024]{1,0:T(8,128)(2,1)}, u32[]{:S(2)}) copy-start(bf16[512,1024]{1,0:T(8,128)(2,1)} %copy-done.10) | copy-start | bytes 3145732
  71.3 29.6 %copy-start.25 = (f32[64,128]{1,0:T(8,128)S(1)}, f32[64,128]{1,0:T(8,128)}, u32[]{:S(2)}) copy-start(f32[64,128]{1,0:T(8,128)} %copy-done.24) | copy-start | bytes 98308
  95.1 8.2 %copy-start.15 = (bf16[128,1280]{1,0:T(8,128)(2,1)S(1)}, bf16[128,1280]{1,0:T(8,128)(2,1)}, u32[]{:S(2)}) copy-start(bf16[128,1280]{1,0:T(8,128)(2,1)} %copy-done.14) | copy-start | bytes 983044
  96.3 6.9 %collective-permute-start.7 = (f32[64,256]{1,0:T(8,128)S(1)}, f32[64,256]{1,0:T(8,128)S(1)}, u32[]{:S(2)}, u32[]{:S(2)}) collective-permute-start(f32[64,256]{1,0:T(8,128)S(1)} %shard_map.160.s0), channel_id=1, source_target_pairs={{0,1},{1,2},{2,3},{3,0},{4,5},{5,6},{6,7},{7,4},{8,9},{9,10},{10,1... | collective-permute-start | bytes 196616 | tf_op jit(solution)/shard_map/ppermute | solution.py:57
  96.5 6.7 %collective-permute-start.8 = (f32[64,256]{1,0:T(8,128)S(1)}, f32[64,256]{1,0:T(8,128)S(1)}, u32[]{:S(2)}, u32[]{:S(2)}) collective-permute-start(f32[64,256]{1,0:T(8,128)S(1)} %shard_map.160.s0), channel_id=1, source_target_pairs={{0,2},{1,3},{2,0},{3,1},{4,6},{5,7},{6,4},{7,5},{8,10},{9,11},{10,... | collective-permute-start | bytes 196616 | tf_op jit(solution)/shard_map/ppermute | solution.py:57
  98.4 4.9 %collective-permute-start.9 = (f32[64,256]{1,0:T(8,128)S(1)}, f32[64,256]{1,0:T(8,128)S(1)}, u32[]{:S(2)}, u32[]{:S(2)}) collective-permute-start(f32[64,256]{1,0:T(8,128)S(1)} %shard_map.160.s0), channel_id=1, source_target_pairs={{0,3},{1,0},{2,1},{3,2},{4,7},{5,4},{6,5},{7,6},{8,11},{9,8},{10,9... | collective-permute-start | bytes 196616 | tf_op jit(solution)/shard_map/ppermute | solution.py:57
  103.1 1.7 copy-start.16
  103.1 1.7 copy-start.40
  104.8 17.8 %copy-start.38 = (s32[4]{0:T(128)S(1)}, s32[4]{0:T(128)}, u32[]{:S(2)}) copy-start(s32[4]{0:T(128)} %compare_select_fusion.where_ref) | copy-start | bytes 52
  104.8 29.6 %all-to-all-start.3 = ((f32[32,24,128]{2,1,0:T(8,128)}), f32[32,24,128]{2,1,0:T(8,128)}, u32[]{:S(2)}, u32[]{:S(2)}) async-start(f32[32,24,128]{2,1,0:T(8,128)} %bitcast.33), calls=%async_computation.3 | async-start | bytes 786432 | tf_op jit(solution)/shard_map/all_to_all | solution.py:65
  114.7 7.2 %copy-start.17 = (f32[32,16,128]{2,1,0:T(8,128)S(1)}, f32[32,16,128]{2,1,0:T(8,128)}, u32[]{:S(2)}) copy-start(f32[32,16,128]{2,1,0:T(8,128)} %copy-done.16) | copy-start | bytes 786436
  114.7 7.1 %collective-permute-start.12 = (f32[32,16,128]{2,1,0:T(8,128)}, f32[32,16,128]{2,1,0:T(8,128)S(1)}, u32[]{:S(2)}, u32[]{:S(2)}) collective-permute-start(f32[32,16,128]{2,1,0:T(8,128)} %copy-done.40), channel_id=1, source_target_pairs={{0,4},{4,0},{1,5},{5,1},{2,6},{6,2},{3,7},{7,3},{8,12},{12,8},{9,1... | collective-permute-start | bytes 786440 | tf_op jit(solution)/shard_map/ppermute | solution.py:53
  116.7 33.4 %collective-permute-start.16 = (bf16[256,1024]{1,0:T(8,128)(2,1)}, bf16[256,1024]{1,0:T(8,128)(2,1)}, u32[]{:S(2)}, u32[]{:S(2)}) collective-permute-start(bf16[256,1024]{1,0:T(8,128)(2,1)} %slice.12), channel_id=1, source_target_pairs={{0,1},{1,2},{2,3},{3,0},{4,5},{5,6},{6,7},{7,4},{8,9},{9,10},{10,1... | collective-permute-start | bytes 1572872 | tf_op jit(solution)/shard_map/ppermute | solution.py:57
  120.0 30.2 %collective-permute-start.17 = (bf16[256,1024]{1,0:T(8,128)(2,1)}, bf16[256,1024]{1,0:T(8,128)(2,1)}, u32[]{:S(2)}, u32[]{:S(2)}) collective-permute-start(bf16[256,1024]{1,0:T(8,128)(2,1)} %slice.13), channel_id=1, source_target_pairs={{0,3},{1,0},{2,1},{3,2},{4,7},{5,4},{6,5},{7,6},{8,11},{9,8},{10,9... | collective-permute-start | bytes 1572872 | tf_op jit(solution)/shard_map/ppermute | solution.py:57
  122.6 3.4 %copy-start.1 = (bf16[4096,1024]{1,0:T(8,128)(2,1)S(1)}, bf16[4096,1024]{1,0:T(8,128)(2,1)}, u32[]{:S(2)}) copy-start(bf16[4096,1024]{1,0:T(8,128)(2,1)} %all-gather.2.cloned.1.call-done) | copy-start | bytes 25165828
  126.0 8.4 %copy-start.30 = (f32[8,128]{1,0:T(8,128)S(1)}, f32[8,128]{1,0:T(8,128)}, u32[]{:S(2)}) copy-start(f32[8,128]{1,0:T(8,128)} %copy-done.29) | copy-start | bytes 12292
  126.0 8.4 %copy-start.36 = (s32[2]{0:T(128)S(1)}, s32[2]{0:T(128)}, u32[]{:S(2)}) copy-start(s32[2]{0:T(128)} %refs_0_.3) | copy-start | bytes 28
  133.1 1.3 copy-start.4
  134.4 15.8 %copy-start.39 = (s32[4]{0:T(128)S(1)}, s32[4]{0:T(128)}, u32[]{:S(2)}) copy-start(s32[4]{0:T(128)} %compare_select_fusion.where_ref) | copy-start | bytes 52
  136.8 13.4 %collective-permute-start.13 = (f32[24,128]{1,0:T(8,128)S(1)}, f32[24,128]{1,0:T(8,128)S(1)}, u32[]{:S(2)}, u32[]{:S(2)}) collective-permute-start(f32[24,128]{1,0:T(8,128)S(1)} %get-tuple-element.64.s0), channel_id=1, source_target_pairs={{0,1},{1,2},{2,3},{3,0},{4,5},{5,6},{6,7},{7,4},{8,9},{9,10},{10,1... | collective-permute-start | bytes 36872 | tf_op jit(solution)/shard_map/ppermute | solution.py:57
  136.9 13.3 %collective-permute-start.14 = (f32[24,128]{1,0:T(8,128)S(1)}, f32[24,128]{1,0:T(8,128)S(1)}, u32[]{:S(2)}, u32[]{:S(2)}) collective-permute-start(f32[24,128]{1,0:T(8,128)S(1)} %get-tuple-element.64.s0), channel_id=1, source_target_pairs={{0,2},{1,3},{2,0},{3,1},{4,6},{5,7},{6,4},{7,5},{8,10},{9,11},{10,... | collective-permute-start | bytes 36872 | tf_op jit(solution)/shard_map/ppermute | solution.py:57
  139.7 10.5 %collective-permute-start.15 = (f32[24,128]{1,0:T(8,128)S(1)}, f32[24,128]{1,0:T(8,128)S(1)}, u32[]{:S(2)}, u32[]{:S(2)}) collective-permute-start(f32[24,128]{1,0:T(8,128)S(1)} %get-tuple-element.64.s0), channel_id=1, source_target_pairs={{0,3},{1,0},{2,1},{3,2},{4,7},{5,4},{6,5},{7,6},{8,11},{9,8},{10,9... | collective-permute-start | bytes 36872 | tf_op jit(solution)/shard_map/ppermute | solution.py:57
  140.3 27.8 %all-to-all-start.4 = ((f32[32,16,128]{2,1,0:T(8,128)}), f32[32,16,128]{2,1,0:T(8,128)}, u32[]{:S(2)}, u32[]{:S(2)}) async-start(f32[32,16,128]{2,1,0:T(8,128)} %add.7), calls=%async_computation.4 | async-start | bytes 524288 | tf_op jit(solution)/shard_map/all_to_all | solution.py:65
  150.2 3.4 %copy-start.2 = (bf16[4096,1024]{1,0:T(8,128)(2,1)S(1)}, bf16[4096,1024]{1,0:T(8,128)(2,1)}, u32[]{:S(2)}) copy-start(bf16[4096,1024]{1,0:T(8,128)(2,1)} %all-gather.2.cloned.1.call-done) | copy-start | bytes 25165828
  153.6 1.6 copy-start.5
  162.8 5.3 %collective-permute-start.18 = (f32[8,1024]{1,0:T(8,128)S(1)}, f32[8,1024]{1,0:T(8,128)S(1)}, u32[]{:S(2)}, u32[]{:S(2)}) collective-permute-start(f32[8,1024]{1,0:T(8,128)S(1)} %get-tuple-element.69.c0), channel_id=1, source_target_pairs={{0,1},{1,2},{2,3},{3,0},{4,5},{5,6},{6,7},{7,4},{8,9},{9,10},{10,1... | collective-permute-start | bytes 98312 | tf_op jit(solution)/shard_map/ppermute | solution.py:57
  164.3 5.5 %collective-permute-start.19 = (f32[8,1024]{1,0:T(8,128)S(1)}, f32[8,1024]{1,0:T(8,128)S(1)}, u32[]{:S(2)}, u32[]{:S(2)}) collective-permute-start(f32[8,1024]{1,0:T(8,128)S(1)} %get-tuple-element.69.c0), channel_id=1, source_target_pairs={{0,2},{1,3},{2,0},{3,1},{4,6},{5,7},{6,4},{7,5},{8,10},{9,11},{10,... | collective-permute-start | bytes 98312 | tf_op jit(solution)/shard_map/ppermute | solution.py:57
  165.5 4.3 %collective-permute-start.20 = (f32[8,1024]{1,0:T(8,128)S(1)}, f32[8,1024]{1,0:T(8,128)S(1)}, u32[]{:S(2)}, u32[]{:S(2)}) collective-permute-start(f32[8,1024]{1,0:T(8,128)S(1)} %get-tuple-element.69.c0), channel_id=1, source_target_pairs={{0,3},{1,0},{2,1},{3,2},{4,7},{5,4},{6,5},{7,6},{8,11},{9,8},{10,9... | collective-permute-start | bytes 98312 | tf_op jit(solution)/shard_map/ppermute | solution.py:57
  (19 other events, 12.9 us)
Sparse Core Ops, SparseCore 0:
  16.7 90.4 all-gather.1

commit v7 on v6

--- a/solution.py
+++ b/solution.py
@@ -21,9 +21,8 @@
 QKV_ROWS = 24
 KEY_ROW = ROLLS * HEADS_TP
 STATE_ROW = KEY_ROW + 2 * ROLLS
-GRANT = 40
+GRANT = 56
 SMALL_GRANT = 24
-DECODE_HINT = 128
 
 adapter_scale = 2.0
 f32 = jnp.float32
@@ -340,54 +339,21 @@
     return pltpu.roll(b.astype(f32), RANK, 1)
 
 
-def near_kernel(where_ref, own, left, right, w_ref, low, b_ref, out):
-    acc = nt_dot(own[...], w_ref[where_ref[0]])
-    acc = acc + nt_dot(left[...], w_ref[where_ref[1]])
-    acc = acc + nt_dot(right[...], w_ref[where_ref[3]])
-    out[...] = acc + adapter_scale * nt_dot(low[...], turned_up(b_ref).astype(bf16))
-
-
-def near_rows(where, own, left, right, w, low, b):
-    n, width, depth = w.shape
+def rows_kernel(
+    where_ref, own, left, right, far_a, far_b, w_ref, low, b_ref, s0, s1, s2, s3, owned, out, cols, x
+):
     rows = own.shape[0]
-    tile = 256
-    whole = lambda a: pl.BlockSpec(a.shape, lambda j, s: (0, 0))
-    return pl.pallas_call(
-        near_kernel,
-        out_shape=shape(rows, width),
-        grid_spec=pltpu.PrefetchScalarGridSpec(
-            num_scalar_prefetch=1,
-            grid=(width // tile,),
-            in_specs=[
-                whole(own),
-                whole(left),
-                whole(right),
-                pl.BlockSpec((n, tile, depth), lambda j, s: (0, j, 0)),
-                whole(low),
-                pl.BlockSpec((tile, b.shape[1]), lambda j, s: (j, 0)),
-            ],
-            out_specs=pl.BlockSpec((rows, tile), lambda j, s: (0, j)),
-        ),
-        compiler_params=pltpu.CompilerParams(vmem_limit_bytes=GRANT << 20),
-        cost_estimate=pl.CostEstimate(
-            flops=2 * rows * width * depth * (n - 1),
-            bytes_accessed=2 * (n * width * depth + n * rows * depth) + 4 * rows * width,
-            transcendentals=0,
-        ),
-    )(where, own, left, right, w, low, b)
-
-
-def last_kernel(
-    where_ref, s0, s1, s2, s3, w_ref, b_ref, owned, near, far_a, far_b, out, rows_out, heads, acc
-):
+    half = far_a.shape[0]
     sent = (s0, s1, s2, s3)
-    k = pl.program_id(0)
-    half = far_a.shape[0]
-    mid = len(sent) // 2
-
-    @pl.when(k == 0)
+
+    @pl.when(pl.program_id(0) == 0)
     def _():
-        for i, s in enumerate(sent):
+        x[0, :rows, :] = own[...]
+        x[1, :rows, :] = left[...]
+        x[2, :half, :] = far_a[...]
+        x[2, half:rows, :] = far_b[...]
+        x[3, :rows, :] = right[...]
+        for k, s in enumerate(sent):
             flat = [
                 jnp.concatenate(
                     [s[b * HEADS_TP + h : b * HEADS_TP + h + 1, :] for h in range(HEADS_TP)],
@@ -396,63 +362,57 @@
                 for b in range(ROLLS)
             ]
             flat.append(jnp.zeros((16 - ROLLS, HEADS_TP * HD), f32))
-            heads[i] = jnp.concatenate(flat, axis=0).astype(bf16)
-        acc[...] = jnp.zeros_like(acc)
-
-    @pl.when(k != mid)
-    def _():
-        acc[...] += nt_dot(w_ref[0], heads[k])
-
-    @pl.when(k == mid)
-    def _():
-        w = w_ref[0]
-        acc[...] += nt_dot(w, heads[k])
-        rows_out[:half, :] = near[:half, :] + nt_dot(far_a[...], w)
-        rows_out[half:, :] = near[half:, :] + nt_dot(far_b[...], w)
-
-    @pl.when(k == pl.num_programs(0) - 1)
-    def _():
-        top = ROLLS * HEADS_TP
-        low = s0[top:, :] + s1[top:, :] + s2[top:, :] + s3[top:, :]
-        got = acc[...].T[:8] + adapter_scale * nt_dot(low, turned_up(b_ref), precision=HIGH)
-        out[...] = got
-        out[:ROLLS, :] += owned[...]
-
-
-def last_products(where, sent, w, b, owned, near, far_a, far_b):
+            x[k, rows:, :] = jnp.concatenate(flat, axis=0).astype(bf16)
+
+    b_turned = turned_up(b_ref)
+    acc = nt_dot(x[0], w_ref[where_ref[0]])
+    for k in range(1, len(sent)):
+        acc = acc + nt_dot(x[k], w_ref[where_ref[k]])
+    out[...] = acc[:rows] + adapter_scale * nt_dot(low[...], b_turned.astype(bf16))
+    top = ROLLS * HEADS_TP
+    low_sum = s0[top:, :] + s1[top:, :] + s2[top:, :] + s3[top:, :]
+    got = adapter_scale * nt_dot(low_sum, b_turned, precision=HIGH)
+    cols[...] = got + acc[rows : rows + 8]
+    cols[:ROLLS, :] += owned[...]
+
+
+def output_rows(where, own, left, right, far_a, far_b, w, low, b, sent, owned):
     n, width, depth = w.shape
-    whole = lambda a: pl.BlockSpec(a.shape, lambda k, s: (0, 0))
+    rows = own.shape[0]
+    tile = 256
+    tiles = width // tile
+    whole = lambda a: pl.BlockSpec(a.shape, lambda j, s: (0, 0))
     return pl.pallas_call(
-        last_kernel,
-        out_shape=(shape(8, width), shape(*near.shape)),
+        rows_kernel,
+        out_shape=(shape(rows, width), shape(8, width)),
         grid_spec=pltpu.PrefetchScalarGridSpec(
             num_scalar_prefetch=1,
-            grid=(n,),
+            grid=(tiles,),
             in_specs=[
-                *(whole(s) for s in sent),
-                pl.BlockSpec((1, width, depth), lambda k, s: (s[k], 0, 0)),
-                whole(b),
-                pl.BlockSpec((ROLLS, width), lambda k, s: (0, s[0])),
-                whole(near),
+                whole(own),
+                whole(left),
+                whole(right),
                 whole(far_a),
                 whole(far_b),
+                pl.BlockSpec((n, tile, depth), lambda j, s: (0, j, 0)),
+                whole(low),
+                pl.BlockSpec((tile, b.shape[1]), lambda j, s: (j, 0)),
+                *(whole(s) for s in sent),
+                pl.BlockSpec((ROLLS, tile), lambda j, s: (0, s[0] * tiles + j)),
             ],
             out_specs=(
-                pl.BlockSpec((8, width), lambda k, s: (0, 0)),
-                whole(near),
+                pl.BlockSpec((rows, tile), lambda j, s: (0, j)),
+                pl.BlockSpec((8, tile), lambda j, s: (0, j)),
             ),
-            scratch_shapes=[
-                pltpu.VMEM((n, 16, depth), bf16),
-                pltpu.VMEM((width, 16), f32),
-            ],
+            scratch_shapes=[pltpu.VMEM((n, rows + 16, depth), bf16)],
         ),
         compiler_params=pltpu.CompilerParams(vmem_limit_bytes=GRANT << 20),
         cost_estimate=pl.CostEstimate(
-            flops=DECODE_HINT * 2 * 16 * width * depth * n,
-            bytes_accessed=2 * n * width * depth,
+            flops=2 * rows * width * depth * n,
+            bytes_accessed=2 * (n * width * depth + n * rows * depth) + 4 * rows * width,
             transcendentals=0,
         ),
-    )(where, *sent, w, b, owned, near, far_a, far_b)
+    )(where, own, left, right, far_a, far_b, w, low, b, *sent, owned)
 
 
 def place_kernel(c0, c1, c2, c3, out):
@@ -508,12 +468,10 @@
     turned = lax.ppermute(
         w_cols, ("y", "t"), [(a * nt + b, b * nt + a) for a in range(ny) for b in range(nt)]
     )
-    turned, message, where = together(turned, message, where)
+    arrived = exchange(message, CHIPS)
+    turned, _ = together(turned, arrived)
     w_block = lax.all_gather(turned, DP, axis=0, tiled=True)
     w_block = w_block.reshape(nt, shard_width, w_cols.shape[1])
-
-
-    arrived = exchange(message, CHIPS)
     gain = attention_norm_gain[None, :]
     sent, state, w_both = call(
         qkv_first_kernel,
@@ -596,14 +554,22 @@
     far_a = shift(left_far[:half], 1, nt)
     far_b = shift(right_far[half:], nt - 1, nt)
     kept = kept + swapped(given)
-    near = near_rows(where, attention_rows, left, right, w_block, low_back, ab)
-    came, near = together(came, near)
 
     attended, owned = attend(True, cache_fill_lengths, came.reshape(-1, LANES), cache, kv, ab)
     attended, kept = together(attended, kept)
     summed = exchange(kept, CHIPS)
-    cols, adapted = last_products(
-        where, shifts(attended, nt), w_block, ab, owned.reshape(ROLLS, width), near, far_a, far_b
+    adapted, cols = output_rows(
+        where,
+        attention_rows,
+        left,
+        right,
+        far_a,
+        far_b,
+        w_block,
+        low_back,
+        ab,
+        shifts(attended, nt),
+        owned.reshape(ROLLS, width),
     )
     arriving = shifts(cols, nt)
     arriving[1], summed = together(arriving[1], summed)

time: 179 us -> 168 us (0.939)
  blocking collectives: 46.6 us -> 17.4 us
  waiting for transfers between devices: 1.83 us -> 20.9 us
  starting transfers between devices: 53.3 us -> 67.4 us
  local copies, waits for them, and re-layouts: 32.7 us -> 20.5 us
  Pallas kernels: 26.2 us -> 23.6 us
    all_to_all x2 -> x1, blocking collectives: 46.6 us -> 17.4 us  [exchange(): return lax.all_to_all(x, axes, split_axis=0, concat_axis=0, tiled=True)]
    all_to_all x3 -> x4, starting transfers between devices: 26 us -> 41.9 us  [exchange(): return lax.all_to_all(x, axes, split_axis=0, concat_axis=0, tiled=True)]
    unnamed x84 -> x78, local copies, waits for them, and re-layouts: 27.5 us -> 14.8 us
    ppermute x16, waiting for transfers between devices: 1.14 us -> 8.27 us  [shift(): return lax.ppermute(x, 't', [(i, (i + by) % n) for i in range(n)])]
    ppermute x1, waiting for transfers between devices: 0.01 us -> 5.72 us  [shards(): lax.ppermute(w_cols, ('y', 't'), [(a * nt + b, b * nt + a) for a in range...]
    all_to_all x3 -> x4, waiting for transfers between devices: 0.01 us -> 4.54 us  [exchange(): return lax.all_to_all(x, axes, split_axis=0, concat_axis=0, tiled=True)]
    pallas_call x2 -> x1, Pallas kernels: 14.7 us -> 11.1 us  [output_rows(): pl.pallas_call(rows_kernel, out_shape=(shape(rows, width), shape(8, width...]
  transfers between devices with their start and end apart: 25 -> 26, of which waited for: 3 -> 11; matrix products, arithmetic and copies ran while one was open for 4% -> 5% of each run, Pallas kernels for 14% -> 13%
where the time goes in v7:
time: 168 us; the launch traced here: 166 us
  starting transfers between devices  67.4 us (40%)
  Pallas kernels  23.6 us (14%)
  waiting for transfers between devices  20.9 us (12%)
  local copies, waits for them, and re-layouts  20.5 us (12%)
  blocking collectives  17.4 us (10%)
  between operations  14.4 us (9%)
  other arithmetic  2.25 us (1%)
    all_to_all x4, starting transfers between devices, exchange(): return lax.all_to_all(x, axes, split_axis=0, concat_axis=0, tiled=True)  41.9 us
    ppermute x16, starting transfers between devices, shift(): return lax.ppermute(x, 't', [(i, (i + by) % n) for i in range(n)])  21.7 us
    all_to_all x1, blocking collectives, exchange(): return lax.all_to_all(x, axes, split_axis=0, concat_axis=0, tiled=True)  17.4 us
    unnamed x78, local copies, waits for them, and re-layouts  14.8 us
    pallas_call x9, Pallas kernels, call(): pl.pallas_call(kernel, out_shape=out, in_specs=[pl.BlockSpec(memory_space...  12.5 us
    pallas_call x1, Pallas kernels, output_rows(): pl.pallas_call(rows_kernel, out_shape=(shape(rows, width), shape(8, width...  11.1 us
    ppermute x16, waiting for transfers between devices, shift(): return lax.ppermute(x, 't', [(i, (i + by) % n) for i in range(n)])  8.27 us
    ppermute x1, waiting for transfers between devices, shards(): lax.ppermute(w_cols, ('y', 't'), [(a * nt + b, b * nt + a) for a in range...  5.72 us
  transfers between devices with their start and end apart: 26, of which 11 were waited for; matrix products, arithmetic and copies ran while one was open for 5% of the time, Pallas kernels for 13%

profile of v7, /device:TPU:8, one launch (start us, length us, event | category | flops | bytes accessed | tf_op | source)
XLA Modules:
  0.0 166.4 jit_solution(15519172098358501498)
XLA Ops:
  7.2 0.8 copy-done.19
  8.0 0.7 copy-done.20
  8.7 0.7 copy-done.21
  10.7 1.3 shard_map.156
  12.0 11.8 %all-to-all-start = ((bf16[32,24,128]{2,1,0:T(8,128)(2,1)}), bf16[32,24,128]{2,1,0:T(8,128)(2,1)S(1)}, u32[]{:S(2)}, u32[]{:S(2)}) async-start(bf16[32,24,128]{2,1,0:T(8,128)(2,1)} %shard_map.156), calls=%async_computation | async-start | bytes 393216 | tf_op jit(solution)/shard_map/all_to_all | solution.py:64
  23.9 3.1 %collective-permute-start.13 = (bf16[64,1024]{1,0:T(8,128)(2,1)}, bf16[64,1024]{1,0:T(8,128)(2,1)S(1)}, u32[]{:S(2)}, u32[]{:S(2)}) collective-permute-start(bf16[64,1024]{1,0:T(8,128)(2,1)} %bitcast.34), channel_id=1, source_target_pairs={{0,0},{1,64},{2,128},{3,192},{64,1},{65,65},{66,129},{67,193},{128... | collective-permute-start | bytes 393224 | tf_op jit(solution)/shard_map/ppermute | solution.py:468
  26.9 5.7 %collective-permute-done.13 = bf16[64,1024]{1,0:T(8,128)(2,1)S(1)} collective-permute-done((bf16[64,1024]{1,0:T(8,128)(2,1)}, bf16[64,1024]{1,0:T(8,128)(2,1)S(1)}, u32[]{:S(2)}, u32[]{:S(2)}) %collective-permute-start.13) | collective-permute-done | bytes 131104 | tf_op jit(solution)/shard_map/ppermute | solution.py:468
  32.7 1.3 all-to-all-done.arrived.own
  34.6 0.7 broadcast_in_dim.9.gain
  35.9 0.9 copy-done.12
  37.2 0.8 copy-done.7
  37.9 0.7 copy-done.8
  39.3 13.1 %all-to-all-start.1 = ((f32[32,24,128]{2,1,0:T(8,128)}), f32[32,24,128]{2,1,0:T(8,128)}, u32[]{:S(2)}, u32[]{:S(2)}) async-start(f32[32,24,128]{2,1,0:T(8,128)} %bitcast.31), calls=%async_computation.1 | async-start | bytes 786432 | tf_op jit(solution)/shard_map/all_to_all | solution.py:64
  52.5 3.2 %collective-permute-start.3 = (bf16[512,1024]{1,0:T(8,128)(2,1)S(1)}, bf16[512,1024]{1,0:T(8,128)(2,1)}, u32[]{:S(2)}, u32[]{:S(2)}) collective-permute-start(bf16[512,1024]{1,0:T(8,128)(2,1)S(1)} %copy-done.1), channel_id=1, source_target_pairs={{0,3},{1,0},{2,1},{3,2},{4,7},{5,4},{6,5},{7,6},{8,11},{9,8},{10,9... | collective-permute-start | bytes 3145736 | tf_op jit(solution)/shard_map/ppermute | solution.py:56
  55.7 1.2 copy-done.2
  58.9 2.3 %shard_map.158 = (bf16[512,1024]{1,0:T(8,128)(2,1)S(1)}, bf16[32,32,128]{2,1,0:T(8,128)(2,1)S(1)}, f32[640,128]{1,0:T(8,128)}) custom-call(f32[2]{0:T(128)S(1)} %copy-done.25, s32[2]{0:T(128)S(1)} %copy-done.27, s32[2]{0:T(128)S(1)} %copy-done.30, bf16[32,24,128]{2,1,0:T(8,128)(2,1)S(1)} %all-to-all-done.arrived.own, ...), custom_call_target="tpu_custom_call" | custom-call | flops 268435456 | bytes 4128792 | tf_op jit(solution)/shard_map/pallas_call | solution.py:84
  61.2 1.0 copy-done.3
  62.1 0.7 copy-done.5
  62.8 1.5 collective-permute-start.5
  65.0 1.8 %collective-permute-start.6 = (f32[640,128]{1,0:T(8,128)}, f32[640,128]{1,0:T(8,128)}, u32[]{:S(2)}, u32[]{:S(2)}) collective-permute-start(f32[640,128]{1,0:T(8,128)} %get-tuple-element.39.p0), channel_id=1, source_target_pairs={{0,3},{1,0},{2,1},{3,2},{4,7},{5,4},{6,5},{7,6},{8,11},{9,8},{10,9... | collective-permute-start | bytes 983048 | tf_op jit(solution)/shard_map/ppermute | solution.py:56
  66.7 1.4 all-to-all-done.1
  68.2 0.7 copy-done.28
  68.9 2.2 %shard_map.159 = (bf16[32,16,128]{2,1,0:T(8,128)(2,1)S(1)}, f32[8,128]{1,0:T(8,128)S(1)}) custom-call(s32[2]{0:T(128)S(1)} %copy-done.28, f32[768,128]{1,0:T(8,128)} %bitcast.6.refs_1_, bf16[2,2048,256]{2,1,0:T(8,128)(2,1)S(1)} %bitcast.25), custom_call_target="tpu_custom_call" | custom-call | flops 67108864 | bytes 2625544 | tf_op jit(solution)/shard_map/pallas_call | solution.py:84
  71.8 17.4 %all_to_all.25.came = bf16[32,16,128]{2,1,0:T(8,128)(2,1)S(1)} all-to-all(bf16[32,16,128]{2,1,0:T(8,128)(2,1)S(1)} %get-tuple-element.41), channel_id=1, replica_groups=mesh['y'=4,'z'=8,'c'=2,'t'=4] {'y','z'}, dimensions={0} | all-to-all | bytes 262144 | tf_op jit(solution)/shard_map/all_to_all | solution.py:64
  89.4 3.2 %collective-permute-done.4.p1 = f32[640,128]{1,0:T(8,128)} collective-permute-done((f32[640,128]{1,0:T(8,128)}, f32[640,128]{1,0:T(8,128)}, u32[]{:S(2)}, u32[]{:S(2)}) %collective-permute-start.4) | collective-permute-done | bytes 327712 | tf_op jit(solution)/shard_map/ppermute | solution.py:56
  92.6 2.0 %collective-permute-start.8 = (f32[64,256]{1,0:T(8,128)S(1)}, f32[64,256]{1,0:T(8,128)S(1)}, u32[]{:S(2)}, u32[]{:S(2)}) collective-permute-start(f32[64,256]{1,0:T(8,128)S(1)} %shard_map.160.s0), channel_id=1, source_target_pairs={{0,1},{1,2},{2,3},{3,0},{4,5},{5,6},{6,7},{7,4},{8,9},{9,10},{10,1... | collective-permute-start | bytes 196616 | tf_op jit(solution)/shard_map/ppermute | solution.py:56
  94.8 2.2 %shard_map.161 = (bf16[512,128]{1,0:T(8,128)(2,1)S(1)}, f32[192,128]{1,0:T(8,128)S(1)}, f32[32,16,128]{2,1,0:T(8,128)S(1)}, f32[32,16,128]{2,1,0:T(8,128)S(1)}) custom-call(f32[640,128]{1,0:T(8,128)} %get-tuple-element.39.p0, f32[640,128]{1,0:T(8,128)} %collective-permute-done.4.p1, f32[640,128]{1,0:T(8,128)} %collective-permute-done.5.p2, ...), custom_call_target="tpu_custom_call" | custom-call | flops 268435456 | bytes 4194304 | tf_op jit(solution)/shard_map/pallas_call | solution.py:84
  97.0 1.0 collective-permute-done.8.s1
  98.0 2.3 %collective-permute-done.9.s2 = f32[64,256]{1,0:T(8,128)S(1)} collective-permute-done((f32[64,256]{1,0:T(8,128)S(1)}, f32[64,256]{1,0:T(8,128)S(1)}, u32[]{:S(2)}, u32[]{:S(2)}) %collective-permute-start.9) | collective-permute-done | bytes 65568 | tf_op jit(solution)/shard_map/ppermute | solution.py:56
  100.4 1.4 shard_map.162
  101.8 9.9 %all-to-all-start.3 = ((f32[32,24,128]{2,1,0:T(8,128)}), f32[32,24,128]{2,1,0:T(8,128)S(1)}, u32[]{:S(2)}, u32[]{:S(2)}) async-start(f32[32,24,128]{2,1,0:T(8,128)} %bitcast.13), calls=%async_computation.3 | async-start | bytes 786432 | tf_op jit(solution)/shard_map/all_to_all | solution.py:64
  111.8 1.9 %slice.12 = bf16[256,1024]{1,0:T(8,128)(2,1)} slice(bf16[512,1024]{1,0:T(8,128)(2,1)} %collective-permute-done.2.left), slice={[0:256], [0:1024]} | slice | bytes 1048576 | tf_op jit(solution)/shard_map/slice | solution.py:554
  113.9 1.9 %slice.13 = bf16[256,1024]{1,0:T(8,128)(2,1)} slice(bf16[512,1024]{1,0:T(8,128)(2,1)} %collective-permute-done.3.right), slice={[256:512], [0:1024]} | slice | bytes 1048576 | tf_op jit(solution)/shard_map/slice | solution.py:555
  115.8 2.9 %collective-permute-start.12 = (bf16[256,1024]{1,0:T(8,128)(2,1)}, bf16[256,1024]{1,0:T(8,128)(2,1)}, u32[]{:S(2)}, u32[]{:S(2)}) collective-permute-start(bf16[256,1024]{1,0:T(8,128)(2,1)} %slice.13), channel_id=1, source_target_pairs={{0,3},{1,0},{2,1},{3,2},{4,7},{5,4},{6,5},{7,6},{8,11},{9,8},{10,9... | collective-permute-start | bytes 1572872 | tf_op jit(solution)/shard_map/ppermute | solution.py:56
  118.8 1.7 %collective-permute-done.14 = f32[32,16,128]{2,1,0:T(8,128)} collective-permute-done((f32[32,16,128]{2,1,0:T(8,128)S(1)}, f32[32,16,128]{2,1,0:T(8,128)}, u32[]{:S(2)}, u32[]{:S(2)}) %collective-permute-start.14) | collective-permute-done | bytes 262176 | tf_op jit(solution)/shard_map/ppermute | solution.py:52
  120.4 1.7 %add.7 = f32[32,16,128]{2,1,0:T(8,128)} add(f32[32,16,128]{2,1,0:T(8,128)S(1)} %copy-done.11, f32[32,16,128]{2,1,0:T(8,128)} %collective-permute-done.14) | non-fusion elementwise | flops 65536 | bytes 786432 | tf_op jit(solution)/shard_map/add | solution.py:556
  122.1 1.8 %all-to-all-done.3 = f32[32,24,128]{2,1,0:T(8,128)S(1)} async-done(((f32[32,24,128]{2,1,0:T(8,128)}), f32[32,24,128]{2,1,0:T(8,128)S(1)}, u32[]{:S(2)}, u32[]{:S(2)}) %all-to-all-start.3) | async-done | bytes 393248 | tf_op jit(solution)/shard_map/all_to_all | solution.py:64
  124.0 1.9 %shard_map.163 = (f32[24,128]{1,0:T(8,128)S(1)}, f32[64,128]{1,0:T(8,128)S(1)}) custom-call(s32[2]{0:T(128)S(1)} %copy-done.29, f32[768,128]{1,0:T(8,128)S(1)} %bitcast.27, bf16[2,2048,256]{2,1,0:T(8,128)(2,1)S(1)} %bitcast.26, f32[8,128]{1,0:T(8,128)S(1)} %copy-done.23, bf16[1024,128]{1,0:T(8,128)(2,1)S(1)} %bitcast.30), custom_call_target="tpu_custom_call" | custom-call | flops 67108864 | bytes 2801672 | tf_op jit(solution)/shard_map/pallas_call | solution.py:84
  125.9 1.7 collective-permute-start.15
  127.5 2.7 %collective-permute-start.16 = (f32[24,128]{1,0:T(8,128)S(1)}, f32[24,128]{1,0:T(8,128)S(1)}, u32[]{:S(2)}, u32[]{:S(2)}) collective-permute-start(f32[24,128]{1,0:T(8,128)S(1)} %get-tuple-element.59.s0), channel_id=1, source_target_pairs={{0,2},{1,3},{2,0},{3,1},{4,6},{5,7},{6,4},{7,5},{8,10},{9,11},{10,... | collective-permute-start | bytes 36872 | tf_op jit(solution)/shard_map/ppermute | solution.py:56
  130.2 1.1 collective-permute-start.17
  131.3 7.1 %all-to-all-start.4 = ((f32[32,16,128]{2,1,0:T(8,128)}), f32[32,16,128]{2,1,0:T(8,128)S(1)}, u32[]{:S(2)}, u32[]{:S(2)}) async-start(f32[32,16,128]{2,1,0:T(8,128)} %add.7), calls=%async_computation.4 | async-start | bytes 524288 | tf_op jit(solution)/shard_map/all_to_all | solution.py:64
  140.2 11.1 %shard_map.164 = (f32[512,1024]{1,0:T(8,128)}, f32[8,1024]{1,0:T(8,128)}) custom-call(s32[4]{0:T(128)} %compare_select_fusion.where_ref, bf16[512,1024]{1,0:T(8,128)(2,1)} %own.1, bf16[512,1024]{1,0:T(8,128)(2,1)} %collective-permute-done.2.left, bf16[512,1024]{1,0:T(8,128)(2,1)} %collective-permute-done.3.right, ...), custom_call_target="tpu_custom_call" | custom-call | flops 4294967296 | bytes 14680064 | tf_op jit(solution)/shard_map/pallas_call | solution.py:385
  151.3 1.1 collective-permute-start.18
  153.2 2.5 %collective-permute-start.20 = (f32[8,1024]{1,0:T(8,128)}, f32[8,1024]{1,0:T(8,128)S(1)}, u32[]{:S(2)}, u32[]{:S(2)}) collective-permute-start(f32[8,1024]{1,0:T(8,128)} %get-tuple-element.61.c0), channel_id=1, source_target_pairs={{0,3},{1,0},{2,1},{3,2},{4,7},{5,4},{6,5},{7,6},{8,11},{9,8},{10,9... | collective-permute-start | bytes 98312 | tf_op jit(solution)/shard_map/ppermute | solution.py:56
  155.7 1.1 collective-permute-done.18.c1
  156.8 0.7 slice_bitcast_fusion
  158.1 0.8 copy-done.18
  (102 shorter events, 11.4 us)
Async XLA Ops:
  7.2 45.2 %copy-start.1 = (bf16[512,1024]{1,0:T(8,128)(2,1)S(1)}, bf16[512,1024]{1,0:T(8,128)(2,1)}, u32[]{:S(2)}) copy-start(bf16[512,1024]{1,0:T(8,128)(2,1)} %own.1) | copy-start | bytes 3145732
  7.2 0.8 copy-start.19
  12.0 56.2 %copy-start = (bf16[2,2048,1,256]{3,1,2,0:T(8,128)(2,1)S(1)}, bf16[2,2048,1,256]{3,1,2,0:T(8,128)(2,1)}, u32[]{:S(2)}) copy-start(bf16[2,2048,1,256]{3,1,2,0:T(8,128)(2,1)} %param.16) | copy-start | bytes 6291460
  12.0 22.0 %all-to-all-start = ((bf16[32,24,128]{2,1,0:T(8,128)(2,1)}), bf16[32,24,128]{2,1,0:T(8,128)(2,1)S(1)}, u32[]{:S(2)}, u32[]{:S(2)}) async-start(bf16[32,24,128]{2,1,0:T(8,128)(2,1)} %shard_map.156), calls=%async_computation | async-start | bytes 393216 | tf_op jit(solution)/shard_map/all_to_all | solution.py:64
  23.8 115.8 %all-gather.2.cloned.1.call-start = ((), (), s32[]{:S(2)}) async-start(), calls=%async_computation.5 | async-start | bytes 8519680 | tf_op jit(solution)/shard_map/all_gather | solution.py:473
  23.9 8.8 %collective-permute-start.13 = (bf16[64,1024]{1,0:T(8,128)(2,1)}, bf16[64,1024]{1,0:T(8,128)(2,1)S(1)}, u32[]{:S(2)}, u32[]{:S(2)}) collective-permute-start(bf16[64,1024]{1,0:T(8,128)(2,1)} %bitcast.34), channel_id=1, source_target_pairs={{0,0},{1,64},{2,128},{3,192},{64,1},{65,65},{66,129},{67,193},{128... | collective-permute-start | bytes 393224 | tf_op jit(solution)/shard_map/ppermute | solution.py:468
  32.7 1.3 copy-start.35
  34.0 5.3 %collective-permute-start.1 = (bf16[32,24,128]{2,1,0:T(8,128)(2,1)S(1)}, bf16[32,24,128]{2,1,0:T(8,128)(2,1)S(1)}, u32[]{:S(2)}, u32[]{:S(2)}) collective-permute-start(bf16[32,24,128]{2,1,0:T(8,128)(2,1)S(1)} %all-to-all-done.arrived.own), channel_id=1, source_target_pairs={{0,4},{4,0},{1,5},{5,1},{2,6},{6,2},{3,7},{7,3},{8,12},{12,8},{9,1... | collective-permute-start | bytes 589832 | tf_op jit(solution)/shard_map/ppermute | solution.py:52
  34.1 1.9 %collective-permute-start = (bf16[64,1280]{1,0:T(8,128)(2,1)}, bf16[64,1280]{1,0:T(8,128)(2,1)S(1)}, u32[]{:S(2)}, u32[]{:S(2)}) collective-permute-start(bf16[64,1280]{1,0:T(8,128)(2,1)} %bitcast.32), channel_id=1, source_target_pairs={{0,4},{4,0},{1,5},{5,1},{2,6},{6,2},{3,7},{7,3},{8,12},{12,8},{9,1... | collective-permute-start | bytes 491528 | tf_op jit(solution)/shard_map/ppermute | solution.py:52
  35.9 0.9 copy-start.12
  37.2 0.8 copy-start.7
  39.3 28.9 %all-to-all-start.1 = ((f32[32,24,128]{2,1,0:T(8,128)}), f32[32,24,128]{2,1,0:T(8,128)}, u32[]{:S(2)}, u32[]{:S(2)}) async-start(f32[32,24,128]{2,1,0:T(8,128)} %bitcast.31), calls=%async_computation.1 | async-start | bytes 786432 | tf_op jit(solution)/shard_map/all_to_all | solution.py:64
  52.4 49.4 %collective-permute-start.2 = (bf16[512,1024]{1,0:T(8,128)(2,1)S(1)}, bf16[512,1024]{1,0:T(8,128)(2,1)}, u32[]{:S(2)}, u32[]{:S(2)}) collective-permute-start(bf16[512,1024]{1,0:T(8,128)(2,1)S(1)} %copy-done.1), channel_id=1, source_target_pairs={{0,1},{1,2},{2,3},{3,0},{4,5},{5,6},{6,7},{7,4},{8,9},{9,10},{10,1... | collective-permute-start | bytes 3145736 | tf_op jit(solution)/shard_map/ppermute | solution.py:56
  52.5 49.3 %collective-permute-start.3 = (bf16[512,1024]{1,0:T(8,128)(2,1)S(1)}, bf16[512,1024]{1,0:T(8,128)(2,1)}, u32[]{:S(2)}, u32[]{:S(2)}) collective-permute-start(bf16[512,1024]{1,0:T(8,128)(2,1)S(1)} %copy-done.1), channel_id=1, source_target_pairs={{0,3},{1,0},{2,1},{3,2},{4,7},{5,4},{6,5},{7,6},{8,11},{9,8},{10,9... | collective-permute-start | bytes 3145736 | tf_op jit(solution)/shard_map/ppermute | solution.py:56
  55.7 8.6 %collective-permute-start.7 = (bf16[64,1024]{1,0:T(8,128)(2,1)}, bf16[64,1024]{1,0:T(8,128)(2,1)S(1)}, u32[]{:S(2)}, u32[]{:S(2)}) collective-permute-start(bf16[64,1024]{1,0:T(8,128)(2,1)} %bitcast.35), channel_id=1, source_target_pairs={{0,4},{4,0},{1,5},{5,1},{2,6},{6,2},{3,7},{7,3},{8,12},{12,8},{9,1... | collective-permute-start | bytes 393224 | tf_op jit(solution)/shard_map/ppermute | solution.py:52
  55.7 1.2 copy-start.2
  61.2 1.0 copy-start.3
  62.8 26.3 %copy-start.13 = (bf16[1,1024,64]{1,2,0:T(8,128)(2,1)S(1)}, bf16[1,1024,64]{1,2,0:T(8,128)(2,1)}, u32[]{:S(2)}) copy-start(bf16[1,1024,64]{1,2,0:T(8,128)(2,1)} %param.18) | copy-start | bytes 393220
  62.8 26.3 %copy-start.6 = (bf16[32,32,128]{2,1,0:T(8,128)(2,1)S(1)}, bf16[32,32,128]{2,1,0:T(8,128)(2,1)}, u32[]{:S(2)}) copy-start(bf16[32,32,128]{2,1,0:T(8,128)(2,1)} %copy-done.5) | copy-start | bytes 786436
  62.8 29.7 %collective-permute-start.4 = (f32[640,128]{1,0:T(8,128)}, f32[640,128]{1,0:T(8,128)}, u32[]{:S(2)}, u32[]{:S(2)}) collective-permute-start(f32[640,128]{1,0:T(8,128)} %get-tuple-element.39.p0), channel_id=1, source_target_pairs={{0,1},{1,2},{2,3},{3,0},{4,5},{5,6},{6,7},{7,4},{8,9},{9,10},{10,1... | collective-permute-start | bytes 983048 | tf_op jit(solution)/shard_map/ppermute | solution.py:56
  62.8 29.7 %collective-permute-start.5 = (f32[640,128]{1,0:T(8,128)}, f32[640,128]{1,0:T(8,128)}, u32[]{:S(2)}, u32[]{:S(2)}) collective-permute-start(f32[640,128]{1,0:T(8,128)} %get-tuple-element.39.p0), channel_id=1, source_target_pairs={{0,2},{1,3},{2,0},{3,1},{4,6},{5,7},{6,4},{7,5},{8,10},{9,11},{10,... | collective-permute-start | bytes 983048 | tf_op jit(solution)/shard_map/ppermute | solution.py:56
  65.0 29.6 %collective-permute-start.6 = (f32[640,128]{1,0:T(8,128)}, f32[640,128]{1,0:T(8,128)}, u32[]{:S(2)}, u32[]{:S(2)}) collective-permute-start(f32[640,128]{1,0:T(8,128)} %get-tuple-element.39.p0), channel_id=1, source_target_pairs={{0,3},{1,0},{2,1},{3,2},{4,7},{5,4},{6,5},{7,6},{8,11},{9,8},{10,9... | collective-permute-start | bytes 983048 | tf_op jit(solution)/shard_map/ppermute | solution.py:56
  68.2 21.0 %copy-start.15 = (bf16[64,1024]{1,0:T(8,128)(2,1)S(1)}, bf16[64,1024]{1,0:T(8,128)(2,1)}, u32[]{:S(2)}) copy-start(bf16[64,1024]{1,0:T(8,128)(2,1)} %copy-done.14) | copy-start | bytes 393220
  68.2 26.6 %copy-start.4 = (bf16[512,1024]{1,0:T(8,128)(2,1)S(1)}, bf16[512,1024]{1,0:T(8,128)(2,1)}, u32[]{:S(2)}) copy-start(bf16[512,1024]{1,0:T(8,128)(2,1)} %copy-done.3) | copy-start | bytes 3145732
  68.2 26.6 %copy-start.17 = (f32[64,128]{1,0:T(8,128)S(1)}, f32[64,128]{1,0:T(8,128)}, u32[]{:S(2)}) copy-start(f32[64,128]{1,0:T(8,128)} %copy-done.16) | copy-start | bytes 98308
  89.1 11.2 %copy-start.9 = (bf16[128,1280]{1,0:T(8,128)(2,1)S(1)}, bf16[128,1280]{1,0:T(8,128)(2,1)}, u32[]{:S(2)}) copy-start(bf16[128,1280]{1,0:T(8,128)(2,1)} %copy-done.8) | copy-start | bytes 983044
  92.6 4.4 %collective-permute-start.10 = (f32[64,256]{1,0:T(8,128)S(1)}, f32[64,256]{1,0:T(8,128)S(1)}, u32[]{:S(2)}, u32[]{:S(2)}) collective-permute-start(f32[64,256]{1,0:T(8,128)S(1)} %shard_map.160.s0), channel_id=1, source_target_pairs={{0,3},{1,0},{2,1},{3,2},{4,7},{5,4},{6,5},{7,6},{8,11},{9,8},{10,9... | collective-permute-start | bytes 196616 | tf_op jit(solution)/shard_map/ppermute | solution.py:56
  92.6 5.5 %collective-permute-start.8 = (f32[64,256]{1,0:T(8,128)S(1)}, f32[64,256]{1,0:T(8,128)S(1)}, u32[]{:S(2)}, u32[]{:S(2)}) collective-permute-start(f32[64,256]{1,0:T(8,128)S(1)} %shard_map.160.s0), channel_id=1, source_target_pairs={{0,1},{1,2},{2,3},{3,0},{4,5},{5,6},{6,7},{7,4},{8,9},{9,10},{10,1... | collective-permute-start | bytes 196616 | tf_op jit(solution)/shard_map/ppermute | solution.py:56
  94.6 5.8 %collective-permute-start.9 = (f32[64,256]{1,0:T(8,128)S(1)}, f32[64,256]{1,0:T(8,128)S(1)}, u32[]{:S(2)}, u32[]{:S(2)}) collective-permute-start(f32[64,256]{1,0:T(8,128)S(1)} %shard_map.160.s0), channel_id=1, source_target_pairs={{0,2},{1,3},{2,0},{3,1},{4,6},{5,7},{6,4},{7,5},{8,10},{9,11},{10,... | collective-permute-start | bytes 196616 | tf_op jit(solution)/shard_map/ppermute | solution.py:56
  97.0 4.8 %copy-start.10 = (f32[32,16,128]{2,1,0:T(8,128)}, f32[32,16,128]{2,1,0:T(8,128)S(1)}, u32[]{:S(2)}) copy-start(f32[32,16,128]{2,1,0:T(8,128)S(1)} %get-tuple-element.57) | copy-start | bytes 786436
  97.0 4.8 %copy-start.31 = (f32[32,16,128]{2,1,0:T(8,128)}, f32[32,16,128]{2,1,0:T(8,128)S(1)}, u32[]{:S(2)}) copy-start(f32[32,16,128]{2,1,0:T(8,128)S(1)} %get-tuple-element.58) | copy-start | bytes 786436
  97.0 4.8 %copy-start.33 = (bf16[512,128]{1,0:T(8,128)(2,1)}, bf16[512,128]{1,0:T(8,128)(2,1)S(1)}, u32[]{:S(2)}) copy-start(bf16[512,128]{1,0:T(8,128)(2,1)S(1)} %get-tuple-element.53.low) | copy-start | bytes 393220
  101.8 22.2 %copy-start.23 = (f32[8,128]{1,0:T(8,128)S(1)}, f32[8,128]{1,0:T(8,128)}, u32[]{:S(2)}) copy-start(f32[8,128]{1,0:T(8,128)} %copy-done.22) | copy-start | bytes 12292
  101.8 22.2 %copy-start.29 = (s32[2]{0:T(128)S(1)}, s32[2]{0:T(128)}, u32[]{:S(2)}) copy-start(s32[2]{0:T(128)} %refs_0_.3) | copy-start | bytes 28
  101.8 18.6 %copy-start.11 = (f32[32,16,128]{2,1,0:T(8,128)S(1)}, f32[32,16,128]{2,1,0:T(8,128)}, u32[]{:S(2)}) copy-start(f32[32,16,128]{2,1,0:T(8,128)} %copy-done.10) | copy-start | bytes 786436
  101.8 16.9 %copy-start.32 = (f32[32,16,128]{2,1,0:T(8,128)S(1)}, f32[32,16,128]{2,1,0:T(8,128)}, u32[]{:S(2)}) copy-start(f32[32,16,128]{2,1,0:T(8,128)} %copy-done.31) | copy-start | bytes 786436
  101.8 22.1 %all-to-all-start.3 = ((f32[32,24,128]{2,1,0:T(8,128)}), f32[32,24,128]{2,1,0:T(8,128)S(1)}, u32[]{:S(2)}, u32[]{:S(2)}) async-start(f32[32,24,128]{2,1,0:T(8,128)} %bitcast.13), calls=%async_computation.3 | async-start | bytes 786432 | tf_op jit(solution)/shard_map/all_to_all | solution.py:64
  113.7 25.9 %collective-permute-start.11 = (bf16[256,1024]{1,0:T(8,128)(2,1)}, bf16[256,1024]{1,0:T(8,128)(2,1)}, u32[]{:S(2)}, u32[]{:S(2)}) collective-permute-start(bf16[256,1024]{1,0:T(8,128)(2,1)} %slice.12), channel_id=1, source_target_pairs={{0,1},{1,2},{2,3},{3,0},{4,5},{5,6},{6,7},{7,4},{8,9},{9,10},{10,1... | collective-permute-start | bytes 1572872 | tf_op jit(solution)/shard_map/ppermute | solution.py:56
  115.8 23.8 %collective-permute-start.12 = (bf16[256,1024]{1,0:T(8,128)(2,1)}, bf16[256,1024]{1,0:T(8,128)(2,1)}, u32[]{:S(2)}, u32[]{:S(2)}) collective-permute-start(bf16[256,1024]{1,0:T(8,128)(2,1)} %slice.13), channel_id=1, source_target_pairs={{0,3},{1,0},{2,1},{3,2},{4,7},{5,4},{6,5},{7,6},{8,11},{9,8},{10,9... | collective-permute-start | bytes 1572872 | tf_op jit(solution)/shard_map/ppermute | solution.py:56
  118.8 1.7 %collective-permute-start.14 = (f32[32,16,128]{2,1,0:T(8,128)S(1)}, f32[32,16,128]{2,1,0:T(8,128)}, u32[]{:S(2)}, u32[]{:S(2)}) collective-permute-start(f32[32,16,128]{2,1,0:T(8,128)S(1)} %copy-done.32), channel_id=1, source_target_pairs={{0,4},{4,0},{1,5},{5,1},{2,6},{6,2},{3,7},{7,3},{8,12},{12,8},{9,1... | collective-permute-start | bytes 786440 | tf_op jit(solution)/shard_map/ppermute | solution.py:52
  125.9 13.8 %copy-start.34 = (f32[24,128]{1,0:T(8,128)}, f32[24,128]{1,0:T(8,128)S(1)}, u32[]{:S(2)}) copy-start(f32[24,128]{1,0:T(8,128)S(1)} %get-tuple-element.59.s0) | copy-start | bytes 36868
  125.9 13.7 %collective-permute-start.15 = (f32[24,128]{1,0:T(8,128)S(1)}, f32[24,128]{1,0:T(8,128)S(1)}, u32[]{:S(2)}, u32[]{:S(2)}) collective-permute-start(f32[24,128]{1,0:T(8,128)S(1)} %get-tuple-element.59.s0), channel_id=1, source_target_pairs={{0,1},{1,2},{2,3},{3,0},{4,5},{5,6},{6,7},{7,4},{8,9},{9,10},{10,1... | collective-permute-start | bytes 36872 | tf_op jit(solution)/shard_map/ppermute | solution.py:56
  127.5 12.1 %collective-permute-start.16 = (f32[24,128]{1,0:T(8,128)S(1)}, f32[24,128]{1,0:T(8,128)S(1)}, u32[]{:S(2)}, u32[]{:S(2)}) collective-permute-start(f32[24,128]{1,0:T(8,128)S(1)} %get-tuple-element.59.s0), channel_id=1, source_target_pairs={{0,2},{1,3},{2,0},{3,1},{4,6},{5,7},{6,4},{7,5},{8,10},{9,11},{10,... | collective-permute-start | bytes 36872 | tf_op jit(solution)/shard_map/ppermute | solution.py:56
  130.2 9.4 %collective-permute-start.17 = (f32[24,128]{1,0:T(8,128)S(1)}, f32[24,128]{1,0:T(8,128)S(1)}, u32[]{:S(2)}, u32[]{:S(2)}) collective-permute-start(f32[24,128]{1,0:T(8,128)S(1)} %get-tuple-element.59.s0), channel_id=1, source_target_pairs={{0,3},{1,0},{2,1},{3,2},{4,7},{5,4},{6,5},{7,6},{8,11},{9,8},{10,9... | collective-permute-start | bytes 36872 | tf_op jit(solution)/shard_map/ppermute | solution.py:56
  131.3 24.4 %all-to-all-start.4 = ((f32[32,16,128]{2,1,0:T(8,128)}), f32[32,16,128]{2,1,0:T(8,128)S(1)}, u32[]{:S(2)}, u32[]{:S(2)}) async-start(f32[32,16,128]{2,1,0:T(8,128)} %add.7), calls=%async_computation.4 | async-start | bytes 524288 | tf_op jit(solution)/shard_map/all_to_all | solution.py:64
  151.3 5.4 %collective-permute-start.18 = (f32[8,1024]{1,0:T(8,128)}, f32[8,1024]{1,0:T(8,128)S(1)}, u32[]{:S(2)}, u32[]{:S(2)}) collective-permute-start(f32[8,1024]{1,0:T(8,128)} %get-tuple-element.61.c0), channel_id=1, source_target_pairs={{0,1},{1,2},{2,3},{3,0},{4,5},{5,6},{6,7},{7,4},{8,9},{9,10},{10,1... | collective-permute-start | bytes 98312 | tf_op jit(solution)/shard_map/ppermute | solution.py:56
  152.5 5.6 %collective-permute-start.19 = (f32[8,1024]{1,0:T(8,128)}, f32[8,1024]{1,0:T(8,128)S(1)}, u32[]{:S(2)}, u32[]{:S(2)}) collective-permute-start(f32[8,1024]{1,0:T(8,128)} %get-tuple-element.61.c0), channel_id=1, source_target_pairs={{0,2},{1,3},{2,0},{3,1},{4,6},{5,7},{6,4},{7,5},{8,10},{9,11},{10,... | collective-permute-start | bytes 98312 | tf_op jit(solution)/shard_map/ppermute | solution.py:56
  153.2 5.0 %collective-permute-start.20 = (f32[8,1024]{1,0:T(8,128)}, f32[8,1024]{1,0:T(8,128)S(1)}, u32[]{:S(2)}, u32[]{:S(2)}) collective-permute-start(f32[8,1024]{1,0:T(8,128)} %get-tuple-element.61.c0), channel_id=1, source_target_pairs={{0,3},{1,0},{2,1},{3,2},{4,7},{5,4},{6,5},{7,6},{8,11},{9,8},{10,9... | collective-permute-start | bytes 98312 | tf_op jit(solution)/shard_map/ppermute | solution.py:56
  (17 other events, 11.3 us)
Sparse Core Ops, SparseCore 0:
  34.1 89.0 all-gather.1

commit v8 on v7

--- a/solution.py
+++ b/solution.py
@@ -96,7 +96,13 @@
     return jax.ShapeDtypeStruct(dims, dtype)
 
 
-def message_kernel(rewards, prompts, a_ref, b_ref, hidden, out):
+def message_kernel(rewards, prompts, a_far, b_far, hidden_far, out_far, a_ref, b_ref, hidden, out, sem):
+    pairs = ((a_far, a_ref), (b_far, b_ref), (hidden_far, hidden))
+    copies = [pltpu.make_async_copy(p, q, sem.at[i]) for i, (p, q) in enumerate(pairs)]
+    for copy in copies:
+        copy.start()
+    for copy in copies:
+        copy.wait()
     pieces = jnp.concatenate([a_ref[...], b_ref[...]], axis=1)
     out[:, :PIECE, :] = jnp.broadcast_to(pieces, (CHIP_COUNT, PIECE, LANES))
     lane = lane_iota((1, LANES))
@@ -109,6 +115,26 @@
     for m in range(CHIP_COUNT):
         cut = hidden[:, m * LANES : (m + 1) * LANES].astype(f32)
         out[m, PIECE:, :] = jnp.concatenate([cut, tail], axis=0).astype(bf16)
+    copy = pltpu.make_async_copy(out, out_far, sem.at[len(pairs)])
+    copy.start()
+    copy.wait()
+
+
+def first_message(rewards, prompts, a, b, hidden):
+    out = shape(CHIP_COUNT, FIRST_ROWS, LANES, dtype=bf16)
+    smem = pl.BlockSpec(memory_space=SMEM)
+    hbm = pl.BlockSpec(memory_space=pltpu.HBM)
+    return pl.pallas_call(
+        message_kernel,
+        out_shape=out,
+        in_specs=[smem, smem, hbm, hbm, hbm],
+        out_specs=hbm,
+        scratch_shapes=[
+            *(pltpu.VMEM(v.shape, v.dtype) for v in (a, b, hidden, out)),
+            pltpu.SemaphoreType.DMA((4,)),
+        ],
+        compiler_params=pltpu.CompilerParams(vmem_limit_bytes=GRANT << 20),
+    )(rewards, prompts, a, b, hidden)
 
 
 def spread_qkv(state, gain, w, out):
@@ -145,17 +171,22 @@
     return gain[:, pl.ds(start, LANES)].astype(f32)
 
 
-def qkv_first_kernel(arrived, gain, w_own, w_other, out, state_out, w_out, held):
+def state_of(arrived, held):
     held[...] = arrived[...].astype(f32).reshape(CHIP_COUNT * FIRST_ROWS, LANES)
-    state = jnp.concatenate(
+    return jnp.concatenate(
         [held[pl.ds(PIECE + b, CHIP_COUNT, stride=FIRST_ROWS), :] for b in range(ROLLS)], axis=0
     )
-    state_out[...] = state
+
+
+def in_core_order(own, other):
     first = first_core()
-    rows = w_own.shape[0]
-    w_out[:rows, :] = jnp.where(first, w_own[...], w_other[...])
-    w_out[rows:, :] = jnp.where(first, w_other[...], w_own[...])
-    spread_qkv(state, gain_of(gain), w_out[...], out)
+    even = jnp.where(first, own[...], other[...])
+    odd = jnp.where(first, other[...], own[...])
+    return jnp.concatenate([even, odd], axis=0)
+
+
+def qkv_first_kernel(arrived, gain, w_own, w_other, out, held):
+    spread_qkv(state_of(arrived, held), gain_of(gain), in_core_order(w_own, w_other), out)
 
 
 def qkv_later_kernel(held, gain, w, s0, s1, s2, s3, out):
@@ -264,8 +295,24 @@
 
 
 def adapter_kernel(
-    rewards, prompts, live, own, other, rows, upstream, weighted_out, ab_out, part
+    rewards,
+    prompts,
+    live,
+    own,
+    other,
+    rows,
+    upstream,
+    w_own,
+    w_other,
+    weighted_out,
+    ab_out,
+    part,
+    state_out,
+    w_out,
+    held,
 ):
+    state_out[...] = state_of(own, held)
+    w_out[...] = in_core_order(w_own, w_other)
     first = first_core()
     even = jnp.where(first, own[...], other[...])
     odd = jnp.where(first, other[...], own[...])
@@ -446,17 +493,12 @@
     cache = key_value_cache[:, :, 0, :]
     where = lax.rem(t - jnp.arange(nt, dtype=jnp.int32) + nt, nt)
 
-    message = call(
-        message_kernel,
-        shape(CHIP_COUNT, FIRST_ROWS, LANES, dtype=bf16),
-        [SMEM, SMEM, VMEM, VMEM, VMEM],
-        (
-            rewards,
-            prompt_group_index,
-            adapter_down_transposed[:, 0, :].T,
-            adapter_up_matrix[:, 0, :].T,
-            hidden,
-        ),
+    message = first_message(
+        rewards,
+        prompt_group_index,
+        adapter_down_transposed[:, 0, :].T,
+        adapter_up_matrix[:, 0, :].T,
+        hidden,
     )
 
     w_rows = query_key_value_weight[:, 0, :]
@@ -469,17 +511,14 @@
         w_cols, ("y", "t"), [(a * nt + b, b * nt + a) for a in range(ny) for b in range(nt)]
     )
     arrived = exchange(message, CHIPS)
+    turned, gain, w_rows_other = together(turned, attention_norm_gain[None, :], w_rows_other)
     turned, _ = together(turned, arrived)
     w_block = lax.all_gather(turned, DP, axis=0, tiled=True)
     w_block = w_block.reshape(nt, shard_width, w_cols.shape[1])
-    gain = attention_norm_gain[None, :]
-    sent, state, w_both = call(
+    arrived, gain, w_rows_other = together(arrived, gain, w_rows_other)
+    sent = call(
         qkv_first_kernel,
-        (
-            shape(CHIP_COUNT * QKV_ROWS, LANES),
-            shape(ROLLS * CHIP_COUNT, LANES),
-            shape(2 * w_rows.shape[0], w_rows.shape[1], dtype=bf16),
-        ),
+        shape(CHIP_COUNT * QKV_ROWS, LANES),
         [VMEM] * 4,
         (arrived, gain, w_rows, w_rows_other),
         scratch=[pltpu.VMEM((CHIP_COUNT * FIRST_ROWS, LANES), f32)],
@@ -494,14 +533,16 @@
     right = shift(own_rows, nt - 1, nt)
     rows = attention_rows.shape[0]
     half = rows // 2
-    weighted, ab, part = call(
+    weighted, ab, part, state, w_both = call(
         adapter_kernel,
         (
             shape(rows, shard_width, dtype=bf16),
             shape(CHIP_COUNT, 2 * PIECE, LANES, dtype=bf16),
             shape(rows + LANES, LANES),
+            shape(ROLLS * CHIP_COUNT, LANES),
+            shape(2 * w_rows.shape[0], w_rows.shape[1], dtype=bf16),
         ),
-        [SMEM] * 3 + [VMEM] * 4,
+        [SMEM] * 3 + [VMEM] * 6,
         (
             rewards,
             prompt_group_index,
@@ -510,7 +551,10 @@
             arrived_other,
             attention_rows,
             upstream,
+            w_rows,
+            w_rows_other,
         ),
+        scratch=[pltpu.VMEM((CHIP_COUNT * FIRST_ROWS, LANES), f32)],
         flops=4 * rows * shard_width * LANES,
     )
     ab = ab.reshape(shard_width, LANES)

time: 168 us -> 166 us (0.988)
  waiting for transfers between devices: 20.9 us -> 17 us
    ppermute x16, waiting for transfers between devices: 8.27 us -> 3.75 us  [shift(): return lax.ppermute(x, 't', [(i, (i + by) % n) for i in range(n)])]
    pallas_call x0 -> x1, Pallas kernels: none -> 2.35 us  [first_message(): pl.pallas_call(message_kernel, out_shape=out, in_specs=[smem, smem, hbm,...]
    ppermute x16, starting transfers between devices: 21.7 us -> 23.9 us  [shift(): return lax.ppermute(x, 't', [(i, (i + by) % n) for i in range(n)])]
    pallas_call x9 -> x8, Pallas kernels: 12.5 us -> 11.3 us  [call(): pl.pallas_call(kernel, out_shape=out, in_specs=[pl.BlockSpec(memory_space...]
    unnamed x78 -> x72, local copies, waits for them, and re-layouts: 14.8 us -> 14.9 us
  transfers between devices with their start and end apart: 26 -> 26, of which waited for: 11 -> 7; matrix products, arithmetic and copies ran while one was open for 5% -> 4% of each run, Pallas kernels for 13% -> 13%
where the time goes in v8:
time: 166 us; the launch traced here: 165 us
  starting transfers between devices  67.9 us (41%)
  Pallas kernels  24.7 us (15%)
  local copies, waits for them, and re-layouts  20.7 us (12%)
  blocking collectives  18.8 us (11%)
  waiting for transfers between devices  17 us (10%)
  between operations  14.4 us (9%)
    all_to_all x4, starting transfers between devices, exchange(): return lax.all_to_all(x, axes, split_axis=0, concat_axis=0, tiled=True)  40.8 us
    ppermute x16, starting transfers between devices, shift(): return lax.ppermute(x, 't', [(i, (i + by) % n) for i in range(n)])  23.9 us
    all_to_all x1, blocking collectives, exchange(): return lax.all_to_all(x, axes, split_axis=0, concat_axis=0, tiled=True)  18.8 us
    unnamed x72, local copies, waits for them, and re-layouts  14.9 us
    pallas_call x8, Pallas kernels, call(): pl.pallas_call(kernel, out_shape=out, in_specs=[pl.BlockSpec(memory_space...  11.3 us
    pallas_call x1, Pallas kernels, output_rows(): pl.pallas_call(rows_kernel, out_shape=(shape(rows, width), shape(8, width...  11.1 us
    all_to_all x4, waiting for transfers between devices, exchange(): return lax.all_to_all(x, axes, split_axis=0, concat_axis=0, tiled=True)  6.07 us
    ppermute x1, waiting for transfers between devices, shards(): lax.ppermute(w_cols, ('y', 't'), [(a * nt + b, b * nt + a) for a in range...  5.57 us
  transfers between devices with their start and end apart: 26, of which 7 were waited for; matrix products, arithmetic and copies ran while one was open for 4% of the time, Pallas kernels for 13%

profile of v8, /device:TPU:8, one launch (start us, length us, event | category | flops | bytes accessed | tf_op | source)
XLA Modules:
  0.0 164.7 jit_solution(8159351668107341718)
XLA Ops:
  7.2 2.4 %shard_map.156 = bf16[32,24,128]{2,1,0:T(8,128)(2,1)} custom-call(f32[2]{0:T(128)} %rewards.3, s32[2]{0:T(128)} %prompts.3, bf16[16,64]{1,0:T(8,128)(2,1)} %bitcast.38, bf16[16,64]{1,0:T(8,128)(2,1)} %bitcast.39, bf16[2,4096]{1,0:T(2,128)(2,1)} %hidden_far.1), custom_call_target="tpu_custom_call" | custom-call | tf_op jit(solution)/shard_map/pallas_call | solution.py:127
  9.5 11.7 %all-to-all-start = ((bf16[32,24,128]{2,1,0:T(8,128)(2,1)}), bf16[32,24,128]{2,1,0:T(8,128)(2,1)S(1)}, u32[]{:S(2)}, u32[]{:S(2)}) async-start(bf16[32,24,128]{2,1,0:T(8,128)(2,1)} %shard_map.156), calls=%async_computation | async-start | bytes 393216 | tf_op jit(solution)/shard_map/all_to_all | solution.py:64
  21.4 3.1 %collective-permute-start = (bf16[64,1024]{1,0:T(8,128)(2,1)}, bf16[64,1024]{1,0:T(8,128)(2,1)S(1)}, u32[]{:S(2)}, u32[]{:S(2)}) collective-permute-start(bf16[64,1024]{1,0:T(8,128)(2,1)} %bitcast.35), channel_id=1, source_target_pairs={{0,0},{1,64},{2,128},{3,192},{64,1},{65,65},{66,129},{67,193},{128... | collective-permute-start | bytes 393224 | tf_op jit(solution)/shard_map/ppermute | solution.py:510
  24.5 0.7 broadcast_in_dim.9.gain
  25.2 5.6 %collective-permute-done = bf16[64,1024]{1,0:T(8,128)(2,1)S(1)} collective-permute-done((bf16[64,1024]{1,0:T(8,128)(2,1)}, bf16[64,1024]{1,0:T(8,128)(2,1)S(1)}, u32[]{:S(2)}, u32[]{:S(2)}) %collective-permute-start) | collective-permute-done | bytes 131104 | tf_op jit(solution)/shard_map/ppermute | solution.py:510
  31.6 1.0 copy-done.9
  32.9 0.7 copy-done.2
  33.7 0.7 copy-done.15
  34.3 14.4 %all-to-all-start.1 = ((f32[32,24,128]{2,1,0:T(8,128)}), f32[32,24,128]{2,1,0:T(8,128)}, u32[]{:S(2)}, u32[]{:S(2)}) async-start(f32[32,24,128]{2,1,0:T(8,128)} %bitcast.27), calls=%async_computation.1 | async-start | bytes 786432 | tf_op jit(solution)/shard_map/all_to_all | solution.py:64
  48.8 3.2 %collective-permute-start.4 = (bf16[512,1024]{1,0:T(8,128)(2,1)S(1)}, bf16[512,1024]{1,0:T(8,128)(2,1)}, u32[]{:S(2)}, u32[]{:S(2)}) collective-permute-start(bf16[512,1024]{1,0:T(8,128)(2,1)S(1)} %copy-done.1), channel_id=1, source_target_pairs={{0,3},{1,0},{2,1},{3,2},{4,7},{5,4},{6,5},{7,6},{8,11},{9,8},{10,9... | collective-permute-start | bytes 3145736 | tf_op jit(solution)/shard_map/ppermute | solution.py:56
  52.0 1.2 copy-done.3
  53.3 0.9 copy-done.10
  54.2 0.9 copy-done.16
  55.1 0.7 copy-done.25
  55.8 0.7 copy-done.26
  56.4 0.7 copy-done.29
  57.1 2.3 %shard_map.158 = (bf16[512,1024]{1,0:T(8,128)(2,1)S(1)}, bf16[32,32,128]{2,1,0:T(8,128)(2,1)S(1)}, f32[640,128]{1,0:T(8,128)}, f32[64,128]{1,0:T(8,128)S(1)}, bf16[128,1280]{1,0:T(8,128)(2,1)S(1)}) custom-call(f32[2]{0:T(128)S(1)} %copy-done.25, s32[2]{0:T(128)S(1)} %copy-done.26, s32[2]{0:T(128)S(1)} %copy-done.29, ...), custom_call_target="tpu_custom_call" | custom-call | flops 268435456 | bytes 4816920 | tf_op jit(solution)/shard_map/pallas_call | solution.py:84
  59.4 1.0 copy-done.4
  60.4 0.7 copy-done.6
  61.1 0.7 copy-done.11
  62.4 1.5 collective-permute-start.6
  64.5 1.8 %collective-permute-start.7 = (f32[640,128]{1,0:T(8,128)}, f32[640,128]{1,0:T(8,128)}, u32[]{:S(2)}, u32[]{:S(2)}) collective-permute-start(f32[640,128]{1,0:T(8,128)} %get-tuple-element.48.p0), channel_id=1, source_target_pairs={{0,3},{1,0},{2,1},{3,2},{4,7},{5,4},{6,5},{7,6},{8,11},{9,8},{10,9... | collective-permute-start | bytes 983048 | tf_op jit(solution)/shard_map/ppermute | solution.py:56
  66.4 0.7 copy-done.27
  67.1 2.2 %shard_map.159 = (bf16[32,16,128]{2,1,0:T(8,128)(2,1)S(1)}, f32[8,128]{1,0:T(8,128)S(1)}) custom-call(s32[2]{0:T(128)S(1)} %copy-done.27, f32[768,128]{1,0:T(8,128)} %bitcast.8.refs_1_, bf16[2,2048,256]{2,1,0:T(8,128)(2,1)S(1)} %bitcast.25), custom_call_target="tpu_custom_call" | custom-call | flops 67108864 | bytes 2625544 | tf_op jit(solution)/shard_map/pallas_call | solution.py:84
  69.9 18.8 %all_to_all.25.came = bf16[32,16,128]{2,1,0:T(8,128)(2,1)S(1)} all-to-all(bf16[32,16,128]{2,1,0:T(8,128)(2,1)S(1)} %get-tuple-element.50), channel_id=1, replica_groups=mesh['y'=4,'z'=8,'c'=2,'t'=4] {'y','z'}, dimensions={0} | all-to-all | bytes 262144 | tf_op jit(solution)/shard_map/all_to_all | solution.py:64
  89.0 3.0 %collective-permute-start.10 = (f32[64,256]{1,0:T(8,128)S(1)}, f32[64,256]{1,0:T(8,128)S(1)}, u32[]{:S(2)}, u32[]{:S(2)}) collective-permute-start(f32[64,256]{1,0:T(8,128)S(1)} %shard_map.160.s0), channel_id=1, source_target_pairs={{0,2},{1,3},{2,0},{3,1},{4,6},{5,7},{6,4},{7,5},{8,10},{9,11},{10,... | collective-permute-start | bytes 196616 | tf_op jit(solution)/shard_map/ppermute | solution.py:56
  92.6 1.4 collective-permute-start.9
  94.0 2.2 %shard_map.161 = (bf16[512,128]{1,0:T(8,128)(2,1)S(1)}, f32[192,128]{1,0:T(8,128)S(1)}, f32[32,16,128]{2,1,0:T(8,128)S(1)}, f32[32,16,128]{2,1,0:T(8,128)S(1)}) custom-call(f32[640,128]{1,0:T(8,128)} %get-tuple-element.48.p0, f32[640,128]{1,0:T(8,128)} %collective-permute-done.5.p1, f32[640,128]{1,0:T(8,128)} %collective-permute-done.6.p2, ...), custom_call_target="tpu_custom_call" | custom-call | flops 268435456 | bytes 4194304 | tf_op jit(solution)/shard_map/pallas_call | solution.py:84
  96.3 1.9 %collective-permute-done.9.s1 = f32[64,256]{1,0:T(8,128)S(1)} collective-permute-done((f32[64,256]{1,0:T(8,128)S(1)}, f32[64,256]{1,0:T(8,128)S(1)}, u32[]{:S(2)}, u32[]{:S(2)}) %collective-permute-start.9) | collective-permute-done | bytes 65568 | tf_op jit(solution)/shard_map/ppermute | solution.py:56
  98.1 1.5 shard_map.162
  99.6 8.0 %all-to-all-start.3 = ((f32[32,24,128]{2,1,0:T(8,128)}), f32[32,24,128]{2,1,0:T(8,128)S(1)}, u32[]{:S(2)}, u32[]{:S(2)}) async-start(f32[32,24,128]{2,1,0:T(8,128)} %bitcast.13), calls=%async_computation.3 | async-start | bytes 786432 | tf_op jit(solution)/shard_map/all_to_all | solution.py:64
  107.6 1.9 %slice.12 = bf16[256,1024]{1,0:T(8,128)(2,1)} slice(bf16[512,1024]{1,0:T(8,128)(2,1)} %collective-permute-done.3.left), slice={[0:256], [0:1024]} | slice | bytes 1048576 | tf_op jit(solution)/shard_map/slice | solution.py:598
  109.5 1.9 %slice.13 = bf16[256,1024]{1,0:T(8,128)(2,1)} slice(bf16[512,1024]{1,0:T(8,128)(2,1)} %collective-permute-done.4.right), slice={[256:512], [0:1024]} | slice | bytes 1048576 | tf_op jit(solution)/shard_map/slice | solution.py:599
  111.4 3.2 %collective-permute-start.13 = (bf16[256,1024]{1,0:T(8,128)(2,1)}, bf16[256,1024]{1,0:T(8,128)(2,1)}, u32[]{:S(2)}, u32[]{:S(2)}) collective-permute-start(bf16[256,1024]{1,0:T(8,128)(2,1)} %slice.13), channel_id=1, source_target_pairs={{0,3},{1,0},{2,1},{3,2},{4,7},{5,4},{6,5},{7,6},{8,11},{9,8},{10,9... | collective-permute-start | bytes 1572872 | tf_op jit(solution)/shard_map/ppermute | solution.py:56
  114.7 1.5 collective-permute-done.14
  116.2 0.7 add.7
  116.9 5.5 %all-to-all-done.3 = f32[32,24,128]{2,1,0:T(8,128)S(1)} async-done(((f32[32,24,128]{2,1,0:T(8,128)}), f32[32,24,128]{2,1,0:T(8,128)S(1)}, u32[]{:S(2)}, u32[]{:S(2)}) %all-to-all-start.3) | async-done | bytes 393248 | tf_op jit(solution)/shard_map/all_to_all | solution.py:64
  122.4 0.9 copy-done.8
  123.3 1.9 %shard_map.163 = (f32[24,128]{1,0:T(8,128)S(1)}, f32[64,128]{1,0:T(8,128)S(1)}) custom-call(s32[2]{0:T(128)S(1)} %copy-done.28, f32[768,128]{1,0:T(8,128)S(1)} %bitcast.28, bf16[2,2048,256]{2,1,0:T(8,128)(2,1)S(1)} %bitcast.26, f32[8,128]{1,0:T(8,128)S(1)} %copy-done.24, bf16[1024,128]{1,0:T(8,128)(2,1)S(1)} %bitcast.31), custom_call_target="tpu_custom_call" | custom-call | flops 67108864 | bytes 2801672 | tf_op jit(solution)/shard_map/pallas_call | solution.py:84
  125.5 3.2 %collective-permute-start.16 = (f32[24,128]{1,0:T(8,128)S(1)}, f32[24,128]{1,0:T(8,128)S(1)}, u32[]{:S(2)}, u32[]{:S(2)}) collective-permute-start(f32[24,128]{1,0:T(8,128)S(1)} %get-tuple-element.69.s0), channel_id=1, source_target_pairs={{0,2},{1,3},{2,0},{3,1},{4,6},{5,7},{6,4},{7,5},{8,10},{9,11},{10,... | collective-permute-start | bytes 36872 | tf_op jit(solution)/shard_map/ppermute | solution.py:56
  128.7 1.5 collective-permute-start.17
  130.2 6.7 %all-to-all-start.4 = ((f32[32,16,128]{2,1,0:T(8,128)}), f32[32,16,128]{2,1,0:T(8,128)S(1)}, u32[]{:S(2)}, u32[]{:S(2)}) async-start(f32[32,16,128]{2,1,0:T(8,128)} %add.7), calls=%async_computation.4 | async-start | bytes 524288 | tf_op jit(solution)/shard_map/all_to_all | solution.py:64
  138.7 11.1 %shard_map.164 = (f32[512,1024]{1,0:T(8,128)}, f32[8,1024]{1,0:T(8,128)}) custom-call(s32[4]{0:T(128)} %compare_select_fusion.where_ref, bf16[512,1024]{1,0:T(8,128)(2,1)} %own.1, bf16[512,1024]{1,0:T(8,128)(2,1)} %collective-permute-done.3.left, bf16[512,1024]{1,0:T(8,128)(2,1)} %collective-permute-done.4.right, ...), custom_call_target="tpu_custom_call" | custom-call | flops 4294967296 | bytes 14680064 | tf_op jit(solution)/shard_map/pallas_call | solution.py:432
  149.8 1.0 collective-permute-start.18
  151.4 2.5 %collective-permute-start.20 = (f32[8,1024]{1,0:T(8,128)}, f32[8,1024]{1,0:T(8,128)S(1)}, u32[]{:S(2)}, u32[]{:S(2)}) collective-permute-start(f32[8,1024]{1,0:T(8,128)} %get-tuple-element.71.c0), channel_id=1, source_target_pairs={{0,3},{1,0},{2,1},{3,2},{4,7},{5,4},{6,5},{7,6},{8,11},{9,8},{10,9... | collective-permute-start | bytes 98312 | tf_op jit(solution)/shard_map/ppermute | solution.py:56
  153.9 1.2 collective-permute-done.18.c1
  155.2 0.7 slice_bitcast_fusion
  156.4 0.8 copy-done.22
  (96 shorter events, 8.0 us)
Async XLA Ops:
  7.2 41.5 %copy-start.1 = (bf16[512,1024]{1,0:T(8,128)(2,1)S(1)}, bf16[512,1024]{1,0:T(8,128)(2,1)}, u32[]{:S(2)}) copy-start(bf16[512,1024]{1,0:T(8,128)(2,1)} %own.1) | copy-start | bytes 3145732
  9.5 21.8 %all-to-all-start = ((bf16[32,24,128]{2,1,0:T(8,128)(2,1)}), bf16[32,24,128]{2,1,0:T(8,128)(2,1)S(1)}, u32[]{:S(2)}, u32[]{:S(2)}) async-start(bf16[32,24,128]{2,1,0:T(8,128)(2,1)} %shard_map.156), calls=%async_computation | async-start | bytes 393216 | tf_op jit(solution)/shard_map/all_to_all | solution.py:64
  21.3 116.9 %all-gather.2.cloned.1.call-start = ((), (), s32[]{:S(2)}) async-start(), calls=%async_computation.5 | async-start | bytes 8519680 | tf_op jit(solution)/shard_map/all_gather | solution.py:516
  21.3 9.5 %collective-permute-start.1 = (bf16[64,1280]{1,0:T(8,128)(2,1)}, bf16[64,1280]{1,0:T(8,128)(2,1)S(1)}, u32[]{:S(2)}, u32[]{:S(2)}) collective-permute-start(bf16[64,1280]{1,0:T(8,128)(2,1)} %bitcast.32), channel_id=1, source_target_pairs={{0,4},{4,0},{1,5},{5,1},{2,6},{6,2},{3,7},{7,3},{8,12},{12,8},{9,1... | collective-permute-start | bytes 491528 | tf_op jit(solution)/shard_map/ppermute | solution.py:52
  21.4 9.4 %collective-permute-start = (bf16[64,1024]{1,0:T(8,128)(2,1)}, bf16[64,1024]{1,0:T(8,128)(2,1)S(1)}, u32[]{:S(2)}, u32[]{:S(2)}) collective-permute-start(bf16[64,1024]{1,0:T(8,128)(2,1)} %bitcast.35), channel_id=1, source_target_pairs={{0,0},{1,64},{2,128},{3,192},{64,1},{65,65},{66,129},{67,193},{128... | collective-permute-start | bytes 393224 | tf_op jit(solution)/shard_map/ppermute | solution.py:510
  31.5 34.9 %copy-start = (bf16[2,2048,1,256]{3,1,2,0:T(8,128)(2,1)S(1)}, bf16[2,2048,1,256]{3,1,2,0:T(8,128)(2,1)}, u32[]{:S(2)}) copy-start(bf16[2,2048,1,256]{3,1,2,0:T(8,128)(2,1)} %param.16) | copy-start | bytes 6291460
  31.5 2.2 %collective-permute-start.2 = (bf16[32,24,128]{2,1,0:T(8,128)(2,1)S(1)}, bf16[32,24,128]{2,1,0:T(8,128)(2,1)S(1)}, u32[]{:S(2)}, u32[]{:S(2)}) collective-permute-start(bf16[32,24,128]{2,1,0:T(8,128)(2,1)S(1)} %all-to-all-done.arrived.own), channel_id=1, source_target_pairs={{0,4},{4,0},{1,5},{5,1},{2,6},{6,2},{3,7},{7,3},{8,12},{12,8},{9,1... | collective-permute-start | bytes 589832 | tf_op jit(solution)/shard_map/ppermute | solution.py:52
  31.6 1.0 copy-start.9
  34.3 32.0 %all-to-all-start.1 = ((f32[32,24,128]{2,1,0:T(8,128)}), f32[32,24,128]{2,1,0:T(8,128)}, u32[]{:S(2)}, u32[]{:S(2)}) async-start(f32[32,24,128]{2,1,0:T(8,128)} %bitcast.27), calls=%async_computation.1 | async-start | bytes 786432 | tf_op jit(solution)/shard_map/all_to_all | solution.py:64
  48.7 50.9 %collective-permute-start.3 = (bf16[512,1024]{1,0:T(8,128)(2,1)S(1)}, bf16[512,1024]{1,0:T(8,128)(2,1)}, u32[]{:S(2)}, u32[]{:S(2)}) collective-permute-start(bf16[512,1024]{1,0:T(8,128)(2,1)S(1)} %copy-done.1), channel_id=1, source_target_pairs={{0,1},{1,2},{2,3},{3,0},{4,5},{5,6},{6,7},{7,4},{8,9},{9,10},{10,1... | collective-permute-start | bytes 3145736 | tf_op jit(solution)/shard_map/ppermute | solution.py:56
  48.8 50.8 %collective-permute-start.4 = (bf16[512,1024]{1,0:T(8,128)(2,1)S(1)}, bf16[512,1024]{1,0:T(8,128)(2,1)}, u32[]{:S(2)}, u32[]{:S(2)}) collective-permute-start(bf16[512,1024]{1,0:T(8,128)(2,1)S(1)} %copy-done.1), channel_id=1, source_target_pairs={{0,3},{1,0},{2,1},{3,2},{4,7},{5,4},{6,5},{7,6},{8,11},{9,8},{10,9... | collective-permute-start | bytes 3145736 | tf_op jit(solution)/shard_map/ppermute | solution.py:56
  52.0 11.9 %collective-permute-start.8 = (bf16[64,1024]{1,0:T(8,128)(2,1)}, bf16[64,1024]{1,0:T(8,128)(2,1)S(1)}, u32[]{:S(2)}, u32[]{:S(2)}) collective-permute-start(bf16[64,1024]{1,0:T(8,128)(2,1)} %bitcast.36), channel_id=1, source_target_pairs={{0,4},{4,0},{1,5},{5,1},{2,6},{6,2},{3,7},{7,3},{8,12},{12,8},{9,1... | collective-permute-start | bytes 393224 | tf_op jit(solution)/shard_map/ppermute | solution.py:52
  52.0 1.2 copy-start.3
  53.3 0.9 copy-start.10
  54.2 0.9 copy-start.16
  59.4 1.0 copy-start.4
  62.4 26.3 %copy-start.17 = (bf16[1,1024,64]{1,2,0:T(8,128)(2,1)S(1)}, bf16[1,1024,64]{1,2,0:T(8,128)(2,1)}, u32[]{:S(2)}) copy-start(bf16[1,1024,64]{1,2,0:T(8,128)(2,1)} %param.18) | copy-start | bytes 393220
  62.4 26.3 %copy-start.7 = (bf16[32,32,128]{2,1,0:T(8,128)(2,1)S(1)}, bf16[32,32,128]{2,1,0:T(8,128)(2,1)}, u32[]{:S(2)}) copy-start(bf16[32,32,128]{2,1,0:T(8,128)(2,1)} %copy-done.6) | copy-start | bytes 786436
  62.4 26.6 %collective-permute-start.5 = (f32[640,128]{1,0:T(8,128)}, f32[640,128]{1,0:T(8,128)}, u32[]{:S(2)}, u32[]{:S(2)}) collective-permute-start(f32[640,128]{1,0:T(8,128)} %get-tuple-element.48.p0), channel_id=1, source_target_pairs={{0,1},{1,2},{2,3},{3,0},{4,5},{5,6},{6,7},{7,4},{8,9},{9,10},{10,1... | collective-permute-start | bytes 983048 | tf_op jit(solution)/shard_map/ppermute | solution.py:56
  62.4 29.6 %collective-permute-start.6 = (f32[640,128]{1,0:T(8,128)}, f32[640,128]{1,0:T(8,128)}, u32[]{:S(2)}, u32[]{:S(2)}) collective-permute-start(f32[640,128]{1,0:T(8,128)} %get-tuple-element.48.p0), channel_id=1, source_target_pairs={{0,2},{1,3},{2,0},{3,1},{4,6},{5,7},{6,4},{7,5},{8,10},{9,11},{10,... | collective-permute-start | bytes 983048 | tf_op jit(solution)/shard_map/ppermute | solution.py:56
  64.5 28.1 %collective-permute-start.7 = (f32[640,128]{1,0:T(8,128)}, f32[640,128]{1,0:T(8,128)}, u32[]{:S(2)}, u32[]{:S(2)}) collective-permute-start(f32[640,128]{1,0:T(8,128)} %get-tuple-element.48.p0), channel_id=1, source_target_pairs={{0,3},{1,0},{2,1},{3,2},{4,7},{5,4},{6,5},{7,6},{8,11},{9,8},{10,9... | collective-permute-start | bytes 983048 | tf_op jit(solution)/shard_map/ppermute | solution.py:56
  66.3 22.4 %copy-start.19 = (bf16[64,1024]{1,0:T(8,128)(2,1)S(1)}, bf16[64,1024]{1,0:T(8,128)(2,1)}, u32[]{:S(2)}) copy-start(bf16[64,1024]{1,0:T(8,128)(2,1)} %copy-done.18) | copy-start | bytes 393220
  66.3 27.7 %copy-start.5 = (bf16[512,1024]{1,0:T(8,128)(2,1)S(1)}, bf16[512,1024]{1,0:T(8,128)(2,1)}, u32[]{:S(2)}) copy-start(bf16[512,1024]{1,0:T(8,128)(2,1)} %copy-done.4) | copy-start | bytes 3145732
  66.3 27.7 %copy-start.21 = (f32[64,128]{1,0:T(8,128)S(1)}, f32[64,128]{1,0:T(8,128)}, u32[]{:S(2)}) copy-start(f32[64,128]{1,0:T(8,128)} %copy-done.20) | copy-start | bytes 98308
  66.3 0.8 copy-start.27
  88.7 9.4 %copy-start.12 = (bf16[128,1280]{1,0:T(8,128)(2,1)S(1)}, bf16[128,1280]{1,0:T(8,128)(2,1)}, u32[]{:S(2)}) copy-start(bf16[128,1280]{1,0:T(8,128)(2,1)} %copy-done.11) | copy-start | bytes 983044
  89.0 7.2 %collective-permute-start.10 = (f32[64,256]{1,0:T(8,128)S(1)}, f32[64,256]{1,0:T(8,128)S(1)}, u32[]{:S(2)}, u32[]{:S(2)}) collective-permute-start(f32[64,256]{1,0:T(8,128)S(1)} %shard_map.160.s0), channel_id=1, source_target_pairs={{0,2},{1,3},{2,0},{3,1},{4,6},{5,7},{6,4},{7,5},{8,10},{9,11},{10,... | collective-permute-start | bytes 196616 | tf_op jit(solution)/shard_map/ppermute | solution.py:56
  92.0 4.3 %collective-permute-start.11 = (f32[64,256]{1,0:T(8,128)S(1)}, f32[64,256]{1,0:T(8,128)S(1)}, u32[]{:S(2)}, u32[]{:S(2)}) collective-permute-start(f32[64,256]{1,0:T(8,128)S(1)} %shard_map.160.s0), channel_id=1, source_target_pairs={{0,3},{1,0},{2,1},{3,2},{4,7},{5,4},{6,5},{7,6},{8,11},{9,8},{10,9... | collective-permute-start | bytes 196616 | tf_op jit(solution)/shard_map/ppermute | solution.py:56
  92.6 5.5 %collective-permute-start.9 = (f32[64,256]{1,0:T(8,128)S(1)}, f32[64,256]{1,0:T(8,128)S(1)}, u32[]{:S(2)}, u32[]{:S(2)}) collective-permute-start(f32[64,256]{1,0:T(8,128)S(1)} %shard_map.160.s0), channel_id=1, source_target_pairs={{0,1},{1,2},{2,3},{3,0},{4,5},{5,6},{6,7},{7,4},{8,9},{9,10},{10,1... | collective-permute-start | bytes 196616 | tf_op jit(solution)/shard_map/ppermute | solution.py:56
  96.2 3.4 %copy-start.13 = (f32[32,16,128]{2,1,0:T(8,128)}, f32[32,16,128]{2,1,0:T(8,128)S(1)}, u32[]{:S(2)}) copy-start(f32[32,16,128]{2,1,0:T(8,128)S(1)} %get-tuple-element.67) | copy-start | bytes 786436
  96.2 3.4 %copy-start.30 = (bf16[512,128]{1,0:T(8,128)(2,1)}, bf16[512,128]{1,0:T(8,128)(2,1)S(1)}, u32[]{:S(2)}) copy-start(bf16[512,128]{1,0:T(8,128)(2,1)S(1)} %get-tuple-element.63.low) | copy-start | bytes 393220
  99.6 22.8 %copy-start.24 = (f32[8,128]{1,0:T(8,128)S(1)}, f32[8,128]{1,0:T(8,128)}, u32[]{:S(2)}) copy-start(f32[8,128]{1,0:T(8,128)} %copy-done.23) | copy-start | bytes 12292
  99.6 22.8 %copy-start.28 = (s32[2]{0:T(128)S(1)}, s32[2]{0:T(128)}, u32[]{:S(2)}) copy-start(s32[2]{0:T(128)} %refs_0_.3) | copy-start | bytes 28
  99.6 16.6 %copy-start.14 = (f32[32,16,128]{2,1,0:T(8,128)S(1)}, f32[32,16,128]{2,1,0:T(8,128)}, u32[]{:S(2)}) copy-start(f32[32,16,128]{2,1,0:T(8,128)} %copy-done.13) | copy-start | bytes 786436
  99.6 22.8 %all-to-all-start.3 = ((f32[32,24,128]{2,1,0:T(8,128)}), f32[32,24,128]{2,1,0:T(8,128)S(1)}, u32[]{:S(2)}, u32[]{:S(2)}) async-start(f32[32,24,128]{2,1,0:T(8,128)} %bitcast.13), calls=%async_computation.3 | async-start | bytes 786432 | tf_op jit(solution)/shard_map/all_to_all | solution.py:64
  109.5 28.5 %collective-permute-start.12 = (bf16[256,1024]{1,0:T(8,128)(2,1)}, bf16[256,1024]{1,0:T(8,128)(2,1)}, u32[]{:S(2)}, u32[]{:S(2)}) collective-permute-start(bf16[256,1024]{1,0:T(8,128)(2,1)} %slice.12), channel_id=1, source_target_pairs={{0,1},{1,2},{2,3},{3,0},{4,5},{5,6},{6,7},{7,4},{8,9},{9,10},{10,1... | collective-permute-start | bytes 1572872 | tf_op jit(solution)/shard_map/ppermute | solution.py:56
  111.4 26.6 %collective-permute-start.13 = (bf16[256,1024]{1,0:T(8,128)(2,1)}, bf16[256,1024]{1,0:T(8,128)(2,1)}, u32[]{:S(2)}, u32[]{:S(2)}) collective-permute-start(bf16[256,1024]{1,0:T(8,128)(2,1)} %slice.13), channel_id=1, source_target_pairs={{0,3},{1,0},{2,1},{3,2},{4,7},{5,4},{6,5},{7,6},{8,11},{9,8},{10,9... | collective-permute-start | bytes 1572872 | tf_op jit(solution)/shard_map/ppermute | solution.py:56
  114.7 1.5 collective-permute-start.14
  122.4 1.0 copy-start.8
  125.3 12.9 %copy-start.31 = (f32[24,128]{1,0:T(8,128)}, f32[24,128]{1,0:T(8,128)S(1)}, u32[]{:S(2)}) copy-start(f32[24,128]{1,0:T(8,128)S(1)} %get-tuple-element.69.s0) | copy-start | bytes 36868
  125.3 12.8 %collective-permute-start.15 = (f32[24,128]{1,0:T(8,128)S(1)}, f32[24,128]{1,0:T(8,128)S(1)}, u32[]{:S(2)}, u32[]{:S(2)}) collective-permute-start(f32[24,128]{1,0:T(8,128)S(1)} %get-tuple-element.69.s0), channel_id=1, source_target_pairs={{0,1},{1,2},{2,3},{3,0},{4,5},{5,6},{6,7},{7,4},{8,9},{9,10},{10,1... | collective-permute-start | bytes 36872 | tf_op jit(solution)/shard_map/ppermute | solution.py:56
  125.5 12.6 %collective-permute-start.16 = (f32[24,128]{1,0:T(8,128)S(1)}, f32[24,128]{1,0:T(8,128)S(1)}, u32[]{:S(2)}, u32[]{:S(2)}) collective-permute-start(f32[24,128]{1,0:T(8,128)S(1)} %get-tuple-element.69.s0), channel_id=1, source_target_pairs={{0,2},{1,3},{2,0},{3,1},{4,6},{5,7},{6,4},{7,5},{8,10},{9,11},{10,... | collective-permute-start | bytes 36872 | tf_op jit(solution)/shard_map/ppermute | solution.py:56
  128.7 9.4 %collective-permute-start.17 = (f32[24,128]{1,0:T(8,128)S(1)}, f32[24,128]{1,0:T(8,128)S(1)}, u32[]{:S(2)}, u32[]{:S(2)}) collective-permute-start(f32[24,128]{1,0:T(8,128)S(1)} %get-tuple-element.69.s0), channel_id=1, source_target_pairs={{0,3},{1,0},{2,1},{3,2},{4,7},{5,4},{6,5},{7,6},{8,11},{9,8},{10,9... | collective-permute-start | bytes 36872 | tf_op jit(solution)/shard_map/ppermute | solution.py:56
  130.2 23.8 %all-to-all-start.4 = ((f32[32,16,128]{2,1,0:T(8,128)}), f32[32,16,128]{2,1,0:T(8,128)S(1)}, u32[]{:S(2)}, u32[]{:S(2)}) async-start(f32[32,16,128]{2,1,0:T(8,128)} %add.7), calls=%async_computation.4 | async-start | bytes 524288 | tf_op jit(solution)/shard_map/all_to_all | solution.py:64
  149.8 5.4 %collective-permute-start.18 = (f32[8,1024]{1,0:T(8,128)}, f32[8,1024]{1,0:T(8,128)S(1)}, u32[]{:S(2)}, u32[]{:S(2)}) collective-permute-start(f32[8,1024]{1,0:T(8,128)} %get-tuple-element.71.c0), channel_id=1, source_target_pairs={{0,1},{1,2},{2,3},{3,0},{4,5},{5,6},{6,7},{7,4},{8,9},{9,10},{10,1... | collective-permute-start | bytes 98312 | tf_op jit(solution)/shard_map/ppermute | solution.py:56
  150.8 5.6 %collective-permute-start.19 = (f32[8,1024]{1,0:T(8,128)}, f32[8,1024]{1,0:T(8,128)S(1)}, u32[]{:S(2)}, u32[]{:S(2)}) collective-permute-start(f32[8,1024]{1,0:T(8,128)} %get-tuple-element.71.c0), channel_id=1, source_target_pairs={{0,2},{1,3},{2,0},{3,1},{4,6},{5,7},{6,4},{7,5},{8,10},{9,11},{10,... | collective-permute-start | bytes 98312 | tf_op jit(solution)/shard_map/ppermute | solution.py:56
  151.4 5.1 %collective-permute-start.20 = (f32[8,1024]{1,0:T(8,128)}, f32[8,1024]{1,0:T(8,128)S(1)}, u32[]{:S(2)}, u32[]{:S(2)}) collective-permute-start(f32[8,1024]{1,0:T(8,128)} %get-tuple-element.71.c0), channel_id=1, source_target_pairs={{0,3},{1,0},{2,1},{3,2},{4,7},{5,4},{6,5},{7,6},{8,11},{9,8},{10,9... | collective-permute-start | bytes 98312 | tf_op jit(solution)/shard_map/ppermute | solution.py:56
  156.4 0.8 copy-start.22
  (14 other events, 9.1 us)
Sparse Core Ops, SparseCore 0:
  31.6 91.5 all-gather.1

commit v9 on v8

--- a/solution.py
+++ b/solution.py
@@ -96,7 +96,9 @@
     return jax.ShapeDtypeStruct(dims, dtype)
 
 
-def message_kernel(rewards, prompts, a_far, b_far, hidden_far, out_far, a_ref, b_ref, hidden, out, sem):
+def message_kernel(
+    rewards, prompts, live, a_far, b_far, hidden_far, out_far, a_ref, b_ref, hidden, out, sem
+):
     pairs = ((a_far, a_ref), (b_far, b_ref), (hidden_far, hidden))
     copies = [pltpu.make_async_copy(p, q, sem.at[i]) for i, (p, q) in enumerate(pairs)]
     for copy in copies:
@@ -108,10 +110,11 @@
     lane = lane_iota((1, LANES))
     value = jnp.where(lane == 0, rewards[0], jnp.where(lane == 1, rewards[1], 0.0))
     prompt = jnp.where(lane == 0, prompts[0], jnp.where(lane == 1, prompts[1], 0)).astype(f32)
+    length = jnp.where(lane == 0, live[0], jnp.where(lane == 1, live[1], 0)).astype(f32)
     high = value.astype(bf16).astype(f32)
     mid = (value - high).astype(bf16).astype(f32)
     low = value - high - mid
-    tail = jnp.concatenate([high, mid, low, prompt, jnp.zeros((2, LANES), f32)], axis=0)
+    tail = jnp.concatenate([high, mid, low, prompt, length, jnp.zeros((1, LANES), f32)], axis=0)
     for m in range(CHIP_COUNT):
         cut = hidden[:, m * LANES : (m + 1) * LANES].astype(f32)
         out[m, PIECE:, :] = jnp.concatenate([cut, tail], axis=0).astype(bf16)
@@ -120,21 +123,21 @@
     copy.wait()
 
 
-def first_message(rewards, prompts, a, b, hidden):
+def first_message(rewards, prompts, live, a, b, hidden):
     out = shape(CHIP_COUNT, FIRST_ROWS, LANES, dtype=bf16)
     smem = pl.BlockSpec(memory_space=SMEM)
     hbm = pl.BlockSpec(memory_space=pltpu.HBM)
     return pl.pallas_call(
         message_kernel,
         out_shape=out,
-        in_specs=[smem, smem, hbm, hbm, hbm],
+        in_specs=[smem, smem, smem, hbm, hbm, hbm],
         out_specs=hbm,
         scratch_shapes=[
             *(pltpu.VMEM(v.shape, v.dtype) for v in (a, b, hidden, out)),
             pltpu.SemaphoreType.DMA((4,)),
         ],
         compiler_params=pltpu.CompilerParams(vmem_limit_bytes=GRANT << 20),
-    )(rewards, prompts, a, b, hidden)
+    )(rewards, prompts, live, a, b, hidden)
 
 
 def spread_qkv(state, gain, w, out):
@@ -295,21 +298,7 @@
 
 
 def adapter_kernel(
-    rewards,
-    prompts,
-    live,
-    own,
-    other,
-    rows,
-    upstream,
-    w_own,
-    w_other,
-    weighted_out,
-    ab_out,
-    part,
-    state_out,
-    w_out,
-    held,
+    own, other, rows, upstream, w_own, w_other, weighted_out, ab_out, part, state_out, w_out, held
 ):
     state_out[...] = state_of(own, held)
     w_out[...] = in_core_order(w_own, w_other)
@@ -323,14 +312,18 @@
     for side in (own, other):
         tail = side[:, PIECE:, :].astype(f32)
         seen.append((tail[:, 2, :] + tail[:, 3, :] + tail[:, 4, :], tail[:, 5, :]))
+    m = lax.axis_index("y") * lax.axis_size("z") + lax.axis_index("z")
+    mine = own[pl.ds(m, 1), PIECE:, :].astype(f32).reshape(8, LANES)
     count = rows.shape[0]
     index = lax.broadcasted_iota(jnp.int32, (count, 1), 0)
     weight = jnp.zeros((count, 1), f32)
     for b in range(ROLLS):
+        reward = mine[2:3, b : b + 1] + mine[3:4, b : b + 1] + mine[4:5, b : b + 1]
+        live = mine[6:7, b : b + 1]
         total = jnp.zeros((1, 1), f32)
         squares = jnp.zeros((1, 1), f32)
         for value, prompt in seen:
-            hit = (prompt == prompts[b].astype(f32)) & (lane < ROLLS)
+            hit = (prompt == mine[5:6, b : b + 1]) & (lane < ROLLS)
             value = jnp.where(hit, value, 0.0)
             total = total + jnp.sum(jnp.sum(value, axis=0, keepdims=True), axis=1, keepdims=True)
             value = value * value
@@ -339,9 +332,9 @@
             )
         mean = total / GROUP
         std = jnp.sqrt(jnp.maximum(squares / GROUP - mean * mean, 0.09))
-        per_roll = (rewards[b] - mean) / std / live[b].astype(f32)
+        per_roll = (reward - mean) / std / live
         slot = index - b * COMP
-        inside = (slot >= 0) & (slot < COMP) & (slot < live[b])
+        inside = (slot >= 0) & (slot < COMP) & (slot < live.astype(jnp.int32))
         weight = jnp.where(inside, per_roll, weight)
     weighted = (weight * upstream[...].astype(f32)).astype(bf16)
     weighted_out[...] = weighted
@@ -496,6 +489,7 @@
     message = first_message(
         rewards,
         prompt_group_index,
+        completion_live_lengths,
         adapter_down_transposed[:, 0, :].T,
         adapter_up_matrix[:, 0, :].T,
         hidden,
@@ -511,10 +505,7 @@
         w_cols, ("y", "t"), [(a * nt + b, b * nt + a) for a in range(ny) for b in range(nt)]
     )
     arrived = exchange(message, CHIPS)
-    turned, gain, w_rows_other = together(turned, attention_norm_gain[None, :], w_rows_other)
-    turned, _ = together(turned, arrived)
-    w_block = lax.all_gather(turned, DP, axis=0, tiled=True)
-    w_block = w_block.reshape(nt, shard_width, w_cols.shape[1])
+    gain = attention_norm_gain[None, :]
     arrived, gain, w_rows_other = together(arrived, gain, w_rows_other)
     sent = call(
         qkv_first_kernel,
@@ -523,10 +514,11 @@
         (arrived, gain, w_rows, w_rows_other),
         scratch=[pltpu.VMEM((CHIP_COUNT * FIRST_ROWS, LANES), f32)],
     )
+    turned, _ = together(turned, sent)
+    w_block = lax.all_gather(turned, DP, axis=0, tiled=True)
+    w_block = w_block.reshape(nt, shard_width, w_cols.shape[1])
+    sent, arrived, own_rows = together(sent, arrived, attention_rows)
     arrived_other = swapped(arrived)
-    sent, arrived, arrived_other, own_rows = together(
-        sent, arrived, arrived_other, attention_rows
-    )
     came = exchange(sent.reshape(CHIP_COUNT, QKV_ROWS, LANES), CHIPS)
 
     left = shift(own_rows, 1, nt)
@@ -542,18 +534,8 @@
             shape(ROLLS * CHIP_COUNT, LANES),
             shape(2 * w_rows.shape[0], w_rows.shape[1], dtype=bf16),
         ),
-        [SMEM] * 3 + [VMEM] * 6,
-        (
-            rewards,
-            prompt_group_index,
-            completion_live_lengths,
-            arrived,
-            arrived_other,
-            attention_rows,
-            upstream,
-            w_rows,
-            w_rows_other,
-        ),
+        [VMEM] * 6,
+        (arrived, arrived_other, attention_rows, upstream, w_rows, w_rows_other),
         scratch=[pltpu.VMEM((CHIP_COUNT * FIRST_ROWS, LANES), f32)],
         flops=4 * rows * shard_width * LANES,
     )

time: 166 us -> 163 us (0.982)
  local copies, waits for them, and re-layouts: 20.7 us -> 16.9 us
  waiting for transfers between devices: 17 us -> 19.2 us
    all_to_all x4, waiting for transfers between devices: 6.07 us -> 11.8 us  [exchange(): return lax.all_to_all(x, axes, split_axis=0, concat_axis=0, tiled=True)]
    ppermute x1, waiting for transfers between devices: 5.57 us -> 0.01 us  [shards(): lax.ppermute(w_cols, ('y', 't'), [(a * nt + b, b * nt + a) for a in range...]
    unnamed x72 -> x60, local copies, waits for them, and re-layouts: 14.9 us -> 11.1 us
  transfers between devices with their start and end apart: 26 -> 26, of which waited for: 7 -> 8; matrix products, arithmetic and copies ran while one was open for 4% -> 4% of each run, Pallas kernels for 13% -> 13%
where the time goes in v9:
time: 163 us; the launch traced here: 162 us
  starting transfers between devices  66.9 us (41%)
  Pallas kernels  24.5 us (15%)
  waiting for transfers between devices  19.2 us (12%)
  blocking collectives  18.7 us (11%)
  local copies, waits for them, and re-layouts  16.9 us (10%)
  between operations  14.4 us (9%)
    all_to_all x4, starting transfers between devices, exchange(): return lax.all_to_all(x, axes, split_axis=0, concat_axis=0, tiled=True)  40.4 us
    ppermute x16, starting transfers between devices, shift(): return lax.ppermute(x, 't', [(i, (i + by) % n) for i in range(n)])  22.7 us
    all_to_all x1, blocking collectives, exchange(): return lax.all_to_all(x, axes, split_axis=0, concat_axis=0, tiled=True)  18.7 us
    all_to_all x4, waiting for transfers between devices, exchange(): return lax.all_to_all(x, axes, split_axis=0, concat_axis=0, tiled=True)  11.8 us
    unnamed x60, local copies, waits for them, and re-layouts  11.1 us
    pallas_call x1, Pallas kernels, output_rows(): pl.pallas_call(rows_kernel, out_shape=(shape(rows, width), shape(8, width...  11.1 us
    pallas_call x8, Pallas kernels, call(): pl.pallas_call(kernel, out_shape=out, in_specs=[pl.BlockSpec(memory_space...  11.1 us
    ppermute x16, waiting for transfers between devices, shift(): return lax.ppermute(x, 't', [(i, (i + by) % n) for i in range(n)])  4.63 us
  transfers between devices with their start and end apart: 26, of which 8 were waited for; matrix products, arithmetic and copies ran while one was open for 4% of the time, Pallas kernels for 13%

profile of v9, /device:TPU:8, one launch (start us, length us, event | category | flops | bytes accessed | tf_op | source)
XLA Modules:
  0.0 161.8 jit_solution(10261504588954519015)
XLA Ops:
  7.2 2.4 %shard_map.156 = bf16[32,24,128]{2,1,0:T(8,128)(2,1)} custom-call(f32[2]{0:T(128)} %rewards.1, s32[2]{0:T(128)} %prompts.1, s32[2]{0:T(128)} %live.1, bf16[16,64]{1,0:T(8,128)(2,1)} %bitcast.38, bf16[16,64]{1,0:T(8,128)(2,1)} %bitcast.39, bf16[2,4096]{1,0:T(2,128)(2,1)} %hidden_far.1), custom_call_target="tpu_custom_call" | custom-call | tf_op jit(solution)/shard_map/pallas_call | solution.py:130
  9.5 11.7 %all-to-all-start = ((bf16[32,24,128]{2,1,0:T(8,128)(2,1)}), bf16[32,24,128]{2,1,0:T(8,128)(2,1)S(1)}, u32[]{:S(2)}, u32[]{:S(2)}) async-start(bf16[32,24,128]{2,1,0:T(8,128)(2,1)} %shard_map.156), calls=%async_computation | async-start | bytes 393216 | tf_op jit(solution)/shard_map/all_to_all | solution.py:64
  21.4 3.1 %collective-permute-start.13 = (bf16[64,1024]{1,0:T(8,128)(2,1)}, bf16[64,1024]{1,0:T(8,128)(2,1)}, u32[]{:S(2)}, u32[]{:S(2)}) collective-permute-start(bf16[64,1024]{1,0:T(8,128)(2,1)} %bitcast.35), channel_id=1, source_target_pairs={{0,0},{1,64},{2,128},{3,192},{64,1},{65,65},{66,129},{67,193},{128... | collective-permute-start | bytes 393224 | tf_op jit(solution)/shard_map/ppermute | solution.py:504
  24.5 0.7 broadcast_in_dim.9.gain
  25.2 6.2 %all-to-all-done.arrived.own = bf16[32,24,128]{2,1,0:T(8,128)(2,1)S(1)} async-done(((bf16[32,24,128]{2,1,0:T(8,128)(2,1)}), bf16[32,24,128]{2,1,0:T(8,128)(2,1)S(1)}, u32[]{:S(2)}, u32[]{:S(2)}) %all-to-all-start) | async-done | bytes 196640 | tf_op jit(solution)/shard_map/all_to_all | solution.py:64
  31.4 0.9 copy-done.9
  32.6 0.7 copy-done.2
  33.4 11.9 %all-to-all-start.1 = ((f32[32,24,128]{2,1,0:T(8,128)}), f32[32,24,128]{2,1,0:T(8,128)}, u32[]{:S(2)}, u32[]{:S(2)}) async-start(f32[32,24,128]{2,1,0:T(8,128)} %bitcast.27), calls=%async_computation.1 | async-start | bytes 786432 | tf_op jit(solution)/shard_map/all_to_all | solution.py:64
  45.4 3.2 %collective-permute-start.2 = (bf16[512,1024]{1,0:T(8,128)(2,1)S(1)}, bf16[512,1024]{1,0:T(8,128)(2,1)}, u32[]{:S(2)}, u32[]{:S(2)}) collective-permute-start(bf16[512,1024]{1,0:T(8,128)(2,1)S(1)} %copy-done.1), channel_id=1, source_target_pairs={{0,3},{1,0},{2,1},{3,2},{4,7},{5,4},{6,5},{7,6},{8,11},{9,8},{10,9... | collective-permute-start | bytes 3145736 | tf_op jit(solution)/shard_map/ppermute | solution.py:56
  49.1 1.1 collective-permute-done.3.other
  50.2 1.2 copy-done.8
  51.5 0.9 copy-done.10
  52.4 2.0 %shard_map.158 = (bf16[512,1024]{1,0:T(8,128)(2,1)S(1)}, bf16[32,32,128]{2,1,0:T(8,128)(2,1)S(1)}, f32[640,128]{1,0:T(8,128)}, f32[64,128]{1,0:T(8,128)S(1)}, bf16[128,1280]{1,0:T(8,128)(2,1)S(1)}) custom-call(bf16[32,24,128]{2,1,0:T(8,128)(2,1)S(1)} %all-to-all-done.arrived.own, bf16[32,24,128]{2,1,0:T(8,128)(2,1)S(1)} %collective-permute-done.3.other, ...), custom_call_target="tpu_custom_call" | custom-call | flops 268435456 | bytes 4816896 | tf_op jit(solution)/shard_map/pallas_call | solution.py:84
  54.4 1.0 copy-done.3
  55.4 0.7 copy-done.5
  56.1 0.7 copy-done.11
  57.4 1.5 collective-permute-start.5
  58.9 0.6 copy-done.16
  59.5 1.8 %collective-permute-start.6 = (f32[640,128]{1,0:T(8,128)}, f32[640,128]{1,0:T(8,128)}, u32[]{:S(2)}, u32[]{:S(2)}) collective-permute-start(f32[640,128]{1,0:T(8,128)} %get-tuple-element.41.p0), channel_id=1, source_target_pairs={{0,3},{1,0},{2,1},{3,2},{4,7},{5,4},{6,5},{7,6},{8,11},{9,8},{10,9... | collective-permute-start | bytes 983048 | tf_op jit(solution)/shard_map/ppermute | solution.py:56
  61.3 0.7 copy-done.23
  62.1 2.2 %shard_map.159 = (bf16[32,16,128]{2,1,0:T(8,128)(2,1)S(1)}, f32[8,128]{1,0:T(8,128)S(1)}) custom-call(s32[2]{0:T(128)S(1)} %copy-done.23, f32[768,128]{1,0:T(8,128)} %bitcast.6.refs_1_, bf16[2,2048,256]{2,1,0:T(8,128)(2,1)S(1)} %bitcast.25), custom_call_target="tpu_custom_call" | custom-call | flops 67108864 | bytes 2625544 | tf_op jit(solution)/shard_map/pallas_call | solution.py:84
  64.9 18.7 %all_to_all.25.came = bf16[32,16,128]{2,1,0:T(8,128)(2,1)S(1)} all-to-all(bf16[32,16,128]{2,1,0:T(8,128)(2,1)S(1)} %get-tuple-element.43), channel_id=1, replica_groups=mesh['y'=4,'z'=8,'c'=2,'t'=4] {'y','z'}, dimensions={0} | all-to-all | bytes 262144 | tf_op jit(solution)/shard_map/all_to_all | solution.py:64
  83.9 1.1 collective-permute-done.4.p1
  85.0 2.0 %collective-permute-start.8 = (f32[64,256]{1,0:T(8,128)S(1)}, f32[64,256]{1,0:T(8,128)S(1)}, u32[]{:S(2)}, u32[]{:S(2)}) collective-permute-start(f32[64,256]{1,0:T(8,128)S(1)} %shard_map.160.s0), channel_id=1, source_target_pairs={{0,1},{1,2},{2,3},{3,0},{4,5},{5,6},{6,7},{7,4},{8,9},{9,10},{10,1... | collective-permute-start | bytes 196616 | tf_op jit(solution)/shard_map/ppermute | solution.py:56
  87.0 2.1 %collective-permute-start.9 = (f32[64,256]{1,0:T(8,128)S(1)}, f32[64,256]{1,0:T(8,128)S(1)}, u32[]{:S(2)}, u32[]{:S(2)}) collective-permute-start(f32[64,256]{1,0:T(8,128)S(1)} %shard_map.160.s0), channel_id=1, source_target_pairs={{0,2},{1,3},{2,0},{3,1},{4,6},{5,7},{6,4},{7,5},{8,10},{9,11},{10,... | collective-permute-start | bytes 196616 | tf_op jit(solution)/shard_map/ppermute | solution.py:56
  89.1 2.2 %shard_map.161 = (bf16[512,128]{1,0:T(8,128)(2,1)S(1)}, f32[192,128]{1,0:T(8,128)S(1)}, f32[32,16,128]{2,1,0:T(8,128)S(1)}, f32[32,16,128]{2,1,0:T(8,128)S(1)}) custom-call(f32[640,128]{1,0:T(8,128)} %get-tuple-element.41.p0, f32[640,128]{1,0:T(8,128)} %collective-permute-done.4.p1, f32[640,128]{1,0:T(8,128)} %collective-permute-done.5.p2, ...), custom_call_target="tpu_custom_call" | custom-call | flops 268435456 | bytes 4194304 | tf_op jit(solution)/shard_map/pallas_call | solution.py:84
  91.4 1.4 collective-permute-done.9.s2
  92.8 1.5 shard_map.162
  94.3 9.9 %all-to-all-start.3 = ((f32[32,24,128]{2,1,0:T(8,128)}), f32[32,24,128]{2,1,0:T(8,128)S(1)}, u32[]{:S(2)}, u32[]{:S(2)}) async-start(f32[32,24,128]{2,1,0:T(8,128)} %bitcast.13), calls=%async_computation.3 | async-start | bytes 786432 | tf_op jit(solution)/shard_map/all_to_all | solution.py:64
  104.2 1.9 %slice.12 = bf16[256,1024]{1,0:T(8,128)(2,1)} slice(bf16[512,1024]{1,0:T(8,128)(2,1)} %collective-permute-done.1.left), slice={[0:256], [0:1024]} | slice | bytes 1048576 | tf_op jit(solution)/shard_map/slice | solution.py:580
  106.4 1.9 %slice.13 = bf16[256,1024]{1,0:T(8,128)(2,1)} slice(bf16[512,1024]{1,0:T(8,128)(2,1)} %collective-permute-done.2.right), slice={[256:512], [0:1024]} | slice | bytes 1048576 | tf_op jit(solution)/shard_map/slice | solution.py:581
  108.3 3.0 %collective-permute-start.12 = (bf16[256,1024]{1,0:T(8,128)(2,1)}, bf16[256,1024]{1,0:T(8,128)(2,1)}, u32[]{:S(2)}, u32[]{:S(2)}) collective-permute-start(bf16[256,1024]{1,0:T(8,128)(2,1)} %slice.13), channel_id=1, source_target_pairs={{0,3},{1,0},{2,1},{3,2},{4,7},{5,4},{6,5},{7,6},{8,11},{9,8},{10,9... | collective-permute-start | bytes 1572872 | tf_op jit(solution)/shard_map/ppermute | solution.py:56
  111.2 1.5 collective-permute-done.14
  112.8 0.7 add.7
  113.5 5.7 %all-to-all-done.3 = f32[32,24,128]{2,1,0:T(8,128)S(1)} async-done(((f32[32,24,128]{2,1,0:T(8,128)}), f32[32,24,128]{2,1,0:T(8,128)S(1)}, u32[]{:S(2)}, u32[]{:S(2)}) %all-to-all-start.3) | async-done | bytes 393248 | tf_op jit(solution)/shard_map/all_to_all | solution.py:64
  119.2 1.0 copy-done.7
  120.2 1.9 %shard_map.163 = (f32[24,128]{1,0:T(8,128)S(1)}, f32[64,128]{1,0:T(8,128)S(1)}) custom-call(s32[2]{0:T(128)S(1)} %copy-done.24, f32[768,128]{1,0:T(8,128)S(1)} %bitcast.28, bf16[2,2048,256]{2,1,0:T(8,128)(2,1)S(1)} %bitcast.26, f32[8,128]{1,0:T(8,128)S(1)} %copy-done.22, bf16[1024,128]{1,0:T(8,128)(2,1)S(1)} %bitcast.31), custom_call_target="tpu_custom_call" | custom-call | flops 67108864 | bytes 2801672 | tf_op jit(solution)/shard_map/pallas_call | solution.py:84
  122.1 0.8 collective-permute-start.15
  122.9 3.1 %collective-permute-start.16 = (f32[24,128]{1,0:T(8,128)S(1)}, f32[24,128]{1,0:T(8,128)S(1)}, u32[]{:S(2)}, u32[]{:S(2)}) collective-permute-start(f32[24,128]{1,0:T(8,128)S(1)} %get-tuple-element.61.s0), channel_id=1, source_target_pairs={{0,2},{1,3},{2,0},{3,1},{4,6},{5,7},{6,4},{7,5},{8,10},{9,11},{10,... | collective-permute-start | bytes 36872 | tf_op jit(solution)/shard_map/ppermute | solution.py:56
  126.3 6.9 %all-to-all-start.4 = ((f32[32,16,128]{2,1,0:T(8,128)}), f32[32,16,128]{2,1,0:T(8,128)S(1)}, u32[]{:S(2)}, u32[]{:S(2)}) async-start(f32[32,16,128]{2,1,0:T(8,128)} %add.7), calls=%async_computation.4 | async-start | bytes 524288 | tf_op jit(solution)/shard_map/all_to_all | solution.py:64
  133.7 0.6 reshape.35.owned
  135.0 11.1 %shard_map.164 = (f32[512,1024]{1,0:T(8,128)}, f32[8,1024]{1,0:T(8,128)}) custom-call(s32[4]{0:T(128)} %compare_select_fusion.where_ref, bf16[512,1024]{1,0:T(8,128)(2,1)} %own.1, bf16[512,1024]{1,0:T(8,128)(2,1)} %collective-permute-done.1.left, bf16[512,1024]{1,0:T(8,128)(2,1)} %collective-permute-done.2.right, ...), custom_call_target="tpu_custom_call" | custom-call | flops 4294967296 | bytes 14680064 | tf_op jit(solution)/shard_map/pallas_call | solution.py:425
  146.1 1.8 %collective-permute-start.18 = (f32[8,1024]{1,0:T(8,128)}, f32[8,1024]{1,0:T(8,128)S(1)}, u32[]{:S(2)}, u32[]{:S(2)}) collective-permute-start(f32[8,1024]{1,0:T(8,128)} %get-tuple-element.63.c0), channel_id=1, source_target_pairs={{0,1},{1,2},{2,3},{3,0},{4,5},{5,6},{6,7},{7,4},{8,9},{9,10},{10,1... | collective-permute-start | bytes 98312 | tf_op jit(solution)/shard_map/ppermute | solution.py:56
  148.3 2.4 %collective-permute-start.20 = (f32[8,1024]{1,0:T(8,128)}, f32[8,1024]{1,0:T(8,128)S(1)}, u32[]{:S(2)}, u32[]{:S(2)}) collective-permute-start(f32[8,1024]{1,0:T(8,128)} %get-tuple-element.63.c0), channel_id=1, source_target_pairs={{0,3},{1,0},{2,1},{3,2},{4,7},{5,4},{6,5},{7,6},{8,11},{9,8},{10,9... | collective-permute-start | bytes 98312 | tf_op jit(solution)/shard_map/ppermute | solution.py:56
  150.7 0.8 collective-permute-done.18.c1
  151.5 0.7 slice_bitcast_fusion
  152.2 1.3 collective-permute-done.19.c2
  153.5 0.8 copy-done.20
  (84 shorter events, 5.4 us)
Async XLA Ops:
  7.2 38.1 %copy-start.1 = (bf16[512,1024]{1,0:T(8,128)(2,1)S(1)}, bf16[512,1024]{1,0:T(8,128)(2,1)}, u32[]{:S(2)}) copy-start(bf16[512,1024]{1,0:T(8,128)(2,1)} %own.1) | copy-start | bytes 3145732
  9.5 21.8 %all-to-all-start = ((bf16[32,24,128]{2,1,0:T(8,128)(2,1)}), bf16[32,24,128]{2,1,0:T(8,128)(2,1)S(1)}, u32[]{:S(2)}, u32[]{:S(2)}) async-start(bf16[32,24,128]{2,1,0:T(8,128)(2,1)} %shard_map.156), calls=%async_computation | async-start | bytes 393216 | tf_op jit(solution)/shard_map/all_to_all | solution.py:64
  21.3 113.2 %all-gather.2.cloned.1.call-start = ((), (), s32[]{:S(2)}) async-start(), calls=%async_computation.5 | async-start | bytes 8519680 | tf_op jit(solution)/shard_map/all_gather | solution.py:518
  21.3 3.9 %collective-permute-start = (bf16[64,1280]{1,0:T(8,128)(2,1)}, bf16[64,1280]{1,0:T(8,128)(2,1)S(1)}, u32[]{:S(2)}, u32[]{:S(2)}) collective-permute-start(bf16[64,1280]{1,0:T(8,128)(2,1)} %bitcast.32), channel_id=1, source_target_pairs={{0,4},{4,0},{1,5},{5,1},{2,6},{6,2},{3,7},{7,3},{8,12},{12,8},{9,1... | collective-permute-start | bytes 491528 | tf_op jit(solution)/shard_map/ppermute | solution.py:52
  21.4 11.9 %collective-permute-start.13 = (bf16[64,1024]{1,0:T(8,128)(2,1)}, bf16[64,1024]{1,0:T(8,128)(2,1)}, u32[]{:S(2)}, u32[]{:S(2)}) collective-permute-start(bf16[64,1024]{1,0:T(8,128)(2,1)} %bitcast.35), channel_id=1, source_target_pairs={{0,0},{1,64},{2,128},{3,192},{64,1},{65,65},{66,129},{67,193},{128... | collective-permute-start | bytes 393224 | tf_op jit(solution)/shard_map/ppermute | solution.py:504
  31.4 0.9 copy-start.9
  32.6 0.7 copy-start.2
  33.4 28.0 %copy-start = (bf16[2,2048,1,256]{3,1,2,0:T(8,128)(2,1)S(1)}, bf16[2,2048,1,256]{3,1,2,0:T(8,128)(2,1)}, u32[]{:S(2)}) copy-start(bf16[2,2048,1,256]{3,1,2,0:T(8,128)(2,1)} %param.16) | copy-start | bytes 6291460
  33.4 27.9 %all-to-all-start.1 = ((f32[32,24,128]{2,1,0:T(8,128)}), f32[32,24,128]{2,1,0:T(8,128)}, u32[]{:S(2)}, u32[]{:S(2)}) async-start(f32[32,24,128]{2,1,0:T(8,128)} %bitcast.27), calls=%async_computation.1 | async-start | bytes 786432 | tf_op jit(solution)/shard_map/all_to_all | solution.py:64
  45.3 48.9 %collective-permute-start.1 = (bf16[512,1024]{1,0:T(8,128)(2,1)S(1)}, bf16[512,1024]{1,0:T(8,128)(2,1)}, u32[]{:S(2)}, u32[]{:S(2)}) collective-permute-start(bf16[512,1024]{1,0:T(8,128)(2,1)S(1)} %copy-done.1), channel_id=1, source_target_pairs={{0,1},{1,2},{2,3},{3,0},{4,5},{5,6},{6,7},{7,4},{8,9},{9,10},{10,1... | collective-permute-start | bytes 3145736 | tf_op jit(solution)/shard_map/ppermute | solution.py:56
  45.4 48.9 %collective-permute-start.2 = (bf16[512,1024]{1,0:T(8,128)(2,1)S(1)}, bf16[512,1024]{1,0:T(8,128)(2,1)}, u32[]{:S(2)}, u32[]{:S(2)}) collective-permute-start(bf16[512,1024]{1,0:T(8,128)(2,1)S(1)} %copy-done.1), channel_id=1, source_target_pairs={{0,3},{1,0},{2,1},{3,2},{4,7},{5,4},{6,5},{7,6},{8,11},{9,8},{10,9... | collective-permute-start | bytes 3145736 | tf_op jit(solution)/shard_map/ppermute | solution.py:56
  48.6 1.6 %collective-permute-start.3 = (bf16[32,24,128]{2,1,0:T(8,128)(2,1)S(1)}, bf16[32,24,128]{2,1,0:T(8,128)(2,1)S(1)}, u32[]{:S(2)}, u32[]{:S(2)}) collective-permute-start(bf16[32,24,128]{2,1,0:T(8,128)(2,1)S(1)} %all-to-all-done.arrived.own), channel_id=1, source_target_pairs={{0,4},{4,0},{1,5},{5,1},{2,6},{6,2},{3,7},{7,3},{8,12},{12,8},{9,1... | collective-permute-start | bytes 589832 | tf_op jit(solution)/shard_map/ppermute | solution.py:52
  48.6 10.3 %collective-permute-start.7 = (bf16[64,1024]{1,0:T(8,128)(2,1)}, bf16[64,1024]{1,0:T(8,128)(2,1)S(1)}, u32[]{:S(2)}, u32[]{:S(2)}) collective-permute-start(bf16[64,1024]{1,0:T(8,128)(2,1)} %bitcast.36), channel_id=1, source_target_pairs={{0,4},{4,0},{1,5},{5,1},{2,6},{6,2},{3,7},{7,3},{8,12},{12,8},{9,1... | collective-permute-start | bytes 393224 | tf_op jit(solution)/shard_map/ppermute | solution.py:52
  50.2 1.2 copy-start.8
  51.5 0.9 copy-start.10
  54.4 1.0 copy-start.3
  57.4 26.2 %copy-start.15 = (bf16[1,1024,64]{1,2,0:T(8,128)(2,1)S(1)}, bf16[1,1024,64]{1,2,0:T(8,128)(2,1)}, u32[]{:S(2)}) copy-start(bf16[1,1024,64]{1,2,0:T(8,128)(2,1)} %param.18) | copy-start | bytes 393220
  57.4 26.2 %copy-start.6 = (bf16[32,32,128]{2,1,0:T(8,128)(2,1)S(1)}, bf16[32,32,128]{2,1,0:T(8,128)(2,1)}, u32[]{:S(2)}) copy-start(bf16[32,32,128]{2,1,0:T(8,128)(2,1)} %copy-done.5) | copy-start | bytes 786436
  57.4 27.5 %collective-permute-start.4 = (f32[640,128]{1,0:T(8,128)}, f32[640,128]{1,0:T(8,128)}, u32[]{:S(2)}, u32[]{:S(2)}) collective-permute-start(f32[640,128]{1,0:T(8,128)} %get-tuple-element.41.p0), channel_id=1, source_target_pairs={{0,1},{1,2},{2,3},{3,0},{4,5},{5,6},{6,7},{7,4},{8,9},{9,10},{10,1... | collective-permute-start | bytes 983048 | tf_op jit(solution)/shard_map/ppermute | solution.py:56
  57.4 27.6 %collective-permute-start.5 = (f32[640,128]{1,0:T(8,128)}, f32[640,128]{1,0:T(8,128)}, u32[]{:S(2)}, u32[]{:S(2)}) collective-permute-start(f32[640,128]{1,0:T(8,128)} %get-tuple-element.41.p0), channel_id=1, source_target_pairs={{0,2},{1,3},{2,0},{3,1},{4,6},{5,7},{6,4},{7,5},{8,10},{9,11},{10,... | collective-permute-start | bytes 983048 | tf_op jit(solution)/shard_map/ppermute | solution.py:56
  59.5 27.5 %collective-permute-start.6 = (f32[640,128]{1,0:T(8,128)}, f32[640,128]{1,0:T(8,128)}, u32[]{:S(2)}, u32[]{:S(2)}) collective-permute-start(f32[640,128]{1,0:T(8,128)} %get-tuple-element.41.p0), channel_id=1, source_target_pairs={{0,3},{1,0},{2,1},{3,2},{4,7},{5,4},{6,5},{7,6},{8,11},{9,8},{10,9... | collective-permute-start | bytes 983048 | tf_op jit(solution)/shard_map/ppermute | solution.py:56
  61.3 22.3 %copy-start.17 = (bf16[64,1024]{1,0:T(8,128)(2,1)S(1)}, bf16[64,1024]{1,0:T(8,128)(2,1)}, u32[]{:S(2)}) copy-start(bf16[64,1024]{1,0:T(8,128)(2,1)} %copy-done.16) | copy-start | bytes 393220
  61.3 27.8 %copy-start.4 = (bf16[512,1024]{1,0:T(8,128)(2,1)S(1)}, bf16[512,1024]{1,0:T(8,128)(2,1)}, u32[]{:S(2)}) copy-start(bf16[512,1024]{1,0:T(8,128)(2,1)} %copy-done.3) | copy-start | bytes 3145732
  61.3 27.8 %copy-start.19 = (f32[64,128]{1,0:T(8,128)S(1)}, f32[64,128]{1,0:T(8,128)}, u32[]{:S(2)}) copy-start(f32[64,128]{1,0:T(8,128)} %copy-done.18) | copy-start | bytes 98308
  61.3 0.8 copy-start.23
  83.6 9.2 %copy-start.12 = (bf16[128,1280]{1,0:T(8,128)(2,1)S(1)}, bf16[128,1280]{1,0:T(8,128)(2,1)}, u32[]{:S(2)}) copy-start(bf16[128,1280]{1,0:T(8,128)(2,1)} %copy-done.11) | copy-start | bytes 983044
  85.0 6.4 %collective-permute-start.10 = (f32[64,256]{1,0:T(8,128)S(1)}, f32[64,256]{1,0:T(8,128)S(1)}, u32[]{:S(2)}, u32[]{:S(2)}) collective-permute-start(f32[64,256]{1,0:T(8,128)S(1)} %shard_map.160.s0), channel_id=1, source_target_pairs={{0,3},{1,0},{2,1},{3,2},{4,7},{5,4},{6,5},{7,6},{8,11},{9,8},{10,9... | collective-permute-start | bytes 196616 | tf_op jit(solution)/shard_map/ppermute | solution.py:56
  85.0 6.4 %collective-permute-start.8 = (f32[64,256]{1,0:T(8,128)S(1)}, f32[64,256]{1,0:T(8,128)S(1)}, u32[]{:S(2)}, u32[]{:S(2)}) collective-permute-start(f32[64,256]{1,0:T(8,128)S(1)} %shard_map.160.s0), channel_id=1, source_target_pairs={{0,1},{1,2},{2,3},{3,0},{4,5},{5,6},{6,7},{7,4},{8,9},{9,10},{10,1... | collective-permute-start | bytes 196616 | tf_op jit(solution)/shard_map/ppermute | solution.py:56
  87.0 5.8 %collective-permute-start.9 = (f32[64,256]{1,0:T(8,128)S(1)}, f32[64,256]{1,0:T(8,128)S(1)}, u32[]{:S(2)}, u32[]{:S(2)}) collective-permute-start(f32[64,256]{1,0:T(8,128)S(1)} %shard_map.160.s0), channel_id=1, source_target_pairs={{0,2},{1,3},{2,0},{3,1},{4,6},{5,7},{6,4},{7,5},{8,10},{9,11},{10,... | collective-permute-start | bytes 196616 | tf_op jit(solution)/shard_map/ppermute | solution.py:56
  91.3 2.9 %copy-start.13 = (f32[32,16,128]{2,1,0:T(8,128)}, f32[32,16,128]{2,1,0:T(8,128)S(1)}, u32[]{:S(2)}) copy-start(f32[32,16,128]{2,1,0:T(8,128)S(1)} %get-tuple-element.59) | copy-start | bytes 786436
  91.3 2.9 %copy-start.25 = (bf16[512,128]{1,0:T(8,128)(2,1)}, bf16[512,128]{1,0:T(8,128)(2,1)S(1)}, u32[]{:S(2)}) copy-start(bf16[512,128]{1,0:T(8,128)(2,1)S(1)} %get-tuple-element.55.low) | copy-start | bytes 393220
  94.2 25.0 %copy-start.22 = (f32[8,128]{1,0:T(8,128)S(1)}, f32[8,128]{1,0:T(8,128)}, u32[]{:S(2)}) copy-start(f32[8,128]{1,0:T(8,128)} %copy-done.21) | copy-start | bytes 12292
  94.2 25.0 %copy-start.24 = (s32[2]{0:T(128)S(1)}, s32[2]{0:T(128)}, u32[]{:S(2)}) copy-start(s32[2]{0:T(128)} %refs_0_.3) | copy-start | bytes 28
  94.3 18.5 %copy-start.14 = (f32[32,16,128]{2,1,0:T(8,128)S(1)}, f32[32,16,128]{2,1,0:T(8,128)}, u32[]{:S(2)}) copy-start(f32[32,16,128]{2,1,0:T(8,128)} %copy-done.13) | copy-start | bytes 786436
  94.3 24.9 %all-to-all-start.3 = ((f32[32,24,128]{2,1,0:T(8,128)}), f32[32,24,128]{2,1,0:T(8,128)S(1)}, u32[]{:S(2)}, u32[]{:S(2)}) async-start(f32[32,24,128]{2,1,0:T(8,128)} %bitcast.13), calls=%async_computation.3 | async-start | bytes 786432 | tf_op jit(solution)/shard_map/all_to_all | solution.py:64
  106.1 28.3 %collective-permute-start.11 = (bf16[256,1024]{1,0:T(8,128)(2,1)}, bf16[256,1024]{1,0:T(8,128)(2,1)}, u32[]{:S(2)}, u32[]{:S(2)}) collective-permute-start(bf16[256,1024]{1,0:T(8,128)(2,1)} %slice.12), channel_id=1, source_target_pairs={{0,1},{1,2},{2,3},{3,0},{4,5},{5,6},{6,7},{7,4},{8,9},{9,10},{10,1... | collective-permute-start | bytes 1572872 | tf_op jit(solution)/shard_map/ppermute | solution.py:56
  108.3 26.1 %collective-permute-start.12 = (bf16[256,1024]{1,0:T(8,128)(2,1)}, bf16[256,1024]{1,0:T(8,128)(2,1)}, u32[]{:S(2)}, u32[]{:S(2)}) collective-permute-start(bf16[256,1024]{1,0:T(8,128)(2,1)} %slice.13), channel_id=1, source_target_pairs={{0,3},{1,0},{2,1},{3,2},{4,7},{5,4},{6,5},{7,6},{8,11},{9,8},{10,9... | collective-permute-start | bytes 1572872 | tf_op jit(solution)/shard_map/ppermute | solution.py:56
  111.2 1.5 collective-permute-start.14
  119.2 1.0 copy-start.7
  122.1 12.4 %copy-start.26 = (f32[24,128]{1,0:T(8,128)}, f32[24,128]{1,0:T(8,128)S(1)}, u32[]{:S(2)}) copy-start(f32[24,128]{1,0:T(8,128)S(1)} %get-tuple-element.61.s0) | copy-start | bytes 36868
  122.1 12.3 %collective-permute-start.15 = (f32[24,128]{1,0:T(8,128)S(1)}, f32[24,128]{1,0:T(8,128)S(1)}, u32[]{:S(2)}, u32[]{:S(2)}) collective-permute-start(f32[24,128]{1,0:T(8,128)S(1)} %get-tuple-element.61.s0), channel_id=1, source_target_pairs={{0,1},{1,2},{2,3},{3,0},{4,5},{5,6},{6,7},{7,4},{8,9},{9,10},{10,1... | collective-permute-start | bytes 36872 | tf_op jit(solution)/shard_map/ppermute | solution.py:56
  122.9 11.5 %collective-permute-start.16 = (f32[24,128]{1,0:T(8,128)S(1)}, f32[24,128]{1,0:T(8,128)S(1)}, u32[]{:S(2)}, u32[]{:S(2)}) collective-permute-start(f32[24,128]{1,0:T(8,128)S(1)} %get-tuple-element.61.s0), channel_id=1, source_target_pairs={{0,2},{1,3},{2,0},{3,1},{4,6},{5,7},{6,4},{7,5},{8,10},{9,11},{10,... | collective-permute-start | bytes 36872 | tf_op jit(solution)/shard_map/ppermute | solution.py:56
  125.9 8.5 %collective-permute-start.17 = (f32[24,128]{1,0:T(8,128)S(1)}, f32[24,128]{1,0:T(8,128)S(1)}, u32[]{:S(2)}, u32[]{:S(2)}) collective-permute-start(f32[24,128]{1,0:T(8,128)S(1)} %get-tuple-element.61.s0), channel_id=1, source_target_pairs={{0,3},{1,0},{2,1},{3,2},{4,7},{5,4},{6,5},{7,6},{8,11},{9,8},{10,9... | collective-permute-start | bytes 36872 | tf_op jit(solution)/shard_map/ppermute | solution.py:56
  126.3 24.4 %all-to-all-start.4 = ((f32[32,16,128]{2,1,0:T(8,128)}), f32[32,16,128]{2,1,0:T(8,128)S(1)}, u32[]{:S(2)}, u32[]{:S(2)}) async-start(f32[32,16,128]{2,1,0:T(8,128)} %add.7), calls=%async_computation.4 | async-start | bytes 524288 | tf_op jit(solution)/shard_map/all_to_all | solution.py:64
  146.1 5.4 %collective-permute-start.18 = (f32[8,1024]{1,0:T(8,128)}, f32[8,1024]{1,0:T(8,128)S(1)}, u32[]{:S(2)}, u32[]{:S(2)}) collective-permute-start(f32[8,1024]{1,0:T(8,128)} %get-tuple-element.63.c0), channel_id=1, source_target_pairs={{0,1},{1,2},{2,3},{3,0},{4,5},{5,6},{6,7},{7,4},{8,9},{9,10},{10,1... | collective-permute-start | bytes 98312 | tf_op jit(solution)/shard_map/ppermute | solution.py:56
  147.9 5.6 %collective-permute-start.19 = (f32[8,1024]{1,0:T(8,128)}, f32[8,1024]{1,0:T(8,128)S(1)}, u32[]{:S(2)}, u32[]{:S(2)}) collective-permute-start(f32[8,1024]{1,0:T(8,128)} %get-tuple-element.63.c0), channel_id=1, source_target_pairs={{0,2},{1,3},{2,0},{3,1},{4,6},{5,7},{6,4},{7,5},{8,10},{9,11},{10,... | collective-permute-start | bytes 98312 | tf_op jit(solution)/shard_map/ppermute | solution.py:56
  148.3 5.2 %collective-permute-start.20 = (f32[8,1024]{1,0:T(8,128)}, f32[8,1024]{1,0:T(8,128)S(1)}, u32[]{:S(2)}, u32[]{:S(2)}) collective-permute-start(f32[8,1024]{1,0:T(8,128)} %get-tuple-element.63.c0), channel_id=1, source_target_pairs={{0,3},{1,0},{2,1},{3,2},{4,7},{5,4},{6,5},{7,6},{8,11},{9,8},{10,9... | collective-permute-start | bytes 98312 | tf_op jit(solution)/shard_map/ppermute | solution.py:56
  153.5 0.8 copy-start.20
  (8 other events, 5.1 us)
Sparse Core Ops, SparseCore 0:
  33.5 89.2 all-gather.1

commit v10 on v9

--- a/solution.py
+++ b/solution.py
@@ -23,6 +23,7 @@
 STATE_ROW = KEY_ROW + 2 * ROLLS
 GRANT = 56
 SMALL_GRANT = 24
+HINT = 2
 
 adapter_scale = 2.0
 f32 = jnp.float32
@@ -413,7 +414,12 @@
     low_sum = s0[top:, :] + s1[top:, :] + s2[top:, :] + s3[top:, :]
     got = adapter_scale * nt_dot(low_sum, b_turned, precision=HIGH)
     cols[...] = got + acc[rows : rows + 8]
-    cols[:ROLLS, :] += owned[...]
+    wide = cols.shape[1] // LANES
+    start = (where_ref[0] * pl.num_programs(0) + pl.program_id(0)) * wide
+    for b in range(ROLLS):
+        for i in range(wide):
+            block = owned[pl.ds(b * CHIP_COUNT + start + i, 1), :]
+            cols[b : b + 1, i * LANES : (i + 1) * LANES] += block
 
 
 def output_rows(where, own, left, right, far_a, far_b, w, low, b, sent, owned):
@@ -438,7 +444,7 @@
                 whole(low),
                 pl.BlockSpec((tile, b.shape[1]), lambda j, s: (j, 0)),
                 *(whole(s) for s in sent),
-                pl.BlockSpec((ROLLS, tile), lambda j, s: (0, s[0] * tiles + j)),
+                whole(owned),
             ],
             out_specs=(
                 pl.BlockSpec((rows, tile), lambda j, s: (0, j)),
@@ -448,7 +454,7 @@
         ),
         compiler_params=pltpu.CompilerParams(vmem_limit_bytes=GRANT << 20),
         cost_estimate=pl.CostEstimate(
-            flops=2 * rows * width * depth * n,
+            flops=HINT * 2 * rows * width * depth * n,
             bytes_accessed=2 * (n * width * depth + n * rows * depth) + 4 * rows * width,
             transcendentals=0,
         ),
@@ -506,7 +512,9 @@
     )
     arrived = exchange(message, CHIPS)
     gain = attention_norm_gain[None, :]
-    arrived, gain, w_rows_other = together(arrived, gain, w_rows_other)
+    arrived, gain, w_rows_other, w_cols_other, where = together(
+        arrived, gain, w_rows_other, w_cols_other, where
+    )
     sent = call(
         qkv_first_kernel,
         shape(CHIP_COUNT * QKV_ROWS, LANES),
@@ -595,7 +603,7 @@
         low_back,
         ab,
         shifts(attended, nt),
-        owned.reshape(ROLLS, width),
+        owned,
     )
     arriving = shifts(cols, nt)
     arriving[1], summed = together(arriving[1], summed)

time: 163 us -> 161 us (0.988)
  waiting for transfers between devices: 19.2 us -> 22 us
  local copies, waits for them, and re-layouts: 16.9 us -> 15.1 us
  starting transfers between devices: 66.9 us -> 65.2 us
    ppermute x16, waiting for transfers between devices: 4.63 us -> 8.34 us  [shift(): return lax.ppermute(x, 't', [(i, (i + by) % n) for i in range(n)])]
    ppermute x16, starting transfers between devices: 22.7 us -> 20.9 us  [shift(): return lax.ppermute(x, 't', [(i, (i + by) % n) for i in range(n)])]
    unnamed x60 -> x62, local copies, waits for them, and re-layouts: 11.1 us -> 9.97 us
  transfers between devices with their start and end apart: 26 -> 26, of which waited for: 8 -> 10; matrix products, arithmetic and copies ran while one was open for 4% -> 4% of each run, Pallas kernels for 13% -> 13%
where the time goes in v10:
time: 161 us; the launch traced here: 160 us
  starting transfers between devices  65.2 us (40%)
  Pallas kernels  24.4 us (15%)
  waiting for transfers between devices  22 us (14%)
  blocking collectives  18 us (11%)
  local copies, waits for them, and re-layouts  15.1 us (9%)
  between operations  14.4 us (9%)
    all_to_all x4, starting transfers between devices, exchange(): return lax.all_to_all(x, axes, split_axis=0, concat_axis=0, tiled=True)  40.6 us
    ppermute x16, starting transfers between devices, shift(): return lax.ppermute(x, 't', [(i, (i + by) % n) for i in range(n)])  20.9 us
    all_to_all x1, blocking collectives, exchange(): return lax.all_to_all(x, axes, split_axis=0, concat_axis=0, tiled=True)  18 us
    pallas_call x1, Pallas kernels, output_rows(): pl.pallas_call(rows_kernel, out_shape=(shape(rows, width), shape(8, width...  11.1 us
    pallas_call x8, Pallas kernels, call(): pl.pallas_call(kernel, out_shape=out, in_specs=[pl.BlockSpec(memory_space...  10.9 us
    all_to_all x4, waiting for transfers between devices, exchange(): return lax.all_to_all(x, axes, split_axis=0, concat_axis=0, tiled=True)  10.6 us
    unnamed x62, local copies, waits for them, and re-layouts  9.97 us
    ppermute x16, waiting for transfers between devices, shift(): return lax.ppermute(x, 't', [(i, (i + by) % n) for i in range(n)])  8.34 us
  transfers between devices with their start and end apart: 26, of which 10 were waited for; matrix products, arithmetic and copies ran while one was open for 4% of the time, Pallas kernels for 13%

profile of v10, /device:TPU:8, one launch (start us, length us, event | category | flops | bytes accessed | tf_op | source)
XLA Modules:
  0.0 160.4 jit_solution(18398176526161413289)
XLA Ops:
  7.2 2.4 %shard_map.156 = bf16[32,24,128]{2,1,0:T(8,128)(2,1)} custom-call(f32[2]{0:T(128)} %rewards.1, s32[2]{0:T(128)} %prompts.1, s32[2]{0:T(128)} %live.1, bf16[16,64]{1,0:T(8,128)(2,1)} %bitcast.38, bf16[16,64]{1,0:T(8,128)(2,1)} %bitcast.39, bf16[2,4096]{1,0:T(2,128)(2,1)} %hidden_far.1), custom_call_target="tpu_custom_call" | custom-call | tf_op jit(solution)/shard_map/pallas_call | solution.py:131
  9.5 11.7 %all-to-all-start = ((bf16[32,24,128]{2,1,0:T(8,128)(2,1)}), bf16[32,24,128]{2,1,0:T(8,128)(2,1)S(1)}, u32[]{:S(2)}, u32[]{:S(2)}) async-start(bf16[32,24,128]{2,1,0:T(8,128)(2,1)} %shard_map.156), calls=%async_computation | async-start | bytes 393216 | tf_op jit(solution)/shard_map/all_to_all | solution.py:65
  21.9 3.1 %collective-permute-start.13 = (bf16[64,1024]{1,0:T(8,128)(2,1)}, bf16[64,1024]{1,0:T(8,128)(2,1)}, u32[]{:S(2)}, u32[]{:S(2)}) collective-permute-start(bf16[64,1024]{1,0:T(8,128)(2,1)} %bitcast.36), channel_id=1, source_target_pairs={{0,0},{1,64},{2,128},{3,192},{64,1},{65,65},{66,129},{67,193},{128... | collective-permute-start | bytes 393224 | tf_op jit(solution)/shard_map/ppermute | solution.py:510
  25.0 0.7 broadcast_in_dim.9.gain
  26.2 0.7 copy-done.16
  26.9 4.5 %all-to-all-done.arrived.own = bf16[32,24,128]{2,1,0:T(8,128)(2,1)S(1)} async-done(((bf16[32,24,128]{2,1,0:T(8,128)(2,1)}), bf16[32,24,128]{2,1,0:T(8,128)(2,1)S(1)}, u32[]{:S(2)}, u32[]{:S(2)}) %all-to-all-start) | async-done | bytes 196640 | tf_op jit(solution)/shard_map/all_to_all | solution.py:65
  31.4 0.9 copy-done.9
  32.6 0.8 copy-done.2
  33.4 12.0 %all-to-all-start.1 = ((f32[32,24,128]{2,1,0:T(8,128)}), f32[32,24,128]{2,1,0:T(8,128)}, u32[]{:S(2)}, u32[]{:S(2)}) async-start(f32[32,24,128]{2,1,0:T(8,128)} %bitcast.27), calls=%async_computation.1 | async-start | bytes 786432 | tf_op jit(solution)/shard_map/all_to_all | solution.py:65
  45.5 3.2 %collective-permute-start.3 = (bf16[512,1024]{1,0:T(8,128)(2,1)S(1)}, bf16[512,1024]{1,0:T(8,128)(2,1)}, u32[]{:S(2)}, u32[]{:S(2)}) collective-permute-start(bf16[512,1024]{1,0:T(8,128)(2,1)S(1)} %copy-done.1), channel_id=1, source_target_pairs={{0,3},{1,0},{2,1},{3,2},{4,7},{5,4},{6,5},{7,6},{8,11},{9,8},{10,9... | collective-permute-start | bytes 3145736 | tf_op jit(solution)/shard_map/ppermute | solution.py:57
  48.7 1.4 collective-permute-done.4.other
  50.2 1.2 copy-done.8
  51.4 0.9 copy-done.10
  52.3 2.0 %shard_map.158 = (bf16[512,1024]{1,0:T(8,128)(2,1)S(1)}, bf16[32,32,128]{2,1,0:T(8,128)(2,1)S(1)}, f32[640,128]{1,0:T(8,128)}, f32[64,128]{1,0:T(8,128)S(1)}, bf16[128,1280]{1,0:T(8,128)(2,1)S(1)}) custom-call(bf16[32,24,128]{2,1,0:T(8,128)(2,1)S(1)} %all-to-all-done.arrived.own, bf16[32,24,128]{2,1,0:T(8,128)(2,1)S(1)} %collective-permute-done.4.other, ...), custom_call_target="tpu_custom_call" | custom-call | flops 268435456 | bytes 4816896 | tf_op jit(solution)/shard_map/pallas_call | solution.py:85
  54.3 1.0 copy-done.3
  55.3 0.7 copy-done.5
  56.0 0.7 copy-done.11
  56.7 1.5 collective-permute-start.6
  58.2 1.8 %collective-permute-start.7 = (f32[640,128]{1,0:T(8,128)}, f32[640,128]{1,0:T(8,128)}, u32[]{:S(2)}, u32[]{:S(2)}) collective-permute-start(f32[640,128]{1,0:T(8,128)} %get-tuple-element.44.p0), channel_id=1, source_target_pairs={{0,3},{1,0},{2,1},{3,2},{4,7},{5,4},{6,5},{7,6},{8,11},{9,8},{10,9... | collective-permute-start | bytes 983048 | tf_op jit(solution)/shard_map/ppermute | solution.py:57
  60.0 0.7 all-to-all-done.1
  60.7 0.7 copy-done.21
  61.5 2.2 %shard_map.159 = (bf16[32,16,128]{2,1,0:T(8,128)(2,1)S(1)}, f32[8,128]{1,0:T(8,128)S(1)}) custom-call(s32[2]{0:T(128)S(1)} %copy-done.21, f32[768,128]{1,0:T(8,128)} %bitcast.8.refs_1_, bf16[2,2048,256]{2,1,0:T(8,128)(2,1)S(1)} %bitcast.25), custom_call_target="tpu_custom_call" | custom-call | flops 67108864 | bytes 2625544 | tf_op jit(solution)/shard_map/pallas_call | solution.py:85
  63.7 18.0 %all_to_all.25.came = bf16[32,16,128]{2,1,0:T(8,128)(2,1)S(1)} all-to-all(bf16[32,16,128]{2,1,0:T(8,128)(2,1)S(1)} %get-tuple-element.46), channel_id=1, replica_groups=mesh['y'=4,'z'=8,'c'=2,'t'=4] {'y','z'}, dimensions={0} | all-to-all | bytes 262144 | tf_op jit(solution)/shard_map/all_to_all | solution.py:65
  82.0 2.9 %collective-permute-done.5.p1 = f32[640,128]{1,0:T(8,128)} collective-permute-done((f32[640,128]{1,0:T(8,128)}, f32[640,128]{1,0:T(8,128)}, u32[]{:S(2)}, u32[]{:S(2)}) %collective-permute-start.5) | collective-permute-done | bytes 327712 | tf_op jit(solution)/shard_map/ppermute | solution.py:57
  84.9 2.0 %collective-permute-start.8 = (f32[64,256]{1,0:T(8,128)S(1)}, f32[64,256]{1,0:T(8,128)S(1)}, u32[]{:S(2)}, u32[]{:S(2)}) collective-permute-start(f32[64,256]{1,0:T(8,128)S(1)} %shard_map.160.s0), channel_id=1, source_target_pairs={{0,1},{1,2},{2,3},{3,0},{4,5},{5,6},{6,7},{7,4},{8,9},{9,10},{10,1... | collective-permute-start | bytes 196616 | tf_op jit(solution)/shard_map/ppermute | solution.py:57
  87.2 2.1 %shard_map.161 = (bf16[512,128]{1,0:T(8,128)(2,1)S(1)}, f32[192,128]{1,0:T(8,128)S(1)}, f32[32,16,128]{2,1,0:T(8,128)S(1)}, f32[32,16,128]{2,1,0:T(8,128)S(1)}) custom-call(f32[640,128]{1,0:T(8,128)} %get-tuple-element.44.p0, f32[640,128]{1,0:T(8,128)} %collective-permute-done.5.p1, f32[640,128]{1,0:T(8,128)} %collective-permute-done.6.p2, ...), custom_call_target="tpu_custom_call" | custom-call | flops 268435456 | bytes 4194304 | tf_op jit(solution)/shard_map/pallas_call | solution.py:85
  89.4 1.0 collective-permute-done.8.s1
  90.3 2.3 %collective-permute-done.9.s2 = f32[64,256]{1,0:T(8,128)S(1)} collective-permute-done((f32[64,256]{1,0:T(8,128)S(1)}, f32[64,256]{1,0:T(8,128)S(1)}, u32[]{:S(2)}, u32[]{:S(2)}) %collective-permute-start.9) | collective-permute-done | bytes 65568 | tf_op jit(solution)/shard_map/ppermute | solution.py:57
  92.7 1.5 shard_map.162
  94.2 9.9 %all-to-all-start.3 = ((f32[32,24,128]{2,1,0:T(8,128)}), f32[32,24,128]{2,1,0:T(8,128)S(1)}, u32[]{:S(2)}, u32[]{:S(2)}) async-start(f32[32,24,128]{2,1,0:T(8,128)} %bitcast.13), calls=%async_computation.3 | async-start | bytes 786432 | tf_op jit(solution)/shard_map/all_to_all | solution.py:65
  104.1 1.9 %slice.12 = bf16[256,1024]{1,0:T(8,128)(2,1)} slice(bf16[512,1024]{1,0:T(8,128)(2,1)} %collective-permute-done.2.left), slice={[0:256], [0:1024]} | slice | bytes 1048576 | tf_op jit(solution)/shard_map/slice | solution.py:588
  106.3 1.9 %slice.13 = bf16[256,1024]{1,0:T(8,128)(2,1)} slice(bf16[512,1024]{1,0:T(8,128)(2,1)} %collective-permute-done.3.right), slice={[256:512], [0:1024]} | slice | bytes 1048576 | tf_op jit(solution)/shard_map/slice | solution.py:589
  108.2 3.0 %collective-permute-start.12 = (bf16[256,1024]{1,0:T(8,128)(2,1)}, bf16[256,1024]{1,0:T(8,128)(2,1)}, u32[]{:S(2)}, u32[]{:S(2)}) collective-permute-start(bf16[256,1024]{1,0:T(8,128)(2,1)} %slice.13), channel_id=1, source_target_pairs={{0,3},{1,0},{2,1},{3,2},{4,7},{5,4},{6,5},{7,6},{8,11},{9,8},{10,9... | collective-permute-start | bytes 1572872 | tf_op jit(solution)/shard_map/ppermute | solution.py:57
  111.2 1.5 collective-permute-done.14
  112.7 0.7 add.7
  113.4 5.4 %all-to-all-done.3 = f32[32,24,128]{2,1,0:T(8,128)S(1)} async-done(((f32[32,24,128]{2,1,0:T(8,128)}), f32[32,24,128]{2,1,0:T(8,128)S(1)}, u32[]{:S(2)}, u32[]{:S(2)}) %all-to-all-start.3) | async-done | bytes 393248 | tf_op jit(solution)/shard_map/all_to_all | solution.py:65
  118.9 0.9 copy-done.7
  119.8 1.9 %shard_map.163 = (f32[24,128]{1,0:T(8,128)S(1)}, f32[64,128]{1,0:T(8,128)S(1)}) custom-call(s32[2]{0:T(128)S(1)} %copy-done.22, f32[768,128]{1,0:T(8,128)S(1)} %bitcast.28, bf16[2,2048,256]{2,1,0:T(8,128)(2,1)S(1)} %bitcast.26, f32[8,128]{1,0:T(8,128)S(1)} %copy-done.20, bf16[1024,128]{1,0:T(8,128)(2,1)S(1)} %bitcast.31), custom_call_target="tpu_custom_call" | custom-call | flops 67108864 | bytes 2801672 | tf_op jit(solution)/shard_map/pallas_call | solution.py:85
  121.7 0.9 collective-permute-start.15
  122.7 3.2 %collective-permute-start.16 = (f32[24,128]{1,0:T(8,128)S(1)}, f32[24,128]{1,0:T(8,128)S(1)}, u32[]{:S(2)}, u32[]{:S(2)}) collective-permute-start(f32[24,128]{1,0:T(8,128)S(1)} %get-tuple-element.65.s0), channel_id=1, source_target_pairs={{0,2},{1,3},{2,0},{3,1},{4,6},{5,7},{6,4},{7,5},{8,10},{9,11},{10,... | collective-permute-start | bytes 36872 | tf_op jit(solution)/shard_map/ppermute | solution.py:57
  126.0 7.0 %all-to-all-start.4 = ((f32[32,16,128]{2,1,0:T(8,128)}), f32[32,16,128]{2,1,0:T(8,128)S(1)}, u32[]{:S(2)}, u32[]{:S(2)}) async-start(f32[32,16,128]{2,1,0:T(8,128)} %add.7), calls=%async_computation.4 | async-start | bytes 524288 | tf_op jit(solution)/shard_map/all_to_all | solution.py:65
  133.7 11.1 %shard_map.164 = (f32[512,1024]{1,0:T(8,128)}, f32[8,1024]{1,0:T(8,128)}) custom-call(s32[4]{0:T(128)} %compare_select_fusion.where_ref, bf16[512,1024]{1,0:T(8,128)(2,1)} %own.1, bf16[512,1024]{1,0:T(8,128)(2,1)} %collective-permute-done.2.left, bf16[512,1024]{1,0:T(8,128)(2,1)} %collective-permute-done.3.right, ...), custom_call_target="tpu_custom_call" | custom-call | flops 8589934592 | bytes 14680064 | tf_op jit(solution)/shard_map/pallas_call | solution.py:431
  144.7 1.8 %collective-permute-start.18 = (f32[8,1024]{1,0:T(8,128)}, f32[8,1024]{1,0:T(8,128)S(1)}, u32[]{:S(2)}, u32[]{:S(2)}) collective-permute-start(f32[8,1024]{1,0:T(8,128)} %get-tuple-element.67.c0), channel_id=1, source_target_pairs={{0,1},{1,2},{2,3},{3,0},{4,5},{5,6},{6,7},{7,4},{8,9},{9,10},{10,1... | collective-permute-start | bytes 98312 | tf_op jit(solution)/shard_map/ppermute | solution.py:57
  147.0 2.3 %collective-permute-start.20 = (f32[8,1024]{1,0:T(8,128)}, f32[8,1024]{1,0:T(8,128)S(1)}, u32[]{:S(2)}, u32[]{:S(2)}) collective-permute-start(f32[8,1024]{1,0:T(8,128)} %get-tuple-element.67.c0), channel_id=1, source_target_pairs={{0,3},{1,0},{2,1},{3,2},{4,7},{5,4},{6,5},{7,6},{8,11},{9,8},{10,9... | collective-permute-start | bytes 98312 | tf_op jit(solution)/shard_map/ppermute | solution.py:57
  149.3 0.9 collective-permute-done.18.c1
  150.2 0.7 slice_bitcast_fusion
  150.9 1.3 collective-permute-done.19.c2
  152.1 0.8 copy-done.18
  (85 shorter events, 4.4 us)
Async XLA Ops:
  7.2 38.2 %copy-start.1 = (bf16[512,1024]{1,0:T(8,128)(2,1)S(1)}, bf16[512,1024]{1,0:T(8,128)(2,1)}, u32[]{:S(2)}) copy-start(bf16[512,1024]{1,0:T(8,128)(2,1)} %own.1) | copy-start | bytes 3145732
  9.5 21.8 %all-to-all-start = ((bf16[32,24,128]{2,1,0:T(8,128)(2,1)}), bf16[32,24,128]{2,1,0:T(8,128)(2,1)S(1)}, u32[]{:S(2)}, u32[]{:S(2)}) async-start(bf16[32,24,128]{2,1,0:T(8,128)(2,1)} %shard_map.156), calls=%async_computation | async-start | bytes 393216 | tf_op jit(solution)/shard_map/all_to_all | solution.py:65
  21.3 111.8 %all-gather.2.cloned.1.call-start = ((), (), s32[]{:S(2)}) async-start(), calls=%async_computation.5 | async-start | bytes 8519680 | tf_op jit(solution)/shard_map/all_gather | solution.py:526
  21.3 5.6 %collective-permute-start = (bf16[64,1280]{1,0:T(8,128)(2,1)}, bf16[64,1280]{1,0:T(8,128)(2,1)S(1)}, u32[]{:S(2)}, u32[]{:S(2)}) collective-permute-start(bf16[64,1280]{1,0:T(8,128)(2,1)} %bitcast.32), channel_id=1, source_target_pairs={{0,4},{4,0},{1,5},{5,1},{2,6},{6,2},{3,7},{7,3},{8,12},{12,8},{9,1... | collective-permute-start | bytes 491528 | tf_op jit(solution)/shard_map/ppermute | solution.py:53
  21.4 4.8 %collective-permute-start.1 = (bf16[64,1024]{1,0:T(8,128)(2,1)}, bf16[64,1024]{1,0:T(8,128)(2,1)S(1)}, u32[]{:S(2)}, u32[]{:S(2)}) collective-permute-start(bf16[64,1024]{1,0:T(8,128)(2,1)} %bitcast.35), channel_id=1, source_target_pairs={{0,4},{4,0},{1,5},{5,1},{2,6},{6,2},{3,7},{7,3},{8,12},{12,8},{9,1... | collective-permute-start | bytes 393224 | tf_op jit(solution)/shard_map/ppermute | solution.py:53
  21.9 11.5 %collective-permute-start.13 = (bf16[64,1024]{1,0:T(8,128)(2,1)}, bf16[64,1024]{1,0:T(8,128)(2,1)}, u32[]{:S(2)}, u32[]{:S(2)}) collective-permute-start(bf16[64,1024]{1,0:T(8,128)(2,1)} %bitcast.36), channel_id=1, source_target_pairs={{0,0},{1,64},{2,128},{3,192},{64,1},{65,65},{66,129},{67,193},{128... | collective-permute-start | bytes 393224 | tf_op jit(solution)/shard_map/ppermute | solution.py:510
  31.4 0.9 copy-start.9
  33.4 27.3 %copy-start = (bf16[2,2048,1,256]{3,1,2,0:T(8,128)(2,1)S(1)}, bf16[2,2048,1,256]{3,1,2,0:T(8,128)(2,1)}, u32[]{:S(2)}) copy-start(bf16[2,2048,1,256]{3,1,2,0:T(8,128)(2,1)} %param.16) | copy-start | bytes 6291460
  33.4 27.3 %all-to-all-start.1 = ((f32[32,24,128]{2,1,0:T(8,128)}), f32[32,24,128]{2,1,0:T(8,128)}, u32[]{:S(2)}, u32[]{:S(2)}) async-start(f32[32,24,128]{2,1,0:T(8,128)} %bitcast.27), calls=%async_computation.1 | async-start | bytes 786432 | tf_op jit(solution)/shard_map/all_to_all | solution.py:65
  45.4 48.7 %collective-permute-start.2 = (bf16[512,1024]{1,0:T(8,128)(2,1)S(1)}, bf16[512,1024]{1,0:T(8,128)(2,1)}, u32[]{:S(2)}, u32[]{:S(2)}) collective-permute-start(bf16[512,1024]{1,0:T(8,128)(2,1)S(1)} %copy-done.1), channel_id=1, source_target_pairs={{0,1},{1,2},{2,3},{3,0},{4,5},{5,6},{6,7},{7,4},{8,9},{9,10},{10,1... | collective-permute-start | bytes 3145736 | tf_op jit(solution)/shard_map/ppermute | solution.py:57
  45.5 48.6 %collective-permute-start.3 = (bf16[512,1024]{1,0:T(8,128)(2,1)S(1)}, bf16[512,1024]{1,0:T(8,128)(2,1)}, u32[]{:S(2)}, u32[]{:S(2)}) collective-permute-start(bf16[512,1024]{1,0:T(8,128)(2,1)S(1)} %copy-done.1), channel_id=1, source_target_pairs={{0,3},{1,0},{2,1},{3,2},{4,7},{5,4},{6,5},{7,6},{8,11},{9,8},{10,9... | collective-permute-start | bytes 3145736 | tf_op jit(solution)/shard_map/ppermute | solution.py:57
  48.7 1.4 collective-permute-start.4
  50.2 1.2 copy-start.8
  51.4 0.9 copy-start.10
  54.3 1.0 copy-start.3
  56.7 25.0 %copy-start.6 = (bf16[32,32,128]{2,1,0:T(8,128)(2,1)S(1)}, bf16[32,32,128]{2,1,0:T(8,128)(2,1)}, u32[]{:S(2)}) copy-start(bf16[32,32,128]{2,1,0:T(8,128)(2,1)} %copy-done.5) | copy-start | bytes 786436
  56.7 28.1 %collective-permute-start.5 = (f32[640,128]{1,0:T(8,128)}, f32[640,128]{1,0:T(8,128)}, u32[]{:S(2)}, u32[]{:S(2)}) collective-permute-start(f32[640,128]{1,0:T(8,128)} %get-tuple-element.44.p0), channel_id=1, source_target_pairs={{0,1},{1,2},{2,3},{3,0},{4,5},{5,6},{6,7},{7,4},{8,9},{9,10},{10,1... | collective-permute-start | bytes 983048 | tf_op jit(solution)/shard_map/ppermute | solution.py:57
  56.7 28.1 %collective-permute-start.6 = (f32[640,128]{1,0:T(8,128)}, f32[640,128]{1,0:T(8,128)}, u32[]{:S(2)}, u32[]{:S(2)}) collective-permute-start(f32[640,128]{1,0:T(8,128)} %get-tuple-element.44.p0), channel_id=1, source_target_pairs={{0,2},{1,3},{2,0},{3,1},{4,6},{5,7},{6,4},{7,5},{8,10},{9,11},{10,... | collective-permute-start | bytes 983048 | tf_op jit(solution)/shard_map/ppermute | solution.py:57
  58.2 28.7 %collective-permute-start.7 = (f32[640,128]{1,0:T(8,128)}, f32[640,128]{1,0:T(8,128)}, u32[]{:S(2)}, u32[]{:S(2)}) collective-permute-start(f32[640,128]{1,0:T(8,128)} %get-tuple-element.44.p0), channel_id=1, source_target_pairs={{0,3},{1,0},{2,1},{3,2},{4,7},{5,4},{6,5},{7,6},{8,11},{9,8},{10,9... | collective-permute-start | bytes 983048 | tf_op jit(solution)/shard_map/ppermute | solution.py:57
  60.7 21.0 %copy-start.15 = (bf16[1,1024,64]{1,2,0:T(8,128)(2,1)S(1)}, bf16[1,1024,64]{1,2,0:T(8,128)(2,1)}, u32[]{:S(2)}) copy-start(bf16[1,1024,64]{1,2,0:T(8,128)(2,1)} %param.18) | copy-start | bytes 393220
  60.7 21.0 %copy-start.17 = (bf16[64,1024]{1,0:T(8,128)(2,1)S(1)}, bf16[64,1024]{1,0:T(8,128)(2,1)}, u32[]{:S(2)}) copy-start(bf16[64,1024]{1,0:T(8,128)(2,1)} %copy-done.16) | copy-start | bytes 393220
  60.7 26.5 %copy-start.4 = (bf16[512,1024]{1,0:T(8,128)(2,1)S(1)}, bf16[512,1024]{1,0:T(8,128)(2,1)}, u32[]{:S(2)}) copy-start(bf16[512,1024]{1,0:T(8,128)(2,1)} %copy-done.3) | copy-start | bytes 3145732
  63.7 25.6 %copy-start.19 = (f32[8,128]{1,0:T(8,128)}, f32[8,128]{1,0:T(8,128)S(1)}, u32[]{:S(2)}) copy-start(f32[8,128]{1,0:T(8,128)S(1)} %get-tuple-element.61.refs_3_) | copy-start | bytes 12292
  81.7 11.0 %copy-start.12 = (bf16[128,1280]{1,0:T(8,128)(2,1)S(1)}, bf16[128,1280]{1,0:T(8,128)(2,1)}, u32[]{:S(2)}) copy-start(bf16[128,1280]{1,0:T(8,128)(2,1)} %copy-done.11) | copy-start | bytes 983044
  84.9 4.5 %collective-permute-start.10 = (f32[64,256]{1,0:T(8,128)S(1)}, f32[64,256]{1,0:T(8,128)S(1)}, u32[]{:S(2)}, u32[]{:S(2)}) collective-permute-start(f32[64,256]{1,0:T(8,128)S(1)} %shard_map.160.s0), channel_id=1, source_target_pairs={{0,3},{1,0},{2,1},{3,2},{4,7},{5,4},{6,5},{7,6},{8,11},{9,8},{10,9... | collective-permute-start | bytes 196616 | tf_op jit(solution)/shard_map/ppermute | solution.py:57
  84.9 5.5 %collective-permute-start.8 = (f32[64,256]{1,0:T(8,128)S(1)}, f32[64,256]{1,0:T(8,128)S(1)}, u32[]{:S(2)}, u32[]{:S(2)}) collective-permute-start(f32[64,256]{1,0:T(8,128)S(1)} %shard_map.160.s0), channel_id=1, source_target_pairs={{0,1},{1,2},{2,3},{3,0},{4,5},{5,6},{6,7},{7,4},{8,9},{9,10},{10,1... | collective-permute-start | bytes 196616 | tf_op jit(solution)/shard_map/ppermute | solution.py:57
  86.9 5.8 %collective-permute-start.9 = (f32[64,256]{1,0:T(8,128)S(1)}, f32[64,256]{1,0:T(8,128)S(1)}, u32[]{:S(2)}, u32[]{:S(2)}) collective-permute-start(f32[64,256]{1,0:T(8,128)S(1)} %shard_map.160.s0), channel_id=1, source_target_pairs={{0,2},{1,3},{2,0},{3,1},{4,6},{5,7},{6,4},{7,5},{8,10},{9,11},{10,... | collective-permute-start | bytes 196616 | tf_op jit(solution)/shard_map/ppermute | solution.py:57
  89.3 4.8 %copy-start.13 = (f32[32,16,128]{2,1,0:T(8,128)}, f32[32,16,128]{2,1,0:T(8,128)S(1)}, u32[]{:S(2)}) copy-start(f32[32,16,128]{2,1,0:T(8,128)S(1)} %get-tuple-element.63) | copy-start | bytes 786436
  89.3 4.8 %copy-start.23 = (f32[32,16,128]{2,1,0:T(8,128)}, f32[32,16,128]{2,1,0:T(8,128)S(1)}, u32[]{:S(2)}) copy-start(f32[32,16,128]{2,1,0:T(8,128)S(1)} %get-tuple-element.64) | copy-start | bytes 786436
  89.3 4.8 %copy-start.25 = (bf16[512,128]{1,0:T(8,128)(2,1)}, bf16[512,128]{1,0:T(8,128)(2,1)S(1)}, u32[]{:S(2)}) copy-start(bf16[512,128]{1,0:T(8,128)(2,1)S(1)} %get-tuple-element.59.low) | copy-start | bytes 393220
  94.1 24.7 %copy-start.20 = (f32[8,128]{1,0:T(8,128)S(1)}, f32[8,128]{1,0:T(8,128)}, u32[]{:S(2)}) copy-start(f32[8,128]{1,0:T(8,128)} %copy-done.19) | copy-start | bytes 12292
  94.1 24.7 %copy-start.22 = (s32[2]{0:T(128)S(1)}, s32[2]{0:T(128)}, u32[]{:S(2)}) copy-start(s32[2]{0:T(128)} %refs_0_.3) | copy-start | bytes 28
  94.2 18.5 %copy-start.14 = (f32[32,16,128]{2,1,0:T(8,128)S(1)}, f32[32,16,128]{2,1,0:T(8,128)}, u32[]{:S(2)}) copy-start(f32[32,16,128]{2,1,0:T(8,128)} %copy-done.13) | copy-start | bytes 786436
  94.2 17.0 %copy-start.24 = (f32[32,16,128]{2,1,0:T(8,128)S(1)}, f32[32,16,128]{2,1,0:T(8,128)}, u32[]{:S(2)}) copy-start(f32[32,16,128]{2,1,0:T(8,128)} %copy-done.23) | copy-start | bytes 786436
  94.2 24.7 %all-to-all-start.3 = ((f32[32,24,128]{2,1,0:T(8,128)}), f32[32,24,128]{2,1,0:T(8,128)S(1)}, u32[]{:S(2)}, u32[]{:S(2)}) async-start(f32[32,24,128]{2,1,0:T(8,128)} %bitcast.13), calls=%async_computation.3 | async-start | bytes 786432 | tf_op jit(solution)/shard_map/all_to_all | solution.py:65
  106.0 27.0 %collective-permute-start.11 = (bf16[256,1024]{1,0:T(8,128)(2,1)}, bf16[256,1024]{1,0:T(8,128)(2,1)}, u32[]{:S(2)}, u32[]{:S(2)}) collective-permute-start(bf16[256,1024]{1,0:T(8,128)(2,1)} %slice.12), channel_id=1, source_target_pairs={{0,1},{1,2},{2,3},{3,0},{4,5},{5,6},{6,7},{7,4},{8,9},{9,10},{10,1... | collective-permute-start | bytes 1572872 | tf_op jit(solution)/shard_map/ppermute | solution.py:57
  108.2 24.8 %collective-permute-start.12 = (bf16[256,1024]{1,0:T(8,128)(2,1)}, bf16[256,1024]{1,0:T(8,128)(2,1)}, u32[]{:S(2)}, u32[]{:S(2)}) collective-permute-start(bf16[256,1024]{1,0:T(8,128)(2,1)} %slice.13), channel_id=1, source_target_pairs={{0,3},{1,0},{2,1},{3,2},{4,7},{5,4},{6,5},{7,6},{8,11},{9,8},{10,9... | collective-permute-start | bytes 1572872 | tf_op jit(solution)/shard_map/ppermute | solution.py:57
  111.2 1.5 collective-permute-start.14
  118.9 1.0 copy-start.7
  121.7 11.4 %copy-start.26 = (f32[64,128]{1,0:T(8,128)}, f32[64,128]{1,0:T(8,128)S(1)}, u32[]{:S(2)}) copy-start(f32[64,128]{1,0:T(8,128)S(1)} %get-tuple-element.66.owned) | copy-start | bytes 98308
  121.7 11.4 %copy-start.27 = (f32[24,128]{1,0:T(8,128)}, f32[24,128]{1,0:T(8,128)S(1)}, u32[]{:S(2)}) copy-start(f32[24,128]{1,0:T(8,128)S(1)} %get-tuple-element.65.s0) | copy-start | bytes 36868
  121.7 11.3 %collective-permute-start.15 = (f32[24,128]{1,0:T(8,128)S(1)}, f32[24,128]{1,0:T(8,128)S(1)}, u32[]{:S(2)}, u32[]{:S(2)}) collective-permute-start(f32[24,128]{1,0:T(8,128)S(1)} %get-tuple-element.65.s0), channel_id=1, source_target_pairs={{0,1},{1,2},{2,3},{3,0},{4,5},{5,6},{6,7},{7,4},{8,9},{9,10},{10,1... | collective-permute-start | bytes 36872 | tf_op jit(solution)/shard_map/ppermute | solution.py:57
  122.7 10.4 %collective-permute-start.16 = (f32[24,128]{1,0:T(8,128)S(1)}, f32[24,128]{1,0:T(8,128)S(1)}, u32[]{:S(2)}, u32[]{:S(2)}) collective-permute-start(f32[24,128]{1,0:T(8,128)S(1)} %get-tuple-element.65.s0), channel_id=1, source_target_pairs={{0,2},{1,3},{2,0},{3,1},{4,6},{5,7},{6,4},{7,5},{8,10},{9,11},{10,... | collective-permute-start | bytes 36872 | tf_op jit(solution)/shard_map/ppermute | solution.py:57
  125.8 7.2 %collective-permute-start.17 = (f32[24,128]{1,0:T(8,128)S(1)}, f32[24,128]{1,0:T(8,128)S(1)}, u32[]{:S(2)}, u32[]{:S(2)}) collective-permute-start(f32[24,128]{1,0:T(8,128)S(1)} %get-tuple-element.65.s0), channel_id=1, source_target_pairs={{0,3},{1,0},{2,1},{3,2},{4,7},{5,4},{6,5},{7,6},{8,11},{9,8},{10,9... | collective-permute-start | bytes 36872 | tf_op jit(solution)/shard_map/ppermute | solution.py:57
  126.0 23.2 %all-to-all-start.4 = ((f32[32,16,128]{2,1,0:T(8,128)}), f32[32,16,128]{2,1,0:T(8,128)S(1)}, u32[]{:S(2)}, u32[]{:S(2)}) async-start(f32[32,16,128]{2,1,0:T(8,128)} %add.7), calls=%async_computation.4 | async-start | bytes 524288 | tf_op jit(solution)/shard_map/all_to_all | solution.py:65
  144.7 5.4 %collective-permute-start.18 = (f32[8,1024]{1,0:T(8,128)}, f32[8,1024]{1,0:T(8,128)S(1)}, u32[]{:S(2)}, u32[]{:S(2)}) collective-permute-start(f32[8,1024]{1,0:T(8,128)} %get-tuple-element.67.c0), channel_id=1, source_target_pairs={{0,1},{1,2},{2,3},{3,0},{4,5},{5,6},{6,7},{7,4},{8,9},{9,10},{10,1... | collective-permute-start | bytes 98312 | tf_op jit(solution)/shard_map/ppermute | solution.py:57
  146.5 5.6 %collective-permute-start.19 = (f32[8,1024]{1,0:T(8,128)}, f32[8,1024]{1,0:T(8,128)S(1)}, u32[]{:S(2)}, u32[]{:S(2)}) collective-permute-start(f32[8,1024]{1,0:T(8,128)} %get-tuple-element.67.c0), channel_id=1, source_target_pairs={{0,2},{1,3},{2,0},{3,1},{4,6},{5,7},{6,4},{7,5},{8,10},{9,11},{10,... | collective-permute-start | bytes 98312 | tf_op jit(solution)/shard_map/ppermute | solution.py:57
  147.0 5.1 %collective-permute-start.20 = (f32[8,1024]{1,0:T(8,128)}, f32[8,1024]{1,0:T(8,128)S(1)}, u32[]{:S(2)}, u32[]{:S(2)}) collective-permute-start(f32[8,1024]{1,0:T(8,128)} %get-tuple-element.67.c0), channel_id=1, source_target_pairs={{0,3},{1,0},{2,1},{3,2},{4,7},{5,4},{6,5},{7,6},{8,11},{9,8},{10,9... | collective-permute-start | bytes 98312 | tf_op jit(solution)/shard_map/ppermute | solution.py:57
  (9 other events, 6.2 us)
Sparse Core Ops, SparseCore 0:
  33.5 89.2 all-gather.1

commit v11 on v10

--- a/solution.py
+++ b/solution.py
@@ -512,8 +512,9 @@
     )
     arrived = exchange(message, CHIPS)
     gain = attention_norm_gain[None, :]
-    arrived, gain, w_rows_other, w_cols_other, where = together(
-        arrived, gain, w_rows_other, w_cols_other, where
+    lengths = jnp.maximum(cache_fill_lengths, 0)
+    arrived, gain, w_rows_other, w_cols_other, where, lengths = together(
+        arrived, gain, w_rows_other, w_cols_other, where, lengths
     )
     sent = call(
         qkv_first_kernel,
@@ -550,7 +551,7 @@
     ab = ab.reshape(shard_width, LANES)
     parts = shifts(part, nt)
 
-    attended, kv = attend(False, cache_fill_lengths, came.reshape(-1, LANES), cache)
+    attended, kv = attend(False, lengths, came.reshape(-1, LANES), cache)
     everyone = exchange(attended, CHIPS)
 
     share = call(
@@ -589,7 +590,7 @@
     far_b = shift(right_far[half:], nt - 1, nt)
     kept = kept + swapped(given)
 
-    attended, owned = attend(True, cache_fill_lengths, came.reshape(-1, LANES), cache, kv, ab)
+    attended, owned = attend(True, lengths, came.reshape(-1, LANES), cache, kv, ab)
     attended, kept = together(attended, kept)
     summed = exchange(kept, CHIPS)
     adapted, cols = output_rows(

time: 161 us -> 161 us (level)
    unnamed x62 -> x54, local copies, waits for them, and re-layouts: 9.97 us -> 9 us
  transfers between devices with their start and end apart: 26 -> 26, of which waited for: 10 -> 10; matrix products, arithmetic and copies ran while one was open for 4% -> 5% of each run, Pallas kernels for 13% -> 13%
where the time goes in v11:
time: 161 us; the launch traced here: 160 us
  starting transfers between devices  64.8 us (40%)
  Pallas kernels  24.4 us (15%)
  waiting for transfers between devices  21.8 us (14%)
  blocking collectives  17.6 us (11%)
  between operations  14.4 us (9%)
  local copies, waits for them, and re-layouts  14.1 us (9%)
  other arithmetic  2.47 us (2%)
    all_to_all x4, starting transfers between devices, exchange(): return lax.all_to_all(x, axes, split_axis=0, concat_axis=0, tiled=True)  40.5 us
    ppermute x16, starting transfers between devices, shift(): return lax.ppermute(x, 't', [(i, (i + by) % n) for i in range(n)])  20.8 us
    all_to_all x1, blocking collectives, exchange(): return lax.all_to_all(x, axes, split_axis=0, concat_axis=0, tiled=True)  17.6 us
    pallas_call x1, Pallas kernels, output_rows(): pl.pallas_call(rows_kernel, out_shape=(shape(rows, width), shape(8, width...  11.1 us
    pallas_call x8, Pallas kernels, call(): pl.pallas_call(kernel, out_shape=out, in_specs=[pl.BlockSpec(memory_space...  11 us
    all_to_all x4, waiting for transfers between devices, exchange(): return lax.all_to_all(x, axes, split_axis=0, concat_axis=0, tiled=True)  10.3 us
    unnamed x54, local copies, waits for them, and re-layouts  9 us
    ppermute x16, waiting for transfers between devices, shift(): return lax.ppermute(x, 't', [(i, (i + by) % n) for i in range(n)])  8.52 us
  transfers between devices with their start and end apart: 26, of which 10 were waited for; matrix products, arithmetic and copies ran while one was open for 5% of the time, Pallas kernels for 13%

profile of v11, /device:TPU:8, one launch (start us, length us, event | category | flops | bytes accessed | tf_op | source)
XLA Modules:
  0.0 159.6 jit_solution(825453432335911375)
XLA Ops:
  7.2 2.4 %shard_map.156 = bf16[32,24,128]{2,1,0:T(8,128)(2,1)} custom-call(f32[2]{0:T(128)} %rewards.1, s32[2]{0:T(128)} %prompts.1, s32[2]{0:T(128)} %live.1, bf16[16,64]{1,0:T(8,128)(2,1)} %bitcast.38, bf16[16,64]{1,0:T(8,128)(2,1)} %bitcast.39, bf16[2,4096]{1,0:T(2,128)(2,1)} %hidden_far.1), custom_call_target="tpu_custom_call" | custom-call | tf_op jit(solution)/shard_map/pallas_call | solution.py:131
  9.5 11.7 %all-to-all-start = ((bf16[32,24,128]{2,1,0:T(8,128)(2,1)}), bf16[32,24,128]{2,1,0:T(8,128)(2,1)S(1)}, u32[]{:S(2)}, u32[]{:S(2)}) async-start(bf16[32,24,128]{2,1,0:T(8,128)(2,1)} %shard_map.156), calls=%async_computation | async-start | bytes 393216 | tf_op jit(solution)/shard_map/all_to_all | solution.py:65
  21.4 3.1 %collective-permute-start.13 = (bf16[64,1024]{1,0:T(8,128)(2,1)}, bf16[64,1024]{1,0:T(8,128)(2,1)}, u32[]{:S(2)}, u32[]{:S(2)}) collective-permute-start(bf16[64,1024]{1,0:T(8,128)(2,1)} %bitcast.36), channel_id=1, source_target_pairs={{0,0},{1,64},{2,128},{3,192},{64,1},{65,65},{66,129},{67,193},{128... | collective-permute-start | bytes 393224 | tf_op jit(solution)/shard_map/ppermute | solution.py:510
  24.8 1.2 broadcast_maximum_fusion.refs_0_
  26.0 0.7 broadcast_in_dim.9.gain
  27.2 0.7 copy-done.15
  27.9 3.5 %all-to-all-done.arrived.own = bf16[32,24,128]{2,1,0:T(8,128)(2,1)S(1)} async-done(((bf16[32,24,128]{2,1,0:T(8,128)(2,1)}), bf16[32,24,128]{2,1,0:T(8,128)(2,1)S(1)}, u32[]{:S(2)}, u32[]{:S(2)}) %all-to-all-start) | async-done | bytes 196640 | tf_op jit(solution)/shard_map/all_to_all | solution.py:65
  31.4 0.9 copy-done.8
  32.6 0.8 copy-done.2
  33.4 11.9 %all-to-all-start.1 = ((f32[32,24,128]{2,1,0:T(8,128)}), f32[32,24,128]{2,1,0:T(8,128)}, u32[]{:S(2)}, u32[]{:S(2)}) async-start(f32[32,24,128]{2,1,0:T(8,128)} %bitcast.27), calls=%async_computation.1 | async-start | bytes 786432 | tf_op jit(solution)/shard_map/all_to_all | solution.py:65
  45.4 3.2 %collective-permute-start.3 = (bf16[512,1024]{1,0:T(8,128)(2,1)S(1)}, bf16[512,1024]{1,0:T(8,128)(2,1)}, u32[]{:S(2)}, u32[]{:S(2)}) collective-permute-start(bf16[512,1024]{1,0:T(8,128)(2,1)S(1)} %copy-done.1), channel_id=1, source_target_pairs={{0,3},{1,0},{2,1},{3,2},{4,7},{5,4},{6,5},{7,6},{8,11},{9,8},{10,9... | collective-permute-start | bytes 3145736 | tf_op jit(solution)/shard_map/ppermute | solution.py:57
  48.6 1.4 collective-permute-done.4.other
  50.1 1.2 copy-done.7
  51.3 0.9 copy-done.9
  52.2 2.0 %shard_map.158 = (bf16[512,1024]{1,0:T(8,128)(2,1)S(1)}, bf16[32,32,128]{2,1,0:T(8,128)(2,1)S(1)}, f32[640,128]{1,0:T(8,128)}, f32[64,128]{1,0:T(8,128)S(1)}, bf16[128,1280]{1,0:T(8,128)(2,1)S(1)}) custom-call(bf16[32,24,128]{2,1,0:T(8,128)(2,1)S(1)} %all-to-all-done.arrived.own, bf16[32,24,128]{2,1,0:T(8,128)(2,1)S(1)} %collective-permute-done.4.other, ...), custom_call_target="tpu_custom_call" | custom-call | flops 268435456 | bytes 4816896 | tf_op jit(solution)/shard_map/pallas_call | solution.py:85
  54.2 1.0 copy-done.3
  55.2 0.7 copy-done.5
  55.9 0.7 copy-done.10
  56.6 1.5 collective-permute-start.6
  58.1 1.8 %collective-permute-start.7 = (f32[640,128]{1,0:T(8,128)}, f32[640,128]{1,0:T(8,128)}, u32[]{:S(2)}, u32[]{:S(2)}) collective-permute-start(f32[640,128]{1,0:T(8,128)} %get-tuple-element.45.p0), channel_id=1, source_target_pairs={{0,3},{1,0},{2,1},{3,2},{4,7},{5,4},{6,5},{7,6},{8,11},{9,8},{10,9... | collective-permute-start | bytes 983048 | tf_op jit(solution)/shard_map/ppermute | solution.py:57
  59.9 1.1 all-to-all-done.1
  61.0 0.7 copy-done.18
  61.8 2.2 %shard_map.159 = (bf16[32,16,128]{2,1,0:T(8,128)(2,1)S(1)}, f32[8,128]{1,0:T(8,128)S(1)}) custom-call(s32[2]{0:T(128)S(1)} %copy-done.18, f32[768,128]{1,0:T(8,128)} %bitcast.8.refs_1_, bf16[2,2048,256]{2,1,0:T(8,128)(2,1)S(1)} %bitcast.25), custom_call_target="tpu_custom_call" | custom-call | flops 67108864 | bytes 2625544 | tf_op jit(solution)/shard_map/pallas_call | solution.py:85
  64.0 17.6 %all_to_all.25.came = bf16[32,16,128]{2,1,0:T(8,128)(2,1)S(1)} all-to-all(bf16[32,16,128]{2,1,0:T(8,128)(2,1)S(1)} %get-tuple-element.48), channel_id=1, replica_groups=mesh['y'=4,'z'=8,'c'=2,'t'=4] {'y','z'}, dimensions={0} | all-to-all | bytes 262144 | tf_op jit(solution)/shard_map/all_to_all | solution.py:65
  81.9 3.1 %collective-permute-done.5.p1 = f32[640,128]{1,0:T(8,128)} collective-permute-done((f32[640,128]{1,0:T(8,128)}, f32[640,128]{1,0:T(8,128)}, u32[]{:S(2)}, u32[]{:S(2)}) %collective-permute-start.5) | collective-permute-done | bytes 327712 | tf_op jit(solution)/shard_map/ppermute | solution.py:57
  85.0 2.0 %collective-permute-start.8 = (f32[64,256]{1,0:T(8,128)S(1)}, f32[64,256]{1,0:T(8,128)S(1)}, u32[]{:S(2)}, u32[]{:S(2)}) collective-permute-start(f32[64,256]{1,0:T(8,128)S(1)} %shard_map.160.s0), channel_id=1, source_target_pairs={{0,1},{1,2},{2,3},{3,0},{4,5},{5,6},{6,7},{7,4},{8,9},{9,10},{10,1... | collective-permute-start | bytes 196616 | tf_op jit(solution)/shard_map/ppermute | solution.py:57
  87.2 2.1 %shard_map.161 = (bf16[512,128]{1,0:T(8,128)(2,1)S(1)}, f32[192,128]{1,0:T(8,128)S(1)}, f32[32,16,128]{2,1,0:T(8,128)S(1)}, f32[32,16,128]{2,1,0:T(8,128)S(1)}) custom-call(f32[640,128]{1,0:T(8,128)} %get-tuple-element.45.p0, f32[640,128]{1,0:T(8,128)} %collective-permute-done.5.p1, f32[640,128]{1,0:T(8,128)} %collective-permute-done.6.p2, ...), custom_call_target="tpu_custom_call" | custom-call | flops 268435456 | bytes 4194304 | tf_op jit(solution)/shard_map/pallas_call | solution.py:85
  89.4 1.1 collective-permute-done.8.s1
  90.4 2.3 %collective-permute-done.9.s2 = f32[64,256]{1,0:T(8,128)S(1)} collective-permute-done((f32[64,256]{1,0:T(8,128)S(1)}, f32[64,256]{1,0:T(8,128)S(1)}, u32[]{:S(2)}, u32[]{:S(2)}) %collective-permute-start.9) | collective-permute-done | bytes 65568 | tf_op jit(solution)/shard_map/ppermute | solution.py:57
  92.8 1.5 shard_map.162
  94.3 9.9 %all-to-all-start.3 = ((f32[32,24,128]{2,1,0:T(8,128)}), f32[32,24,128]{2,1,0:T(8,128)S(1)}, u32[]{:S(2)}, u32[]{:S(2)}) async-start(f32[32,24,128]{2,1,0:T(8,128)} %bitcast.13), calls=%async_computation.3 | async-start | bytes 786432 | tf_op jit(solution)/shard_map/all_to_all | solution.py:65
  104.2 1.9 %slice.12 = bf16[256,1024]{1,0:T(8,128)(2,1)} slice(bf16[512,1024]{1,0:T(8,128)(2,1)} %collective-permute-done.2.left), slice={[0:256], [0:1024]} | slice | bytes 1048576 | tf_op jit(solution)/shard_map/slice | solution.py:589
  106.4 1.9 %slice.13 = bf16[256,1024]{1,0:T(8,128)(2,1)} slice(bf16[512,1024]{1,0:T(8,128)(2,1)} %collective-permute-done.3.right), slice={[256:512], [0:1024]} | slice | bytes 1048576 | tf_op jit(solution)/shard_map/slice | solution.py:590
  108.3 3.0 %collective-permute-start.12 = (bf16[256,1024]{1,0:T(8,128)(2,1)}, bf16[256,1024]{1,0:T(8,128)(2,1)}, u32[]{:S(2)}, u32[]{:S(2)}) collective-permute-start(bf16[256,1024]{1,0:T(8,128)(2,1)} %slice.13), channel_id=1, source_target_pairs={{0,3},{1,0},{2,1},{3,2},{4,7},{5,4},{6,5},{7,6},{8,11},{9,8},{10,9... | collective-permute-start | bytes 1572872 | tf_op jit(solution)/shard_map/ppermute | solution.py:57
  111.3 1.5 collective-permute-done.14
  112.8 0.7 add.7
  113.6 5.6 %all-to-all-done.3 = f32[32,24,128]{2,1,0:T(8,128)S(1)} async-done(((f32[32,24,128]{2,1,0:T(8,128)}), f32[32,24,128]{2,1,0:T(8,128)S(1)}, u32[]{:S(2)}, u32[]{:S(2)}) %all-to-all-start.3) | async-done | bytes 393248 | tf_op jit(solution)/shard_map/all_to_all | solution.py:65
  119.2 1.9 %shard_map.163 = (f32[24,128]{1,0:T(8,128)S(1)}, f32[64,128]{1,0:T(8,128)S(1)}) custom-call(s32[2]{0:T(128)S(1)} %copy-done.18, f32[768,128]{1,0:T(8,128)S(1)} %bitcast.28, bf16[2,2048,256]{2,1,0:T(8,128)(2,1)S(1)} %bitcast.26, f32[8,128]{1,0:T(8,128)S(1)} %get-tuple-element.63.refs_3_, bf16[1024,128]{1,0:T(8,128)(2,1)S(1)} %bitcast.31), custom_call_target="tpu_custom_call" | custom-call | flops 67108864 | bytes 2801672 | tf_op jit(solution)/shard_map/pallas_call | solution.py:85
  121.1 0.9 collective-permute-start.15
  122.0 2.9 %collective-permute-start.16 = (f32[24,128]{1,0:T(8,128)S(1)}, f32[24,128]{1,0:T(8,128)S(1)}, u32[]{:S(2)}, u32[]{:S(2)}) collective-permute-start(f32[24,128]{1,0:T(8,128)S(1)} %get-tuple-element.67.s0), channel_id=1, source_target_pairs={{0,2},{1,3},{2,0},{3,1},{4,6},{5,7},{6,4},{7,5},{8,10},{9,11},{10,... | collective-permute-start | bytes 36872 | tf_op jit(solution)/shard_map/ppermute | solution.py:57
  125.2 7.0 %all-to-all-start.4 = ((f32[32,16,128]{2,1,0:T(8,128)}), f32[32,16,128]{2,1,0:T(8,128)S(1)}, u32[]{:S(2)}, u32[]{:S(2)}) async-start(f32[32,16,128]{2,1,0:T(8,128)} %add.7), calls=%async_computation.4 | async-start | bytes 524288 | tf_op jit(solution)/shard_map/all_to_all | solution.py:65
  132.9 11.1 %shard_map.164 = (f32[512,1024]{1,0:T(8,128)}, f32[8,1024]{1,0:T(8,128)}) custom-call(s32[4]{0:T(128)} %compare_select_fusion.where_ref, bf16[512,1024]{1,0:T(8,128)(2,1)} %own.1, bf16[512,1024]{1,0:T(8,128)(2,1)} %collective-permute-done.2.left, bf16[512,1024]{1,0:T(8,128)(2,1)} %collective-permute-done.3.right, ...), custom_call_target="tpu_custom_call" | custom-call | flops 8589934592 | bytes 14680064 | tf_op jit(solution)/shard_map/pallas_call | solution.py:431
  144.0 1.8 %collective-permute-start.18 = (f32[8,1024]{1,0:T(8,128)}, f32[8,1024]{1,0:T(8,128)S(1)}, u32[]{:S(2)}, u32[]{:S(2)}) collective-permute-start(f32[8,1024]{1,0:T(8,128)} %get-tuple-element.69.c0), channel_id=1, source_target_pairs={{0,1},{1,2},{2,3},{3,0},{4,5},{5,6},{6,7},{7,4},{8,9},{9,10},{10,1... | collective-permute-start | bytes 98312 | tf_op jit(solution)/shard_map/ppermute | solution.py:57
  146.2 2.4 %collective-permute-start.20 = (f32[8,1024]{1,0:T(8,128)}, f32[8,1024]{1,0:T(8,128)S(1)}, u32[]{:S(2)}, u32[]{:S(2)}) collective-permute-start(f32[8,1024]{1,0:T(8,128)} %get-tuple-element.69.c0), channel_id=1, source_target_pairs={{0,3},{1,0},{2,1},{3,2},{4,7},{5,4},{6,5},{7,6},{8,11},{9,8},{10,9... | collective-permute-start | bytes 98312 | tf_op jit(solution)/shard_map/ppermute | solution.py:57
  148.6 0.8 collective-permute-done.18.c1
  149.4 0.7 slice_bitcast_fusion
  150.1 1.3 collective-permute-done.19.c2
  151.4 0.8 copy-done.17
  (78 shorter events, 4.2 us)
Async XLA Ops:
  7.2 38.1 %copy-start.1 = (bf16[512,1024]{1,0:T(8,128)(2,1)S(1)}, bf16[512,1024]{1,0:T(8,128)(2,1)}, u32[]{:S(2)}) copy-start(bf16[512,1024]{1,0:T(8,128)(2,1)} %own.1) | copy-start | bytes 3145732
  9.5 21.8 %all-to-all-start = ((bf16[32,24,128]{2,1,0:T(8,128)(2,1)}), bf16[32,24,128]{2,1,0:T(8,128)(2,1)S(1)}, u32[]{:S(2)}, u32[]{:S(2)}) async-start(bf16[32,24,128]{2,1,0:T(8,128)(2,1)} %shard_map.156), calls=%async_computation | async-start | bytes 393216 | tf_op jit(solution)/shard_map/all_to_all | solution.py:65
  21.3 111.1 %all-gather.2.cloned.1.call-start = ((), (), s32[]{:S(2)}) async-start(), calls=%async_computation.5 | async-start | bytes 8519680 | tf_op jit(solution)/shard_map/all_gather | solution.py:527
  21.3 5.9 %collective-permute-start.1 = (bf16[64,1024]{1,0:T(8,128)(2,1)}, bf16[64,1024]{1,0:T(8,128)(2,1)S(1)}, u32[]{:S(2)}, u32[]{:S(2)}) collective-permute-start(bf16[64,1024]{1,0:T(8,128)(2,1)} %bitcast.35), channel_id=1, source_target_pairs={{0,4},{4,0},{1,5},{5,1},{2,6},{6,2},{3,7},{7,3},{8,12},{12,8},{9,1... | collective-permute-start | bytes 393224 | tf_op jit(solution)/shard_map/ppermute | solution.py:53
  21.4 12.0 %collective-permute-start.13 = (bf16[64,1024]{1,0:T(8,128)(2,1)}, bf16[64,1024]{1,0:T(8,128)(2,1)}, u32[]{:S(2)}, u32[]{:S(2)}) collective-permute-start(bf16[64,1024]{1,0:T(8,128)(2,1)} %bitcast.36), channel_id=1, source_target_pairs={{0,0},{1,64},{2,128},{3,192},{64,1},{65,65},{66,129},{67,193},{128... | collective-permute-start | bytes 393224 | tf_op jit(solution)/shard_map/ppermute | solution.py:510
  24.5 3.4 %collective-permute-start = (bf16[64,1280]{1,0:T(8,128)(2,1)}, bf16[64,1280]{1,0:T(8,128)(2,1)S(1)}, u32[]{:S(2)}, u32[]{:S(2)}) collective-permute-start(bf16[64,1280]{1,0:T(8,128)(2,1)} %bitcast.32), channel_id=1, source_target_pairs={{0,4},{4,0},{1,5},{5,1},{2,6},{6,2},{3,7},{7,3},{8,12},{12,8},{9,1... | collective-permute-start | bytes 491528 | tf_op jit(solution)/shard_map/ppermute | solution.py:53
  31.4 0.9 copy-start.8
  32.6 0.8 copy-start.2
  33.4 27.6 %copy-start = (bf16[2,2048,1,256]{3,1,2,0:T(8,128)(2,1)S(1)}, bf16[2,2048,1,256]{3,1,2,0:T(8,128)(2,1)}, u32[]{:S(2)}) copy-start(bf16[2,2048,1,256]{3,1,2,0:T(8,128)(2,1)} %param.16) | copy-start | bytes 6291460
  33.4 27.6 %all-to-all-start.1 = ((f32[32,24,128]{2,1,0:T(8,128)}), f32[32,24,128]{2,1,0:T(8,128)}, u32[]{:S(2)}, u32[]{:S(2)}) async-start(f32[32,24,128]{2,1,0:T(8,128)} %bitcast.27), calls=%async_computation.1 | async-start | bytes 786432 | tf_op jit(solution)/shard_map/all_to_all | solution.py:65
  45.3 49.0 %collective-permute-start.2 = (bf16[512,1024]{1,0:T(8,128)(2,1)S(1)}, bf16[512,1024]{1,0:T(8,128)(2,1)}, u32[]{:S(2)}, u32[]{:S(2)}) collective-permute-start(bf16[512,1024]{1,0:T(8,128)(2,1)S(1)} %copy-done.1), channel_id=1, source_target_pairs={{0,1},{1,2},{2,3},{3,0},{4,5},{5,6},{6,7},{7,4},{8,9},{9,10},{10,1... | collective-permute-start | bytes 3145736 | tf_op jit(solution)/shard_map/ppermute | solution.py:57
  45.4 48.9 %collective-permute-start.3 = (bf16[512,1024]{1,0:T(8,128)(2,1)S(1)}, bf16[512,1024]{1,0:T(8,128)(2,1)}, u32[]{:S(2)}, u32[]{:S(2)}) collective-permute-start(bf16[512,1024]{1,0:T(8,128)(2,1)S(1)} %copy-done.1), channel_id=1, source_target_pairs={{0,3},{1,0},{2,1},{3,2},{4,7},{5,4},{6,5},{7,6},{8,11},{9,8},{10,9... | collective-permute-start | bytes 3145736 | tf_op jit(solution)/shard_map/ppermute | solution.py:57
  48.6 1.4 collective-permute-start.4
  50.0 1.2 copy-start.7
  51.3 0.9 copy-start.9
  54.2 1.0 copy-start.3
  55.9 0.7 copy-start.10
  56.6 25.0 %copy-start.6 = (bf16[32,32,128]{2,1,0:T(8,128)(2,1)S(1)}, bf16[32,32,128]{2,1,0:T(8,128)(2,1)}, u32[]{:S(2)}) copy-start(bf16[32,32,128]{2,1,0:T(8,128)(2,1)} %copy-done.5) | copy-start | bytes 786436
  56.6 28.3 %collective-permute-start.5 = (f32[640,128]{1,0:T(8,128)}, f32[640,128]{1,0:T(8,128)}, u32[]{:S(2)}, u32[]{:S(2)}) collective-permute-start(f32[640,128]{1,0:T(8,128)} %get-tuple-element.45.p0), channel_id=1, source_target_pairs={{0,1},{1,2},{2,3},{3,0},{4,5},{5,6},{6,7},{7,4},{8,9},{9,10},{10,1... | collective-permute-start | bytes 983048 | tf_op jit(solution)/shard_map/ppermute | solution.py:57
  56.6 28.3 %collective-permute-start.6 = (f32[640,128]{1,0:T(8,128)}, f32[640,128]{1,0:T(8,128)}, u32[]{:S(2)}, u32[]{:S(2)}) collective-permute-start(f32[640,128]{1,0:T(8,128)} %get-tuple-element.45.p0), channel_id=1, source_target_pairs={{0,2},{1,3},{2,0},{3,1},{4,6},{5,7},{6,4},{7,5},{8,10},{9,11},{10,... | collective-permute-start | bytes 983048 | tf_op jit(solution)/shard_map/ppermute | solution.py:57
  58.1 28.9 %collective-permute-start.7 = (f32[640,128]{1,0:T(8,128)}, f32[640,128]{1,0:T(8,128)}, u32[]{:S(2)}, u32[]{:S(2)}) collective-permute-start(f32[640,128]{1,0:T(8,128)} %get-tuple-element.45.p0), channel_id=1, source_target_pairs={{0,3},{1,0},{2,1},{3,2},{4,7},{5,4},{6,5},{7,6},{8,11},{9,8},{10,9... | collective-permute-start | bytes 983048 | tf_op jit(solution)/shard_map/ppermute | solution.py:57
  61.0 20.6 %copy-start.14 = (bf16[1,1024,64]{1,2,0:T(8,128)(2,1)S(1)}, bf16[1,1024,64]{1,2,0:T(8,128)(2,1)}, u32[]{:S(2)}) copy-start(bf16[1,1024,64]{1,2,0:T(8,128)(2,1)} %param.18) | copy-start | bytes 393220
  61.0 20.6 %copy-start.16 = (bf16[64,1024]{1,0:T(8,128)(2,1)S(1)}, bf16[64,1024]{1,0:T(8,128)(2,1)}, u32[]{:S(2)}) copy-start(bf16[64,1024]{1,0:T(8,128)(2,1)} %copy-done.15) | copy-start | bytes 393220
  61.0 26.2 %copy-start.4 = (bf16[512,1024]{1,0:T(8,128)(2,1)S(1)}, bf16[512,1024]{1,0:T(8,128)(2,1)}, u32[]{:S(2)}) copy-start(bf16[512,1024]{1,0:T(8,128)(2,1)} %copy-done.3) | copy-start | bytes 3145732
  61.0 0.8 copy-start.18
  81.6 11.2 %copy-start.11 = (bf16[128,1280]{1,0:T(8,128)(2,1)S(1)}, bf16[128,1280]{1,0:T(8,128)(2,1)}, u32[]{:S(2)}) copy-start(bf16[128,1280]{1,0:T(8,128)(2,1)} %copy-done.10) | copy-start | bytes 983044
  85.0 4.4 %collective-permute-start.10 = (f32[64,256]{1,0:T(8,128)S(1)}, f32[64,256]{1,0:T(8,128)S(1)}, u32[]{:S(2)}, u32[]{:S(2)}) collective-permute-start(f32[64,256]{1,0:T(8,128)S(1)} %shard_map.160.s0), channel_id=1, source_target_pairs={{0,3},{1,0},{2,1},{3,2},{4,7},{5,4},{6,5},{7,6},{8,11},{9,8},{10,9... | collective-permute-start | bytes 196616 | tf_op jit(solution)/shard_map/ppermute | solution.py:57
  85.0 5.5 %collective-permute-start.8 = (f32[64,256]{1,0:T(8,128)S(1)}, f32[64,256]{1,0:T(8,128)S(1)}, u32[]{:S(2)}, u32[]{:S(2)}) collective-permute-start(f32[64,256]{1,0:T(8,128)S(1)} %shard_map.160.s0), channel_id=1, source_target_pairs={{0,1},{1,2},{2,3},{3,0},{4,5},{5,6},{6,7},{7,4},{8,9},{9,10},{10,1... | collective-permute-start | bytes 196616 | tf_op jit(solution)/shard_map/ppermute | solution.py:57
  87.0 5.8 %collective-permute-start.9 = (f32[64,256]{1,0:T(8,128)S(1)}, f32[64,256]{1,0:T(8,128)S(1)}, u32[]{:S(2)}, u32[]{:S(2)}) collective-permute-start(f32[64,256]{1,0:T(8,128)S(1)} %shard_map.160.s0), channel_id=1, source_target_pairs={{0,2},{1,3},{2,0},{3,1},{4,6},{5,7},{6,4},{7,5},{8,10},{9,11},{10,... | collective-permute-start | bytes 196616 | tf_op jit(solution)/shard_map/ppermute | solution.py:57
  89.3 4.9 %copy-start.12 = (f32[32,16,128]{2,1,0:T(8,128)}, f32[32,16,128]{2,1,0:T(8,128)S(1)}, u32[]{:S(2)}) copy-start(f32[32,16,128]{2,1,0:T(8,128)S(1)} %get-tuple-element.65) | copy-start | bytes 786436
  89.3 4.9 %copy-start.19 = (f32[32,16,128]{2,1,0:T(8,128)}, f32[32,16,128]{2,1,0:T(8,128)S(1)}, u32[]{:S(2)}) copy-start(f32[32,16,128]{2,1,0:T(8,128)S(1)} %get-tuple-element.66) | copy-start | bytes 786436
  89.4 4.9 %copy-start.21 = (bf16[512,128]{1,0:T(8,128)(2,1)}, bf16[512,128]{1,0:T(8,128)(2,1)S(1)}, u32[]{:S(2)}) copy-start(bf16[512,128]{1,0:T(8,128)(2,1)S(1)} %get-tuple-element.61.low) | copy-start | bytes 393220
  94.3 18.5 %copy-start.13 = (f32[32,16,128]{2,1,0:T(8,128)S(1)}, f32[32,16,128]{2,1,0:T(8,128)}, u32[]{:S(2)}) copy-start(f32[32,16,128]{2,1,0:T(8,128)} %copy-done.12) | copy-start | bytes 786436
  94.3 17.0 %copy-start.20 = (f32[32,16,128]{2,1,0:T(8,128)S(1)}, f32[32,16,128]{2,1,0:T(8,128)}, u32[]{:S(2)}) copy-start(f32[32,16,128]{2,1,0:T(8,128)} %copy-done.19) | copy-start | bytes 786436
  94.3 24.9 %all-to-all-start.3 = ((f32[32,24,128]{2,1,0:T(8,128)}), f32[32,24,128]{2,1,0:T(8,128)S(1)}, u32[]{:S(2)}, u32[]{:S(2)}) async-start(f32[32,24,128]{2,1,0:T(8,128)} %bitcast.13), calls=%async_computation.3 | async-start | bytes 786432 | tf_op jit(solution)/shard_map/all_to_all | solution.py:65
  106.1 26.1 %collective-permute-start.11 = (bf16[256,1024]{1,0:T(8,128)(2,1)}, bf16[256,1024]{1,0:T(8,128)(2,1)}, u32[]{:S(2)}, u32[]{:S(2)}) collective-permute-start(bf16[256,1024]{1,0:T(8,128)(2,1)} %slice.12), channel_id=1, source_target_pairs={{0,1},{1,2},{2,3},{3,0},{4,5},{5,6},{6,7},{7,4},{8,9},{9,10},{10,1... | collective-permute-start | bytes 1572872 | tf_op jit(solution)/shard_map/ppermute | solution.py:57
  108.3 23.9 %collective-permute-start.12 = (bf16[256,1024]{1,0:T(8,128)(2,1)}, bf16[256,1024]{1,0:T(8,128)(2,1)}, u32[]{:S(2)}, u32[]{:S(2)}) collective-permute-start(bf16[256,1024]{1,0:T(8,128)(2,1)} %slice.13), channel_id=1, source_target_pairs={{0,3},{1,0},{2,1},{3,2},{4,7},{5,4},{6,5},{7,6},{8,11},{9,8},{10,9... | collective-permute-start | bytes 1572872 | tf_op jit(solution)/shard_map/ppermute | solution.py:57
  111.3 1.5 collective-permute-start.14
  121.1 11.2 %copy-start.22 = (f32[64,128]{1,0:T(8,128)}, f32[64,128]{1,0:T(8,128)S(1)}, u32[]{:S(2)}) copy-start(f32[64,128]{1,0:T(8,128)S(1)} %get-tuple-element.68.owned) | copy-start | bytes 98308
  121.1 11.3 %copy-start.23 = (f32[24,128]{1,0:T(8,128)}, f32[24,128]{1,0:T(8,128)S(1)}, u32[]{:S(2)}) copy-start(f32[24,128]{1,0:T(8,128)S(1)} %get-tuple-element.67.s0) | copy-start | bytes 36868
  121.1 11.2 %collective-permute-start.15 = (f32[24,128]{1,0:T(8,128)S(1)}, f32[24,128]{1,0:T(8,128)S(1)}, u32[]{:S(2)}, u32[]{:S(2)}) collective-permute-start(f32[24,128]{1,0:T(8,128)S(1)} %get-tuple-element.67.s0), channel_id=1, source_target_pairs={{0,1},{1,2},{2,3},{3,0},{4,5},{5,6},{6,7},{7,4},{8,9},{9,10},{10,1... | collective-permute-start | bytes 36872 | tf_op jit(solution)/shard_map/ppermute | solution.py:57
  122.0 10.3 %collective-permute-start.16 = (f32[24,128]{1,0:T(8,128)S(1)}, f32[24,128]{1,0:T(8,128)S(1)}, u32[]{:S(2)}, u32[]{:S(2)}) collective-permute-start(f32[24,128]{1,0:T(8,128)S(1)} %get-tuple-element.67.s0), channel_id=1, source_target_pairs={{0,2},{1,3},{2,0},{3,1},{4,6},{5,7},{6,4},{7,5},{8,10},{9,11},{10,... | collective-permute-start | bytes 36872 | tf_op jit(solution)/shard_map/ppermute | solution.py:57
  124.9 7.4 %collective-permute-start.17 = (f32[24,128]{1,0:T(8,128)S(1)}, f32[24,128]{1,0:T(8,128)S(1)}, u32[]{:S(2)}, u32[]{:S(2)}) collective-permute-start(f32[24,128]{1,0:T(8,128)S(1)} %get-tuple-element.67.s0), channel_id=1, source_target_pairs={{0,3},{1,0},{2,1},{3,2},{4,7},{5,4},{6,5},{7,6},{8,11},{9,8},{10,9... | collective-permute-start | bytes 36872 | tf_op jit(solution)/shard_map/ppermute | solution.py:57
  125.2 23.4 %all-to-all-start.4 = ((f32[32,16,128]{2,1,0:T(8,128)}), f32[32,16,128]{2,1,0:T(8,128)S(1)}, u32[]{:S(2)}, u32[]{:S(2)}) async-start(f32[32,16,128]{2,1,0:T(8,128)} %add.7), calls=%async_computation.4 | async-start | bytes 524288 | tf_op jit(solution)/shard_map/all_to_all | solution.py:65
  144.0 5.4 %collective-permute-start.18 = (f32[8,1024]{1,0:T(8,128)}, f32[8,1024]{1,0:T(8,128)S(1)}, u32[]{:S(2)}, u32[]{:S(2)}) collective-permute-start(f32[8,1024]{1,0:T(8,128)} %get-tuple-element.69.c0), channel_id=1, source_target_pairs={{0,1},{1,2},{2,3},{3,0},{4,5},{5,6},{6,7},{7,4},{8,9},{9,10},{10,1... | collective-permute-start | bytes 98312 | tf_op jit(solution)/shard_map/ppermute | solution.py:57
  145.7 5.6 %collective-permute-start.19 = (f32[8,1024]{1,0:T(8,128)}, f32[8,1024]{1,0:T(8,128)S(1)}, u32[]{:S(2)}, u32[]{:S(2)}) collective-permute-start(f32[8,1024]{1,0:T(8,128)} %get-tuple-element.69.c0), channel_id=1, source_target_pairs={{0,2},{1,3},{2,0},{3,1},{4,6},{5,7},{6,4},{7,5},{8,10},{9,11},{10,... | collective-permute-start | bytes 98312 | tf_op jit(solution)/shard_map/ppermute | solution.py:57
  146.2 5.2 %collective-permute-start.20 = (f32[8,1024]{1,0:T(8,128)}, f32[8,1024]{1,0:T(8,128)S(1)}, u32[]{:S(2)}, u32[]{:S(2)}) collective-permute-start(f32[8,1024]{1,0:T(8,128)} %get-tuple-element.69.c0), channel_id=1, source_target_pairs={{0,3},{1,0},{2,1},{3,2},{4,7},{5,4},{6,5},{7,6},{8,11},{9,8},{10,9... | collective-permute-start | bytes 98312 | tf_op jit(solution)/shard_map/ppermute | solution.py:57
  151.4 0.8 copy-start.17
  (5 other events, 3.2 us)
Sparse Core Ops, SparseCore 0:
  33.5 89.3 all-gather.1
